TPU v7x, 256 devices: a whole 4x4x8 slice. The times are simulated.
256 devices in a mesh: seq: 32 (over x, z), head: 8 (over y, core).
Axes of the slice: x: 4, y: 4, z: 8, core: 2. Of those that a mesh axis runs over, the one named last changes fastest.
Arguments:
- queries: bfloat16 [49152, 4096], P(('seq', 'head')), may hold values from -32 to 32
- cache_keys: bfloat16 [262144, 1024], P('seq', 'head'), may hold values from -12 to 12
- cache_values: bfloat16 [262144, 1024], P('seq', 'head'), may hold values from -6 to 6
- block_ids: int32 [384, 8], P('seq'), may hold values from 0 to 2047, as said below
Outputs:
- attention: bfloat16 [49152, 4096], P(('seq', 'head'))
Inputs may be any that keep to these rules, and one draw needn't show every extreme that they name: `block_ids`: entries 0 to 4 of row r name distinct blocks c with c // 64 == r // 12; the other 3 entries name blocks with another value of c // 64, distinct within the row. Among the far entries of the 12 rows with one value of r // 12, at most 2 name blocks of any one other value of c // 64, and exactly 2 do for some value.
All inputs are finite; a program needn't handle non-finite values.
Results may differ from a plain program's by a relative error of at most 0.0043.
Values may be sent and summed in bfloat16 or wider, within the bound.
No kernel may reach another device: no remote copies, remote signals or barrier semaphores. Data moves between devices by JAX's collectives and lax.ppermute only.
A program may use at most 128 MiB of HBM per device.

v0:
```python
import math

import jax
import jax.numpy as jnp
from jax import lax
from jax.sharding import PartitionSpec as P

HD = 128
BLK = 128
NEAR = 5


def block_partials(query_rows, key_rows, value_rows):
    score_scale = query_rows.shape[-1] ** (-0.5)
    scores = (
        jnp.einsum("aqgrd,apkgd->apgrqk", query_rows, key_rows, preferred_element_type=jnp.float32)
        * score_scale
    )
    block_max = jnp.max(scores, axis=-1)
    exponent = jnp.exp(scores - block_max[..., None])
    block_sum = jnp.sum(exponent, axis=-1)
    partial_value = jnp.einsum(
        "apgrqk,apkgd->apqgrd",
        exponent.astype(jnp.bfloat16),
        value_rows,
        preferred_element_type=jnp.float32,
    )
    return (partial_value, block_max, block_sum)


def merge_picks(partial_value, block_max, block_sum):
    highest = jnp.max(block_max, axis=-4, keepdims=True)
    factor = jnp.exp(block_max - highest)
    denominator = jnp.sum(factor * block_sum, axis=-4)
    numerator = jnp.sum(partial_value * jnp.moveaxis(factor, -1, -3)[..., None], axis=-5)
    return numerator / jnp.moveaxis(denominator, -1, -3)[..., None]


def slot_places(owner_of, seq_count, capacity):
    owner_hits = (owner_of[:, None] == jnp.arange(seq_count, dtype=jnp.int32)[None, :]).astype(
        jnp.int32
    )
    before = jnp.cumsum(owner_hits, axis=0) - owner_hits
    owner_rank = jnp.sum(before * owner_hits, axis=1)
    return owner_of * capacity + owner_rank


def grouped(array, per_step):
    return array.reshape((array.shape[0] // per_step, per_step) + array.shape[1:])


def shards(queries, cache_keys, cache_values, block_ids):
    seq_count = lax.axis_size("seq")
    seq_place = lax.axis_index("seq")
    by_heads = lax.all_to_all(queries, "head", split_axis=1, concat_axis=0, tiled=True)
    kv_local = cache_keys.shape[1] // HD
    q_width = by_heads.shape[1]
    ratio = q_width // (kv_local * HD)
    q_count = by_heads.shape[0] // BLK
    k_count = cache_keys.shape[0] // BLK
    far_count = block_ids.shape[1] - NEAR
    capacity = max(2, (far_count * q_count + seq_count - 2) // (seq_count - 1))
    slot_total = seq_count * capacity
    per_step = math.gcd(q_count, 4)
    q_blocks = by_heads.reshape(q_count, BLK, kv_local, ratio, HD)
    k_blocks = cache_keys.reshape(k_count, BLK, kv_local, HD)
    v_blocks = cache_values.reshape(k_count, BLK, kv_local, HD)
    near_ids = (block_ids[:, :NEAR] - seq_place * k_count).reshape(-1)
    far_ids = block_ids[:, NEAR:].reshape(-1)
    far_owner = far_ids // k_count
    far_within = far_ids - far_owner * k_count
    far_slot = slot_places(far_owner, seq_count, capacity)
    slot_range = jnp.arange(slot_total, dtype=jnp.int32)
    placed = (far_slot[:, None] == slot_range[None, :]).astype(jnp.int32)
    asked = jnp.sum(placed * far_within[:, None], axis=0).reshape(seq_count, capacity)
    wanted = lax.all_to_all(asked, "seq", split_axis=0, concat_axis=0, tiled=True)
    wanted_flat = wanted.reshape(-1)
    near_k = jnp.take(k_blocks, near_ids, axis=0).reshape(q_count, NEAR, BLK, kv_local, HD)
    near_v = jnp.take(v_blocks, near_ids, axis=0).reshape(q_count, NEAR, BLK, kv_local, HD)
    sent_k = jnp.take(k_blocks, wanted_flat, axis=0).reshape(
        seq_count, capacity, BLK, kv_local * HD
    )
    sent_v = jnp.take(v_blocks, wanted_flat, axis=0).reshape(
        seq_count, capacity, BLK, kv_local * HD
    )
    got_k, got_v = (
        lax.all_to_all(sent_k, "seq", split_axis=0, concat_axis=0, tiled=True),
        lax.all_to_all(sent_v, "seq", split_axis=0, concat_axis=0, tiled=True),
    )
    far_k = jnp.take(got_k.reshape(slot_total, BLK, kv_local, HD), far_slot, axis=0).reshape(
        q_count, far_count, BLK, kv_local, HD
    )
    far_v = jnp.take(got_v.reshape(slot_total, BLK, kv_local, HD), far_slot, axis=0).reshape(
        q_count, far_count, BLK, kv_local, HD
    )
    all_k = jnp.concatenate([near_k, far_k], axis=1)
    all_v = jnp.concatenate([near_v, far_v], axis=1)

    def attend(pieces):
        return merge_picks(*block_partials(*pieces)).astype(jnp.bfloat16)

    result = lax.map(
        attend, (grouped(q_blocks, per_step), grouped(all_k, per_step), grouped(all_v, per_step))
    )
    result = result.reshape(q_count * BLK, q_width)
    return lax.all_to_all(result, "head", split_axis=0, concat_axis=1, tiled=True)


def solution(mesh):
    return jax.shard_map(
        shards,
        mesh=mesh,
        in_specs=(P(("seq", "head"), None), P("seq", "head"), P("seq", "head"), P("seq", None)),
        out_specs=P(("seq", "head"), None),
        check_vma=False,
    )
```

profile of v0, /device:TPU:1, one launch (start us, length us, event | category | flops | bytes accessed | tf_op | source)
XLA Modules:
  0.0 239.3 jit_solution(10428355501875917105)
XLA Ops:
  0.0 0.0 copy-start
  0.0 0.8 slice.7
  0.8 0.1 copy.38
  0.9 0.1 reshape.220
  1.0 0.1 fusion.22
  1.1 0.1 reduce_window_sum.11
  1.2 0.2 select_reduce_fusion.1
  1.4 0.1 select_reduce_fusion
  1.5 0.7 all_to_all.38
  2.2 11.9 %all-to-all-start = ((s32[32,1,2]{2,1,0:T(1,128)}), s32[32,1,2]{2,1,0:T(1,128)S(1)}, u32[]{:S(2)}, u32[]{:S(2)}) async-start(s32[32,1,2]{2,1,0:T(1,128)} %bitcast.26), calls=%async_computation | async-start | bytes 32768 | tf_op jit(solution)/shard_map/all_to_all | solution.py:76
  14.1 2.7 %copy.60 = bf16[24,8,8,512]{3,2,0,1:T(8,128)(2,1)} copy(bf16[24,8,8,512]{3,2,1,0:T(8,128)(2,1)} %bitcast.152) | data formatting | bytes 3145728 | tf_op jit(solution)/shard_map/all_to_all | solution.py:55
  16.8 5.9 %all-to-all-done = s32[32,1,2]{2,1,0:T(1,128)S(1)} async-done(((s32[32,1,2]{2,1,0:T(1,128)}), s32[32,1,2]{2,1,0:T(1,128)S(1)}, u32[]{:S(2)}, u32[]{:S(2)}) %all-to-all-start) | async-done | bytes 288 | tf_op jit(solution)/shard_map/all_to_all | solution.py:76
  22.7 6.6 %all-to-all-start.3 = ((bf16[192,8,512]{2,0,1:T(8,128)(2,1)}), bf16[192,8,512]{2,0,1:T(8,128)(2,1)}, u32[]{:S(2)}, u32[]{:S(2)}) async-start(bf16[192,8,512]{2,0,1:T(8,128)(2,1)} %bitcast.147), calls=%async_computation.3 | async-start | bytes 3145728 | tf_op jit(solution)/shard_map/all_to_all | solution.py:55
  29.3 0.6 broadcast.214
  29.8 0.7 reduce.10
  30.6 0.1 reshape.221
  30.7 3.8 %gather_fusion.4 = bf16[64,128,128]{2,1,0:T(8,128)(2,1)} fusion(bf16[64,128,128]{2,1,0:T(8,128)(2,1)} %bitcast.143, s32[1024]{0:T(1024)S(1)} %pad_clamp_fusion.1), kind=kCustom, calls=%fused_computation.4.clone | custom fusion | bytes 4194560 | tf_op jit(solution)/shard_map/jit(_take)/gather | solution.py:80
  34.5 2.1 gather_fusion.1
  36.6 4.6 %bitcast_select_fusion = (bf16[64,128,1,128]{3,1,0,2:T(8,128)(2,1)}, bf16[64,128,1,128]{3,1,0,2:T(8,128)(2,1)}) fusion(bf16[64,128,128]{2,1,0:T(8,128)(2,1)} %gather_fusion.4, pred[64]{0:T(512)(128)(4,1)S(1)} %compare_and_fusion.1, bf16[64,128,128]{2,1,0:T(8,128)(2,1)} %gather_fusion.1), kind=kLoop, calls=%fused_computation.37 | loop fusion | flops 2097152 | bytes 8388672 | tf_op jit(solution)/shard_map/jit(_take)/select_n | solution.py:80
  41.2 8.8 %all-to-all-done.3 = bf16[192,8,512]{2,0,1:T(8,128)(2,1)} async-done(((bf16[192,8,512]{2,0,1:T(8,128)(2,1)}), bf16[192,8,512]{2,0,1:T(8,128)(2,1)}, u32[]{:S(2)}, u32[]{:S(2)}) %all-to-all-start.3) | async-done | bytes 1572896 | tf_op jit(solution)/shard_map/all_to_all | solution.py:55
  50.1 51.9 %all_to_all.54 = bf16[32,2,128,128]{3,2,1,0:T(8,128)(2,1)} all-to-all(bf16[32,2,128,128]{3,2,1,0:T(8,128)(2,1)} %bitcast.142), channel_id=1, replica_groups=mesh['seq'=32,'head'=8] {'seq'}, dimensions={0} | all-to-all | bytes 4194304 | tf_op jit(solution)/shard_map/all_to_all | solution.py:87
  102.0 8.8 %all-to-all-start.1 = ((bf16[32,2,128,128]{3,2,1,0:T(8,128)(2,1)}), bf16[32,2,128,128]{3,2,1,0:T(8,128)(2,1)}, u32[]{:S(2)}, u32[]{:S(2)}) async-start(bf16[32,2,128,128]{3,2,1,0:T(8,128)(2,1)} %bitcast.141), calls=%async_computation.1 | async-start | bytes 4194304 | tf_op jit(solution)/shard_map/all_to_all | solution.py:88
  110.7 0.0 copy-done.3
  110.8 0.1 copy.37
  110.9 0.1 reshape.219
  111.0 2.2 gather_fusion
  113.1 3.7 %gather_fusion.3 = bf16[60,128,128]{2,1,0:T(8,128)(2,1)} fusion(bf16[64,128,128]{2,1,0:T(8,128)(2,1)} %bitcast.144, s32[1024]{0:T(1024)S(1)} %pad_clamp_fusion.2), kind=kCustom, calls=%fused_computation.3.clone | custom fusion | bytes 3932400 | tf_op jit(solution)/shard_map/jit(_take)/gather | solution.py:78
  116.8 4.5 %bitcast_select_fusion.2 = (bf16[60,128,1,128]{3,1,0,2:T(8,128)(2,1)}, bf16[60,128,1,128]{3,1,0,2:T(8,128)(2,1)}) fusion(bf16[60,128,128]{2,1,0:T(8,128)(2,1)} %gather_fusion.3, pred[60]{0:T(512)(128)(4,1)S(1)} %compare_and_fusion.2, bf16[60,128,128]{2,1,0:T(8,128)(2,1)} %gather_fusion), kind=kLoop, calls=%fused_computation.39 | loop fusion | flops 1966080 | bytes 7864380 | tf_op jit(solution)/shard_map/jit(_take)/select_n | solution.py:78
  121.3 4.0 %copy.40 = bf16[3,4,5,128,1,128]{3,5,2,1,4,0:T(8,128)(2,1)} copy(bf16[3,4,5,128,1,128]{5,3,2,1,0,4:T(8,128)(2,1)} %bitcast.146) | data formatting | bytes 3932160 | tf_op jit(solution)/shard_map/concatenate | solution.py:97
  125.3 3.5 %reshape_reshape.3 = bf16[3,4,128,1,4,128]{5,4,2,1,0,3:T(4,128)(2,1)} reshape(bf16[8,192,512]{2,1,0:T(8,128)(2,1)} %bitcast.45) | data formatting | bytes 3145728 | tf_op jit(solution)/shard_map/reshape;reshape | solution.py:49
  128.8 2.4 gather_fusion.5
  131.2 28.3 %all-to-all-done.1 = bf16[32,2,128,128]{3,2,1,0:T(8,128)(2,1)} async-done(((bf16[32,2,128,128]{3,2,1,0:T(8,128)(2,1)}), bf16[32,2,128,128]{3,2,1,0:T(8,128)(2,1)}, u32[]{:S(2)}, u32[]{:S(2)}) %all-to-all-start.1) | async-done | bytes 2097184 | tf_op jit(solution)/shard_map/all_to_all | solution.py:88
  159.4 3.4 %gather_fusion.2 = bf16[36,128,128]{2,1,0:T(8,128)(2,1)} fusion(bf16[64,128,128]{2,1,0:T(8,128)(2,1)} %bitcast.31, s32[1024]{0:T(1024)S(1)} %pad_clamp_fusion), kind=kCustom, calls=%fused_computation.2.clone | custom fusion | bytes 2359440 | tf_op jit(solution)/shard_map/jit(_take)/gather | solution.py:93
  162.8 3.0 %bitcast_select_fusion.4 = (bf16[36,128,1,128]{3,1,0,2:T(8,128)(2,1)}, bf16[36,128,1,128]{3,1,0,2:T(8,128)(2,1)}) fusion(bf16[36,128,128]{2,1,0:T(8,128)(2,1)S(1)} %gather_fusion.5, pred[36]{0:T(512)(128)(4,1)S(1)} %get-tuple-element.68, bf16[36,128,128]{2,1,0:T(8,128)(2,1)} %gather_fusion.2), kind=kLoop, calls=%fused_computation.42 | loop fusion | flops 1179648 | bytes 4718628 | tf_op jit(solution)/shard_map/jit(_take)/select_n | solution.py:90
  165.8 1.7 copy.41
  167.5 0.0 copy-start.1
  167.5 0.0 copy-start.2
  167.5 3.6 %pad_maximum_fusion = bf16[3,4,8,128,1,128]{3,5,2,1,4,0:T(8,128)(2,1)} fusion(bf16[3,4,3,128,1,128]{3,5,2,1,4,0:T(8,128)(2,1)S(1)} %copy.41, bf16[3,4,5,128,1,128]{3,5,2,1,4,0:T(8,128)(2,1)} %copy.40), kind=kLoop, calls=%fused_computation.35 | loop fusion | flops 1572864 | bytes 6291456 | tf_op jit(solution)/shard_map/concatenate | solution.py:97
  171.2 2.0 pad_maximum_fusion.1
  173.2 34.5 %while.10 = (s32[]{:T(128)}, bf16[3,4,128,1,4,128]{5,4,2,1,0,3:T(4,128)(2,1)}, bf16[3,4,8,128,1,128]{3,5,2,1,4,0:T(8,128)(2,1)}, bf16[3,4,8,128,1,128]{5,3,2,1,4...) while((s32[]{:T(128)}, bf16[3,4,128,1,4,128]{5,4,2,1,0,3:T(4,128)(2,1)}, ...), condition=%wide.region_9.13_spmd, body=%wide.region_3.12_spmd.sunk | while | flops 1097101312 | bytes 34186824 | solution.py:102
  173.2 1.2 constant_dynamic-slice_fusion.2
  174.4 2.5 %bitcast_reduce_fusion.3 = (f32[4,8,4,128]{3,2,1,0:T(4,128)S(1)}, f32[4,8,128,128,4]{3,2,4,1,0:T(8,128)S(1)}) fusion(bf16[1,4,128,1,4,128]{5,4,2,1,0,3:T(4,128)(2,1)S(1)} %constant_dynamic-slice_fusion.2, bf16[3,4,8,128,1,128]{5,3,2,1,4,0:T(8,128)(2,1)} %get-tuple-element.134, s32[]{:T(128)} %get-tuple-element.125), kind=kOutput, calls=%fused_computation.10.clone.1 | convolution fusion | flops 541048832 | bytes 10027520 | tf_op jit(solution)/shard_map/while/body/eval_jaxpr/aqgrd,apkgd->apgrqk/dot_general | solution.py:16
  176.9 2.3 fusion.31
  179.3 3.9 %fusion.33 = f32[4,128,4,128]{1,3,2,0:T(8,128)S(1)} fusion(f32[4,8,128,4]{2,3,1,0:T(4,128)S(1)} %fusion.32, f32[4,8,128,128,4]{3,2,4,1,0:T(8,128)S(1)} %get-tuple-element.116, f32[4,8,4,128]{3,2,1,0:T(4,128)S(1)} %get-tuple-element.115, bf16[3,4,8,128,1,128]{3,5,2,1,4,0:T(8,128)(2,1)} %get-tuple-element.133, s32[]{:T(128)} %get-tuple-element.125), kind=kOutput, calls=%fused_computation.7.clone.1 | convolution fusion | flops 547094528 | bytes 10617344 | tf_op jit(solution)/shard_map/while/body/eval_jaxpr/apgrqk,apkgd->apqgrd/dot_general | solution.py:22
  183.2 0.1 fusion.34
  183.3 0.3 copy.64
  183.7 1.0 constant_dynamic-update-slice_fusion.2
  184.6 1.2 constant_dynamic-slice_fusion.2
  185.9 2.5 %bitcast_reduce_fusion.3 = (f32[4,8,4,128]{3,2,1,0:T(4,128)S(1)}, f32[4,8,128,128,4]{3,2,4,1,0:T(8,128)S(1)}) fusion(bf16[1,4,128,1,4,128]{5,4,2,1,0,3:T(4,128)(2,1)S(1)} %constant_dynamic-slice_fusion.2, bf16[3,4,8,128,1,128]{5,3,2,1,4,0:T(8,128)(2,1)} %get-tuple-element.134, s32[]{:T(128)} %get-tuple-element.125), kind=kOutput, calls=%fused_computation.10.clone.1 | convolution fusion | flops 541048832 | bytes 10027520 | tf_op jit(solution)/shard_map/while/body/eval_jaxpr/aqgrd,apkgd->apgrqk/dot_general | solution.py:16
  188.4 2.3 fusion.31
  190.8 3.9 %fusion.33 = f32[4,128,4,128]{1,3,2,0:T(8,128)S(1)} fusion(f32[4,8,128,4]{2,3,1,0:T(4,128)S(1)} %fusion.32, f32[4,8,128,128,4]{3,2,4,1,0:T(8,128)S(1)} %get-tuple-element.116, f32[4,8,4,128]{3,2,1,0:T(4,128)S(1)} %get-tuple-element.115, bf16[3,4,8,128,1,128]{3,5,2,1,4,0:T(8,128)(2,1)} %get-tuple-element.133, s32[]{:T(128)} %get-tuple-element.125), kind=kOutput, calls=%fused_computation.7.clone.1 | convolution fusion | flops 547094528 | bytes 10617344 | tf_op jit(solution)/shard_map/while/body/eval_jaxpr/apgrqk,apkgd->apqgrd/dot_general | solution.py:22
  194.7 0.1 fusion.34
  194.8 0.3 copy.64
  195.2 1.0 constant_dynamic-update-slice_fusion.2
  196.1 1.2 constant_dynamic-slice_fusion.2
  197.4 2.5 %bitcast_reduce_fusion.3 = (f32[4,8,4,128]{3,2,1,0:T(4,128)S(1)}, f32[4,8,128,128,4]{3,2,4,1,0:T(8,128)S(1)}) fusion(bf16[1,4,128,1,4,128]{5,4,2,1,0,3:T(4,128)(2,1)S(1)} %constant_dynamic-slice_fusion.2, bf16[3,4,8,128,1,128]{5,3,2,1,4,0:T(8,128)(2,1)} %get-tuple-element.134, s32[]{:T(128)} %get-tuple-element.125), kind=kOutput, calls=%fused_computation.10.clone.1 | convolution fusion | flops 541048832 | bytes 10027520 | tf_op jit(solution)/shard_map/while/body/eval_jaxpr/aqgrd,apkgd->apgrqk/dot_general | solution.py:16
  199.9 2.3 fusion.31
  202.3 3.9 %fusion.33 = f32[4,128,4,128]{1,3,2,0:T(8,128)S(1)} fusion(f32[4,8,128,4]{2,3,1,0:T(4,128)S(1)} %fusion.32, f32[4,8,128,128,4]{3,2,4,1,0:T(8,128)S(1)} %get-tuple-element.116, f32[4,8,4,128]{3,2,1,0:T(4,128)S(1)} %get-tuple-element.115, bf16[3,4,8,128,1,128]{3,5,2,1,4,0:T(8,128)(2,1)} %get-tuple-element.133, s32[]{:T(128)} %get-tuple-element.125), kind=kOutput, calls=%fused_computation.7.clone.1 | convolution fusion | flops 547094528 | bytes 10617344 | tf_op jit(solution)/shard_map/while/body/eval_jaxpr/apgrqk,apkgd->apqgrd/dot_general | solution.py:22
  206.2 0.1 fusion.34
  206.3 0.3 copy.64
  206.6 1.0 constant_dynamic-update-slice_fusion.2
  207.6 3.7 %all_to_all.45 = bf16[8,192,512]{2,1,0:T(8,128)(2,1)} reshape(bf16[3,4,128,1,4,128]{5,4,2,1,0,3:T(4,128)(2,1)} %get-tuple-element.35) | data formatting | bytes 3145728 | tf_op jit(solution)/shard_map/all_to_all | solution.py:106
  211.3 26.7 %all_to_all.55 = bf16[8,192,512]{2,1,0:T(8,128)(2,1)S(1)} all-to-all(bf16[8,192,512]{2,1,0:T(8,128)(2,1)} %all_to_all.45), channel_id=1, replica_groups=mesh['seq'=32,'head'=8] {'head'}, dimensions={0} | all-to-all | bytes 3145728 | tf_op jit(solution)/shard_map/all_to_all | solution.py:106
  238.0 1.3 copy.54
  (22 shorter events, 0.3 us)
Async XLA Ops:
  0.0 34.5 %copy-start = (bf16[8192,128]{1,0:T(8,128)(2,1)S(1)}, bf16[8192,128]{1,0:T(8,128)(2,1)}, u32[]{:S(2)}) copy-start(bf16[8192,128]{1,0:T(8,128)(2,1)} %param.14) | copy-start | bytes 6291460
  2.2 20.5 %all-to-all-start = ((s32[32,1,2]{2,1,0:T(1,128)}), s32[32,1,2]{2,1,0:T(1,128)S(1)}, u32[]{:S(2)}, u32[]{:S(2)}) async-start(s32[32,1,2]{2,1,0:T(1,128)} %bitcast.26), calls=%async_computation | async-start | bytes 32768 | tf_op jit(solution)/shard_map/all_to_all | solution.py:76
  22.7 27.4 %all-to-all-start.3 = ((bf16[192,8,512]{2,0,1:T(8,128)(2,1)}), bf16[192,8,512]{2,0,1:T(8,128)(2,1)}, u32[]{:S(2)}, u32[]{:S(2)}) async-start(bf16[192,8,512]{2,0,1:T(8,128)(2,1)} %bitcast.147), calls=%async_computation.3 | async-start | bytes 3145728 | tf_op jit(solution)/shard_map/all_to_all | solution.py:55
  102.0 8.8 %copy-start.3 = (s32[12,8]{0,1:T(8,128)S(1)}, s32[12,8]{0,1:T(8,128)}, u32[]{:S(2)}) copy-start(s32[12,8]{0,1:T(8,128)} %param.15) | copy-start | bytes 1156
  102.0 57.4 %all-to-all-start.1 = ((bf16[32,2,128,128]{3,2,1,0:T(8,128)(2,1)}), bf16[32,2,128,128]{3,2,1,0:T(8,128)(2,1)}, u32[]{:S(2)}, u32[]{:S(2)}) async-start(bf16[32,2,128,128]{3,2,1,0:T(8,128)(2,1)} %bitcast.141), calls=%async_computation.1 | async-start | bytes 4194304 | tf_op jit(solution)/shard_map/all_to_all | solution.py:88
  167.5 3.7 %copy-start.1 = (bf16[60,128,1,128]{3,1,0,2:T(8,128)(2,1)S(1)}, bf16[60,128,1,128]{3,1,0,2:T(8,128)(2,1)}, u32[]{:S(2)}) copy-start(bf16[60,128,1,128]{3,1,0,2:T(8,128)(2,1)} %get-tuple-element.74) | copy-start | bytes 5898244
  167.5 3.7 %copy-start.2 = (bf16[36,128,1,128]{3,1,0,2:T(8,128)(2,1)S(1)}, bf16[36,128,1,128]{3,1,0,2:T(8,128)(2,1)}, u32[]{:S(2)}) copy-start(bf16[36,128,1,128]{3,1,0,2:T(8,128)(2,1)} %get-tuple-element.76) | copy-start | bytes 3538948
where the time goes:
time: 241 us; the launch traced here: 239 us
  blocking collectives  78.6 us (33%)
  local copies, waits for them, and re-layouts  44.5 us (18%)
  waiting for transfers between devices  43 us (18%)
  starting transfers between devices  27.2 us (11%)
  other arithmetic  26.4 us (11%)
  matrix products  19.3 us (8%)
    all_to_all x1, blocking collectives, shards(): lax.all_to_all(sent_k, 'seq', split_axis=0, concat_axis=0, tiled=True)  51.9 us
    all_to_all x1, waiting for transfers between devices, shards(): lax.all_to_all(sent_v, 'seq', split_axis=0, concat_axis=0, tiled=True)  28.3 us
    all_to_all x1, blocking collectives, shards(): lax.all_to_all(result, 'head', split_axis=0, concat_axis=1, tiled=True)  26.7 us
    all_to_all x1, starting transfers between devices, shards(): lax.all_to_all(asked, 'seq', split_axis=0, concat_axis=0, tiled=True)  11.9 us
    dot_general x3, matrix products, block_partials(): jnp.einsum('apgrqk,apkgd->apqgrd', exponent.astype(jnp.bfloat16), value_r...  11.8 us
    all_to_all x1, waiting for transfers between devices, shards(): lax.all_to_all(queries, 'head', split_axis=1, concat_axis=0, tiled=True)  8.83 us
    all_to_all x1, starting transfers between devices, shards(): lax.all_to_all(sent_v, 'seq', split_axis=0, concat_axis=0, tiled=True)  8.76 us
    dot_general x3, matrix products, block_partials(): jnp.einsum('aqgrd,apkgd->apgrqk', query_rows, key_rows, preferred_element...  7.55 us
  transfers between devices with their start and end apart: 3, of which 3 were waited for; matrix products, arithmetic and copies ran while one was open for 15% of the time, Pallas kernels for 0%

commit v1 on v0

v1 whole, which is shorter than its diff:
```python
import functools
import math

import jax
import jax.numpy as jnp
from jax import lax
from jax.experimental import pallas as pl
from jax.experimental.pallas import tpu as pltpu
from jax.sharding import PartitionSpec as P

HD = 128
BLK = 128
NEAR = 5
CORES = 2
HBM = pl.BlockSpec(memory_space=pltpu.HBM)
SMEM = pl.BlockSpec(memory_space=pltpu.SMEM)
VMEM = pl.BlockSpec(memory_space=pltpu.VMEM)
LOG2E = 1.4426950408889634


def wait_for(ref, sem):
    pltpu.make_async_copy(ref, ref, sem).wait()


def cost(flops, bytes_accessed, transcendentals=0):
    return pl.CostEstimate(flops=flops, bytes_accessed=bytes_accessed, transcendentals=transcendentals)


def split_queries_kernel(offsets, places_ref, q_ref, *refs):
    outs, sem = refs[:-1], refs[-1]
    width = outs[0].shape[1]
    copies = []
    for i in range(offsets):
        start = pl.multiple_of(places_ref[i] * width, width)
        copies.append(pltpu.make_async_copy(q_ref.at[:, pl.ds(start, width)], outs[i], sem.at[i]))
    for copy in copies:
        copy.start()
    for copy in copies:
        copy.wait()


def split_queries(queries, places):
    count = places.shape[0]
    rows, width = queries.shape[0], queries.shape[1] // count
    return pl.pallas_call(
        functools.partial(split_queries_kernel, count),
        out_shape=[jax.ShapeDtypeStruct((rows, width), queries.dtype)] * count,
        in_specs=[SMEM, HBM],
        out_specs=[HBM] * count,
        scratch_shapes=[pltpu.SemaphoreType.DMA((count,))],
        cost_estimate=cost(0, 4 * queries.size),
    )(places, queries)


def join_outputs_kernel(offsets, places_ref, *refs):
    pieces, out_ref, sem = refs[:offsets], refs[offsets], refs[offsets + 1]
    width = pieces[0].shape[1]
    copies = []
    for i in range(offsets):
        start = pl.multiple_of(places_ref[i] * width, width)
        copies.append(pltpu.make_async_copy(pieces[i], out_ref.at[:, pl.ds(start, width)], sem.at[i]))
    for copy in copies:
        copy.start()
    for copy in copies:
        copy.wait()


def join_outputs(pieces, places):
    count = len(pieces)
    rows, width = pieces[0].shape
    return pl.pallas_call(
        functools.partial(join_outputs_kernel, count),
        out_shape=jax.ShapeDtypeStruct((rows, width * count), pieces[0].dtype),
        in_specs=[SMEM] + [HBM] * count,
        out_specs=HBM,
        scratch_shapes=[pltpu.SemaphoreType.DMA((count,))],
        cost_estimate=cost(0, 4 * rows * width * count),
    )(places, *pieces)


def pack_kernel(wanted_ref, k_ref, v_ref, out_ref, sem):
    count = out_ref.shape[0]

    def start(i, carry):
        rows = pl.ds(pl.multiple_of(wanted_ref[i] * BLK, BLK), BLK)
        pltpu.make_async_copy(k_ref.at[rows], out_ref.at[i, 0], sem).start()
        pltpu.make_async_copy(v_ref.at[rows], out_ref.at[i, 1], sem).start()
        return carry

    lax.fori_loop(0, count, start, 0)
    wait_for(out_ref, sem)


def pack(wanted, keys, values):
    count = wanted.shape[0]
    return pl.pallas_call(
        pack_kernel,
        out_shape=jax.ShapeDtypeStruct((count, 2, BLK, HD), keys.dtype),
        in_specs=[SMEM, HBM, HBM],
        out_specs=HBM,
        scratch_shapes=[pltpu.SemaphoreType.DMA],
        cost_estimate=cost(0, 8 * count * BLK * HD),
    )(wanted, keys, values)


def load_queries(core, qa_ref, qb_ref, q_buf, q_sem):
    half = qa_ref.shape[0]
    copies = []
    for i, (ref, place) in enumerate(((qa_ref, core), (qb_ref, 1 - core))):
        rows = pl.ds(pl.multiple_of(place * half, half), half)
        copies.append(pltpu.make_async_copy(ref, q_buf.at[rows], q_sem.at[i]))
    return copies


def near_kernel(ids_ref, core_ref, qa_ref, qb_ref, k_ref, v_ref, acc_ref, stat_ref, q_buf, k_buf, v_buf, q_sem, k_sem, v_sem):
    blocks, span = k_buf.shape[0], k_buf.shape[1]
    picks, ratio = span // BLK, q_buf.shape[1] // HD
    factor = HD ** (-0.5) * LOG2E
    q_copies = load_queries(core_ref[0], qa_ref, qb_ref, q_buf, q_sem)
    for copy in q_copies:
        copy.start()
    for i in range(blocks):
        for j in range(picks):
            rows = pl.ds(pl.multiple_of(ids_ref[i * picks + j] * BLK, BLK), BLK)
            pltpu.make_async_copy(k_ref.at[rows], k_buf.at[i, pl.ds(j * BLK, BLK)], k_sem.at[i]).start()
            pltpu.make_async_copy(v_ref.at[rows], v_buf.at[i, pl.ds(j * BLK, BLK)], v_sem.at[i]).start()
    for copy in q_copies:
        copy.wait()

    def block(i, carry):
        wait_for(k_buf.at[i], k_sem.at[i])
        wait_for(v_buf.at[i], v_sem.at[i])
        rows = pl.ds(pl.multiple_of(i * BLK, BLK), BLK)
        lane = lax.broadcasted_iota(jnp.int32, (BLK, HD), 1)
        stats = jnp.zeros((BLK, HD), jnp.float32)
        for r in range(ratio):
            columns = pl.ds(r * HD, HD)
            score = lax.dot_general(
                q_buf[rows, columns], k_buf[i], (((1,), (1,)), ((), ())), preferred_element_type=jnp.float32
            )
            highest = jnp.max(score, axis=1, keepdims=True) * factor
            exponent = jnp.exp2(score * factor - highest)
            total = jnp.sum(exponent, axis=1, keepdims=True)
            acc_ref[rows, columns] = jnp.dot(
                exponent.astype(jnp.bfloat16), v_buf[i], preferred_element_type=jnp.float32
            )
            stats = jnp.where(lane == r, highest, stats)
            stats = jnp.where(lane == ratio + r, total, stats)
        stat_ref[rows, :] = stats
        return carry

    lax.fori_loop(0, blocks, block, 0)


def near_attention(ids, core, qa, qb, keys, values):
    blocks, picks = ids.shape
    rows, width = 2 * qa.shape[0], qa.shape[1]
    span = picks * BLK
    work = rows * width * span
    return pl.pallas_call(
        near_kernel,
        out_shape=[
            jax.ShapeDtypeStruct((rows, width), jnp.float32),
            jax.ShapeDtypeStruct((rows, HD), jnp.float32),
        ],
        in_specs=[SMEM, SMEM, HBM, HBM, HBM, HBM],
        out_specs=[VMEM, VMEM],
        scratch_shapes=[
            pltpu.VMEM((rows, width), qa.dtype),
            pltpu.VMEM((blocks, span, HD), keys.dtype),
            pltpu.VMEM((blocks, span, HD), keys.dtype),
            pltpu.SemaphoreType.DMA((2,)),
            pltpu.SemaphoreType.DMA((blocks,)),
            pltpu.SemaphoreType.DMA((blocks,)),
        ],
        cost_estimate=cost(4 * work, 6 * rows * width + 4 * blocks * span * HD, work // HD),
    )(ids.reshape(-1), core, qa, qb, keys, values)


def far_kernel(slots_ref, core_ref, qa_ref, qb_ref, got_ref, acc_ref, stat_ref, oa_ref, ob_ref, q_buf, k_buf, v_buf, o_buf, q_sem, k_sem, v_sem, o_sem):
    blocks, span = k_buf.shape[0], k_buf.shape[1]
    picks, ratio = span // BLK, q_buf.shape[1] // HD
    half = qa_ref.shape[0]
    factor = HD ** (-0.5) * LOG2E
    core = core_ref[0]
    q_copies = load_queries(core, qa_ref, qb_ref, q_buf, q_sem)
    for copy in q_copies:
        copy.start()
    for i in range(blocks):
        for j in range(picks):
            slot = slots_ref[i * picks + j]
            pltpu.make_async_copy(got_ref.at[slot, 0], k_buf.at[i, pl.ds(j * BLK, BLK)], k_sem.at[i]).start()
            pltpu.make_async_copy(got_ref.at[slot, 1], v_buf.at[i, pl.ds(j * BLK, BLK)], v_sem.at[i]).start()
    for copy in q_copies:
        copy.wait()

    def block(i, carry):
        wait_for(k_buf.at[i], k_sem.at[i])
        wait_for(v_buf.at[i], v_sem.at[i])
        rows = pl.ds(pl.multiple_of(i * BLK, BLK), BLK)
        for r in range(ratio):
            columns = pl.ds(r * HD, HD)
            score = lax.dot_general(
                q_buf[rows, columns], k_buf[i], (((1,), (1,)), ((), ())), preferred_element_type=jnp.float32
            )
            before = stat_ref[rows, r : r + 1]
            highest = jnp.maximum(jnp.max(score, axis=1, keepdims=True) * factor, before)
            exponent = jnp.exp2(score * factor - highest)
            kept = jnp.exp2(before - highest)
            total = jnp.sum(exponent, axis=1, keepdims=True) + kept * stat_ref[rows, ratio + r : ratio + r + 1]
            partial = jnp.dot(exponent.astype(jnp.bfloat16), v_buf[i], preferred_element_type=jnp.float32)
            merged = (partial + kept * acc_ref[rows, columns]) / total
            o_buf[rows, columns] = merged.astype(o_buf.dtype)
        return carry

    lax.fori_loop(0, blocks, block, 0)
    copies = []
    for i, (ref, place) in enumerate(((oa_ref, core), (ob_ref, 1 - core))):
        rows = pl.ds(pl.multiple_of(place * half, half), half)
        copies.append(pltpu.make_async_copy(o_buf.at[rows], ref, o_sem.at[i]))
    for copy in copies:
        copy.start()
    for copy in copies:
        copy.wait()


def far_attention(slots, core, qa, qb, got, acc, stats):
    blocks, picks = slots.shape
    half, width = qa.shape
    rows = 2 * half
    span = picks * BLK
    work = rows * width * span
    return pl.pallas_call(
        far_kernel,
        out_shape=[jax.ShapeDtypeStruct((half, width), qa.dtype)] * 2,
        in_specs=[SMEM, SMEM, HBM, HBM, HBM, VMEM, VMEM],
        out_specs=[HBM, HBM],
        scratch_shapes=[
            pltpu.VMEM((rows, width), qa.dtype),
            pltpu.VMEM((blocks, span, HD), got.dtype),
            pltpu.VMEM((blocks, span, HD), got.dtype),
            pltpu.VMEM((rows, width), qa.dtype),
            pltpu.SemaphoreType.DMA((2,)),
            pltpu.SemaphoreType.DMA((blocks,)),
            pltpu.SemaphoreType.DMA((blocks,)),
            pltpu.SemaphoreType.DMA((2,)),
        ],
        cost_estimate=cost(4 * work, 8 * rows * width + 4 * blocks * span * HD, work // HD),
    )(slots.reshape(-1), core, qa, qb, got, acc, stats)


def offset_pairs(chips, chip_step, core_step):
    return [
        (chip * CORES + core, (chip + chip_step) % chips * CORES + (core ^ core_step))
        for chip in range(chips)
        for core in range(CORES)
    ]


def shards(queries, cache_keys, cache_values, block_ids):
    seq_count = lax.axis_size("seq")
    heads = lax.axis_size("head")
    seq_place = lax.axis_index("seq")
    head_place = lax.axis_index("head")
    chips = heads // CORES
    chip, core = head_place // CORES, head_place % CORES
    q_count, k_count = block_ids.shape[0], cache_keys.shape[0] // BLK
    per_chip = q_count // chips
    far_count = block_ids.shape[1] - NEAR
    capacity = max(2, (far_count * q_count + seq_count - 2) // (seq_count - 1))
    slot_total = seq_count * capacity

    far_ids = block_ids[:, NEAR:].reshape(-1)
    far_owner = far_ids // k_count
    far_within = far_ids - far_owner * k_count
    entry = jnp.arange(far_ids.shape[0], dtype=jnp.int32)
    earlier = (far_owner[:, None] == far_owner[None, :]) & (entry[None, :] < entry[:, None])
    far_slot = far_owner * capacity + jnp.sum(earlier.astype(jnp.int32), axis=1)
    placed = far_slot[:, None] == jnp.arange(slot_total, dtype=jnp.int32)[None, :]
    asked = jnp.sum(jnp.where(placed, far_within[:, None], 0), axis=0).reshape(seq_count, capacity)
    wanted = lax.all_to_all(asked, "seq", split_axis=0, concat_axis=0, tiled=True).reshape(-1)

    sent = pack(wanted, cache_keys, cache_values)
    got = lax.all_to_all(
        sent.reshape(seq_count, capacity, 2, BLK, HD), "seq", split_axis=0, concat_axis=0, tiled=True
    ).reshape(slot_total, 2, BLK, HD)

    steps = [(d, e) for d in range(chips) for e in range(CORES)]
    step_chip = jnp.array([d for d, _ in steps], jnp.int32)
    step_core = jnp.array([e for _, e in steps], jnp.int32)
    ahead = (chip + step_chip) % chips * CORES + (core + step_core) % CORES
    pieces = split_queries(queries, ahead)
    rows_of = {}
    for piece, (d, e) in zip(pieces, steps):
        rows_of[d, e] = piece if d == e == 0 else lax.ppermute(piece, "head", offset_pairs(chips, d, e))

    order = (chip - jnp.arange(chips, dtype=jnp.int32)) % chips
    near_ids = jnp.take((block_ids[:, :NEAR] - seq_place * k_count).reshape(chips, per_chip, NEAR), order, axis=0)
    slots = jnp.take(far_slot.reshape(chips, per_chip, far_count), order, axis=0)
    core_operand = core.astype(jnp.int32).reshape(1)

    near = [
        near_attention(near_ids[d], core_operand, rows_of[d, 0], rows_of[d, 1], cache_keys, cache_values)
        for d in range(chips)
    ]
    got, near = lax.optimization_barrier((got, near))
    results = {}
    for d in sorted(range(chips), key=lambda d: -min(d, chips - d)):
        made = far_attention(slots[d], core_operand, rows_of[d, 0], rows_of[d, 1], got, *near[d])
        for e in range(CORES):
            results[d, e] = made[e] if d == e == 0 else lax.ppermute(made[e], "head", offset_pairs(chips, -d, e))
    return join_outputs([results[step] for step in steps], ahead)


def solution(mesh):
    return jax.shard_map(
        shards,
        mesh=mesh,
        in_specs=(P(("seq", "head"), None), P("seq", "head"), P("seq", "head"), P("seq", None)),
        out_specs=P(("seq", "head"), None),
        check_vma=False,
    )
```

time: 241 us -> 359 us (1.49)
  Pallas kernels: 0 us -> 288 us
  blocking collectives: 78.6 us -> 20.3 us
  local copies, waits for them, and re-layouts: 44.5 us -> 12.5 us
  waiting for transfers between devices: 43 us -> 11.2 us
  other arithmetic: 26.4 us -> 1.78 us
  matrix products: 19.3 us -> 0 us
    pallas_call x0 -> x11, Pallas kernels: none -> 288 us  [the longest x1 129 us: pack(): pl.pallas_call(pack_kernel, out_shape=jax.ShapeDtypeStruct((count, 2, BLK...]
    all_to_all x2 -> x1, blocking collectives: 78.6 us -> 20.3 us  [shards(): lax.all_to_all(asked, 'seq', split_axis=0, concat_axis=0, tiled=True)]
    all_to_all x3 -> x1, waiting for transfers between devices: 43 us -> 0.01 us  [shards(): lax.all_to_all(sent.reshape(seq_count, capacity, 2, BLK, HD), 'seq', spli...]
    all_to_all x3 -> x1, starting transfers between devices: 27.2 us -> 5.01 us  [shards(): lax.all_to_all(sent.reshape(seq_count, capacity, 2, BLK, HD), 'seq', spli...]
    dot_general x6 -> x0, matrix products: 19.3 us -> none  [the longest x3 11.8 us: block_partials(): jnp.einsum('apgrqk,apkgd->apqgrd', exponent.astype(jnp.bfloat16), value_r...]
    ppermute x0 -> x14, starting transfers between devices: none -> 18.7 us  [the longest x7 10.9 us: shards(): lax.ppermute(piece, 'head', offset_pairs(chips, d, e))]
    gather x6 -> x2, local copies, waits for them, and re-layouts: 17.5 us -> 1.14 us  [the longest x1 0.57 us: shards(): jnp.take(far_slot.reshape(chips, per_chip, far_count), order, axis=0)]
    select_n x6 -> x3, other arithmetic: 12.1 us -> 0.16 us  [the longest x2 0.09 us: shards(): jnp.take(far_slot.reshape(chips, per_chip, far_count), order, axis=0)]
  transfers between devices with their start and end apart: 3 -> 15, of which waited for: 3 -> 2; matrix products, arithmetic and copies ran while one was open for 15% -> 2% of each run, Pallas kernels for 0% -> 28%
where the time goes in v1:
time: 359 us; the launch traced here: 358 us
  Pallas kernels  288 us (80%)
  starting transfers between devices  23.7 us (7%)
  blocking collectives  20.3 us (6%)
  local copies, waits for them, and re-layouts  12.5 us (3%)
  waiting for transfers between devices  11.2 us (3%)
    pallas_call x1, Pallas kernels, pack(): pl.pallas_call(pack_kernel, out_shape=jax.ShapeDtypeStruct((count, 2, BLK...  129 us
    pallas_call x1, Pallas kernels, join_outputs(): pl.pallas_call(functools.partial(join_outputs_kernel, count), out_shape=j...  49.5 us
    pallas_call x1, Pallas kernels, split_queries(): pl.pallas_call(functools.partial(split_queries_kernel, count), out_shape=...  49.5 us
    pallas_call x4, Pallas kernels, far_attention(): pl.pallas_call(far_kernel, out_shape=[jax.ShapeDtypeStruct((half, width),...  32 us
    pallas_call x4, Pallas kernels, near_attention(): pl.pallas_call(near_kernel, out_shape=[jax.ShapeDtypeStruct((rows, width)...  28.6 us
    all_to_all x1, blocking collectives, shards(): lax.all_to_all(asked, 'seq', split_axis=0, concat_axis=0, tiled=True)  20.3 us
    ppermute x7, waiting for transfers between devices, shards(): lax.ppermute(made[e], 'head', offset_pairs(chips, -d, e))  11.2 us
    ppermute x7, starting transfers between devices, shards(): lax.ppermute(piece, 'head', offset_pairs(chips, d, e))  10.9 us
  transfers between devices with their start and end apart: 15, of which 2 were waited for; matrix products, arithmetic and copies ran while one was open for 2% of the time, Pallas kernels for 28%

profile of v1, /device:TPU:1, one launch (start us, length us, event | category | flops | bytes accessed | tf_op | source)
XLA Modules:
  0.0 358.5 jit_solution(9950859895149297541)
XLA Ops:
  0.0 0.7 slice.30
  0.7 0.1 copy.34
  0.8 0.1 reshape.166
  0.9 0.2 convert_reduce_fusion
  1.1 0.1 select_reduce_fusion
  1.2 0.1 all_to_all.9
  1.3 20.3 %all_to_all.14 = s32[32,1,2]{2,1,0:T(1,128)S(1)} all-to-all(s32[32,1,2]{2,1,0:T(1,128)S(1)} %bitcast.11), channel_id=1, replica_groups=mesh['seq'=32,'head'=8] {'seq'}, dimensions={0} | all-to-all | bytes 512 | tf_op jit(solution)/shard_map/all_to_all | solution.py:281
  21.6 0.5 broadcast.249
  22.1 0.7 reduce.3
  22.8 0.6 reshape.168.wanted_ref
  23.4 128.8 %shard_map.65 = bf16[64,2,128,128]{3,2,1,0:T(8,128)(2,1)} custom-call(s32[64]{0:T(128)} %reshape.168.wanted_ref, bf16[8192,128]{1,0:T(8,128)(2,1)} %k_ref.9, bf16[8192,128]{1,0:T(8,128)(2,1)} %v_ref.9), custom_call_target="tpu_custom_call" | custom-call | bytes 8388608 | tf_op jit(solution)/shard_map/pallas_call | solution.py:96
  152.3 0.0 copy-start.15
  152.3 5.0 %all-to-all-start.1 = ((bf16[32,2,2,128,128]{4,3,2,1,0:T(8,128)(2,1)}), bf16[32,2,2,128,128]{4,3,2,1,0:T(8,128)(2,1)}, u32[]{:S(2)}, u32[]{:S(2)}) async-start(bf16[32,2,2,128,128]{4,3,2,1,0:T(8,128)(2,1)} %bitcast.10), calls=%async_computation.1 | async-start | bytes 8388608 | tf_op jit(solution)/shard_map/all_to_all | solution.py:284
  157.3 0.6 fusion.5.places_ref
  157.9 49.5 %shard_map.64 = (bf16[192,512]{1,0:T(8,128)(2,1)}, bf16[192,512]{1,0:T(8,128)(2,1)}, bf16[192,512]{1,0:T(8,128)(2,1)}, bf16[192,512]{1,0:T(8,128)(2,1)}, bf16[19...) custom-call(s32[8]{0:T(128)} %fusion.5.places_ref, ...), custom_call_target="tpu_custom_call" | custom-call | bytes 3145728 | tf_op jit(solution)/shard_map/pallas_call | solution.py:45
  207.4 2.2 collective-permute-start
  209.6 1.3 collective-permute-start.1
  210.9 1.5 collective-permute-start.2
  212.5 1.3 collective-permute-start.3
  213.7 2.0 collective-permute-start.4
  215.8 0.1 reduce_sum.21
  215.9 0.1 reshape.165
  215.9 0.1 copy.30
  216.1 0.1 reshape.171
  216.1 0.1 copy.36
  216.3 0.6 gather_fusion
  216.9 0.6 gather_fusion.1
  217.5 0.1 broadcast_select_fusion.1
  217.6 0.1 broadcast_select_fusion
  217.6 1.5 collective-permute-start.5
  219.1 1.1 collective-permute-start.6
  220.2 0.6 reshape_squeeze.24.slots_ref
  220.8 0.6 reshape_squeeze.25.ids_ref
  221.4 0.6 reshape_squeeze.26.ids_ref
  222.0 0.6 reshape_squeeze.27.ids_ref
  222.6 0.6 reshape_squeeze.28.ids_ref
  223.2 0.6 reshape_squeeze.29.slots_ref
  223.8 7.1 %shard_map.66 = (f32[384,512]{1,0:T(8,128)}, f32[384,128]{1,0:T(8,128)}) custom-call(s32[15]{0:T(128)} %reshape_squeeze.25.ids_ref, s32[1]{0:T(128)} %bitcast.1.core_ref, bf16[192,512]{1,0:T(8,128)(2,1)} %get-tuple-element.38.qa_ref, bf16[192,512]{1,0:T(8,128)(2,1)} %copy-done.4, bf16[8192,128]{1,0:T(8,128)(2,1)} %k_ref.9, bf16[8192,128]{1,0:T(8,128)(2,1)} %v_ref.9), custom_call_target="tpu_custom_call" | custom-call | flops 503316480 | bytes 2162688 | tf_op jit(solution)/shard_map/pallas_call | solution.py:160
  231.0 0.7 copy-done.3
  231.6 7.1 %shard_map.67 = (f32[384,512]{1,0:T(8,128)}, f32[384,128]{1,0:T(8,128)}) custom-call(s32[15]{0:T(128)} %reshape_squeeze.26.ids_ref, s32[1]{0:T(128)} %bitcast.1.core_ref, bf16[192,512]{1,0:T(8,128)(2,1)} %copy-done.2, bf16[192,512]{1,0:T(8,128)(2,1)} %copy-done.3, bf16[8192,128]{1,0:T(8,128)(2,1)} %k_ref.9, bf16[8192,128]{1,0:T(8,128)(2,1)} %v_ref.9), custom_call_target="tpu_custom_call" | custom-call | flops 503316480 | bytes 2162688 | tf_op jit(solution)/shard_map/pallas_call | solution.py:160
  238.8 0.7 copy-done
  239.5 0.7 copy-done.1
  240.2 7.2 %shard_map.68 = (f32[384,512]{1,0:T(8,128)}, f32[384,128]{1,0:T(8,128)}) custom-call(s32[15]{0:T(128)} %reshape_squeeze.27.ids_ref, s32[1]{0:T(128)} %bitcast.1.core_ref, bf16[192,512]{1,0:T(8,128)(2,1)} %copy-done, bf16[192,512]{1,0:T(8,128)(2,1)} %copy-done.1, bf16[8192,128]{1,0:T(8,128)(2,1)} %k_ref.9, bf16[8192,128]{1,0:T(8,128)(2,1)} %v_ref.9), custom_call_target="tpu_custom_call" | custom-call | flops 503316480 | bytes 2162688 | tf_op jit(solution)/shard_map/pallas_call | solution.py:160
  247.4 0.7 copy-done.5
  248.0 0.7 copy-done.6
  248.7 7.2 %shard_map.69 = (f32[384,512]{1,0:T(8,128)}, f32[384,128]{1,0:T(8,128)}) custom-call(s32[15]{0:T(128)} %reshape_squeeze.28.ids_ref, s32[1]{0:T(128)} %bitcast.1.core_ref, bf16[192,512]{1,0:T(8,128)(2,1)} %copy-done.5, bf16[192,512]{1,0:T(8,128)(2,1)} %copy-done.6, bf16[8192,128]{1,0:T(8,128)(2,1)} %k_ref.9, bf16[8192,128]{1,0:T(8,128)(2,1)} %v_ref.9), custom_call_target="tpu_custom_call" | custom-call | flops 503316480 | bytes 2162688 | tf_op jit(solution)/shard_map/pallas_call | solution.py:160
  255.9 8.0 %shard_map.70 = (bf16[192,512]{1,0:T(8,128)(2,1)}, bf16[192,512]{1,0:T(8,128)(2,1)}) custom-call(s32[9]{0:T(128)} %reshape_squeeze.24.slots_ref, s32[1]{0:T(128)} %bitcast.1.core_ref, bf16[192,512]{1,0:T(8,128)(2,1)} %get-tuple-element.38.qa_ref, bf16[192,512]{1,0:T(8,128)(2,1)} %copy-done.4, bf16[64,2,128,128]{3,2,1,0:T(8,128)(2,1)} %bitcast.4.got_ref, ...), custom_call_target="tpu_custom_call" | custom-call | flops 301989888 | bytes 2162688 | tf_op jit(solution)/shard_map/pallas_call | solution.py:233
  263.9 0.3 collective-permute-start.7
  264.2 8.0 %shard_map.71 = (bf16[192,512]{1,0:T(8,128)(2,1)}, bf16[192,512]{1,0:T(8,128)(2,1)}) custom-call(s32[9]{0:T(128)} %reshape_squeeze.29.slots_ref, s32[1]{0:T(128)} %bitcast.1.core_ref, bf16[192,512]{1,0:T(8,128)(2,1)} %copy-done.2, bf16[192,512]{1,0:T(8,128)(2,1)} %copy-done.3, bf16[64,2,128,128]{3,2,1,0:T(8,128)(2,1)} %bitcast.4.got_ref, ...), custom_call_target="tpu_custom_call" | custom-call | flops 301989888 | bytes 2162688 | tf_op jit(solution)/shard_map/pallas_call | solution.py:233
  272.2 2.3 collective-permute-start.8
  274.5 0.6 reshape_squeeze.30.slots_ref
  275.1 0.6 reshape_squeeze.31.slots_ref
  275.7 0.6 collective-permute-start.9
  276.3 8.0 %shard_map.72 = (bf16[192,512]{1,0:T(8,128)(2,1)}, bf16[192,512]{1,0:T(8,128)(2,1)}) custom-call(s32[9]{0:T(128)} %reshape_squeeze.30.slots_ref, s32[1]{0:T(128)} %bitcast.1.core_ref, bf16[192,512]{1,0:T(8,128)(2,1)} %copy-done, bf16[192,512]{1,0:T(8,128)(2,1)} %copy-done.1, bf16[64,2,128,128]{3,2,1,0:T(8,128)(2,1)} %bitcast.4.got_ref, ...), custom_call_target="tpu_custom_call" | custom-call | flops 301989888 | bytes 2162688 | tf_op jit(solution)/shard_map/pallas_call | solution.py:233
  284.3 1.1 collective-permute-start.10
  285.5 2.3 collective-permute-start.11
  287.8 8.0 %shard_map.73 = (bf16[192,512]{1,0:T(8,128)(2,1)}, bf16[192,512]{1,0:T(8,128)(2,1)}) custom-call(s32[9]{0:T(128)} %reshape_squeeze.31.slots_ref, s32[1]{0:T(128)} %bitcast.1.core_ref, bf16[192,512]{1,0:T(8,128)(2,1)} %copy-done.5, bf16[192,512]{1,0:T(8,128)(2,1)} %copy-done.6, bf16[64,2,128,128]{3,2,1,0:T(8,128)(2,1)} %bitcast.4.got_ref, ...), custom_call_target="tpu_custom_call" | custom-call | flops 301989888 | bytes 2162688 | tf_op jit(solution)/shard_map/pallas_call | solution.py:233
  295.8 1.1 collective-permute-start.12
  296.9 0.0 collective-permute-start.13
  296.9 0.0 collective-permute-done.11.refs_5_
  297.0 6.8 %collective-permute-done.12.refs_6_ = bf16[192,512]{1,0:T(8,128)(2,1)S(1)} collective-permute-done((bf16[192,512]{1,0:T(8,128)(2,1)}, bf16[192,512]{1,0:T(8,128)(2,1)S(1)}, u32[]{:S(2)}, u32[]{:S(2)}) %collective-permute-start.12) | collective-permute-done | bytes 196640 | tf_op jit(solution)/shard_map/ppermute | solution.py:311
  303.8 4.3 %collective-permute-done.13.refs_7_ = bf16[192,512]{1,0:T(8,128)(2,1)S(1)} collective-permute-done((bf16[192,512]{1,0:T(8,128)(2,1)}, bf16[192,512]{1,0:T(8,128)(2,1)S(1)}, u32[]{:S(2)}, u32[]{:S(2)}) %collective-permute-start.13) | collective-permute-done | bytes 196640 | tf_op jit(solution)/shard_map/ppermute | solution.py:311
  308.2 0.6 copy-done.13
  308.8 49.5 %shard_map.74 = bf16[192,4096]{1,0:T(8,128)(2,1)} custom-call(s32[8]{0:T(128)} %fusion.5.places_ref, bf16[192,512]{1,0:T(8,128)(2,1)} %get-tuple-element.57.refs_0_, bf16[192,512]{1,0:T(8,128)(2,1)} %copy-done.7, bf16[192,512]{1,0:T(8,128)(2,1)} %copy-done.8, bf16[192,512]{1,0:T(8,128)(2,1)} %copy-done.9, bf16[192,512]{1,0:T(8,128)(2,1)} %copy-done.10, ...), custom_call_target="tpu_custom_call" | custom-call | bytes 3145728 | tf_op jit(solution)/shard_map/pallas_call | solution.py:71
  (48 shorter events, 0.2 us)
Async XLA Ops:
  152.3 5.1 %copy-start.15 = (s32[8]{0:T(128)S(1)}, s32[8]{0:T(128)}, u32[]{:S(2)}) copy-start(s32[8]{0:T(128)} %constant.109.clone) | copy-start | bytes 100
  152.3 5.1 %copy-start.16 = (s32[8]{0:T(128)S(1)}, s32[8]{0:T(128)}, u32[]{:S(2)}) copy-start(s32[8]{0:T(128)} %constant.110.clone) | copy-start | bytes 100
  152.3 63.8 %copy-start.14 = (s32[12,8]{0,1:T(8,128)S(1)}, s32[12,8]{0,1:T(8,128)}, u32[]{:S(2)}) copy-start(s32[12,8]{0,1:T(8,128)} %param.9) | copy-start | bytes 1156
  152.3 103.6 %all-to-all-start.1 = ((bf16[32,2,2,128,128]{4,3,2,1,0:T(8,128)(2,1)}), bf16[32,2,2,128,128]{4,3,2,1,0:T(8,128)(2,1)}, u32[]{:S(2)}, u32[]{:S(2)}) async-start(bf16[32,2,2,128,128]{4,3,2,1,0:T(8,128)(2,1)} %bitcast.10), calls=%async_computation.1 | async-start | bytes 8388608 | tf_op jit(solution)/shard_map/all_to_all | solution.py:284
  207.4 10.2 %collective-permute-start = (bf16[192,512]{1,0:T(8,128)(2,1)}, bf16[192,512]{1,0:T(8,128)(2,1)S(1)}, u32[]{:S(2)}, u32[]{:S(2)}) collective-permute-start(bf16[192,512]{1,0:T(8,128)(2,1)} %get-tuple-element.39), channel_id=1, source_target_pairs={{0,1},{1,0},{2,3},{3,2},{4,5},{5,4},{6,7},{7,6},{8,9},{9,8},{10,11... | collective-permute-start | bytes 589832 | tf_op jit(solution)/shard_map/ppermute | solution.py:295
  209.6 9.5 %collective-permute-start.1 = (bf16[192,512]{1,0:T(8,128)(2,1)}, bf16[192,512]{1,0:T(8,128)(2,1)S(1)}, u32[]{:S(2)}, u32[]{:S(2)}) collective-permute-start(bf16[192,512]{1,0:T(8,128)(2,1)} %get-tuple-element.42), channel_id=1, source_target_pairs={{0,2},{1,3},{2,4},{3,5},{4,6},{5,7},{6,0},{7,1},{8,10},{9,11},{10,... | collective-permute-start | bytes 589832 | tf_op jit(solution)/shard_map/ppermute | solution.py:295
  210.9 20.0 %collective-permute-start.2 = (bf16[192,512]{1,0:T(8,128)(2,1)}, bf16[192,512]{1,0:T(8,128)(2,1)S(1)}, u32[]{:S(2)}, u32[]{:S(2)}) collective-permute-start(bf16[192,512]{1,0:T(8,128)(2,1)} %get-tuple-element.43), channel_id=1, source_target_pairs={{0,3},{1,2},{2,5},{3,4},{4,7},{5,6},{6,1},{7,0},{8,11},{9,10},{10,... | collective-permute-start | bytes 589832 | tf_op jit(solution)/shard_map/ppermute | solution.py:295
  212.5 26.3 %collective-permute-start.3 = (bf16[192,512]{1,0:T(8,128)(2,1)}, bf16[192,512]{1,0:T(8,128)(2,1)S(1)}, u32[]{:S(2)}, u32[]{:S(2)}) collective-permute-start(bf16[192,512]{1,0:T(8,128)(2,1)} %get-tuple-element.46), channel_id=1, source_target_pairs={{0,4},{1,5},{2,6},{3,7},{4,0},{5,1},{6,2},{7,3},{8,12},{9,13},{10,... | collective-permute-start | bytes 589832 | tf_op jit(solution)/shard_map/ppermute | solution.py:295
  213.7 25.1 %collective-permute-start.4 = (bf16[192,512]{1,0:T(8,128)(2,1)}, bf16[192,512]{1,0:T(8,128)(2,1)S(1)}, u32[]{:S(2)}, u32[]{:S(2)}) collective-permute-start(bf16[192,512]{1,0:T(8,128)(2,1)} %get-tuple-element.47), channel_id=1, source_target_pairs={{0,5},{1,4},{2,7},{3,6},{4,1},{5,0},{6,3},{7,2},{8,13},{9,12},{10,... | collective-permute-start | bytes 589832 | tf_op jit(solution)/shard_map/ppermute | solution.py:295
  217.6 6.2 %copy-start.4 = (bf16[192,512]{1,0:T(8,128)(2,1)}, bf16[192,512]{1,0:T(8,128)(2,1)S(1)}, u32[]{:S(2)}) copy-start(bf16[192,512]{1,0:T(8,128)(2,1)S(1)} %collective-permute-done.qb_ref) | copy-start | bytes 589828
  217.6 29.7 %collective-permute-start.5 = (bf16[192,512]{1,0:T(8,128)(2,1)}, bf16[192,512]{1,0:T(8,128)(2,1)S(1)}, u32[]{:S(2)}, u32[]{:S(2)}) collective-permute-start(bf16[192,512]{1,0:T(8,128)(2,1)} %get-tuple-element.50), channel_id=1, source_target_pairs={{0,6},{1,7},{2,0},{3,1},{4,2},{5,3},{6,4},{7,5},{8,14},{9,15},{10,... | collective-permute-start | bytes 589832 | tf_op jit(solution)/shard_map/ppermute | solution.py:295
  219.1 11.8 %copy-start.2 = (bf16[192,512]{1,0:T(8,128)(2,1)}, bf16[192,512]{1,0:T(8,128)(2,1)S(1)}, u32[]{:S(2)}) copy-start(bf16[192,512]{1,0:T(8,128)(2,1)S(1)} %collective-permute-done.1.qa_ref) | copy-start | bytes 589828
  219.1 28.2 %collective-permute-start.6 = (bf16[192,512]{1,0:T(8,128)(2,1)}, bf16[192,512]{1,0:T(8,128)(2,1)S(1)}, u32[]{:S(2)}, u32[]{:S(2)}) collective-permute-start(bf16[192,512]{1,0:T(8,128)(2,1)} %get-tuple-element.51), channel_id=1, source_target_pairs={{0,7},{1,6},{2,1},{3,0},{4,3},{5,2},{6,5},{7,4},{8,15},{9,14},{10,... | collective-permute-start | bytes 589832 | tf_op jit(solution)/shard_map/ppermute | solution.py:295
  231.0 0.7 copy-start.3
  238.8 0.7 copy-start
  239.5 0.7 copy-start.1
  247.3 0.7 copy-start.5
  248.0 0.7 copy-start.6
  263.9 31.9 %collective-permute-start.7 = (bf16[192,512]{1,0:T(8,128)(2,1)}, bf16[192,512]{1,0:T(8,128)(2,1)S(1)}, u32[]{:S(2)}, u32[]{:S(2)}) collective-permute-start(bf16[192,512]{1,0:T(8,128)(2,1)} %get-tuple-element.58), channel_id=1, source_target_pairs={{0,1},{1,0},{2,3},{3,2},{4,5},{5,4},{6,7},{7,6},{8,9},{9,8},{10,11... | collective-permute-start | bytes 589832 | tf_op jit(solution)/shard_map/ppermute | solution.py:311
  272.2 24.7 %collective-permute-start.8 = (bf16[192,512]{1,0:T(8,128)(2,1)}, bf16[192,512]{1,0:T(8,128)(2,1)S(1)}, u32[]{:S(2)}, u32[]{:S(2)}) collective-permute-start(bf16[192,512]{1,0:T(8,128)(2,1)} %get-tuple-element.61), channel_id=1, source_target_pairs={{0,6},{1,7},{2,0},{3,1},{4,2},{5,3},{6,4},{7,5},{8,14},{9,15},{10,... | collective-permute-start | bytes 589832 | tf_op jit(solution)/shard_map/ppermute | solution.py:311
  275.7 21.2 %collective-permute-start.9 = (bf16[192,512]{1,0:T(8,128)(2,1)}, bf16[192,512]{1,0:T(8,128)(2,1)S(1)}, u32[]{:S(2)}, u32[]{:S(2)}) collective-permute-start(bf16[192,512]{1,0:T(8,128)(2,1)} %get-tuple-element.62), channel_id=1, source_target_pairs={{0,7},{1,6},{2,1},{3,0},{4,3},{5,2},{6,5},{7,4},{8,15},{9,14},{10,... | collective-permute-start | bytes 589832 | tf_op jit(solution)/shard_map/ppermute | solution.py:311
  284.3 12.6 %collective-permute-start.10 = (bf16[192,512]{1,0:T(8,128)(2,1)}, bf16[192,512]{1,0:T(8,128)(2,1)S(1)}, u32[]{:S(2)}, u32[]{:S(2)}) collective-permute-start(bf16[192,512]{1,0:T(8,128)(2,1)} %get-tuple-element.65), channel_id=1, source_target_pairs={{0,4},{1,5},{2,6},{3,7},{4,0},{5,1},{6,2},{7,3},{8,12},{9,13},{10,... | collective-permute-start | bytes 589832 | tf_op jit(solution)/shard_map/ppermute | solution.py:311
  285.5 11.5 %collective-permute-start.11 = (bf16[192,512]{1,0:T(8,128)(2,1)}, bf16[192,512]{1,0:T(8,128)(2,1)S(1)}, u32[]{:S(2)}, u32[]{:S(2)}) collective-permute-start(bf16[192,512]{1,0:T(8,128)(2,1)} %get-tuple-element.66), channel_id=1, source_target_pairs={{0,5},{1,4},{2,7},{3,6},{4,1},{5,0},{6,3},{7,2},{8,13},{9,12},{10,... | collective-permute-start | bytes 589832 | tf_op jit(solution)/shard_map/ppermute | solution.py:311
  295.8 12.4 %copy-start.7 = (bf16[192,512]{1,0:T(8,128)(2,1)}, bf16[192,512]{1,0:T(8,128)(2,1)S(1)}, u32[]{:S(2)}) copy-start(bf16[192,512]{1,0:T(8,128)(2,1)S(1)} %collective-permute-done.7.refs_1_) | copy-start | bytes 589828
  295.8 8.0 %collective-permute-start.12 = (bf16[192,512]{1,0:T(8,128)(2,1)}, bf16[192,512]{1,0:T(8,128)(2,1)S(1)}, u32[]{:S(2)}, u32[]{:S(2)}) collective-permute-start(bf16[192,512]{1,0:T(8,128)(2,1)} %get-tuple-element.69), channel_id=1, source_target_pairs={{0,2},{1,3},{2,4},{3,5},{4,6},{5,7},{6,0},{7,1},{8,10},{9,11},{10,... | collective-permute-start | bytes 589832 | tf_op jit(solution)/shard_map/ppermute | solution.py:311
  296.9 11.3 %copy-start.8 = (bf16[192,512]{1,0:T(8,128)(2,1)}, bf16[192,512]{1,0:T(8,128)(2,1)S(1)}, u32[]{:S(2)}) copy-start(bf16[192,512]{1,0:T(8,128)(2,1)S(1)} %collective-permute-done.8.refs_2_) | copy-start | bytes 589828
  296.9 11.3 %collective-permute-start.13 = (bf16[192,512]{1,0:T(8,128)(2,1)}, bf16[192,512]{1,0:T(8,128)(2,1)S(1)}, u32[]{:S(2)}, u32[]{:S(2)}) collective-permute-start(bf16[192,512]{1,0:T(8,128)(2,1)} %get-tuple-element.70), channel_id=1, source_target_pairs={{0,3},{1,2},{2,5},{3,4},{4,7},{5,6},{6,1},{7,0},{8,11},{9,10},{10,... | collective-permute-start | bytes 589832 | tf_op jit(solution)/shard_map/ppermute | solution.py:311
  296.9 11.2 %copy-start.9 = (bf16[192,512]{1,0:T(8,128)(2,1)}, bf16[192,512]{1,0:T(8,128)(2,1)S(1)}, u32[]{:S(2)}) copy-start(bf16[192,512]{1,0:T(8,128)(2,1)S(1)} %collective-permute-done.9.refs_3_) | copy-start | bytes 589828
  296.9 11.2 %copy-start.10 = (bf16[192,512]{1,0:T(8,128)(2,1)}, bf16[192,512]{1,0:T(8,128)(2,1)S(1)}, u32[]{:S(2)}) copy-start(bf16[192,512]{1,0:T(8,128)(2,1)S(1)} %collective-permute-done.10.refs_4_) | copy-start | bytes 589828
  297.0 11.2 %copy-start.11 = (bf16[192,512]{1,0:T(8,128)(2,1)}, bf16[192,512]{1,0:T(8,128)(2,1)S(1)}, u32[]{:S(2)}) copy-start(bf16[192,512]{1,0:T(8,128)(2,1)S(1)} %collective-permute-done.11.refs_5_) | copy-start | bytes 589828
  303.8 4.4 %copy-start.12 = (bf16[192,512]{1,0:T(8,128)(2,1)}, bf16[192,512]{1,0:T(8,128)(2,1)S(1)}, u32[]{:S(2)}) copy-start(bf16[192,512]{1,0:T(8,128)(2,1)S(1)} %collective-permute-done.12.refs_6_) | copy-start | bytes 589828
  308.1 0.7 copy-start.13

commit v2 on v1

v2 whole, which is shorter than its diff:
```python
import functools
import math

import jax
import jax.numpy as jnp
from jax import lax
from jax.experimental import pallas as pl
from jax.experimental.pallas import tpu as pltpu
from jax.sharding import PartitionSpec as P

HD = 128
BLK = 128
NEAR = 5
CORES = 2
HBM = pl.BlockSpec(memory_space=pltpu.HBM)
SMEM = pl.BlockSpec(memory_space=pltpu.SMEM)
VMEM = pl.BlockSpec(memory_space=pltpu.VMEM)
LOG2E = 1.4426950408889634


def wait_for(ref, sem):
    pltpu.make_async_copy(ref, ref, sem).wait()


def room(mebibytes):
    return pltpu.CompilerParams(vmem_limit_bytes=mebibytes * 1024 * 1024)


def cost(flops, bytes_accessed, transcendentals=0):
    return pl.CostEstimate(flops=flops, bytes_accessed=bytes_accessed, transcendentals=transcendentals)


def split_queries_kernel(places_ref, q_ref, *refs):
    count = len(refs) - 3
    outs, buf, in_sem, out_sem = refs[:count], *refs[count:]
    width = buf.shape[2]
    into, out_of = [], []
    for i in range(count):
        start = pl.multiple_of(places_ref[i] * width, width)
        into.append(pltpu.make_async_copy(q_ref.at[:, pl.ds(start, width)], buf.at[i], in_sem.at[i]))
        out_of.append(pltpu.make_async_copy(buf.at[i], outs[i], out_sem.at[i]))
    for copy in into:
        copy.start()
    for i in range(count):
        into[i].wait()
        out_of[i].start()
    for copy in out_of:
        copy.wait()


def split_queries(queries, places):
    count = places.shape[0]
    rows, width = queries.shape[0], queries.shape[1] // count
    return pl.pallas_call(
        split_queries_kernel,
        out_shape=[jax.ShapeDtypeStruct((rows, width), queries.dtype)] * count,
        in_specs=[SMEM, HBM],
        out_specs=[HBM] * count,
        scratch_shapes=[
            pltpu.VMEM((count, rows, width), queries.dtype),
            pltpu.SemaphoreType.DMA((count,)),
            pltpu.SemaphoreType.DMA((count,)),
        ],
        cost_estimate=cost(0, 4 * queries.size),
    )(places, queries)


def join_outputs_kernel(offsets, places_ref, *refs):
    pieces, out_ref, sem = refs[:offsets], refs[offsets], refs[offsets + 1]
    width = pieces[0].shape[1]
    copies = []
    for i in range(offsets):
        start = pl.multiple_of(places_ref[i] * width, width)
        copies.append(pltpu.make_async_copy(pieces[i], out_ref.at[:, pl.ds(start, width)], sem.at[i]))
    for copy in copies:
        copy.start()
    for copy in copies:
        copy.wait()


def join_outputs(pieces, places):
    count = len(pieces)
    rows, width = pieces[0].shape
    return pl.pallas_call(
        functools.partial(join_outputs_kernel, count),
        out_shape=jax.ShapeDtypeStruct((rows, width * count), pieces[0].dtype),
        in_specs=[SMEM] + [VMEM] * count,
        out_specs=HBM,
        scratch_shapes=[pltpu.SemaphoreType.DMA((count,))],
        compiler_params=room(4),
        cost_estimate=cost(0, 4 * rows * width * count),
    )(places, *pieces)


def pack_kernel(chunks, wanted_ref, k_ref, v_ref, out_ref, buf, in_sem, out_sem):
    span = out_ref.shape[0] // chunks
    for chunk in range(chunks):

        def start(i, carry):
            rows = pl.ds(pl.multiple_of(wanted_ref[i] * BLK, BLK), BLK)
            pltpu.make_async_copy(k_ref.at[rows], buf.at[i, 0], in_sem.at[chunk]).start()
            pltpu.make_async_copy(v_ref.at[rows], buf.at[i, 1], in_sem.at[chunk]).start()
            return carry

        lax.fori_loop(chunk * span, (chunk + 1) * span, start, 0, unroll=True)
    copies = []
    for chunk in range(chunks):
        part = pl.ds(chunk * span, span)
        wait_for(buf.at[part], in_sem.at[chunk])
        copies.append(pltpu.make_async_copy(buf.at[part], out_ref.at[part], out_sem.at[chunk]))
        copies[-1].start()
    for copy in copies:
        copy.wait()


def pack(wanted, keys, values):
    count, chunks = wanted.shape[0], 4
    return pl.pallas_call(
        functools.partial(pack_kernel, chunks),
        out_shape=jax.ShapeDtypeStruct((count, 2, BLK, HD), keys.dtype),
        in_specs=[SMEM, HBM, HBM],
        out_specs=HBM,
        scratch_shapes=[
            pltpu.VMEM((count, 2, BLK, HD), keys.dtype),
            pltpu.SemaphoreType.DMA((chunks,)),
            pltpu.SemaphoreType.DMA((chunks,)),
        ],
        cost_estimate=cost(0, 8 * count * BLK * HD),
    )(wanted, keys, values)


def scores_of(keys, queries):
    return lax.dot_general(keys, queries, (((1,), (1,)), ((), ())), preferred_element_type=jnp.float32)


def weighted(values, weights):
    return lax.dot_general(values, weights, (((0,), (0,)), ((), ())), preferred_element_type=jnp.float32)


def near_kernel(ids_ref, core_ref, qa_ref, qb_ref, k_ref, v_ref, acc_out, stat_out, q_out, q_buf, k_buf, v_buf, acc_ref, stat_ref, q_ref, k_sem, v_sem, out_sem):
    blocks, picks, half = acc_ref.shape[0], k_buf.shape[1] // BLK, qa_ref.shape[0]
    ratio = q_buf.shape[1] // HD
    factor = HD ** (-0.5) * LOG2E
    core = core_ref[0]
    for i in range(blocks):
        for j in range(picks):
            held = pl.ds(pl.multiple_of(ids_ref[i * picks + j] * BLK, BLK), BLK)
            pltpu.make_async_copy(k_ref.at[held], k_buf.at[i, pl.ds(j * BLK, BLK)], k_sem.at[i]).start()
            pltpu.make_async_copy(v_ref.at[held], v_buf.at[i, pl.ds(j * BLK, BLK)], v_sem.at[i]).start()
    q_buf[pl.ds(pl.multiple_of(core * half, half), half), :] = qa_ref[...]
    q_buf[pl.ds(pl.multiple_of((1 - core) * half, half), half), :] = qb_ref[...]
    for i in range(blocks):
        for r in range(ratio):
            q_ref[i, r * BLK : (r + 1) * BLK, :] = q_buf[i * BLK : (i + 1) * BLK, r * HD : (r + 1) * HD]
    copies = [pltpu.make_async_copy(q_ref, q_out, out_sem.at[0])]
    copies[0].start()

    def block(i, carry):
        wait_for(k_buf.at[i], k_sem.at[i])
        wait_for(v_buf.at[i], v_sem.at[i])
        score = scores_of(k_buf[i], q_ref[i])
        highest = jnp.max(score, axis=0, keepdims=True) * factor
        exponent = jnp.exp2(score * factor - highest)
        stat_ref[i, 0:1, :] = highest
        stat_ref[i, 1:2, :] = jnp.sum(exponent, axis=0, keepdims=True)
        acc_ref[i] = weighted(v_buf[i], exponent.astype(jnp.bfloat16))
        return carry

    lax.fori_loop(0, blocks, block, 0)
    copies.append(pltpu.make_async_copy(acc_ref, acc_out, out_sem.at[1]))
    copies.append(pltpu.make_async_copy(stat_ref, stat_out, out_sem.at[2]))
    copies[1].start()
    copies[2].start()
    for copy in copies:
        copy.wait()


def near_attention(ids, core, qa, qb, keys, values):
    blocks, picks = ids.shape
    rows, width = 2 * qa.shape[0], qa.shape[1]
    span, wide = picks * BLK, BLK * (width // HD)
    work = rows * width * span
    kept = [((blocks, HD, wide), jnp.float32), ((blocks, 8, wide), jnp.float32), ((blocks, wide, HD), qa.dtype)]
    return pl.pallas_call(
        near_kernel,
        out_shape=[jax.ShapeDtypeStruct(*what) for what in kept],
        in_specs=[SMEM, SMEM, VMEM, VMEM, HBM, HBM],
        out_specs=[HBM] * 3,
        scratch_shapes=[
            pltpu.VMEM((rows, width), qa.dtype),
            pltpu.VMEM((blocks, span, HD), keys.dtype),
            pltpu.VMEM((blocks, span, HD), keys.dtype),
            *[pltpu.VMEM(*what) for what in kept],
            pltpu.SemaphoreType.DMA((blocks,)),
            pltpu.SemaphoreType.DMA((blocks,)),
            pltpu.SemaphoreType.DMA((3,)),
        ],
        cost_estimate=cost(4 * work, 8 * rows * width + 4 * blocks * span * HD, work // HD),
    )(ids.reshape(-1), core, qa, qb, keys, values)


def far_kernel(slots_ref, core_ref, got_ref, acc_in, stat_in, q_in, oa_ref, ob_ref, k_buf, v_buf, acc_ref, stat_ref, q_ref, o_buf, k_sem, v_sem, in_sem, out_sem):
    blocks, picks = k_buf.shape[0], k_buf.shape[1] // BLK
    half, ratio = oa_ref.shape[0], oa_ref.shape[1] // HD
    factor = HD ** (-0.5) * LOG2E
    core = core_ref[0]
    kept_copies = []
    for i in range(blocks):
        copy = pltpu.make_async_copy(q_in.at[i], q_ref.at[i], in_sem.at[i, 0])
        copy.start()
        for j in range(picks):
            slot = slots_ref[i * picks + j]
            pltpu.make_async_copy(got_ref.at[slot, 0], k_buf.at[i, pl.ds(j * BLK, BLK)], k_sem.at[i]).start()
            pltpu.make_async_copy(got_ref.at[slot, 1], v_buf.at[i, pl.ds(j * BLK, BLK)], v_sem.at[i]).start()
        stat_copy = pltpu.make_async_copy(stat_in.at[i], stat_ref.at[i], in_sem.at[i, 1])
        acc_copy = pltpu.make_async_copy(acc_in.at[i], acc_ref.at[i], in_sem.at[i, 2])
        stat_copy.start()
        acc_copy.start()
        kept_copies.append((copy, stat_copy, acc_copy))
    for i in range(blocks):
        wait_for(k_buf.at[i], k_sem.at[i])
        wait_for(v_buf.at[i], v_sem.at[i])
        for copy in kept_copies[i]:
            copy.wait()
        score = scores_of(k_buf[i], q_ref[i])
        before = stat_ref[i, 0:1, :]
        highest = jnp.maximum(jnp.max(score, axis=0, keepdims=True) * factor, before)
        exponent = jnp.exp2(score * factor - highest)
        kept = jnp.exp2(before - highest)
        total = jnp.sum(exponent, axis=0, keepdims=True) + kept * stat_ref[i, 1:2, :]
        partial = weighted(v_buf[i], exponent.astype(jnp.bfloat16))
        merged = (partial + kept * acc_ref[i]) * (1.0 / total)
        for r in range(ratio):
            columns = slice(r * BLK, (r + 1) * BLK)
            o_buf[i * BLK : (i + 1) * BLK, columns] = merged[:, columns].T.astype(o_buf.dtype)
    copies = []
    for i, (ref, place) in enumerate(((oa_ref, core), (ob_ref, 1 - core))):
        rows = pl.ds(pl.multiple_of(place * half, half), half)
        copies.append(pltpu.make_async_copy(o_buf.at[rows], ref, out_sem.at[i]))
    for copy in copies:
        copy.start()
    for copy in copies:
        copy.wait()


def far_attention(slots, core, got, acc, stats, q):
    blocks, picks = slots.shape
    rows, width = blocks * BLK, q.shape[1] // BLK * HD
    span = picks * BLK
    work = rows * width * span
    return pl.pallas_call(
        far_kernel,
        out_shape=[jax.ShapeDtypeStruct((rows // 2, width), q.dtype)] * 2,
        in_specs=[SMEM, SMEM, HBM, HBM, HBM, HBM],
        out_specs=[HBM, HBM],
        scratch_shapes=[
            pltpu.VMEM((blocks, span, HD), got.dtype),
            pltpu.VMEM((blocks, span, HD), got.dtype),
            pltpu.VMEM(acc.shape, acc.dtype),
            pltpu.VMEM(stats.shape, stats.dtype),
            pltpu.VMEM(q.shape, q.dtype),
            pltpu.VMEM((rows, width), q.dtype),
            pltpu.SemaphoreType.DMA((blocks,)),
            pltpu.SemaphoreType.DMA((blocks,)),
            pltpu.SemaphoreType.DMA((blocks, 3)),
            pltpu.SemaphoreType.DMA((2,)),
        ],
        cost_estimate=cost(4 * work, 8 * rows * width + 4 * blocks * span * HD, work // HD),
    )(slots.reshape(-1), core, got, acc, stats, q)


def offset_pairs(chips, chip_step, core_step):
    return [
        (chip * CORES + core, (chip + chip_step) % chips * CORES + (core ^ core_step))
        for chip in range(chips)
        for core in range(CORES)
    ]


def shards(queries, cache_keys, cache_values, block_ids):
    seq_count = lax.axis_size("seq")
    heads = lax.axis_size("head")
    seq_place = lax.axis_index("seq")
    head_place = lax.axis_index("head")
    chips = heads // CORES
    chip, core = head_place // CORES, head_place % CORES
    q_count, k_count = block_ids.shape[0], cache_keys.shape[0] // BLK
    per_chip = q_count // chips
    far_count = block_ids.shape[1] - NEAR
    capacity = max(2, (far_count * q_count + seq_count - 2) // (seq_count - 1))
    slot_total = seq_count * capacity

    far_ids = block_ids[:, NEAR:].reshape(-1)
    far_owner = far_ids // k_count
    far_within = far_ids - far_owner * k_count
    entry = jnp.arange(far_ids.shape[0], dtype=jnp.int32)
    earlier = (far_owner[:, None] == far_owner[None, :]) & (entry[None, :] < entry[:, None])
    far_slot = far_owner * capacity + jnp.sum(earlier.astype(jnp.int32), axis=1)
    placed = far_slot[:, None] == jnp.arange(slot_total, dtype=jnp.int32)[None, :]
    asked = jnp.sum(jnp.where(placed, far_within[:, None], 0), axis=0).reshape(seq_count, capacity)
    wanted = lax.all_to_all(asked, "seq", split_axis=0, concat_axis=0, tiled=True).reshape(-1)

    sent = pack(wanted, cache_keys, cache_values)
    got = lax.all_to_all(
        sent.reshape(seq_count, capacity, 2, BLK, HD), "seq", split_axis=0, concat_axis=0, tiled=True
    ).reshape(slot_total, 2, BLK, HD)

    steps = [(d, e) for d in range(chips) for e in range(CORES)]
    step_chip = jnp.array([d for d, _ in steps], jnp.int32)
    step_core = jnp.array([e for _, e in steps], jnp.int32)
    ahead = (chip + step_chip) % chips * CORES + (core + step_core) % CORES
    pieces = split_queries(queries, ahead)
    rows_of = {}
    for piece, (d, e) in zip(pieces, steps):
        rows_of[d, e] = piece if d == e == 0 else lax.ppermute(piece, "head", offset_pairs(chips, d, e))

    order = (chip - jnp.arange(chips, dtype=jnp.int32)) % chips
    near_ids = jnp.take((block_ids[:, :NEAR] - seq_place * k_count).reshape(chips, per_chip, NEAR), order, axis=0)
    slots = jnp.take(far_slot.reshape(chips, per_chip, far_count), order, axis=0)
    core_operand = core.astype(jnp.int32).reshape(1)

    near = [
        near_attention(near_ids[d], core_operand, rows_of[d, 0], rows_of[d, 1], cache_keys, cache_values)
        for d in range(chips)
    ]
    got, near = lax.optimization_barrier((got, near))
    results = {}
    for d in sorted(range(chips), key=lambda d: -min(d, chips - d)):
        made = far_attention(slots[d], core_operand, got, *near[d])
        for e in range(CORES):
            results[d, e] = made[e] if d == e == 0 else lax.ppermute(made[e], "head", offset_pairs(chips, -d, e))
    return join_outputs([results[step] for step in steps], ahead)


def solution(mesh):
    return jax.shard_map(
        shards,
        mesh=mesh,
        in_specs=(P(("seq", "head"), None), P("seq", "head"), P("seq", "head"), P("seq", None)),
        out_specs=P(("seq", "head"), None),
        check_vma=False,
    )
```

time: 359 us -> 177 us (0.49)
  Pallas kernels: 288 us -> 52.8 us
  waiting for transfers between devices: 11.2 us -> 63.1 us
    pallas_call x10, Pallas kernels: 239 us -> 51.1 us  [the longest x4 21.6 us: near_attention(): pl.pallas_call(near_kernel, out_shape=[jax.ShapeDtypeStruct(*what) for wh...]
    all_to_all x1, waiting for transfers between devices: 0.01 us -> 51.3 us  [shards(): lax.all_to_all(sent.reshape(seq_count, capacity, 2, BLK, HD), 'seq', spli...]
    pallas_call x1, Pallas kernels: 49.5 us -> 1.74 us  [join_outputs(): pl.pallas_call(functools.partial(join_outputs_kernel, count), out_shape=j...]
  transfers between devices with their start and end apart: 15 -> 15, of which waited for: 2 -> 5; matrix products, arithmetic and copies ran while one was open for 2% -> 4% of each run, Pallas kernels for 28% -> 22%
where the time goes in v2:
time: 177 us; the launch traced here: 176 us
  waiting for transfers between devices  63.1 us (36%)
  Pallas kernels  52.8 us (30%)
  starting transfers between devices  25.8 us (15%)
  blocking collectives  20.3 us (11%)
  local copies, waits for them, and re-layouts  12.1 us (7%)
    all_to_all x1, waiting for transfers between devices, shards(): lax.all_to_all(sent.reshape(seq_count, capacity, 2, BLK, HD), 'seq', spli...  51.3 us
    pallas_call x4, Pallas kernels, near_attention(): pl.pallas_call(near_kernel, out_shape=[jax.ShapeDtypeStruct(*what) for wh...  21.6 us
    all_to_all x1, blocking collectives, shards(): lax.all_to_all(asked, 'seq', split_axis=0, concat_axis=0, tiled=True)  20.3 us
    pallas_call x4, Pallas kernels, far_attention(): pl.pallas_call(far_kernel, out_shape=[jax.ShapeDtypeStruct((rows // 2, wi...  19.3 us
    ppermute x7, waiting for transfers between devices, shards(): lax.ppermute(made[e], 'head', offset_pairs(chips, -d, e))  11.8 us
    ppermute x7, starting transfers between devices, shards(): lax.ppermute(piece, 'head', offset_pairs(chips, d, e))  10.9 us
    ppermute x7, starting transfers between devices, shards(): lax.ppermute(made[e], 'head', offset_pairs(chips, -d, e))  9.85 us
    pallas_call x1, Pallas kernels, pack(): pl.pallas_call(functools.partial(pack_kernel, chunks), out_shape=jax.Shap...  7.2 us
  transfers between devices with their start and end apart: 15, of which 5 were waited for; matrix products, arithmetic and copies ran while one was open for 4% of the time, Pallas kernels for 22%

profile of v2, /device:TPU:1, one launch (start us, length us, event | category | flops | bytes accessed | tf_op | source)
XLA Modules:
  0.0 176.4 jit_solution(7852191406749419845)
XLA Ops:
  0.0 0.7 slice.30
  0.7 0.1 copy.34
  0.8 0.1 reshape.166
  0.9 0.2 convert_reduce_fusion
  1.1 0.1 select_reduce_fusion
  1.2 0.1 all_to_all.9
  1.3 20.3 %all_to_all.14 = s32[32,1,2]{2,1,0:T(1,128)S(1)} all-to-all(s32[32,1,2]{2,1,0:T(1,128)S(1)} %bitcast.11), channel_id=1, replica_groups=mesh['seq'=32,'head'=8] {'seq'}, dimensions={0} | all-to-all | bytes 512 | tf_op jit(solution)/shard_map/all_to_all | solution.py:301
  21.6 0.5 broadcast.249
  22.1 0.7 reduce.3
  22.8 0.6 reshape.168.wanted_ref
  23.4 7.2 %shard_map.64 = bf16[64,2,128,128]{3,2,1,0:T(8,128)(2,1)} custom-call(s32[64]{0:T(128)} %reshape.168.wanted_ref, bf16[8192,128]{1,0:T(8,128)(2,1)} %k_ref.9, bf16[8192,128]{1,0:T(8,128)(2,1)} %v_ref.9), custom_call_target="tpu_custom_call" | custom-call | bytes 8388608 | tf_op jit(solution)/shard_map/pallas_call | solution.py:118
  30.6 0.0 copy-start.11
  30.7 5.0 %all-to-all-start.1 = ((bf16[32,2,2,128,128]{4,3,2,1,0:T(8,128)(2,1)}), bf16[32,2,2,128,128]{4,3,2,1,0:T(8,128)(2,1)}, u32[]{:S(2)}, u32[]{:S(2)}) async-start(bf16[32,2,2,128,128]{4,3,2,1,0:T(8,128)(2,1)} %bitcast.10), calls=%async_computation.1 | async-start | bytes 8388608 | tf_op jit(solution)/shard_map/all_to_all | solution.py:304
  35.7 0.6 fusion.5.places_ref
  36.3 3.0 %shard_map.65 = (bf16[192,512]{1,0:T(8,128)(2,1)}, bf16[192,512]{1,0:T(8,128)(2,1)}, bf16[192,512]{1,0:T(8,128)(2,1)}, bf16[192,512]{1,0:T(8,128)(2,1)}, bf16[19...) custom-call(s32[8]{0:T(128)} %fusion.5.places_ref, ...), custom_call_target="tpu_custom_call" | custom-call | bytes 3145728 | tf_op jit(solution)/shard_map/pallas_call | solution.py:54
  39.2 2.2 %collective-permute-start = (bf16[192,512]{1,0:T(8,128)(2,1)}, bf16[192,512]{1,0:T(8,128)(2,1)S(1)}, u32[]{:S(2)}, u32[]{:S(2)}) collective-permute-start(bf16[192,512]{1,0:T(8,128)(2,1)} %get-tuple-element.47), channel_id=1, source_target_pairs={{0,1},{1,0},{2,3},{3,2},{4,5},{5,4},{6,7},{7,6},{8,9},{9,8},{10,11... | collective-permute-start | bytes 589832 | tf_op jit(solution)/shard_map/ppermute | solution.py:315
  41.4 1.3 collective-permute-start.1
  42.7 1.5 collective-permute-start.2
  44.3 1.3 collective-permute-start.3
  45.6 2.0 %collective-permute-start.4 = (bf16[192,512]{1,0:T(8,128)(2,1)}, bf16[192,512]{1,0:T(8,128)(2,1)S(1)}, u32[]{:S(2)}, u32[]{:S(2)}) collective-permute-start(bf16[192,512]{1,0:T(8,128)(2,1)} %get-tuple-element.57), channel_id=1, source_target_pairs={{0,5},{1,4},{2,7},{3,6},{4,1},{5,0},{6,3},{7,2},{8,13},{9,12},{10,... | collective-permute-start | bytes 589832 | tf_op jit(solution)/shard_map/ppermute | solution.py:315
  47.6 0.1 reduce_sum.21
  47.7 0.1 reshape.165
  47.8 0.1 copy.30
  47.9 0.1 reshape.171
  48.0 0.1 copy.36
  48.1 0.6 gather_fusion
  48.7 0.6 gather_fusion.1
  49.3 0.1 broadcast_select_fusion.1
  49.4 0.1 broadcast_select_fusion
  49.5 1.5 collective-permute-start.5
  50.9 1.1 collective-permute-start.6
  52.1 0.6 reshape_squeeze.24.slots_ref
  52.7 0.6 reshape_squeeze.25.ids_ref
  53.3 0.6 reshape_squeeze.26.ids_ref
  54.0 0.6 reshape_squeeze.27.ids_ref
  54.6 0.7 reshape_squeeze.28.ids_ref
  55.2 0.6 reshape_squeeze.29.slots_ref
  55.8 5.4 %shard_map.66 = (f32[3,128,512]{2,1,0:T(8,128)}, f32[3,8,512]{2,1,0:T(8,128)}, bf16[3,512,128]{2,1,0:T(8,128)(2,1)}) custom-call(s32[15]{0:T(128)} %reshape_squeeze.25.ids_ref, s32[1]{0:T(128)} %bitcast.1.core_ref, bf16[192,512]{1,0:T(8,128)(2,1)} %get-tuple-element.46.qa_ref, bf16[192,512]{1,0:T(8,128)(2,1)} %copy-done.6, bf16[8192,128]{1,0:T(8,128)(2,1)} %k_ref.9, ...), custom_call_target="tpu_custom_call" | custom-call | flops 503316480 | bytes 2555904 | tf_op jit(solution)/shard_map/pallas_call | solution.py:184
  61.2 0.7 copy-done.5
  61.9 5.5 %shard_map.67 = (f32[3,128,512]{2,1,0:T(8,128)}, f32[3,8,512]{2,1,0:T(8,128)}, bf16[3,512,128]{2,1,0:T(8,128)(2,1)}) custom-call(s32[15]{0:T(128)} %reshape_squeeze.26.ids_ref, s32[1]{0:T(128)} %bitcast.1.core_ref, bf16[192,512]{1,0:T(8,128)(2,1)} %copy-done.4, bf16[192,512]{1,0:T(8,128)(2,1)} %copy-done.5, bf16[8192,128]{1,0:T(8,128)(2,1)} %k_ref.9, ...), custom_call_target="tpu_custom_call" | custom-call | flops 503316480 | bytes 2555904 | tf_op jit(solution)/shard_map/pallas_call | solution.py:184
  67.4 0.7 copy-done.2
  68.0 0.7 copy-done.3
  68.7 5.4 %shard_map.68 = (f32[3,128,512]{2,1,0:T(8,128)}, f32[3,8,512]{2,1,0:T(8,128)}, bf16[3,512,128]{2,1,0:T(8,128)(2,1)}) custom-call(s32[15]{0:T(128)} %reshape_squeeze.27.ids_ref, s32[1]{0:T(128)} %bitcast.1.core_ref, bf16[192,512]{1,0:T(8,128)(2,1)} %copy-done.2, bf16[192,512]{1,0:T(8,128)(2,1)} %copy-done.3, bf16[8192,128]{1,0:T(8,128)(2,1)} %k_ref.9, ...), custom_call_target="tpu_custom_call" | custom-call | flops 503316480 | bytes 2555904 | tf_op jit(solution)/shard_map/pallas_call | solution.py:184
  74.2 0.7 copy-done.7
  74.8 0.7 copy-done.8
  75.5 5.4 %shard_map.69 = (f32[3,128,512]{2,1,0:T(8,128)}, f32[3,8,512]{2,1,0:T(8,128)}, bf16[3,512,128]{2,1,0:T(8,128)(2,1)}) custom-call(s32[15]{0:T(128)} %reshape_squeeze.28.ids_ref, s32[1]{0:T(128)} %bitcast.1.core_ref, bf16[192,512]{1,0:T(8,128)(2,1)} %copy-done.7, bf16[192,512]{1,0:T(8,128)(2,1)} %copy-done.8, bf16[8192,128]{1,0:T(8,128)(2,1)} %k_ref.9, ...), custom_call_target="tpu_custom_call" | custom-call | flops 503316480 | bytes 2555904 | tf_op jit(solution)/shard_map/pallas_call | solution.py:184
  80.9 51.3 %all-to-all-done.1 = bf16[32,2,2,128,128]{4,3,2,1,0:T(8,128)(2,1)} async-done(((bf16[32,2,2,128,128]{4,3,2,1,0:T(8,128)(2,1)}), bf16[32,2,2,128,128]{4,3,2,1,0:T(8,128)(2,1)}, u32[]{:S(2)}, u32[]{:S(2)}) %all-to-all-start.1) | async-done | bytes 4194336 | tf_op jit(solution)/shard_map/all_to_all | solution.py:304
  132.2 4.8 %shard_map.70 = (bf16[192,512]{1,0:T(8,128)(2,1)}, bf16[192,512]{1,0:T(8,128)(2,1)}) custom-call(s32[9]{0:T(128)} %reshape_squeeze.24.slots_ref, s32[1]{0:T(128)} %bitcast.1.core_ref, bf16[64,2,128,128]{3,2,1,0:T(8,128)(2,1)} %bitcast.4.got_ref, f32[3,128,512]{2,1,0:T(8,128)} %get-tuple-element.67.acc_in, f32[3,8,512]{2,1,0:T(8,128)} %get-tuple-element.68.stat_in, ...), custom_call_target="tpu_custom_call" | custom-call | flops 301989888 | bytes 2162688 | tf_op jit(solution)/shard_map/pallas_call | solution.py:251
  137.1 1.8 %collective-permute-start.7 = (bf16[192,512]{1,0:T(8,128)(2,1)}, bf16[192,512]{1,0:T(8,128)(2,1)S(1)}, u32[]{:S(2)}, u32[]{:S(2)}) collective-permute-start(bf16[192,512]{1,0:T(8,128)(2,1)} %get-tuple-element.71), channel_id=1, source_target_pairs={{0,1},{1,0},{2,3},{3,2},{4,5},{5,4},{6,7},{7,6},{8,9},{9,8},{10,11... | collective-permute-start | bytes 589832 | tf_op jit(solution)/shard_map/ppermute | solution.py:331
  138.9 4.8 %shard_map.71 = (bf16[192,512]{1,0:T(8,128)(2,1)}, bf16[192,512]{1,0:T(8,128)(2,1)}) custom-call(s32[9]{0:T(128)} %reshape_squeeze.29.slots_ref, s32[1]{0:T(128)} %bitcast.1.core_ref, bf16[64,2,128,128]{3,2,1,0:T(8,128)(2,1)} %bitcast.4.got_ref, f32[3,128,512]{2,1,0:T(8,128)} %get-tuple-element.72.acc_in, f32[3,8,512]{2,1,0:T(8,128)} %get-tuple-element.73.stat_in, ...), custom_call_target="tpu_custom_call" | custom-call | flops 301989888 | bytes 2162688 | tf_op jit(solution)/shard_map/pallas_call | solution.py:251
  143.7 2.8 %collective-permute-start.8 = (bf16[192,512]{1,0:T(8,128)(2,1)}, bf16[192,512]{1,0:T(8,128)(2,1)S(1)}, u32[]{:S(2)}, u32[]{:S(2)}) collective-permute-start(bf16[192,512]{1,0:T(8,128)(2,1)} %get-tuple-element.75), channel_id=1, source_target_pairs={{0,6},{1,7},{2,0},{3,1},{4,2},{5,3},{6,4},{7,5},{8,14},{9,15},{10,... | collective-permute-start | bytes 589832 | tf_op jit(solution)/shard_map/ppermute | solution.py:331
  146.5 0.6 reshape_squeeze.30.slots_ref
  147.1 0.7 reshape_squeeze.31.slots_ref
  147.8 0.6 collective-permute-start.9
  148.5 4.8 %shard_map.72 = (bf16[192,512]{1,0:T(8,128)(2,1)}, bf16[192,512]{1,0:T(8,128)(2,1)}) custom-call(s32[9]{0:T(128)} %reshape_squeeze.30.slots_ref, s32[1]{0:T(128)} %bitcast.1.core_ref, bf16[64,2,128,128]{3,2,1,0:T(8,128)(2,1)} %bitcast.4.got_ref, f32[3,128,512]{2,1,0:T(8,128)} %get-tuple-element.77.acc_in, f32[3,8,512]{2,1,0:T(8,128)} %get-tuple-element.78.stat_in, ...), custom_call_target="tpu_custom_call" | custom-call | flops 301989888 | bytes 2162688 | tf_op jit(solution)/shard_map/pallas_call | solution.py:251
  153.3 0.1 collective-permute-start.10
  153.4 3.3 %collective-permute-start.11 = (bf16[192,512]{1,0:T(8,128)(2,1)}, bf16[192,512]{1,0:T(8,128)(2,1)S(1)}, u32[]{:S(2)}, u32[]{:S(2)}) collective-permute-start(bf16[192,512]{1,0:T(8,128)(2,1)} %get-tuple-element.81), channel_id=1, source_target_pairs={{0,5},{1,4},{2,7},{3,6},{4,1},{5,0},{6,3},{7,2},{8,13},{9,12},{10,... | collective-permute-start | bytes 589832 | tf_op jit(solution)/shard_map/ppermute | solution.py:331
  156.7 4.8 %shard_map.73 = (bf16[192,512]{1,0:T(8,128)(2,1)}, bf16[192,512]{1,0:T(8,128)(2,1)}) custom-call(s32[9]{0:T(128)} %reshape_squeeze.31.slots_ref, s32[1]{0:T(128)} %bitcast.1.core_ref, bf16[64,2,128,128]{3,2,1,0:T(8,128)(2,1)} %bitcast.4.got_ref, f32[3,128,512]{2,1,0:T(8,128)} %get-tuple-element.82.acc_in, f32[3,8,512]{2,1,0:T(8,128)} %get-tuple-element.83.stat_in, ...), custom_call_target="tpu_custom_call" | custom-call | flops 301989888 | bytes 2162688 | tf_op jit(solution)/shard_map/pallas_call | solution.py:251
  161.6 1.1 collective-permute-start.12
  162.7 1.0 collective-permute-done.9.refs_3_
  163.7 2.9 %collective-permute-done.11.refs_5_ = bf16[192,512]{1,0:T(8,128)(2,1)S(1)} collective-permute-done((bf16[192,512]{1,0:T(8,128)(2,1)}, bf16[192,512]{1,0:T(8,128)(2,1)S(1)}, u32[]{:S(2)}, u32[]{:S(2)}) %collective-permute-start.11) | collective-permute-done | bytes 196640 | tf_op jit(solution)/shard_map/ppermute | solution.py:331
  166.5 3.7 %collective-permute-done.12.refs_6_ = bf16[192,512]{1,0:T(8,128)(2,1)S(1)} collective-permute-done((bf16[192,512]{1,0:T(8,128)(2,1)}, bf16[192,512]{1,0:T(8,128)(2,1)S(1)}, u32[]{:S(2)}, u32[]{:S(2)}) %collective-permute-start.12) | collective-permute-done | bytes 196640 | tf_op jit(solution)/shard_map/ppermute | solution.py:331
  170.3 4.2 %collective-permute-done.13.refs_7_ = bf16[192,512]{1,0:T(8,128)(2,1)S(1)} collective-permute-done((bf16[192,512]{1,0:T(8,128)(2,1)}, bf16[192,512]{1,0:T(8,128)(2,1)S(1)}, u32[]{:S(2)}, u32[]{:S(2)}) %collective-permute-start.13) | collective-permute-done | bytes 196640 | tf_op jit(solution)/shard_map/ppermute | solution.py:331
  174.5 1.7 shard_map.74
  (38 shorter events, 0.2 us)
Async XLA Ops:
  30.6 5.1 %copy-start.10 = (s32[8]{0:T(128)S(1)}, s32[8]{0:T(128)}, u32[]{:S(2)}) copy-start(s32[8]{0:T(128)} %constant.109.clone) | copy-start | bytes 100
  30.6 5.1 %copy-start.11 = (s32[8]{0:T(128)S(1)}, s32[8]{0:T(128)}, u32[]{:S(2)}) copy-start(s32[8]{0:T(128)} %constant.110.clone) | copy-start | bytes 100
  30.6 17.2 %copy-start.9 = (s32[12,8]{0,1:T(8,128)S(1)}, s32[12,8]{0,1:T(8,128)}, u32[]{:S(2)}) copy-start(s32[12,8]{0,1:T(8,128)} %param.9) | copy-start | bytes 1156
  30.7 101.6 %all-to-all-start.1 = ((bf16[32,2,2,128,128]{4,3,2,1,0:T(8,128)(2,1)}), bf16[32,2,2,128,128]{4,3,2,1,0:T(8,128)(2,1)}, u32[]{:S(2)}, u32[]{:S(2)}) async-start(bf16[32,2,2,128,128]{4,3,2,1,0:T(8,128)(2,1)} %bitcast.10), calls=%async_computation.1 | async-start | bytes 8388608 | tf_op jit(solution)/shard_map/all_to_all | solution.py:304
  39.2 10.2 %collective-permute-start = (bf16[192,512]{1,0:T(8,128)(2,1)}, bf16[192,512]{1,0:T(8,128)(2,1)S(1)}, u32[]{:S(2)}, u32[]{:S(2)}) collective-permute-start(bf16[192,512]{1,0:T(8,128)(2,1)} %get-tuple-element.47), channel_id=1, source_target_pairs={{0,1},{1,0},{2,3},{3,2},{4,5},{5,4},{6,7},{7,6},{8,9},{9,8},{10,11... | collective-permute-start | bytes 589832 | tf_op jit(solution)/shard_map/ppermute | solution.py:315
  41.4 9.5 %collective-permute-start.1 = (bf16[192,512]{1,0:T(8,128)(2,1)}, bf16[192,512]{1,0:T(8,128)(2,1)S(1)}, u32[]{:S(2)}, u32[]{:S(2)}) collective-permute-start(bf16[192,512]{1,0:T(8,128)(2,1)} %get-tuple-element.51), channel_id=1, source_target_pairs={{0,2},{1,3},{2,4},{3,5},{4,6},{5,7},{6,0},{7,1},{8,10},{9,11},{10,... | collective-permute-start | bytes 589832 | tf_op jit(solution)/shard_map/ppermute | solution.py:315
  42.7 18.4 %collective-permute-start.2 = (bf16[192,512]{1,0:T(8,128)(2,1)}, bf16[192,512]{1,0:T(8,128)(2,1)S(1)}, u32[]{:S(2)}, u32[]{:S(2)}) collective-permute-start(bf16[192,512]{1,0:T(8,128)(2,1)} %get-tuple-element.52), channel_id=1, source_target_pairs={{0,3},{1,2},{2,5},{3,4},{4,7},{5,6},{6,1},{7,0},{8,11},{9,10},{10,... | collective-permute-start | bytes 589832 | tf_op jit(solution)/shard_map/ppermute | solution.py:315
  44.3 23.1 %collective-permute-start.3 = (bf16[192,512]{1,0:T(8,128)(2,1)}, bf16[192,512]{1,0:T(8,128)(2,1)S(1)}, u32[]{:S(2)}, u32[]{:S(2)}) collective-permute-start(bf16[192,512]{1,0:T(8,128)(2,1)} %get-tuple-element.56), channel_id=1, source_target_pairs={{0,4},{1,5},{2,6},{3,7},{4,0},{5,1},{6,2},{7,3},{8,12},{9,13},{10,... | collective-permute-start | bytes 589832 | tf_op jit(solution)/shard_map/ppermute | solution.py:315
  45.6 21.8 %collective-permute-start.4 = (bf16[192,512]{1,0:T(8,128)(2,1)}, bf16[192,512]{1,0:T(8,128)(2,1)S(1)}, u32[]{:S(2)}, u32[]{:S(2)}) collective-permute-start(bf16[192,512]{1,0:T(8,128)(2,1)} %get-tuple-element.57), channel_id=1, source_target_pairs={{0,5},{1,4},{2,7},{3,6},{4,1},{5,0},{6,3},{7,2},{8,13},{9,12},{10,... | collective-permute-start | bytes 589832 | tf_op jit(solution)/shard_map/ppermute | solution.py:315
  49.5 6.3 %copy-start.6 = (bf16[192,512]{1,0:T(8,128)(2,1)}, bf16[192,512]{1,0:T(8,128)(2,1)S(1)}, u32[]{:S(2)}) copy-start(bf16[192,512]{1,0:T(8,128)(2,1)S(1)} %collective-permute-done.qb_ref) | copy-start | bytes 589828
  49.5 24.7 %collective-permute-start.5 = (bf16[192,512]{1,0:T(8,128)(2,1)}, bf16[192,512]{1,0:T(8,128)(2,1)S(1)}, u32[]{:S(2)}, u32[]{:S(2)}) collective-permute-start(bf16[192,512]{1,0:T(8,128)(2,1)} %get-tuple-element.61), channel_id=1, source_target_pairs={{0,6},{1,7},{2,0},{3,1},{4,2},{5,3},{6,4},{7,5},{8,14},{9,15},{10,... | collective-permute-start | bytes 589832 | tf_op jit(solution)/shard_map/ppermute | solution.py:315
  50.9 10.3 %copy-start.4 = (bf16[192,512]{1,0:T(8,128)(2,1)}, bf16[192,512]{1,0:T(8,128)(2,1)S(1)}, u32[]{:S(2)}) copy-start(bf16[192,512]{1,0:T(8,128)(2,1)S(1)} %collective-permute-done.1.qa_ref) | copy-start | bytes 589828
  50.9 23.2 %collective-permute-start.6 = (bf16[192,512]{1,0:T(8,128)(2,1)}, bf16[192,512]{1,0:T(8,128)(2,1)S(1)}, u32[]{:S(2)}, u32[]{:S(2)}) collective-permute-start(bf16[192,512]{1,0:T(8,128)(2,1)} %get-tuple-element.62), channel_id=1, source_target_pairs={{0,7},{1,6},{2,1},{3,0},{4,3},{5,2},{6,5},{7,4},{8,15},{9,14},{10,... | collective-permute-start | bytes 589832 | tf_op jit(solution)/shard_map/ppermute | solution.py:315
  61.2 0.7 copy-start.5
  67.4 0.7 copy-start.2
  68.0 0.7 copy-start.3
  74.1 0.7 copy-start.7
  74.8 0.7 copy-start.8
  137.1 24.5 %collective-permute-start.7 = (bf16[192,512]{1,0:T(8,128)(2,1)}, bf16[192,512]{1,0:T(8,128)(2,1)S(1)}, u32[]{:S(2)}, u32[]{:S(2)}) collective-permute-start(bf16[192,512]{1,0:T(8,128)(2,1)} %get-tuple-element.71), channel_id=1, source_target_pairs={{0,1},{1,0},{2,3},{3,2},{4,5},{5,4},{6,7},{7,6},{8,9},{9,8},{10,11... | collective-permute-start | bytes 589832 | tf_op jit(solution)/shard_map/ppermute | solution.py:331
  143.7 19.0 %collective-permute-start.8 = (bf16[192,512]{1,0:T(8,128)(2,1)}, bf16[192,512]{1,0:T(8,128)(2,1)S(1)}, u32[]{:S(2)}, u32[]{:S(2)}) collective-permute-start(bf16[192,512]{1,0:T(8,128)(2,1)} %get-tuple-element.75), channel_id=1, source_target_pairs={{0,6},{1,7},{2,0},{3,1},{4,2},{5,3},{6,4},{7,5},{8,14},{9,15},{10,... | collective-permute-start | bytes 589832 | tf_op jit(solution)/shard_map/ppermute | solution.py:331
  147.8 15.9 %collective-permute-start.9 = (bf16[192,512]{1,0:T(8,128)(2,1)}, bf16[192,512]{1,0:T(8,128)(2,1)S(1)}, u32[]{:S(2)}, u32[]{:S(2)}) collective-permute-start(bf16[192,512]{1,0:T(8,128)(2,1)} %get-tuple-element.76), channel_id=1, source_target_pairs={{0,7},{1,6},{2,1},{3,0},{4,3},{5,2},{6,5},{7,4},{8,15},{9,14},{10,... | collective-permute-start | bytes 589832 | tf_op jit(solution)/shard_map/ppermute | solution.py:331
  153.3 10.4 %collective-permute-start.10 = (bf16[192,512]{1,0:T(8,128)(2,1)}, bf16[192,512]{1,0:T(8,128)(2,1)S(1)}, u32[]{:S(2)}, u32[]{:S(2)}) collective-permute-start(bf16[192,512]{1,0:T(8,128)(2,1)} %get-tuple-element.80), channel_id=1, source_target_pairs={{0,4},{1,5},{2,6},{3,7},{4,0},{5,1},{6,2},{7,3},{8,12},{9,13},{10,... | collective-permute-start | bytes 589832 | tf_op jit(solution)/shard_map/ppermute | solution.py:331
  153.4 21.1 %copy-start = (bf16[192,512]{1,0:T(8,128)(2,1)S(1)}, bf16[192,512]{1,0:T(8,128)(2,1)}, u32[]{:S(2)}) copy-start(bf16[192,512]{1,0:T(8,128)(2,1)} %get-tuple-element.70.refs_0_) | copy-start | bytes 589828
  153.4 21.1 %copy-start.1 = (s32[8]{0:T(128)S(1)}, s32[8]{0:T(128)}, u32[]{:S(2)}) copy-start(s32[8]{0:T(128)} %fusion.5.places_ref) | copy-start | bytes 100
  153.4 13.1 %collective-permute-start.11 = (bf16[192,512]{1,0:T(8,128)(2,1)}, bf16[192,512]{1,0:T(8,128)(2,1)S(1)}, u32[]{:S(2)}, u32[]{:S(2)}) collective-permute-start(bf16[192,512]{1,0:T(8,128)(2,1)} %get-tuple-element.81), channel_id=1, source_target_pairs={{0,5},{1,4},{2,7},{3,6},{4,1},{5,0},{6,3},{7,2},{8,13},{9,12},{10,... | collective-permute-start | bytes 589832 | tf_op jit(solution)/shard_map/ppermute | solution.py:331
  161.6 8.7 %collective-permute-start.12 = (bf16[192,512]{1,0:T(8,128)(2,1)}, bf16[192,512]{1,0:T(8,128)(2,1)S(1)}, u32[]{:S(2)}, u32[]{:S(2)}) collective-permute-start(bf16[192,512]{1,0:T(8,128)(2,1)} %get-tuple-element.85), channel_id=1, source_target_pairs={{0,2},{1,3},{2,4},{3,5},{4,6},{5,7},{6,0},{7,1},{8,10},{9,11},{10,... | collective-permute-start | bytes 589832 | tf_op jit(solution)/shard_map/ppermute | solution.py:331
  162.7 11.8 %collective-permute-start.13 = (bf16[192,512]{1,0:T(8,128)(2,1)}, bf16[192,512]{1,0:T(8,128)(2,1)S(1)}, u32[]{:S(2)}, u32[]{:S(2)}) collective-permute-start(bf16[192,512]{1,0:T(8,128)(2,1)} %get-tuple-element.86), channel_id=1, source_target_pairs={{0,3},{1,2},{2,5},{3,4},{4,7},{5,6},{6,1},{7,0},{8,11},{9,10},{10,... | collective-permute-start | bytes 589832 | tf_op jit(solution)/shard_map/ppermute | solution.py:331

commit v3 on v2

v3 whole, which is shorter than its diff:
```python
import functools

import jax
import jax.numpy as jnp
from jax import lax
from jax.experimental import pallas as pl
from jax.experimental.pallas import tpu as pltpu
from jax.sharding import PartitionSpec as P

HD = 128
BLK = 128
NEAR = 5
CORES = 2
HBM = pl.BlockSpec(memory_space=pltpu.HBM)
SMEM = pl.BlockSpec(memory_space=pltpu.SMEM)
VMEM = pl.BlockSpec(memory_space=pltpu.VMEM)
LOG2E = 1.4426950408889634


def wait_for(ref, sem):
    pltpu.make_async_copy(ref, ref, sem).wait()


def room(mebibytes):
    return pltpu.CompilerParams(vmem_limit_bytes=mebibytes * 1024 * 1024)


def cost(flops, bytes_accessed, transcendentals=0):
    return pl.CostEstimate(flops=flops, bytes_accessed=bytes_accessed, transcendentals=transcendentals)


def split_queries_kernel(places_ref, q_ref, *refs):
    count = len(refs) - 3
    outs, buf, in_sem, out_sem = refs[:count], *refs[count:]
    width = buf.shape[2]
    into, out_of = [], []
    for i in range(count):
        start = pl.multiple_of(places_ref[i] * width, width)
        into.append(pltpu.make_async_copy(q_ref.at[:, pl.ds(start, width)], buf.at[i], in_sem.at[i]))
        out_of.append(pltpu.make_async_copy(buf.at[i], outs[i], out_sem.at[i]))
    for copy in into:
        copy.start()
    for i in range(count):
        into[i].wait()
        out_of[i].start()
    for copy in out_of:
        copy.wait()


def split_queries(queries, places):
    count = places.shape[0]
    rows, width = queries.shape[0], queries.shape[1] // count
    return pl.pallas_call(
        split_queries_kernel,
        out_shape=[jax.ShapeDtypeStruct((rows, width), queries.dtype)] * count,
        in_specs=[SMEM, HBM],
        out_specs=[HBM] * count,
        scratch_shapes=[
            pltpu.VMEM((count, rows, width), queries.dtype),
            pltpu.SemaphoreType.DMA((count,)),
            pltpu.SemaphoreType.DMA((count,)),
        ],
        cost_estimate=cost(0, 4 * queries.size),
    )(places, queries)


def join_outputs_kernel(places_ref, *refs):
    count = len(refs) - 2
    pieces, out_ref, sem = refs[:count], refs[count], refs[count + 1]
    width = pieces[0].shape[2]
    copies = []
    for i in range(count):
        start = pl.multiple_of(places_ref[i] * width, width)
        copies.append(pltpu.make_async_copy(pieces[i].at[i % CORES], out_ref.at[:, pl.ds(start, width)], sem.at[i]))
    for copy in copies:
        copy.start()
    for copy in copies:
        copy.wait()


def join_outputs(pieces, places):
    count = len(pieces)
    _, rows, width = pieces[0].shape
    return pl.pallas_call(
        join_outputs_kernel,
        out_shape=jax.ShapeDtypeStruct((rows, width * count), pieces[0].dtype),
        in_specs=[SMEM] + [VMEM] * count,
        out_specs=HBM,
        scratch_shapes=[pltpu.SemaphoreType.DMA((count,))],
        compiler_params=room(6),
        cost_estimate=cost(0, 4 * rows * width * count),
    )(places, *pieces)


def pack_kernel(chunks, ahead, wanted_ref, k_ref, v_ref, out_ref, buf, in_sem, out_sem):
    span, capacity = out_ref.shape[0] // chunks, wanted_ref.shape[2]

    def fetch(chunk):
        for i in range(chunk * span, (chunk + 1) * span):
            rows = pl.ds(pl.multiple_of(wanted_ref[i // capacity, 0, i % capacity] * BLK, BLK), BLK)
            pltpu.make_async_copy(k_ref.at[rows], buf.at[i, 0], in_sem.at[chunk]).start()
            pltpu.make_async_copy(v_ref.at[rows], buf.at[i, 1], in_sem.at[chunk]).start()

    copies = []
    for chunk in range(min(ahead, chunks)):
        fetch(chunk)
    for chunk in range(chunks):
        part = pl.ds(chunk * span, span)
        wait_for(buf.at[part], in_sem.at[chunk])
        copies.append(pltpu.make_async_copy(buf.at[part], out_ref.at[part], out_sem.at[chunk]))
        copies[-1].start()
        if chunk + ahead < chunks:
            fetch(chunk + ahead)
    for copy in copies:
        copy.wait()


def pack(wanted, keys, values, chunks=8, ahead=2):
    count = wanted.shape[0] * wanted.shape[2]
    return pl.pallas_call(
        functools.partial(pack_kernel, chunks, ahead),
        out_shape=jax.ShapeDtypeStruct((count, 2, BLK, HD), keys.dtype),
        in_specs=[SMEM, HBM, HBM],
        out_specs=HBM,
        scratch_shapes=[
            pltpu.VMEM((count, 2, BLK, HD), keys.dtype),
            pltpu.SemaphoreType.DMA((chunks,)),
            pltpu.SemaphoreType.DMA((chunks,)),
        ],
        cost_estimate=cost(0, 8 * count * BLK * HD),
    )(wanted, keys, values)


def scores_of(keys, queries):
    return lax.dot_general(keys, queries, (((1,), (1,)), ((), ())), preferred_element_type=jnp.float32)


def weighted(values, weights):
    return lax.dot_general(values, weights, (((0,), (0,)), ((), ())), preferred_element_type=jnp.float32)


def near_kernel(first, ids_ref, core_ref, qa_ref, qb_ref, k_ref, v_ref, acc_out, stat_out, q_out, q_buf, k_buf, v_buf, acc_ref, stat_ref, q_ref, k_sem, v_sem, out_sem):
    blocks, picks, half = acc_ref.shape[0], k_buf.shape[1] // BLK, qa_ref.shape[0]
    ratio = q_buf.shape[1] // HD
    factor = HD ** (-0.5) * LOG2E
    core = core_ref[0]
    for i in range(blocks):
        for j in range(picks):
            held = pl.ds(pl.multiple_of(ids_ref[first + i, j] * BLK, BLK), BLK)
            pltpu.make_async_copy(k_ref.at[held], k_buf.at[i, pl.ds(j * BLK, BLK)], k_sem.at[i]).start()
            pltpu.make_async_copy(v_ref.at[held], v_buf.at[i, pl.ds(j * BLK, BLK)], v_sem.at[i]).start()
    q_buf[pl.ds(pl.multiple_of(core * half, half), half), :] = qa_ref[...]
    q_buf[pl.ds(pl.multiple_of((1 - core) * half, half), half), :] = qb_ref[...]
    for i in range(blocks):
        for r in range(ratio):
            q_ref[i, r * BLK : (r + 1) * BLK, :] = q_buf[i * BLK : (i + 1) * BLK, r * HD : (r + 1) * HD]
    copies = [pltpu.make_async_copy(q_ref, q_out, out_sem.at[0])]
    copies[0].start()

    def block(i, carry):
        wait_for(k_buf.at[i], k_sem.at[i])
        wait_for(v_buf.at[i], v_sem.at[i])
        score = scores_of(k_buf[i], q_ref[i])
        highest = jnp.max(score, axis=0, keepdims=True) * factor
        exponent = jnp.exp2(score * factor - highest)
        stat_ref[i, 0:1, :] = highest
        stat_ref[i, 1:2, :] = jnp.sum(exponent, axis=0, keepdims=True)
        acc_ref[i] = weighted(v_buf[i], exponent.astype(jnp.bfloat16))
        return carry

    lax.fori_loop(0, blocks, block, 0)
    copies.append(pltpu.make_async_copy(acc_ref, acc_out, out_sem.at[1]))
    copies.append(pltpu.make_async_copy(stat_ref, stat_out, out_sem.at[2]))
    copies[1].start()
    copies[2].start()
    for copy in copies:
        copy.wait()


def near_attention(ids, first, core, qa, qb, keys, values):
    picks = ids.shape[1]
    rows, width = 2 * qa.shape[0], qa.shape[1]
    blocks = rows // BLK
    span, wide = picks * BLK, BLK * (width // HD)
    work = rows * width * span
    kept = [((blocks, HD, wide), jnp.float32), ((blocks, 8, wide), jnp.float32), ((blocks, wide, HD), qa.dtype)]
    return pl.pallas_call(
        functools.partial(near_kernel, first),
        out_shape=[jax.ShapeDtypeStruct(*what) for what in kept],
        in_specs=[SMEM, SMEM, VMEM, VMEM, HBM, HBM],
        out_specs=[HBM] * 3,
        scratch_shapes=[
            pltpu.VMEM((rows, width), qa.dtype),
            pltpu.VMEM((blocks, span, HD), keys.dtype),
            pltpu.VMEM((blocks, span, HD), keys.dtype),
            *[pltpu.VMEM(*what) for what in kept],
            pltpu.SemaphoreType.DMA((blocks,)),
            pltpu.SemaphoreType.DMA((blocks,)),
            pltpu.SemaphoreType.DMA((3,)),
        ],
        cost_estimate=cost(4 * work, 8 * rows * width + 4 * blocks * span * HD, work // HD),
    )(ids, core, qa, qb, keys, values)


def far_kernel(firsts, slots_ref, core_ref, got_ref, *refs):
    groups = len(firsts)
    kept_in, o_refs = refs[: 3 * groups], refs[3 * groups : 4 * groups]
    k_buf, v_buf, acc_ref, stat_ref, q_ref, o_buf, k_sem, v_sem, in_sem, out_sem = refs[4 * groups :]
    picks, half = k_buf.shape[1] // BLK, o_buf.shape[2]
    ratio, blocks = o_buf.shape[3] // HD, k_buf.shape[0] // groups
    factor = HD ** (-0.5) * LOG2E
    core = core_ref[0]
    eye = lax.broadcasted_iota(jnp.int32, (HD, HD), 0) == lax.broadcasted_iota(jnp.int32, (HD, HD), 1)
    eye = eye.astype(jnp.float32).astype(jnp.bfloat16)

    def kept_copies(n):
        g, i = divmod(n, blocks)
        acc_in, stat_in, q_in = kept_in[3 * g : 3 * g + 3]
        return (
            pltpu.make_async_copy(q_in.at[i], q_ref.at[n], in_sem.at[n, 0]),
            pltpu.make_async_copy(stat_in.at[i], stat_ref.at[n], in_sem.at[n, 1]),
            pltpu.make_async_copy(acc_in.at[i], acc_ref.at[n], in_sem.at[n, 2]),
        )

    def fetch(n):
        g, i = divmod(n, blocks)
        copies = kept_copies(n)
        copies[0].start()
        for side, (buf, sem) in enumerate(((k_buf, k_sem), (v_buf, v_sem))):
            for j in range(picks):
                source = got_ref.at[slots_ref[firsts[g] + i, j], side]
                pltpu.make_async_copy(source, buf.at[n, pl.ds(j * BLK, BLK)], sem.at[n]).start()
        copies[1].start()
        copies[2].start()

    sent = []
    for n in range(2):
        fetch(n)
    for n in range(groups * blocks):
        g, i = divmod(n, blocks)
        if n + 2 < groups * blocks:
            fetch(n + 2)
        copies = kept_copies(n)
        copies[0].wait()
        wait_for(k_buf.at[n], k_sem.at[n])
        score = scores_of(k_buf[n], q_ref[n])
        copies[1].wait()
        before = stat_ref[n, 0:1, :]
        highest = jnp.maximum(jnp.max(score, axis=0, keepdims=True) * factor, before)
        exponent = jnp.exp2(score * factor - highest)
        kept = jnp.exp2(before - highest)
        total = jnp.sum(exponent, axis=0, keepdims=True) + kept * stat_ref[n, 1:2, :]
        wait_for(v_buf.at[n], v_sem.at[n])
        partial = weighted(v_buf[n], exponent.astype(jnp.bfloat16))
        copies[2].wait()
        merged = ((partial + kept * acc_ref[n]) * (1.0 / total)).astype(o_buf.dtype)
        for r in range(ratio):
            turned = scores_of(eye, merged[:, r * BLK : (r + 1) * BLK]).astype(o_buf.dtype)
            for part in range(CORES):
                low, high = max(i * BLK, part * half), min((i + 1) * BLK, (part + 1) * half)
                if low < high:
                    o_buf[g, part, low - part * half : high - part * half, r * HD : (r + 1) * HD] = turned[
                        low - i * BLK : high - i * BLK
                    ]
        for part in range(CORES):
            if -(-(part + 1) * half // BLK) == i + 1:
                place = core if part == 0 else 1 - core
                sent.append(pltpu.make_async_copy(o_buf.at[g, part], o_refs[g].at[place], out_sem.at[g, part]))
                sent[-1].start()
    for copy in sent:
        copy.wait()


def far_attention(slots, firsts, core, got, kept):
    groups, picks = len(firsts), slots.shape[1]
    acc, stats, q = kept[0]
    blocks, wide = q.shape[0], q.shape[1]
    count = groups * blocks
    half, width = blocks * BLK // CORES, wide // BLK * HD
    span = picks * BLK
    work = count * BLK * width * span
    return pl.pallas_call(
        functools.partial(far_kernel, firsts),
        out_shape=[jax.ShapeDtypeStruct((CORES, half, width), q.dtype)] * groups,
        in_specs=[SMEM, SMEM] + [HBM] * (1 + 3 * groups),
        out_specs=[HBM] * groups,
        scratch_shapes=[
            pltpu.VMEM((count, span, HD), got.dtype),
            pltpu.VMEM((count, span, HD), got.dtype),
            pltpu.VMEM((count,) + acc.shape[1:], acc.dtype),
            pltpu.VMEM((count,) + stats.shape[1:], stats.dtype),
            pltpu.VMEM((count,) + q.shape[1:], q.dtype),
            pltpu.VMEM((groups, CORES, half, width), q.dtype),
            pltpu.SemaphoreType.DMA((count,)),
            pltpu.SemaphoreType.DMA((count,)),
            pltpu.SemaphoreType.DMA((count, 3)),
            pltpu.SemaphoreType.DMA((groups, CORES)),
        ],
        cost_estimate=cost(4 * work, 4 * count * (2 * BLK * width + span * HD), work // HD),
    )(slots, core, got, *[array for group in kept for array in group])


def offset_pairs(chips, chip_step, core_step):
    return [
        (chip * CORES + core, (chip + chip_step) % chips * CORES + (core ^ core_step))
        for chip in range(chips)
        for core in range(CORES)
    ]


def shards(queries, cache_keys, cache_values, block_ids):
    seq_count = lax.axis_size("seq")
    heads = lax.axis_size("head")
    seq_place = lax.axis_index("seq")
    head_place = lax.axis_index("head")
    chips = heads // CORES
    chip, core = head_place // CORES, head_place % CORES
    q_count, k_count = block_ids.shape[0], cache_keys.shape[0] // BLK
    per_chip = q_count // chips
    far_count = block_ids.shape[1] - NEAR
    capacity = max(2, (far_count * q_count + seq_count - 2) // (seq_count - 1))
    slot_total = seq_count * capacity

    far_ids = block_ids[:, NEAR:].reshape(-1)
    far_owner = far_ids // k_count
    far_within = far_ids - far_owner * k_count
    entry = jnp.arange(far_ids.shape[0], dtype=jnp.int32)
    earlier = (far_owner[:, None] == far_owner[None, :]) & (entry[None, :] < entry[:, None])
    far_slot = far_owner * capacity + jnp.sum(earlier.astype(jnp.int32), axis=1)
    slot_range = jnp.arange(slot_total, dtype=jnp.int32)
    unasked = slot_range % k_count
    placed = far_slot[:, None] == slot_range[None, :]
    asked = unasked + jnp.sum(jnp.where(placed, far_within[:, None] - unasked[None, :], 0), axis=0)
    wanted = lax.all_to_all(asked.reshape(seq_count, 1, capacity), "seq", split_axis=0, concat_axis=0, tiled=True)

    sent = pack(wanted, cache_keys, cache_values)
    got = lax.all_to_all(
        sent.reshape(seq_count, capacity, 2, BLK, HD), "seq", split_axis=0, concat_axis=0, tiled=True
    ).reshape(slot_total, 2, BLK, HD)

    steps = [(d, e) for d in range(chips) for e in range(CORES)]
    step_chip = jnp.array([d for d, _ in steps], jnp.int32)
    step_core = jnp.array([e for _, e in steps], jnp.int32)
    ahead = (chip + step_chip) % chips * CORES + (core + step_core) % CORES
    pieces = split_queries(queries, ahead)
    rows_of = {}
    for piece, (d, e) in zip(pieces, steps):
        rows_of[d, e] = piece if d == e == 0 else lax.ppermute(piece, "head", offset_pairs(chips, d, e))

    order = (chip - jnp.arange(chips, dtype=jnp.int32)) % chips
    own_ids = jnp.concatenate([block_ids[:, :NEAR] - seq_place * k_count, far_slot.reshape(q_count, far_count)], axis=1)
    own_ids = jnp.take(own_ids.reshape(chips, per_chip, -1), order, axis=0).reshape(q_count, -1)
    near_ids, slots = own_ids[:, :NEAR], own_ids[:, NEAR:]
    core_operand = core.astype(jnp.int32).reshape(1)
    near = [
        near_attention(near_ids, d * per_chip, core_operand, rows_of[d, 0], rows_of[d, 1], cache_keys, cache_values)
        for d in range(chips)
    ]
    got, near, slots = lax.optimization_barrier((got, near, slots))

    results = [None] * chips
    distance = lambda d: min(d, chips - d)
    for hops in range(chips // 2, -1, -1):
        group = [d for d in range(chips) if distance(d) == hops]
        made = far_attention(slots, tuple(d * per_chip for d in group), core_operand, got, [near[d] for d in group])
        if hops:
            made, got = lax.optimization_barrier((made, got))
        for d, rows in zip(group, made):
            results[d] = lax.ppermute(rows, "head", offset_pairs(chips, -d, 0)) if d else rows
    joined = []
    for d in range(chips):
        joined += [results[d], lax.ppermute(results[d], "head", offset_pairs(chips, 0, 1))]
    return join_outputs(joined, ahead)


def solution(mesh):
    return jax.shard_map(
        shards,
        mesh=mesh,
        in_specs=(P(("seq", "head"), None), P("seq", "head"), P("seq", "head"), P("seq", None)),
        out_specs=P(("seq", "head"), None),
        check_vma=False,
    )
```

time: 177 us -> 174 us (0.983)
  starting transfers between devices: 25.8 us -> 32.7 us
  local copies, waits for them, and re-layouts: 12.1 us -> 7.05 us
  waiting for transfers between devices: 63.1 us -> 58.8 us
    ppermute x7, waiting for transfers between devices: 11.8 us -> 4.24 us  [the longest x3 2.9 us: shards(): lax.ppermute(rows, 'head', offset_pairs(chips, -d, 0))]
    ppermute x7, starting transfers between devices: 9.85 us -> 16.3 us  [the longest x4 12.4 us: shards(): lax.ppermute(results[d], 'head', offset_pairs(chips, 0, 1))]
    another operation x8 -> x0, local copies, waits for them, and re-layouts: 5.01 us -> none  [the longest x4 2.54 us: near_attention(): ids.reshape(-1)]
    all_to_all x1, waiting for transfers between devices: 51.3 us -> 54.5 us  [shards(): lax.all_to_all(sent.reshape(seq_count, capacity, 2, BLK, HD), 'seq', spli...]
    pallas_call x10 -> x9, Pallas kernels: 49.9 us -> 48.7 us  [the longest x4 21.6 us: near_attention(): pl.pallas_call(functools.partial(near_kernel, first), out_shape=[jax.Shap...]
    unnamed x24 -> x29, local copies, waits for them, and re-layouts: 3.38 us -> 4.48 us
  transfers between devices with their start and end apart: 15 -> 15, of which waited for: 5 -> 3; matrix products, arithmetic and copies ran while one was open for 4% -> 1% of each run, Pallas kernels for 22% -> 17%
where the time goes in v3:
time: 174 us; the launch traced here: 172 us
  waiting for transfers between devices  58.8 us (34%)
  Pallas kernels  51.7 us (30%)
  starting transfers between devices  32.7 us (19%)
  blocking collectives  20.4 us (12%)
  local copies, waits for them, and re-layouts  7.05 us (4%)
    all_to_all x1, waiting for transfers between devices, shards(): lax.all_to_all(sent.reshape(seq_count, capacity, 2, BLK, HD), 'seq', spli...  54.5 us
    pallas_call x4, Pallas kernels, near_attention(): pl.pallas_call(functools.partial(near_kernel, first), out_shape=[jax.Shap...  21.6 us
    all_to_all x1, blocking collectives, shards(): lax.all_to_all(asked.reshape(seq_count, 1, capacity), 'seq', split_axis=0...  20.4 us
    pallas_call x3, Pallas kernels, far_attention(): pl.pallas_call(functools.partial(far_kernel, firsts), out_shape=[jax.Shap...  18.2 us
    ppermute x4, starting transfers between devices, shards(): lax.ppermute(results[d], 'head', offset_pairs(chips, 0, 1))  12.4 us
    ppermute x7, starting transfers between devices, shards(): lax.ppermute(piece, 'head', offset_pairs(chips, d, e))  11.5 us
    pallas_call x1, Pallas kernels, pack(): pl.pallas_call(functools.partial(pack_kernel, chunks, ahead), out_shape=j...  7.08 us
    all_to_all x1, starting transfers between devices, shards(): lax.all_to_all(sent.reshape(seq_count, capacity, 2, BLK, HD), 'seq', spli...  5.01 us
  transfers between devices with their start and end apart: 15, of which 3 were waited for; matrix products, arithmetic and copies ran while one was open for 1% of the time, Pallas kernels for 17%

profile of v3, /device:TPU:1, one launch (start us, length us, event | category | flops | bytes accessed | tf_op | source)
XLA Modules:
  0.0 172.2 jit_solution(3347820615171652255)
XLA Ops:
  0.0 0.7 slice.12
  0.7 0.1 copy.22
  0.8 0.1 reshape.223
  0.9 0.2 convert_reduce_fusion
  1.1 0.1 select_reduce_fusion
  1.2 0.1 reduce_sum.24
  1.3 20.4 %all_to_all.10.wanted_ref = s32[32,1,2]{2,1,0:T(1,128)} all-to-all(s32[32,1,2]{2,1,0:T(1,128)S(1)} %fusion.1), channel_id=1, replica_groups=mesh['seq'=32,'head'=8] {'seq'}, dimensions={0} | all-to-all | bytes 512 | tf_op jit(solution)/shard_map/all_to_all | solution.py:334
  21.7 7.1 %shard_map.64 = bf16[64,2,128,128]{3,2,1,0:T(8,128)(2,1)} custom-call(s32[32,1,2]{2,1,0:T(1,128)} %all_to_all.10.wanted_ref, bf16[8192,128]{1,0:T(8,128)(2,1)} %k_ref.9, bf16[8192,128]{1,0:T(8,128)(2,1)} %v_ref.9), custom_call_target="tpu_custom_call" | custom-call | bytes 8388608 | tf_op jit(solution)/shard_map/pallas_call | solution.py:120
  28.8 0.0 copy-start.12
  28.8 0.0 copy-start.13
  28.8 0.0 copy-start.11
  28.9 5.0 %all-to-all-start.1 = ((bf16[32,2,2,128,128]{4,3,2,1,0:T(8,128)(2,1)}), bf16[32,2,2,128,128]{4,3,2,1,0:T(8,128)(2,1)}, u32[]{:S(2)}, u32[]{:S(2)}) async-start(bf16[32,2,2,128,128]{4,3,2,1,0:T(8,128)(2,1)} %bitcast.9), calls=%async_computation.1 | async-start | bytes 8388608 | tf_op jit(solution)/shard_map/all_to_all | solution.py:337
  33.9 0.5 fusion.7.places_ref
  34.5 3.0 %shard_map.65 = (bf16[192,512]{1,0:T(8,128)(2,1)}, bf16[192,512]{1,0:T(8,128)(2,1)}, bf16[192,512]{1,0:T(8,128)(2,1)}, bf16[192,512]{1,0:T(8,128)(2,1)}, bf16[19...) custom-call(s32[8]{0:T(128)} %fusion.7.places_ref, ...), custom_call_target="tpu_custom_call" | custom-call | bytes 3145728 | tf_op jit(solution)/shard_map/pallas_call | solution.py:53
  37.4 2.0 %collective-permute-start = (bf16[192,512]{1,0:T(8,128)(2,1)}, bf16[192,512]{1,0:T(8,128)(2,1)S(1)}, u32[]{:S(2)}, u32[]{:S(2)}) collective-permute-start(bf16[192,512]{1,0:T(8,128)(2,1)} %get-tuple-element.47), channel_id=1, source_target_pairs={{0,1},{1,0},{2,3},{3,2},{4,5},{5,4},{6,7},{7,6},{8,9},{9,8},{10,11... | collective-permute-start | bytes 589832 | tf_op jit(solution)/shard_map/ppermute | solution.py:348
  39.5 1.3 collective-permute-start.1
  40.8 1.5 collective-permute-start.2
  42.3 1.3 collective-permute-start.3
  43.6 2.0 %collective-permute-start.4 = (bf16[192,512]{1,0:T(8,128)(2,1)}, bf16[192,512]{1,0:T(8,128)(2,1)S(1)}, u32[]{:S(2)}, u32[]{:S(2)}) collective-permute-start(bf16[192,512]{1,0:T(8,128)(2,1)} %get-tuple-element.57), channel_id=1, source_target_pairs={{0,5},{1,4},{2,7},{3,6},{4,1},{5,0},{6,3},{7,2},{8,13},{9,12},{10,... | collective-permute-start | bytes 589832 | tf_op jit(solution)/shard_map/ppermute | solution.py:348
  45.6 0.1 reduce_sum.25
  45.8 0.1 concatenate.8
  45.8 0.1 copy.19
  46.0 0.1 pad_add_fusion
  46.0 0.6 gather_fusion
  46.6 0.1 broadcast_in_dim.27
  46.7 0.1 broadcast_in_dim.28
  46.8 0.0 collective-permute-done.qb_ref
  46.8 1.5 collective-permute-start.5
  48.3 0.0 collective-permute-done.1.qa_ref
  48.3 1.8 %collective-permute-start.6 = (bf16[192,512]{1,0:T(8,128)(2,1)}, bf16[192,512]{1,0:T(8,128)(2,1)S(1)}, u32[]{:S(2)}, u32[]{:S(2)}) collective-permute-start(bf16[192,512]{1,0:T(8,128)(2,1)} %get-tuple-element.62), channel_id=1, source_target_pairs={{0,7},{1,6},{2,1},{3,0},{4,3},{5,2},{6,5},{7,4},{8,15},{9,14},{10,... | collective-permute-start | bytes 589832 | tf_op jit(solution)/shard_map/ppermute | solution.py:348
  50.1 0.1 broadcast_select_fusion
  50.2 0.7 slice.19.slots_ref
  50.8 5.4 %shard_map.66 = (f32[3,128,512]{2,1,0:T(8,128)}, f32[3,8,512]{2,1,0:T(8,128)}, bf16[3,512,128]{2,1,0:T(8,128)(2,1)}) custom-call(s32[12,5]{1,0:T(8,128)} %bitcast.10, s32[1]{0:T(128)} %bitcast.4.core_ref, bf16[192,512]{1,0:T(8,128)(2,1)} %get-tuple-element.46.qa_ref, bf16[192,512]{1,0:T(8,128)(2,1)} %copy-done.8, bf16[8192,128]{1,0:T(8,128)(2,1)} %k_ref.9, ...), custom_call_target="tpu_custom_call" | custom-call | flops 503316480 | bytes 2555904 | tf_op jit(solution)/shard_map/pallas_call | solution.py:187
  56.2 0.0 collective-permute-done.2.qb_ref
  56.2 0.7 copy-done.7
  56.9 5.5 %shard_map.67 = (f32[3,128,512]{2,1,0:T(8,128)}, f32[3,8,512]{2,1,0:T(8,128)}, bf16[3,512,128]{2,1,0:T(8,128)(2,1)}) custom-call(s32[12,5]{1,0:T(8,128)} %bitcast.11, s32[1]{0:T(128)} %bitcast.4.core_ref, bf16[192,512]{1,0:T(8,128)(2,1)} %copy-done.6, bf16[192,512]{1,0:T(8,128)(2,1)} %copy-done.7, bf16[8192,128]{1,0:T(8,128)(2,1)} %k_ref.9, ...), custom_call_target="tpu_custom_call" | custom-call | flops 503316480 | bytes 2555904 | tf_op jit(solution)/shard_map/pallas_call | solution.py:187
  62.4 0.0 collective-permute-done.3.qa_ref
  62.4 0.0 collective-permute-done.4.qb_ref
  62.4 0.7 copy-done.4
  63.1 0.7 copy-done.5
  63.7 5.4 %shard_map.68 = (f32[3,128,512]{2,1,0:T(8,128)}, f32[3,8,512]{2,1,0:T(8,128)}, bf16[3,512,128]{2,1,0:T(8,128)(2,1)}) custom-call(s32[12,5]{1,0:T(8,128)} %bitcast.12, s32[1]{0:T(128)} %bitcast.4.core_ref, bf16[192,512]{1,0:T(8,128)(2,1)} %copy-done.4, bf16[192,512]{1,0:T(8,128)(2,1)} %copy-done.5, bf16[8192,128]{1,0:T(8,128)(2,1)} %k_ref.9, ...), custom_call_target="tpu_custom_call" | custom-call | flops 503316480 | bytes 2555904 | tf_op jit(solution)/shard_map/pallas_call | solution.py:187
  69.2 0.0 collective-permute-done.5.qa_ref
  69.2 0.0 collective-permute-done.6.qb_ref
  69.2 0.7 copy-done.9
  69.8 0.7 copy-done.10
  70.5 5.4 %shard_map.69 = (f32[3,128,512]{2,1,0:T(8,128)}, f32[3,8,512]{2,1,0:T(8,128)}, bf16[3,512,128]{2,1,0:T(8,128)(2,1)}) custom-call(s32[12,5]{1,0:T(8,128)} %bitcast.13, s32[1]{0:T(128)} %bitcast.4.core_ref, bf16[192,512]{1,0:T(8,128)(2,1)} %copy-done.9, bf16[192,512]{1,0:T(8,128)(2,1)} %copy-done.10, bf16[8192,128]{1,0:T(8,128)(2,1)} %k_ref.9, ...), custom_call_target="tpu_custom_call" | custom-call | flops 503316480 | bytes 2555904 | tf_op jit(solution)/shard_map/pallas_call | solution.py:187
  75.9 54.5 %all-to-all-done.1 = bf16[32,2,2,128,128]{4,3,2,1,0:T(8,128)(2,1)} async-done(((bf16[32,2,2,128,128]{4,3,2,1,0:T(8,128)(2,1)}), bf16[32,2,2,128,128]{4,3,2,1,0:T(8,128)(2,1)}, u32[]{:S(2)}, u32[]{:S(2)}) %all-to-all-start.1) | async-done | bytes 4194336 | tf_op jit(solution)/shard_map/all_to_all | solution.py:337
  130.5 5.1 %shard_map.70 = bf16[2,192,512]{2,1,0:T(8,128)(2,1)} custom-call(s32[12,3]{1,0:T(8,128)} %slice.19.slots_ref, s32[1]{0:T(128)} %bitcast.4.core_ref, bf16[64,2,128,128]{3,2,1,0:T(8,128)(2,1)} %bitcast.2.got_ref, f32[3,128,512]{2,1,0:T(8,128)} %get-tuple-element.68.refs_0_, f32[3,8,512]{2,1,0:T(8,128)} %get-tuple-element.69.refs_1_, ...), custom_call_target="tpu_custom_call" | custom-call | flops 301989888 | bytes 2162688 | tf_op jit(solution)/shard_map/pallas_call | solution.py:282
  135.6 8.0 %shard_map.71 = (bf16[2,192,512]{2,1,0:T(8,128)(2,1)}, bf16[2,192,512]{2,1,0:T(8,128)(2,1)}) custom-call(s32[12,3]{1,0:T(8,128)} %slice.19.slots_ref, s32[1]{0:T(128)} %bitcast.4.core_ref, bf16[64,2,128,128]{3,2,1,0:T(8,128)(2,1)} %bitcast.2.got_ref, f32[3,128,512]{2,1,0:T(8,128)} %get-tuple-element.72.refs_0_, f32[3,8,512]{2,1,0:T(8,128)} %get-tuple-element.73.refs_1_, ...), custom_call_target="tpu_custom_call" | custom-call | flops 603979776 | bytes 4325376 | tf_op jit(solution)/shard_map/pallas_call | solution.py:282
  143.6 2.8 %collective-permute-start.8 = (bf16[2,192,512]{2,1,0:T(8,128)(2,1)}, bf16[2,192,512]{2,1,0:T(8,128)(2,1)S(1)}, u32[]{:S(2)}, u32[]{:S(2)}) collective-permute-start(bf16[2,192,512]{2,1,0:T(8,128)(2,1)} %get-tuple-element.84), channel_id=1, source_target_pairs={{0,6},{1,7},{2,0},{3,1},{4,2},{5,3},{6,4},{7,5},{8,14},{9,15},{10,... | collective-permute-start | bytes 1179656 | tf_op jit(solution)/shard_map/ppermute | solution.py:369
  146.5 0.3 collective-permute-start.10
  146.8 0.7 collective-permute-start.12
  147.5 5.1 %shard_map.72.refs_0_ = bf16[2,192,512]{2,1,0:T(8,128)(2,1)} custom-call(s32[12,3]{1,0:T(8,128)} %slice.19.slots_ref, s32[1]{0:T(128)} %bitcast.4.core_ref, bf16[64,2,128,128]{3,2,1,0:T(8,128)(2,1)} %bitcast.2.got_ref, f32[3,128,512]{2,1,0:T(8,128)} %get-tuple-element.81.refs_0_, f32[3,8,512]{2,1,0:T(8,128)} %get-tuple-element.82.refs_1_, ...), custom_call_target="tpu_custom_call" | custom-call | flops 301989888 | bytes 2162688 | tf_op jit(solution)/shard_map/pallas_call | solution.py:282
  152.6 2.5 %collective-permute-start.7 = (bf16[2,192,512]{2,1,0:T(8,128)(2,1)}, bf16[2,192,512]{2,1,0:T(8,128)(2,1)S(1)}, u32[]{:S(2)}, u32[]{:S(2)}) collective-permute-start(bf16[2,192,512]{2,1,0:T(8,128)(2,1)} %shard_map.72.refs_0_), channel_id=1, source_target_pairs={{0,1},{1,0},{2,3},{3,2},{4,5},{5,4},{6,7},{7,6},{8,9},{9,8},{10,11... | collective-permute-start | bytes 1179656 | tf_op jit(solution)/shard_map/ppermute | solution.py:372
  155.1 9.4 %collective-permute-start.9 = (bf16[2,192,512]{2,1,0:T(8,128)(2,1)S(1)}, bf16[2,192,512]{2,1,0:T(8,128)(2,1)S(1)}, u32[]{:S(2)}, u32[]{:S(2)}) collective-permute-start(bf16[2,192,512]{2,1,0:T(8,128)(2,1)S(1)} %collective-permute-done.8.refs_2_), channel_id=1, source_target_pairs={{0,1},{1,0},{2,3},{3,2},{4,5},{5,4},{6,7},{7,6},{8,9},{9,8},{10,11... | collective-permute-start | bytes 1179656 | tf_op jit(solution)/shard_map/ppermute | solution.py:372
  164.5 0.0 collective-permute-done.10.refs_4_
  164.5 0.0 collective-permute-start.11
  164.5 2.9 %collective-permute-done.12.refs_6_ = bf16[2,192,512]{2,1,0:T(8,128)(2,1)S(1)} collective-permute-done((bf16[2,192,512]{2,1,0:T(8,128)(2,1)}, bf16[2,192,512]{2,1,0:T(8,128)(2,1)S(1)}, u32[]{:S(2)}, u32[]{:S(2)}) %collective-permute-start.12) | collective-permute-done | bytes 393248 | tf_op jit(solution)/shard_map/ppermute | solution.py:369
  167.4 0.5 collective-permute-start.13
  167.9 0.0 collective-permute-done.9.refs_3_
  167.9 0.0 collective-permute-done.11.refs_5_
  167.9 1.3 collective-permute-done.13.refs_7_
  169.3 1.0 copy-done
  170.3 1.7 %shard_map.73 = bf16[192,4096]{1,0:T(8,128)(2,1)} custom-call(s32[8]{0:T(128)S(1)} %copy-done.1, bf16[2,192,512]{2,1,0:T(8,128)(2,1)S(1)} %copy-done, bf16[2,192,512]{2,1,0:T(8,128)(2,1)S(1)} %collective-permute-done.7.refs_1_, bf16[2,192,512]{2,1,0:T(8,128)(2,1)S(1)} %collective-permute-done.8.refs_2_, ...), custom_call_target="tpu_custom_call" | custom-call | bytes 3145728 | tf_op jit(solution)/shard_map/pallas_call | solution.py:84
  (32 shorter events, 0.2 us)
Async XLA Ops:
  28.8 5.1 %copy-start.12 = (s32[8]{0:T(128)S(1)}, s32[8]{0:T(128)}, u32[]{:S(2)}) copy-start(s32[8]{0:T(128)} %constant.114.clone) | copy-start | bytes 100
  28.8 5.1 %copy-start.13 = (s32[8]{0:T(128)S(1)}, s32[8]{0:T(128)}, u32[]{:S(2)}) copy-start(s32[8]{0:T(128)} %constant.115.clone) | copy-start | bytes 100
  28.8 16.9 %copy-start.11 = (s32[12,8]{0,1:T(8,128)S(1)}, s32[12,8]{0,1:T(8,128)}, u32[]{:S(2)}) copy-start(s32[12,8]{0,1:T(8,128)} %param.9) | copy-start | bytes 1156
  28.9 101.6 %all-to-all-start.1 = ((bf16[32,2,2,128,128]{4,3,2,1,0:T(8,128)(2,1)}), bf16[32,2,2,128,128]{4,3,2,1,0:T(8,128)(2,1)}, u32[]{:S(2)}, u32[]{:S(2)}) async-start(bf16[32,2,2,128,128]{4,3,2,1,0:T(8,128)(2,1)} %bitcast.9), calls=%async_computation.1 | async-start | bytes 8388608 | tf_op jit(solution)/shard_map/all_to_all | solution.py:337
  37.4 9.4 %collective-permute-start = (bf16[192,512]{1,0:T(8,128)(2,1)}, bf16[192,512]{1,0:T(8,128)(2,1)S(1)}, u32[]{:S(2)}, u32[]{:S(2)}) collective-permute-start(bf16[192,512]{1,0:T(8,128)(2,1)} %get-tuple-element.47), channel_id=1, source_target_pairs={{0,1},{1,0},{2,3},{3,2},{4,5},{5,4},{6,7},{7,6},{8,9},{9,8},{10,11... | collective-permute-start | bytes 589832 | tf_op jit(solution)/shard_map/ppermute | solution.py:348
  39.5 8.8 %collective-permute-start.1 = (bf16[192,512]{1,0:T(8,128)(2,1)}, bf16[192,512]{1,0:T(8,128)(2,1)S(1)}, u32[]{:S(2)}, u32[]{:S(2)}) collective-permute-start(bf16[192,512]{1,0:T(8,128)(2,1)} %get-tuple-element.51), channel_id=1, source_target_pairs={{0,2},{1,3},{2,4},{3,5},{4,6},{5,7},{6,0},{7,1},{8,10},{9,11},{10,... | collective-permute-start | bytes 589832 | tf_op jit(solution)/shard_map/ppermute | solution.py:348
  40.8 15.4 %collective-permute-start.2 = (bf16[192,512]{1,0:T(8,128)(2,1)}, bf16[192,512]{1,0:T(8,128)(2,1)S(1)}, u32[]{:S(2)}, u32[]{:S(2)}) collective-permute-start(bf16[192,512]{1,0:T(8,128)(2,1)} %get-tuple-element.52), channel_id=1, source_target_pairs={{0,3},{1,2},{2,5},{3,4},{4,7},{5,6},{6,1},{7,0},{8,11},{9,10},{10,... | collective-permute-start | bytes 589832 | tf_op jit(solution)/shard_map/ppermute | solution.py:348
  42.3 20.1 %collective-permute-start.3 = (bf16[192,512]{1,0:T(8,128)(2,1)}, bf16[192,512]{1,0:T(8,128)(2,1)S(1)}, u32[]{:S(2)}, u32[]{:S(2)}) collective-permute-start(bf16[192,512]{1,0:T(8,128)(2,1)} %get-tuple-element.56), channel_id=1, source_target_pairs={{0,4},{1,5},{2,6},{3,7},{4,0},{5,1},{6,2},{7,3},{8,12},{9,13},{10,... | collective-permute-start | bytes 589832 | tf_op jit(solution)/shard_map/ppermute | solution.py:348
  43.6 18.8 %collective-permute-start.4 = (bf16[192,512]{1,0:T(8,128)(2,1)}, bf16[192,512]{1,0:T(8,128)(2,1)S(1)}, u32[]{:S(2)}, u32[]{:S(2)}) collective-permute-start(bf16[192,512]{1,0:T(8,128)(2,1)} %get-tuple-element.57), channel_id=1, source_target_pairs={{0,5},{1,4},{2,7},{3,6},{4,1},{5,0},{6,3},{7,2},{8,13},{9,12},{10,... | collective-permute-start | bytes 589832 | tf_op jit(solution)/shard_map/ppermute | solution.py:348
  46.8 4.0 %copy-start.8 = (bf16[192,512]{1,0:T(8,128)(2,1)}, bf16[192,512]{1,0:T(8,128)(2,1)S(1)}, u32[]{:S(2)}) copy-start(bf16[192,512]{1,0:T(8,128)(2,1)S(1)} %collective-permute-done.qb_ref) | copy-start | bytes 589828
  46.8 22.3 %collective-permute-start.5 = (bf16[192,512]{1,0:T(8,128)(2,1)}, bf16[192,512]{1,0:T(8,128)(2,1)S(1)}, u32[]{:S(2)}, u32[]{:S(2)}) collective-permute-start(bf16[192,512]{1,0:T(8,128)(2,1)} %get-tuple-element.61), channel_id=1, source_target_pairs={{0,6},{1,7},{2,0},{3,1},{4,2},{5,3},{6,4},{7,5},{8,14},{9,15},{10,... | collective-permute-start | bytes 589832 | tf_op jit(solution)/shard_map/ppermute | solution.py:348
  48.3 8.0 %copy-start.6 = (bf16[192,512]{1,0:T(8,128)(2,1)}, bf16[192,512]{1,0:T(8,128)(2,1)S(1)}, u32[]{:S(2)}) copy-start(bf16[192,512]{1,0:T(8,128)(2,1)S(1)} %collective-permute-done.1.qa_ref) | copy-start | bytes 589828
  48.3 20.9 %collective-permute-start.6 = (bf16[192,512]{1,0:T(8,128)(2,1)}, bf16[192,512]{1,0:T(8,128)(2,1)S(1)}, u32[]{:S(2)}, u32[]{:S(2)}) collective-permute-start(bf16[192,512]{1,0:T(8,128)(2,1)} %get-tuple-element.62), channel_id=1, source_target_pairs={{0,7},{1,6},{2,1},{3,0},{4,3},{5,2},{6,5},{7,4},{8,15},{9,14},{10,... | collective-permute-start | bytes 589832 | tf_op jit(solution)/shard_map/ppermute | solution.py:348
  50.2 0.7 copy-start.3
  56.2 0.7 copy-start.7
  62.4 0.7 copy-start.4
  63.1 0.7 copy-start.5
  69.2 0.7 copy-start.9
  69.8 0.7 copy-start.10
  135.6 10.9 %copy-start.2 = (bf16[2,192,512]{2,1,0:T(8,128)(2,1)S(1)}, bf16[2,192,512]{2,1,0:T(8,128)(2,1)}, u32[]{:S(2)}) copy-start(bf16[2,192,512]{2,1,0:T(8,128)(2,1)} %shard_map.70) | copy-start | bytes 1179652
  143.6 25.6 %copy-start.1 = (s32[8]{0:T(128)S(1)}, s32[8]{0:T(128)}, u32[]{:S(2)}) copy-start(s32[8]{0:T(128)} %fusion.7.places_ref) | copy-start | bytes 100
  143.6 11.4 %collective-permute-start.8 = (bf16[2,192,512]{2,1,0:T(8,128)(2,1)}, bf16[2,192,512]{2,1,0:T(8,128)(2,1)S(1)}, u32[]{:S(2)}, u32[]{:S(2)}) collective-permute-start(bf16[2,192,512]{2,1,0:T(8,128)(2,1)} %get-tuple-element.84), channel_id=1, source_target_pairs={{0,6},{1,7},{2,0},{3,1},{4,2},{5,3},{6,4},{7,5},{8,14},{9,15},{10,... | collective-permute-start | bytes 1179656 | tf_op jit(solution)/shard_map/ppermute | solution.py:369
  146.5 18.1 %collective-permute-start.10 = (bf16[2,192,512]{2,1,0:T(8,128)(2,1)S(1)}, bf16[2,192,512]{2,1,0:T(8,128)(2,1)S(1)}, u32[]{:S(2)}, u32[]{:S(2)}) collective-permute-start(bf16[2,192,512]{2,1,0:T(8,128)(2,1)S(1)} %copy-done.2), channel_id=1, source_target_pairs={{0,4},{1,5},{2,6},{3,7},{4,0},{5,1},{6,2},{7,3},{8,12},{9,13},{10,... | collective-permute-start | bytes 1179656 | tf_op jit(solution)/shard_map/ppermute | solution.py:369
  146.8 20.6 %collective-permute-start.12 = (bf16[2,192,512]{2,1,0:T(8,128)(2,1)}, bf16[2,192,512]{2,1,0:T(8,128)(2,1)S(1)}, u32[]{:S(2)}, u32[]{:S(2)}) collective-permute-start(bf16[2,192,512]{2,1,0:T(8,128)(2,1)} %get-tuple-element.86), channel_id=1, source_target_pairs={{0,2},{1,3},{2,4},{3,5},{4,6},{5,7},{6,0},{7,1},{8,10},{9,11},{10,... | collective-permute-start | bytes 1179656 | tf_op jit(solution)/shard_map/ppermute | solution.py:369
  152.6 15.3 %collective-permute-start.7 = (bf16[2,192,512]{2,1,0:T(8,128)(2,1)}, bf16[2,192,512]{2,1,0:T(8,128)(2,1)S(1)}, u32[]{:S(2)}, u32[]{:S(2)}) collective-permute-start(bf16[2,192,512]{2,1,0:T(8,128)(2,1)} %shard_map.72.refs_0_), channel_id=1, source_target_pairs={{0,1},{1,0},{2,3},{3,2},{4,5},{5,4},{6,7},{7,6},{8,9},{9,8},{10,11... | collective-permute-start | bytes 1179656 | tf_op jit(solution)/shard_map/ppermute | solution.py:372
  155.1 12.8 %collective-permute-start.9 = (bf16[2,192,512]{2,1,0:T(8,128)(2,1)S(1)}, bf16[2,192,512]{2,1,0:T(8,128)(2,1)S(1)}, u32[]{:S(2)}, u32[]{:S(2)}) collective-permute-start(bf16[2,192,512]{2,1,0:T(8,128)(2,1)S(1)} %collective-permute-done.8.refs_2_), channel_id=1, source_target_pairs={{0,1},{1,0},{2,3},{3,2},{4,5},{5,4},{6,7},{7,6},{8,9},{9,8},{10,11... | collective-permute-start | bytes 1179656 | tf_op jit(solution)/shard_map/ppermute | solution.py:372
  164.5 3.4 %collective-permute-start.11 = (bf16[2,192,512]{2,1,0:T(8,128)(2,1)S(1)}, bf16[2,192,512]{2,1,0:T(8,128)(2,1)S(1)}, u32[]{:S(2)}, u32[]{:S(2)}) collective-permute-start(bf16[2,192,512]{2,1,0:T(8,128)(2,1)S(1)} %collective-permute-done.10.refs_4_), channel_id=1, source_target_pairs={{0,1},{1,0},{2,3},{3,2},{4,5},{5,4},{6,7},{7,6},{8,9},{9,8},{10,11... | collective-permute-start | bytes 1179656 | tf_op jit(solution)/shard_map/ppermute | solution.py:372
  167.4 1.8 %collective-permute-start.13 = (bf16[2,192,512]{2,1,0:T(8,128)(2,1)S(1)}, bf16[2,192,512]{2,1,0:T(8,128)(2,1)S(1)}, u32[]{:S(2)}, u32[]{:S(2)}) collective-permute-start(bf16[2,192,512]{2,1,0:T(8,128)(2,1)S(1)} %collective-permute-done.12.refs_6_), channel_id=1, source_target_pairs={{0,1},{1,0},{2,3},{3,2},{4,5},{5,4},{6,7},{7,6},{8,9},{9,8},{10,11... | collective-permute-start | bytes 1179656 | tf_op jit(solution)/shard_map/ppermute | solution.py:372
  169.3 1.0 copy-start

commit v4 on v3

--- a/solution.py
+++ b/solution.py
@@ -15,6 +15,7 @@
 SMEM = pl.BlockSpec(memory_space=pltpu.SMEM)
 VMEM = pl.BlockSpec(memory_space=pltpu.VMEM)
 LOG2E = 1.4426950408889634
+HIGHEST, TOTAL, KEPT_ROWS = HD, HD + 1, HD + 8
 
 
 def wait_for(ref, sem):
@@ -115,7 +116,7 @@
         copy.wait()
 
 
-def pack(wanted, keys, values, chunks=8, ahead=2):
+def pack(wanted, keys, values, chunks=4, ahead=4):
     count = wanted.shape[0] * wanted.shape[2]
     return pl.pallas_call(
         functools.partial(pack_kernel, chunks, ahead),
@@ -139,8 +140,8 @@
     return lax.dot_general(values, weights, (((0,), (0,)), ((), ())), preferred_element_type=jnp.float32)
 
 
-def near_kernel(first, ids_ref, core_ref, qa_ref, qb_ref, k_ref, v_ref, acc_out, stat_out, q_out, q_buf, k_buf, v_buf, acc_ref, stat_ref, q_ref, k_sem, v_sem, out_sem):
-    blocks, picks, half = acc_ref.shape[0], k_buf.shape[1] // BLK, qa_ref.shape[0]
+def near_kernel(first, ids_ref, core_ref, qa_ref, qb_ref, k_ref, v_ref, kept_out, q_out, q_buf, k_buf, v_buf, kept_ref, q_ref, k_sem, v_sem, out_sem):
+    blocks, picks, half = q_ref.shape[0], k_buf.shape[1] // BLK, qa_ref.shape[0]
     ratio = q_buf.shape[1] // HD
     factor = HD ** (-0.5) * LOG2E
     core = core_ref[0]
@@ -154,8 +155,8 @@
     for i in range(blocks):
         for r in range(ratio):
             q_ref[i, r * BLK : (r + 1) * BLK, :] = q_buf[i * BLK : (i + 1) * BLK, r * HD : (r + 1) * HD]
-    copies = [pltpu.make_async_copy(q_ref, q_out, out_sem.at[0])]
-    copies[0].start()
+    q_copy = pltpu.make_async_copy(q_ref, q_out, out_sem.at[0])
+    q_copy.start()
 
     def block(i, carry):
         wait_for(k_buf.at[i], k_sem.at[i])
@@ -163,18 +164,16 @@
         score = scores_of(k_buf[i], q_ref[i])
         highest = jnp.max(score, axis=0, keepdims=True) * factor
         exponent = jnp.exp2(score * factor - highest)
-        stat_ref[i, 0:1, :] = highest
-        stat_ref[i, 1:2, :] = jnp.sum(exponent, axis=0, keepdims=True)
-        acc_ref[i] = weighted(v_buf[i], exponent.astype(jnp.bfloat16))
+        kept_ref[i, HIGHEST : HIGHEST + 1, :] = highest
+        kept_ref[i, TOTAL : TOTAL + 1, :] = jnp.sum(exponent, axis=0, keepdims=True)
+        kept_ref[i, 0:HD, :] = weighted(v_buf[i], exponent.astype(jnp.bfloat16))
         return carry
 
     lax.fori_loop(0, blocks, block, 0)
-    copies.append(pltpu.make_async_copy(acc_ref, acc_out, out_sem.at[1]))
-    copies.append(pltpu.make_async_copy(stat_ref, stat_out, out_sem.at[2]))
-    copies[1].start()
-    copies[2].start()
-    for copy in copies:
-        copy.wait()
+    kept_copy = pltpu.make_async_copy(kept_ref, kept_out, out_sem.at[1])
+    kept_copy.start()
+    q_copy.wait()
+    kept_copy.wait()
 
 
 def near_attention(ids, first, core, qa, qb, keys, values):
@@ -183,12 +182,12 @@
     blocks = rows // BLK
     span, wide = picks * BLK, BLK * (width // HD)
     work = rows * width * span
-    kept = [((blocks, HD, wide), jnp.float32), ((blocks, 8, wide), jnp.float32), ((blocks, wide, HD), qa.dtype)]
+    kept = [((blocks, KEPT_ROWS, wide), jnp.float32), ((blocks, wide, HD), qa.dtype)]
     return pl.pallas_call(
         functools.partial(near_kernel, first),
         out_shape=[jax.ShapeDtypeStruct(*what) for what in kept],
         in_specs=[SMEM, SMEM, VMEM, VMEM, HBM, HBM],
-        out_specs=[HBM] * 3,
+        out_specs=[HBM] * 2,
         scratch_shapes=[
             pltpu.VMEM((rows, width), qa.dtype),
             pltpu.VMEM((blocks, span, HD), keys.dtype),
@@ -196,7 +195,7 @@
             *[pltpu.VMEM(*what) for what in kept],
             pltpu.SemaphoreType.DMA((blocks,)),
             pltpu.SemaphoreType.DMA((blocks,)),
-            pltpu.SemaphoreType.DMA((3,)),
+            pltpu.SemaphoreType.DMA((2,)),
         ],
         cost_estimate=cost(4 * work, 8 * rows * width + 4 * blocks * span * HD, work // HD),
     )(ids, core, qa, qb, keys, values)
@@ -204,100 +203,55 @@
 
 def far_kernel(firsts, slots_ref, core_ref, got_ref, *refs):
     groups = len(firsts)
-    kept_in, o_refs = refs[: 3 * groups], refs[3 * groups : 4 * groups]
-    k_buf, v_buf, acc_ref, stat_ref, q_ref, o_buf, k_sem, v_sem, in_sem, out_sem = refs[4 * groups :]
-    picks, half = k_buf.shape[1] // BLK, o_buf.shape[2]
-    ratio, blocks = o_buf.shape[3] // HD, k_buf.shape[0] // groups
+    near_refs, o_refs = refs[: 2 * groups], refs[2 * groups : 3 * groups]
+    far_buf, far_sem = refs[3 * groups :]
+    picks, half = far_buf.shape[1], o_refs[0].shape[1]
+    ratio, blocks = o_refs[0].shape[2] // HD, far_buf.shape[0] // groups
     factor = HD ** (-0.5) * LOG2E
     core = core_ref[0]
-    eye = lax.broadcasted_iota(jnp.int32, (HD, HD), 0) == lax.broadcasted_iota(jnp.int32, (HD, HD), 1)
-    eye = eye.astype(jnp.float32).astype(jnp.bfloat16)
-
-    def kept_copies(n):
-        g, i = divmod(n, blocks)
-        acc_in, stat_in, q_in = kept_in[3 * g : 3 * g + 3]
-        return (
-            pltpu.make_async_copy(q_in.at[i], q_ref.at[n], in_sem.at[n, 0]),
-            pltpu.make_async_copy(stat_in.at[i], stat_ref.at[n], in_sem.at[n, 1]),
-            pltpu.make_async_copy(acc_in.at[i], acc_ref.at[n], in_sem.at[n, 2]),
-        )
-
-    def fetch(n):
-        g, i = divmod(n, blocks)
-        copies = kept_copies(n)
-        copies[0].start()
-        for side, (buf, sem) in enumerate(((k_buf, k_sem), (v_buf, v_sem))):
-            for j in range(picks):
-                source = got_ref.at[slots_ref[firsts[g] + i, j], side]
-                pltpu.make_async_copy(source, buf.at[n, pl.ds(j * BLK, BLK)], sem.at[n]).start()
-        copies[1].start()
-        copies[2].start()
-
-    sent = []
-    for n in range(2):
-        fetch(n)
     for n in range(groups * blocks):
         g, i = divmod(n, blocks)
-        if n + 2 < groups * blocks:
-            fetch(n + 2)
-        copies = kept_copies(n)
-        copies[0].wait()
-        wait_for(k_buf.at[n], k_sem.at[n])
-        score = scores_of(k_buf[n], q_ref[n])
-        copies[1].wait()
-        before = stat_ref[n, 0:1, :]
+        for j in range(picks):
+            pltpu.make_async_copy(got_ref.at[slots_ref[firsts[g] + i, j]], far_buf.at[n, j], far_sem.at[n]).start()
+    for n in range(groups * blocks):
+        g, i = divmod(n, blocks)
+        kept_ref, q_ref = near_refs[2 * g : 2 * g + 2]
+        wait_for(far_buf.at[n], far_sem.at[n])
+        score = scores_of(jnp.concatenate([far_buf[n, j, 0] for j in range(picks)], axis=0), q_ref[i])
+        before = kept_ref[i, HIGHEST : HIGHEST + 1, :]
         highest = jnp.maximum(jnp.max(score, axis=0, keepdims=True) * factor, before)
         exponent = jnp.exp2(score * factor - highest)
         kept = jnp.exp2(before - highest)
-        total = jnp.sum(exponent, axis=0, keepdims=True) + kept * stat_ref[n, 1:2, :]
-        wait_for(v_buf.at[n], v_sem.at[n])
-        partial = weighted(v_buf[n], exponent.astype(jnp.bfloat16))
-        copies[2].wait()
-        merged = ((partial + kept * acc_ref[n]) * (1.0 / total)).astype(o_buf.dtype)
+        total = jnp.sum(exponent, axis=0, keepdims=True) + kept * kept_ref[i, TOTAL : TOTAL + 1, :]
+        partial = weighted(
+            jnp.concatenate([far_buf[n, j, 1] for j in range(picks)], axis=0), exponent.astype(jnp.bfloat16)
+        )
+        merged = (partial + kept * kept_ref[i, 0:HD, :]) * (1.0 / total)
         for r in range(ratio):
-            turned = scores_of(eye, merged[:, r * BLK : (r + 1) * BLK]).astype(o_buf.dtype)
+            turned = merged[:, r * BLK : (r + 1) * BLK].T.astype(o_refs[g].dtype)
             for part in range(CORES):
                 low, high = max(i * BLK, part * half), min((i + 1) * BLK, (part + 1) * half)
                 if low < high:
-                    o_buf[g, part, low - part * half : high - part * half, r * HD : (r + 1) * HD] = turned[
-                        low - i * BLK : high - i * BLK
-                    ]
-        for part in range(CORES):
-            if -(-(part + 1) * half // BLK) == i + 1:
-                place = core if part == 0 else 1 - core
-                sent.append(pltpu.make_async_copy(o_buf.at[g, part], o_refs[g].at[place], out_sem.at[g, part]))
-                sent[-1].start()
-    for copy in sent:
-        copy.wait()
-
-
-def far_attention(slots, firsts, core, got, kept):
+                    place = core if part == 0 else 1 - core
+                    rows = slice(low - part * half, high - part * half)
+                    o_refs[g][place, rows, r * HD : (r + 1) * HD] = turned[low - i * BLK : high - i * BLK]
+
+
+def far_attention(slots, firsts, core, got, near):
     groups, picks = len(firsts), slots.shape[1]
-    acc, stats, q = kept[0]
+    _, q = near[0]
     blocks, wide = q.shape[0], q.shape[1]
     count = groups * blocks
     half, width = blocks * BLK // CORES, wide // BLK * HD
-    span = picks * BLK
-    work = count * BLK * width * span
     return pl.pallas_call(
         functools.partial(far_kernel, firsts),
         out_shape=[jax.ShapeDtypeStruct((CORES, half, width), q.dtype)] * groups,
-        in_specs=[SMEM, SMEM] + [HBM] * (1 + 3 * groups),
-        out_specs=[HBM] * groups,
-        scratch_shapes=[
-            pltpu.VMEM((count, span, HD), got.dtype),
-            pltpu.VMEM((count, span, HD), got.dtype),
-            pltpu.VMEM((count,) + acc.shape[1:], acc.dtype),
-            pltpu.VMEM((count,) + stats.shape[1:], stats.dtype),
-            pltpu.VMEM((count,) + q.shape[1:], q.dtype),
-            pltpu.VMEM((groups, CORES, half, width), q.dtype),
-            pltpu.SemaphoreType.DMA((count,)),
-            pltpu.SemaphoreType.DMA((count,)),
-            pltpu.SemaphoreType.DMA((count, 3)),
-            pltpu.SemaphoreType.DMA((groups, CORES)),
-        ],
-        cost_estimate=cost(4 * work, 4 * count * (2 * BLK * width + span * HD), work // HD),
-    )(slots, core, got, *[array for group in kept for array in group])
+        in_specs=[SMEM, SMEM, HBM] + [VMEM] * (2 * groups),
+        out_specs=[VMEM] * groups,
+        scratch_shapes=[pltpu.VMEM((count, picks) + got.shape[1:], got.dtype), pltpu.SemaphoreType.DMA((count,))],
+        compiler_params=room(16),
+        cost_estimate=cost(1, 1),
+    )(slots, core, got, *[array for group in near for array in group])
 
 
 def offset_pairs(chips, chip_step, core_step):
@@ -362,6 +316,8 @@
     distance = lambda d: min(d, chips - d)
     for hops in range(chips // 2, -1, -1):
         group = [d for d in range(chips) if distance(d) == hops]
+        if not hops:
+            got, results[chips // 2] = lax.optimization_barrier((got, results[chips // 2]))
         made = far_attention(slots, tuple(d * per_chip for d in group), core_operand, got, [near[d] for d in group])
         if hops:
             made, got = lax.optimization_barrier((made, got))

time: 174 us -> 160 us (0.920)
  starting transfers between devices: 32.7 us -> 26.4 us
  Pallas kernels: 51.7 us -> 45.7 us
    ppermute x4, starting transfers between devices: 12.4 us -> 5.25 us  [shards(): lax.ppermute(results[d], 'head', offset_pairs(chips, 0, 1))]
    pallas_call x3, Pallas kernels: 18.2 us -> 13.3 us  [far_attention(): pl.pallas_call(functools.partial(far_kernel, firsts), out_shape=[jax.Shap...]
    unnamed x29 -> x41, local copies, waits for them, and re-layouts: 4.48 us -> 4.07 us
  transfers between devices with their start and end apart: 15 -> 15, of which waited for: 3 -> 5; matrix products, arithmetic and copies ran while one was open for 1% -> 1% of each run, Pallas kernels for 17% -> 21%
where the time goes in v4:
time: 160 us; the launch traced here: 159 us
  waiting for transfers between devices  59 us (37%)
  Pallas kernels  45.7 us (29%)
  starting transfers between devices  26.4 us (16%)
  blocking collectives  20.4 us (13%)
  local copies, waits for them, and re-layouts  6.04 us (4%)
    all_to_all x1, waiting for transfers between devices, shards(): lax.all_to_all(sent.reshape(seq_count, capacity, 2, BLK, HD), 'seq', spli...  54.6 us
    pallas_call x4, Pallas kernels, near_attention(): pl.pallas_call(functools.partial(near_kernel, first), out_shape=[jax.Shap...  21.6 us
    all_to_all x1, blocking collectives, shards(): lax.all_to_all(asked.reshape(seq_count, 1, capacity), 'seq', split_axis=0...  20.4 us
    pallas_call x3, Pallas kernels, far_attention(): pl.pallas_call(functools.partial(far_kernel, firsts), out_shape=[jax.Shap...  13.3 us
    ppermute x7, starting transfers between devices, shards(): lax.ppermute(piece, 'head', offset_pairs(chips, d, e))  11.5 us
    pallas_call x1, Pallas kernels, pack(): pl.pallas_call(functools.partial(pack_kernel, chunks, ahead), out_shape=j...  6.08 us
    ppermute x4, starting transfers between devices, shards(): lax.ppermute(results[d], 'head', offset_pairs(chips, 0, 1))  5.25 us
    all_to_all x1, starting transfers between devices, shards(): lax.all_to_all(sent.reshape(seq_count, capacity, 2, BLK, HD), 'seq', spli...  5 us
  transfers between devices with their start and end apart: 15, of which 5 were waited for; matrix products, arithmetic and copies ran while one was open for 1% of the time, Pallas kernels for 21%

profile of v4, /device:TPU:1, one launch (start us, length us, event | category | flops | bytes accessed | tf_op | source)
XLA Modules:
  0.0 159.2 jit_solution(6432558005587020900)
XLA Ops:
  0.0 0.7 slice.12
  0.7 0.1 copy.22
  0.8 0.1 reshape.223
  0.9 0.2 convert_reduce_fusion
  1.1 0.1 select_reduce_fusion
  1.2 0.1 reduce_sum.24
  1.3 20.4 %all_to_all.10.wanted_ref = s32[32,1,2]{2,1,0:T(1,128)} all-to-all(s32[32,1,2]{2,1,0:T(1,128)S(1)} %fusion.1), channel_id=1, replica_groups=mesh['seq'=32,'head'=8] {'seq'}, dimensions={0} | all-to-all | bytes 512 | tf_op jit(solution)/shard_map/all_to_all | solution.py:288
  21.7 6.1 %shard_map.64 = bf16[64,2,128,128]{3,2,1,0:T(8,128)(2,1)} custom-call(s32[32,1,2]{2,1,0:T(1,128)} %all_to_all.10.wanted_ref, bf16[8192,128]{1,0:T(8,128)(2,1)} %k_ref.9, bf16[8192,128]{1,0:T(8,128)(2,1)} %v_ref.9), custom_call_target="tpu_custom_call" | custom-call | bytes 8388608 | tf_op jit(solution)/shard_map/pallas_call | solution.py:121
  27.8 0.0 copy-start.18
  27.8 0.0 copy-start.19
  27.8 0.0 copy-start.17
  27.9 5.0 %all-to-all-start.1 = ((bf16[32,2,2,128,128]{4,3,2,1,0:T(8,128)(2,1)}), bf16[32,2,2,128,128]{4,3,2,1,0:T(8,128)(2,1)}, u32[]{:S(2)}, u32[]{:S(2)}) async-start(bf16[32,2,2,128,128]{4,3,2,1,0:T(8,128)(2,1)} %bitcast.9), calls=%async_computation.1 | async-start | bytes 8388608 | tf_op jit(solution)/shard_map/all_to_all | solution.py:291
  32.9 0.5 fusion.7.places_ref
  33.4 3.0 %shard_map.65 = (bf16[192,512]{1,0:T(8,128)(2,1)}, bf16[192,512]{1,0:T(8,128)(2,1)}, bf16[192,512]{1,0:T(8,128)(2,1)}, bf16[192,512]{1,0:T(8,128)(2,1)}, bf16[19...) custom-call(s32[8]{0:T(128)} %fusion.7.places_ref, ...), custom_call_target="tpu_custom_call" | custom-call | bytes 3145728 | tf_op jit(solution)/shard_map/pallas_call | solution.py:54
  36.4 2.0 %collective-permute-start = (bf16[192,512]{1,0:T(8,128)(2,1)}, bf16[192,512]{1,0:T(8,128)(2,1)S(1)}, u32[]{:S(2)}, u32[]{:S(2)}) collective-permute-start(bf16[192,512]{1,0:T(8,128)(2,1)} %get-tuple-element.41), channel_id=1, source_target_pairs={{0,1},{1,0},{2,3},{3,2},{4,5},{5,4},{6,7},{7,6},{8,9},{9,8},{10,11... | collective-permute-start | bytes 589832 | tf_op jit(solution)/shard_map/ppermute | solution.py:302
  38.4 1.3 collective-permute-start.1
  39.8 1.5 collective-permute-start.2
  41.3 1.3 collective-permute-start.3
  42.6 2.0 %collective-permute-start.4 = (bf16[192,512]{1,0:T(8,128)(2,1)}, bf16[192,512]{1,0:T(8,128)(2,1)S(1)}, u32[]{:S(2)}, u32[]{:S(2)}) collective-permute-start(bf16[192,512]{1,0:T(8,128)(2,1)} %get-tuple-element.49), channel_id=1, source_target_pairs={{0,5},{1,4},{2,7},{3,6},{4,1},{5,0},{6,3},{7,2},{8,13},{9,12},{10,... | collective-permute-start | bytes 589832 | tf_op jit(solution)/shard_map/ppermute | solution.py:302
  44.6 0.1 reduce_sum.25
  44.7 0.1 concatenate.8
  44.8 0.1 copy.19
  44.9 0.1 pad_add_fusion
  45.0 0.6 gather_fusion
  45.6 0.1 broadcast_in_dim.27
  45.7 0.1 broadcast_in_dim.28
  45.8 0.0 collective-permute-done.qb_ref
  45.8 1.5 collective-permute-start.5
  47.2 0.0 collective-permute-done.1.qa_ref
  47.3 1.8 %collective-permute-start.6 = (bf16[192,512]{1,0:T(8,128)(2,1)}, bf16[192,512]{1,0:T(8,128)(2,1)S(1)}, u32[]{:S(2)}, u32[]{:S(2)}) collective-permute-start(bf16[192,512]{1,0:T(8,128)(2,1)} %get-tuple-element.53), channel_id=1, source_target_pairs={{0,7},{1,6},{2,1},{3,0},{4,3},{5,2},{6,5},{7,4},{8,15},{9,14},{10,... | collective-permute-start | bytes 589832 | tf_op jit(solution)/shard_map/ppermute | solution.py:302
  49.1 0.1 broadcast_select_fusion
  49.1 0.1 slice.19.slots_ref
  49.2 0.5 copy-done.9
  49.7 5.4 %shard_map.66 = (f32[3,136,512]{2,1,0:T(8,128)}, bf16[3,512,128]{2,1,0:T(8,128)(2,1)}) custom-call(s32[12,5]{1,0:T(8,128)} %bitcast.10, s32[1]{0:T(128)} %bitcast.4.core_ref, bf16[192,512]{1,0:T(8,128)(2,1)} %get-tuple-element.40.qa_ref, bf16[192,512]{1,0:T(8,128)(2,1)} %copy-done.14, bf16[8192,128]{1,0:T(8,128)(2,1)} %k_ref.9, bf16[8192,128]{1,0:T(8,128)(2,1)} %v_ref.9), custom_call_target="tpu_custom_call" | custom-call | flops 503316480 | bytes 2555904 | tf_op jit(solution)/shard_map/pallas_call | solution.py:186
  55.1 0.0 collective-permute-done.2.qb_ref
  55.2 0.7 copy-done.13
  55.9 5.4 %shard_map.67 = (f32[3,136,512]{2,1,0:T(8,128)}, bf16[3,512,128]{2,1,0:T(8,128)(2,1)}) custom-call(s32[12,5]{1,0:T(8,128)} %bitcast.11, s32[1]{0:T(128)} %bitcast.4.core_ref, bf16[192,512]{1,0:T(8,128)(2,1)} %copy-done.12, bf16[192,512]{1,0:T(8,128)(2,1)} %copy-done.13, bf16[8192,128]{1,0:T(8,128)(2,1)} %k_ref.9, bf16[8192,128]{1,0:T(8,128)(2,1)} %v_ref.9), custom_call_target="tpu_custom_call" | custom-call | flops 503316480 | bytes 2555904 | tf_op jit(solution)/shard_map/pallas_call | solution.py:186
  61.3 0.0 collective-permute-done.3.qa_ref
  61.3 0.0 collective-permute-done.4.qb_ref
  61.3 0.7 copy-done.10
  62.0 0.7 copy-done.11
  62.7 5.4 %shard_map.68 = (f32[3,136,512]{2,1,0:T(8,128)}, bf16[3,512,128]{2,1,0:T(8,128)(2,1)}) custom-call(s32[12,5]{1,0:T(8,128)} %bitcast.12, s32[1]{0:T(128)} %bitcast.4.core_ref, bf16[192,512]{1,0:T(8,128)(2,1)} %copy-done.10, bf16[192,512]{1,0:T(8,128)(2,1)} %copy-done.11, bf16[8192,128]{1,0:T(8,128)(2,1)} %k_ref.9, bf16[8192,128]{1,0:T(8,128)(2,1)} %v_ref.9), custom_call_target="tpu_custom_call" | custom-call | flops 503316480 | bytes 2555904 | tf_op jit(solution)/shard_map/pallas_call | solution.py:186
  68.0 0.0 collective-permute-done.5.qa_ref
  68.1 0.0 collective-permute-done.6.qb_ref
  68.1 0.7 copy-done.15
  68.7 0.7 copy-done.16
  69.4 5.5 %shard_map.69 = (f32[3,136,512]{2,1,0:T(8,128)}, bf16[3,512,128]{2,1,0:T(8,128)(2,1)}) custom-call(s32[12,5]{1,0:T(8,128)} %bitcast.13, s32[1]{0:T(128)} %bitcast.4.core_ref, bf16[192,512]{1,0:T(8,128)(2,1)} %copy-done.15, bf16[192,512]{1,0:T(8,128)(2,1)} %copy-done.16, bf16[8192,128]{1,0:T(8,128)(2,1)} %k_ref.9, bf16[8192,128]{1,0:T(8,128)(2,1)} %v_ref.9), custom_call_target="tpu_custom_call" | custom-call | flops 503316480 | bytes 2555904 | tf_op jit(solution)/shard_map/pallas_call | solution.py:186
  74.9 54.6 %all-to-all-done.1 = bf16[32,2,2,128,128]{4,3,2,1,0:T(8,128)(2,1)} async-done(((bf16[32,2,2,128,128]{4,3,2,1,0:T(8,128)(2,1)}), bf16[32,2,2,128,128]{4,3,2,1,0:T(8,128)(2,1)}, u32[]{:S(2)}, u32[]{:S(2)}) %all-to-all-start.1) | async-done | bytes 4194336 | tf_op jit(solution)/shard_map/all_to_all | solution.py:291
  129.5 3.8 %shard_map.70 = bf16[2,192,512]{2,1,0:T(8,128)(2,1)S(1)} custom-call(s32[12,3]{1,0:T(8,128)S(1)} %slice.19.slots_ref, s32[1]{0:T(128)} %bitcast.4.core_ref, bf16[64,2,128,128]{3,2,1,0:T(8,128)(2,1)} %bitcast.2.got_ref, f32[3,136,512]{2,1,0:T(8,128)S(1)} %copy-done.2, bf16[3,512,128]{2,1,0:T(8,128)(2,1)S(1)} %copy-done.5), custom_call_target="tpu_custom_call" | custom-call | flops 1 | bytes 1 | tf_op jit(solution)/shard_map/pallas_call | solution.py:246
  133.3 0.0 copy-start
  133.3 3.2 %collective-permute-start.7 = (bf16[2,192,512]{2,1,0:T(8,128)(2,1)S(1)}, bf16[2,192,512]{2,1,0:T(8,128)(2,1)S(1)}, u32[]{:S(2)}, u32[]{:S(2)}) collective-permute-start(bf16[2,192,512]{2,1,0:T(8,128)(2,1)S(1)} %shard_map.70), channel_id=1, source_target_pairs={{0,4},{1,5},{2,6},{3,7},{4,0},{5,1},{6,2},{7,3},{8,12},{9,13},{10,... | collective-permute-start | bytes 1179656 | tf_op jit(solution)/shard_map/ppermute | solution.py:325
  136.5 5.8 %shard_map.71 = (bf16[2,192,512]{2,1,0:T(8,128)(2,1)S(1)}, bf16[2,192,512]{2,1,0:T(8,128)(2,1)S(1)}) custom-call(s32[12,3]{1,0:T(8,128)S(1)} %slice.19.slots_ref, s32[1]{0:T(128)} %bitcast.4.core_ref, bf16[64,2,128,128]{3,2,1,0:T(8,128)(2,1)} %bitcast.2.got_ref, f32[3,136,512]{2,1,0:T(8,128)S(1)} %copy-done.1, bf16[3,512,128]{2,1,0:T(8,128)(2,1)S(1)} %copy-done.6, ...), custom_call_target="tpu_custom_call" | custom-call | flops 1 | bytes 1 | tf_op jit(solution)/shard_map/pallas_call | solution.py:246
  142.3 0.9 collective-permute-start.9
  143.2 0.7 collective-permute-start.12
  143.9 0.3 collective-permute-done.7.refs_4_
  144.1 3.7 %shard_map.72.refs_0_ = bf16[2,192,512]{2,1,0:T(8,128)(2,1)S(1)} custom-call(s32[12,3]{1,0:T(8,128)S(1)} %slice.19.slots_ref, s32[1]{0:T(128)} %bitcast.4.core_ref, bf16[64,2,128,128]{3,2,1,0:T(8,128)(2,1)} %bitcast.2.got_ref, f32[3,136,512]{2,1,0:T(8,128)S(1)} %copy-done, bf16[3,512,128]{2,1,0:T(8,128)(2,1)S(1)} %copy-done.4), custom_call_target="tpu_custom_call" | custom-call | flops 1 | bytes 1 | tf_op jit(solution)/shard_map/pallas_call | solution.py:246
  147.9 2.8 %collective-permute-start.8 = (bf16[2,192,512]{2,1,0:T(8,128)(2,1)S(1)}, bf16[2,192,512]{2,1,0:T(8,128)(2,1)S(1)}, u32[]{:S(2)}, u32[]{:S(2)}) collective-permute-start(bf16[2,192,512]{2,1,0:T(8,128)(2,1)S(1)} %shard_map.72.refs_0_), channel_id=1, source_target_pairs={{0,1},{1,0},{2,3},{3,2},{4,5},{5,4},{6,7},{7,6},{8,9},{9,8},{10,11... | collective-permute-start | bytes 1179656 | tf_op jit(solution)/shard_map/ppermute | solution.py:328
  150.7 0.1 collective-permute-start.11
  150.8 2.8 %collective-permute-done.9.refs_2_ = bf16[2,192,512]{2,1,0:T(8,128)(2,1)S(1)} collective-permute-done((bf16[2,192,512]{2,1,0:T(8,128)(2,1)S(1)}, bf16[2,192,512]{2,1,0:T(8,128)(2,1)S(1)}, u32[]{:S(2)}, u32[]{:S(2)}) %collective-permute-start.9) | collective-permute-done | bytes 393248 | tf_op jit(solution)/shard_map/ppermute | solution.py:325
  153.6 1.8 %collective-permute-start.10 = (bf16[2,192,512]{2,1,0:T(8,128)(2,1)S(1)}, bf16[2,192,512]{2,1,0:T(8,128)(2,1)S(1)}, u32[]{:S(2)}, u32[]{:S(2)}) collective-permute-start(bf16[2,192,512]{2,1,0:T(8,128)(2,1)S(1)} %collective-permute-done.9.refs_2_), channel_id=1, source_target_pairs={{0,1},{1,0},{2,3},{3,2},{4,5},{5,4},{6,7},{7,6},{8,9},{9,8},{10,11... | collective-permute-start | bytes 1179656 | tf_op jit(solution)/shard_map/ppermute | solution.py:328
  155.4 0.5 collective-permute-start.13
  155.9 0.8 collective-permute-done.10.refs_3_
  156.7 0.6 collective-permute-done.13.refs_7_
  157.3 1.7 %shard_map.73 = bf16[192,4096]{1,0:T(8,128)(2,1)} custom-call(s32[8]{0:T(128)S(1)} %copy-done.8, bf16[2,192,512]{2,1,0:T(8,128)(2,1)S(1)} %shard_map.72.refs_0_, bf16[2,192,512]{2,1,0:T(8,128)(2,1)S(1)} %collective-permute-done.8.refs_1_, bf16[2,192,512]{2,1,0:T(8,128)(2,1)S(1)} %collective-permute-done.9.refs_2_, ...), custom_call_target="tpu_custom_call" | custom-call | bytes 3145728 | tf_op jit(solution)/shard_map/pallas_call | solution.py:85
  (44 shorter events, 0.2 us)
Async XLA Ops:
  27.8 5.1 %copy-start.18 = (s32[8]{0:T(128)S(1)}, s32[8]{0:T(128)}, u32[]{:S(2)}) copy-start(s32[8]{0:T(128)} %constant.114.clone) | copy-start | bytes 100
  27.8 5.1 %copy-start.19 = (s32[8]{0:T(128)S(1)}, s32[8]{0:T(128)}, u32[]{:S(2)}) copy-start(s32[8]{0:T(128)} %constant.115.clone) | copy-start | bytes 100
  27.8 16.9 %copy-start.17 = (s32[12,8]{0,1:T(8,128)S(1)}, s32[12,8]{0,1:T(8,128)}, u32[]{:S(2)}) copy-start(s32[12,8]{0,1:T(8,128)} %param.9) | copy-start | bytes 1156
  27.9 101.6 %all-to-all-start.1 = ((bf16[32,2,2,128,128]{4,3,2,1,0:T(8,128)(2,1)}), bf16[32,2,2,128,128]{4,3,2,1,0:T(8,128)(2,1)}, u32[]{:S(2)}, u32[]{:S(2)}) async-start(bf16[32,2,2,128,128]{4,3,2,1,0:T(8,128)(2,1)} %bitcast.9), calls=%async_computation.1 | async-start | bytes 8388608 | tf_op jit(solution)/shard_map/all_to_all | solution.py:291
  36.4 9.4 %collective-permute-start = (bf16[192,512]{1,0:T(8,128)(2,1)}, bf16[192,512]{1,0:T(8,128)(2,1)S(1)}, u32[]{:S(2)}, u32[]{:S(2)}) collective-permute-start(bf16[192,512]{1,0:T(8,128)(2,1)} %get-tuple-element.41), channel_id=1, source_target_pairs={{0,1},{1,0},{2,3},{3,2},{4,5},{5,4},{6,7},{7,6},{8,9},{9,8},{10,11... | collective-permute-start | bytes 589832 | tf_op jit(solution)/shard_map/ppermute | solution.py:302
  38.4 8.8 %collective-permute-start.1 = (bf16[192,512]{1,0:T(8,128)(2,1)}, bf16[192,512]{1,0:T(8,128)(2,1)S(1)}, u32[]{:S(2)}, u32[]{:S(2)}) collective-permute-start(bf16[192,512]{1,0:T(8,128)(2,1)} %get-tuple-element.44), channel_id=1, source_target_pairs={{0,2},{1,3},{2,4},{3,5},{4,6},{5,7},{6,0},{7,1},{8,10},{9,11},{10,... | collective-permute-start | bytes 589832 | tf_op jit(solution)/shard_map/ppermute | solution.py:302
  39.8 15.4 %collective-permute-start.2 = (bf16[192,512]{1,0:T(8,128)(2,1)}, bf16[192,512]{1,0:T(8,128)(2,1)S(1)}, u32[]{:S(2)}, u32[]{:S(2)}) collective-permute-start(bf16[192,512]{1,0:T(8,128)(2,1)} %get-tuple-element.45), channel_id=1, source_target_pairs={{0,3},{1,2},{2,5},{3,4},{4,7},{5,6},{6,1},{7,0},{8,11},{9,10},{10,... | collective-permute-start | bytes 589832 | tf_op jit(solution)/shard_map/ppermute | solution.py:302
  41.3 20.0 %collective-permute-start.3 = (bf16[192,512]{1,0:T(8,128)(2,1)}, bf16[192,512]{1,0:T(8,128)(2,1)S(1)}, u32[]{:S(2)}, u32[]{:S(2)}) collective-permute-start(bf16[192,512]{1,0:T(8,128)(2,1)} %get-tuple-element.48), channel_id=1, source_target_pairs={{0,4},{1,5},{2,6},{3,7},{4,0},{5,1},{6,2},{7,3},{8,12},{9,13},{10,... | collective-permute-start | bytes 589832 | tf_op jit(solution)/shard_map/ppermute | solution.py:302
  42.6 18.7 %collective-permute-start.4 = (bf16[192,512]{1,0:T(8,128)(2,1)}, bf16[192,512]{1,0:T(8,128)(2,1)S(1)}, u32[]{:S(2)}, u32[]{:S(2)}) collective-permute-start(bf16[192,512]{1,0:T(8,128)(2,1)} %get-tuple-element.49), channel_id=1, source_target_pairs={{0,5},{1,4},{2,7},{3,6},{4,1},{5,0},{6,3},{7,2},{8,13},{9,12},{10,... | collective-permute-start | bytes 589832 | tf_op jit(solution)/shard_map/ppermute | solution.py:302
  45.8 3.4 %copy-start.14 = (bf16[192,512]{1,0:T(8,128)(2,1)}, bf16[192,512]{1,0:T(8,128)(2,1)S(1)}, u32[]{:S(2)}) copy-start(bf16[192,512]{1,0:T(8,128)(2,1)S(1)} %collective-permute-done.qb_ref) | copy-start | bytes 589828
  45.8 22.3 %collective-permute-start.5 = (bf16[192,512]{1,0:T(8,128)(2,1)}, bf16[192,512]{1,0:T(8,128)(2,1)S(1)}, u32[]{:S(2)}, u32[]{:S(2)}) collective-permute-start(bf16[192,512]{1,0:T(8,128)(2,1)} %get-tuple-element.52), channel_id=1, source_target_pairs={{0,6},{1,7},{2,0},{3,1},{4,2},{5,3},{6,4},{7,5},{8,14},{9,15},{10,... | collective-permute-start | bytes 589832 | tf_op jit(solution)/shard_map/ppermute | solution.py:302
  47.3 7.9 %copy-start.12 = (bf16[192,512]{1,0:T(8,128)(2,1)}, bf16[192,512]{1,0:T(8,128)(2,1)S(1)}, u32[]{:S(2)}) copy-start(bf16[192,512]{1,0:T(8,128)(2,1)S(1)} %collective-permute-done.1.qa_ref) | copy-start | bytes 589828
  47.3 20.8 %collective-permute-start.6 = (bf16[192,512]{1,0:T(8,128)(2,1)}, bf16[192,512]{1,0:T(8,128)(2,1)S(1)}, u32[]{:S(2)}, u32[]{:S(2)}) collective-permute-start(bf16[192,512]{1,0:T(8,128)(2,1)} %get-tuple-element.53), channel_id=1, source_target_pairs={{0,7},{1,6},{2,1},{3,0},{4,3},{5,2},{6,5},{7,4},{8,15},{9,14},{10,... | collective-permute-start | bytes 589832 | tf_op jit(solution)/shard_map/ppermute | solution.py:302
  49.1 0.6 copy-start.9
  55.2 0.7 copy-start.13
  61.3 0.7 copy-start.10
  62.0 0.7 copy-start.11
  68.0 61.4 %copy-start.2 = (f32[3,136,512]{2,1,0:T(8,128)S(1)}, f32[3,136,512]{2,1,0:T(8,128)}, u32[]{:S(2)}) copy-start(f32[3,136,512]{2,1,0:T(8,128)} %get-tuple-element.58.refs_0_) | copy-start | bytes 2506756
  68.0 61.4 %copy-start.5 = (bf16[3,512,128]{2,1,0:T(8,128)(2,1)S(1)}, bf16[3,512,128]{2,1,0:T(8,128)(2,1)}, u32[]{:S(2)}) copy-start(bf16[3,512,128]{2,1,0:T(8,128)(2,1)} %get-tuple-element.59.refs_1_) | copy-start | bytes 1179652
  68.1 0.7 copy-start.15
  68.7 0.7 copy-start.16
  129.5 7.0 %copy-start.1 = (f32[3,136,512]{2,1,0:T(8,128)S(1)}, f32[3,136,512]{2,1,0:T(8,128)}, u32[]{:S(2)}) copy-start(f32[3,136,512]{2,1,0:T(8,128)} %get-tuple-element.61.refs_0_) | copy-start | bytes 2506756
  129.5 7.0 %copy-start.3 = (f32[3,136,512]{2,1,0:T(8,128)S(1)}, f32[3,136,512]{2,1,0:T(8,128)}, u32[]{:S(2)}) copy-start(f32[3,136,512]{2,1,0:T(8,128)} %get-tuple-element.63.refs_2_) | copy-start | bytes 2506756
  129.5 7.0 %copy-start.6 = (bf16[3,512,128]{2,1,0:T(8,128)(2,1)S(1)}, bf16[3,512,128]{2,1,0:T(8,128)(2,1)}, u32[]{:S(2)}) copy-start(bf16[3,512,128]{2,1,0:T(8,128)(2,1)} %get-tuple-element.62.refs_1_) | copy-start | bytes 1179652
  129.5 7.0 %copy-start.7 = (bf16[3,512,128]{2,1,0:T(8,128)(2,1)S(1)}, bf16[3,512,128]{2,1,0:T(8,128)(2,1)}, u32[]{:S(2)}) copy-start(bf16[3,512,128]{2,1,0:T(8,128)(2,1)} %get-tuple-element.64.refs_3_) | copy-start | bytes 1179652
  133.3 10.9 %copy-start = (f32[3,136,512]{2,1,0:T(8,128)S(1)}, f32[3,136,512]{2,1,0:T(8,128)}, u32[]{:S(2)}) copy-start(f32[3,136,512]{2,1,0:T(8,128)} %get-tuple-element.70.refs_0_) | copy-start | bytes 2506756
  133.3 10.9 %copy-start.4 = (bf16[3,512,128]{2,1,0:T(8,128)(2,1)S(1)}, bf16[3,512,128]{2,1,0:T(8,128)(2,1)}, u32[]{:S(2)}) copy-start(bf16[3,512,128]{2,1,0:T(8,128)(2,1)} %get-tuple-element.71.refs_1_) | copy-start | bytes 1179652
  133.3 10.9 %collective-permute-start.7 = (bf16[2,192,512]{2,1,0:T(8,128)(2,1)S(1)}, bf16[2,192,512]{2,1,0:T(8,128)(2,1)S(1)}, u32[]{:S(2)}, u32[]{:S(2)}) collective-permute-start(bf16[2,192,512]{2,1,0:T(8,128)(2,1)S(1)} %shard_map.70), channel_id=1, source_target_pairs={{0,4},{1,5},{2,6},{3,7},{4,0},{5,1},{6,2},{7,3},{8,12},{9,13},{10,... | collective-permute-start | bytes 1179656 | tf_op jit(solution)/shard_map/ppermute | solution.py:325
  142.3 15.0 %copy-start.8 = (s32[8]{0:T(128)S(1)}, s32[8]{0:T(128)}, u32[]{:S(2)}) copy-start(s32[8]{0:T(128)} %fusion.7.places_ref) | copy-start | bytes 100
  142.3 11.3 %collective-permute-start.9 = (bf16[2,192,512]{2,1,0:T(8,128)(2,1)S(1)}, bf16[2,192,512]{2,1,0:T(8,128)(2,1)S(1)}, u32[]{:S(2)}, u32[]{:S(2)}) collective-permute-start(bf16[2,192,512]{2,1,0:T(8,128)(2,1)S(1)} %get-tuple-element.72), channel_id=1, source_target_pairs={{0,6},{1,7},{2,0},{3,1},{4,2},{5,3},{6,4},{7,5},{8,14},{9,15},{10,... | collective-permute-start | bytes 1179656 | tf_op jit(solution)/shard_map/ppermute | solution.py:325
  143.2 12.2 %collective-permute-start.12 = (bf16[2,192,512]{2,1,0:T(8,128)(2,1)S(1)}, bf16[2,192,512]{2,1,0:T(8,128)(2,1)S(1)}, u32[]{:S(2)}, u32[]{:S(2)}) collective-permute-start(bf16[2,192,512]{2,1,0:T(8,128)(2,1)S(1)} %get-tuple-element.74), channel_id=1, source_target_pairs={{0,2},{1,3},{2,4},{3,5},{4,6},{5,7},{6,0},{7,1},{8,10},{9,11},{10,... | collective-permute-start | bytes 1179656 | tf_op jit(solution)/shard_map/ppermute | solution.py:325
  147.9 8.0 %collective-permute-start.8 = (bf16[2,192,512]{2,1,0:T(8,128)(2,1)S(1)}, bf16[2,192,512]{2,1,0:T(8,128)(2,1)S(1)}, u32[]{:S(2)}, u32[]{:S(2)}) collective-permute-start(bf16[2,192,512]{2,1,0:T(8,128)(2,1)S(1)} %shard_map.72.refs_0_), channel_id=1, source_target_pairs={{0,1},{1,0},{2,3},{3,2},{4,5},{5,4},{6,7},{7,6},{8,9},{9,8},{10,11... | collective-permute-start | bytes 1179656 | tf_op jit(solution)/shard_map/ppermute | solution.py:328
  150.7 6.0 %collective-permute-start.11 = (bf16[2,192,512]{2,1,0:T(8,128)(2,1)S(1)}, bf16[2,192,512]{2,1,0:T(8,128)(2,1)S(1)}, u32[]{:S(2)}, u32[]{:S(2)}) collective-permute-start(bf16[2,192,512]{2,1,0:T(8,128)(2,1)S(1)} %collective-permute-done.7.refs_4_), channel_id=1, source_target_pairs={{0,1},{1,0},{2,3},{3,2},{4,5},{5,4},{6,7},{7,6},{8,9},{9,8},{10,11... | collective-permute-start | bytes 1179656 | tf_op jit(solution)/shard_map/ppermute | solution.py:328
  153.6 3.1 %collective-permute-start.10 = (bf16[2,192,512]{2,1,0:T(8,128)(2,1)S(1)}, bf16[2,192,512]{2,1,0:T(8,128)(2,1)S(1)}, u32[]{:S(2)}, u32[]{:S(2)}) collective-permute-start(bf16[2,192,512]{2,1,0:T(8,128)(2,1)S(1)} %collective-permute-done.9.refs_2_), channel_id=1, source_target_pairs={{0,1},{1,0},{2,3},{3,2},{4,5},{5,4},{6,7},{7,6},{8,9},{9,8},{10,11... | collective-permute-start | bytes 1179656 | tf_op jit(solution)/shard_map/ppermute | solution.py:328
  155.4 1.9 %collective-permute-start.13 = (bf16[2,192,512]{2,1,0:T(8,128)(2,1)S(1)}, bf16[2,192,512]{2,1,0:T(8,128)(2,1)S(1)}, u32[]{:S(2)}, u32[]{:S(2)}) collective-permute-start(bf16[2,192,512]{2,1,0:T(8,128)(2,1)S(1)} %collective-permute-done.12.refs_6_), channel_id=1, source_target_pairs={{0,1},{1,0},{2,3},{3,2},{4,5},{5,4},{6,7},{7,6},{8,9},{9,8},{10,11... | collective-permute-start | bytes 1179656 | tf_op jit(solution)/shard_map/ppermute | solution.py:328

commit v5 on v4

--- a/solution.py
+++ b/solution.py
@@ -65,32 +65,33 @@
     )(places, queries)
 
 
-def join_outputs_kernel(places_ref, *refs):
-    count = len(refs) - 2
-    pieces, out_ref, sem = refs[:count], refs[count], refs[count + 1]
-    width = pieces[0].shape[2]
+def join_outputs_kernel(count, chosen, places_ref, *refs):
+    pieces, out_ref, sem = refs[: len(chosen)], refs[-2], refs[-1]
+    width = out_ref.shape[1] // count
     copies = []
-    for i in range(count):
+    for piece, i in zip(pieces, chosen):
         start = pl.multiple_of(places_ref[i] * width, width)
-        copies.append(pltpu.make_async_copy(pieces[i].at[i % CORES], out_ref.at[:, pl.ds(start, width)], sem.at[i]))
+        copies.append(pltpu.make_async_copy(piece.at[i % CORES], out_ref.at[:, pl.ds(start, width)], sem.at[i]))
     for copy in copies:
         copy.start()
     for copy in copies:
         copy.wait()
 
 
-def join_outputs(pieces, places):
+def join_outputs(pieces, chosen, places, out=None):
     count = len(pieces)
     _, rows, width = pieces[0].shape
-    return pl.pallas_call(
-        join_outputs_kernel,
+    rest = [] if out is None else [out]
+    return pl.pallas_call(
+        functools.partial(join_outputs_kernel, count, chosen),
         out_shape=jax.ShapeDtypeStruct((rows, width * count), pieces[0].dtype),
-        in_specs=[SMEM] + [VMEM] * count,
+        in_specs=[SMEM] + [VMEM] * len(chosen) + [HBM] * len(rest),
         out_specs=HBM,
         scratch_shapes=[pltpu.SemaphoreType.DMA((count,))],
+        input_output_aliases={1 + len(chosen): 0} if rest else {},
         compiler_params=room(6),
-        cost_estimate=cost(0, 4 * rows * width * count),
-    )(places, *pieces)
+        cost_estimate=cost(0, 4 * rows * width * len(chosen)),
+    )(places, *[pieces[i] for i in chosen], *rest)
 
 
 def pack_kernel(chunks, ahead, wanted_ref, k_ref, v_ref, out_ref, buf, in_sem, out_sem):
@@ -217,18 +218,19 @@
         g, i = divmod(n, blocks)
         kept_ref, q_ref = near_refs[2 * g : 2 * g + 2]
         wait_for(far_buf.at[n], far_sem.at[n])
-        score = scores_of(jnp.concatenate([far_buf[n, j, 0] for j in range(picks)], axis=0), q_ref[i])
-        before = kept_ref[i, HIGHEST : HIGHEST + 1, :]
-        highest = jnp.maximum(jnp.max(score, axis=0, keepdims=True) * factor, before)
-        exponent = jnp.exp2(score * factor - highest)
-        kept = jnp.exp2(before - highest)
-        total = jnp.sum(exponent, axis=0, keepdims=True) + kept * kept_ref[i, TOTAL : TOTAL + 1, :]
-        partial = weighted(
-            jnp.concatenate([far_buf[n, j, 1] for j in range(picks)], axis=0), exponent.astype(jnp.bfloat16)
-        )
-        merged = (partial + kept * kept_ref[i, 0:HD, :]) * (1.0 / total)
+        keys = jnp.concatenate([far_buf[n, j, 0] for j in range(picks)], axis=0)
+        values = jnp.concatenate([far_buf[n, j, 1] for j in range(picks)], axis=0)
         for r in range(ratio):
-            turned = merged[:, r * BLK : (r + 1) * BLK].T.astype(o_refs[g].dtype)
+            queries = slice(r * BLK, (r + 1) * BLK)
+            score = scores_of(keys, q_ref[i, queries, :])
+            before = kept_ref[i, HIGHEST : HIGHEST + 1, queries]
+            highest = jnp.maximum(jnp.max(score, axis=0, keepdims=True) * factor, before)
+            exponent = jnp.exp2(score * factor - highest)
+            kept = jnp.exp2(before - highest)
+            total = jnp.sum(exponent, axis=0, keepdims=True) + kept * kept_ref[i, TOTAL : TOTAL + 1, queries]
+            partial = weighted(values, exponent.astype(jnp.bfloat16))
+            merged = (partial + kept * kept_ref[i, 0:HD, queries]) * (1.0 / total)
+            turned = merged.T.astype(o_refs[g].dtype)
             for part in range(CORES):
                 low, high = max(i * BLK, part * half), min((i + 1) * BLK, (part + 1) * half)
                 if low < high:
@@ -326,7 +328,9 @@
     joined = []
     for d in range(chips):
         joined += [results[d], lax.ppermute(results[d], "head", offset_pairs(chips, 0, 1))]
-    return join_outputs(joined, ahead)
+    early = tuple(i for i in range(heads) if i // CORES in (0, chips // 2))
+    late = tuple(i for i in range(heads) if i not in early)
+    return join_outputs(joined, late, ahead, join_outputs(joined, early, ahead))
 
 
 def solution(mesh):

time: 160 us -> 160 us (level)
  transfers between devices with their start and end apart: 15 -> 15, of which waited for: 5 -> 3; matrix products, arithmetic and copies ran while one was open for 1% -> 1% of each run, Pallas kernels for 21% -> 22%
where the time goes in v5:
time: 160 us; the launch traced here: 159 us
  waiting for transfers between devices  57.6 us (36%)
  Pallas kernels  46.4 us (29%)
  starting transfers between devices  26.6 us (17%)
  blocking collectives  20.4 us (13%)
  local copies, waits for them, and re-layouts  6.03 us (4%)
    all_to_all x1, waiting for transfers between devices, shards(): lax.all_to_all(sent.reshape(seq_count, capacity, 2, BLK, HD), 'seq', spli...  54.5 us
    pallas_call x4, Pallas kernels, near_attention(): pl.pallas_call(functools.partial(near_kernel, first), out_shape=[jax.Shap...  21.7 us
    all_to_all x1, blocking collectives, shards(): lax.all_to_all(asked.reshape(seq_count, 1, capacity), 'seq', split_axis=0...  20.4 us
    pallas_call x3, Pallas kernels, far_attention(): pl.pallas_call(functools.partial(far_kernel, firsts), out_shape=[jax.Shap...  13.1 us
    ppermute x7, starting transfers between devices, shards(): lax.ppermute(piece, 'head', offset_pairs(chips, d, e))  11.5 us
    pallas_call x1, Pallas kernels, pack(): pl.pallas_call(functools.partial(pack_kernel, chunks, ahead), out_shape=j...  5.73 us
    ppermute x4, starting transfers between devices, shards(): lax.ppermute(results[d], 'head', offset_pairs(chips, 0, 1))  5.36 us
    all_to_all x1, starting transfers between devices, shards(): lax.all_to_all(sent.reshape(seq_count, capacity, 2, BLK, HD), 'seq', spli...  5 us
  transfers between devices with their start and end apart: 15, of which 3 were waited for; matrix products, arithmetic and copies ran while one was open for 1% of the time, Pallas kernels for 22%

profile of v5, /device:TPU:1, one launch (start us, length us, event | category | flops | bytes accessed | tf_op | source)
XLA Modules:
  0.0 158.6 jit_solution(3558212535907570778)
XLA Ops:
  0.0 0.7 slice.12
  0.7 0.1 copy.23
  0.8 0.1 reshape.223
  0.9 0.2 convert_reduce_fusion
  1.1 0.1 select_reduce_fusion
  1.2 0.1 reduce_sum.24
  1.3 20.4 %all_to_all.10.wanted_ref = s32[32,1,2]{2,1,0:T(1,128)} all-to-all(s32[32,1,2]{2,1,0:T(1,128)S(1)} %fusion.1), channel_id=1, replica_groups=mesh['seq'=32,'head'=8] {'seq'}, dimensions={0} | all-to-all | bytes 512 | tf_op jit(solution)/shard_map/all_to_all | solution.py:290
  21.7 5.7 %shard_map.64 = bf16[64,2,128,128]{3,2,1,0:T(8,128)(2,1)} custom-call(s32[32,1,2]{2,1,0:T(1,128)} %all_to_all.10.wanted_ref, bf16[8192,128]{1,0:T(8,128)(2,1)} %k_ref.9, bf16[8192,128]{1,0:T(8,128)(2,1)} %v_ref.9), custom_call_target="tpu_custom_call" | custom-call | bytes 8388608 | tf_op jit(solution)/shard_map/pallas_call | solution.py:122
  27.5 0.0 copy-start.18
  27.5 0.0 copy-start.19
  27.5 0.0 copy-start.17
  27.5 5.0 %all-to-all-start.1 = ((bf16[32,2,2,128,128]{4,3,2,1,0:T(8,128)(2,1)}), bf16[32,2,2,128,128]{4,3,2,1,0:T(8,128)(2,1)}, u32[]{:S(2)}, u32[]{:S(2)}) async-start(bf16[32,2,2,128,128]{4,3,2,1,0:T(8,128)(2,1)} %bitcast.9), calls=%async_computation.1 | async-start | bytes 8388608 | tf_op jit(solution)/shard_map/all_to_all | solution.py:293
  32.6 0.5 fusion.7.places_ref
  33.1 3.0 %shard_map.65 = (bf16[192,512]{1,0:T(8,128)(2,1)}, bf16[192,512]{1,0:T(8,128)(2,1)}, bf16[192,512]{1,0:T(8,128)(2,1)}, bf16[192,512]{1,0:T(8,128)(2,1)}, bf16[19...) custom-call(s32[8]{0:T(128)} %fusion.7.places_ref, ...), custom_call_target="tpu_custom_call" | custom-call | bytes 3145728 | tf_op jit(solution)/shard_map/pallas_call | solution.py:54
  36.1 2.0 %collective-permute-start = (bf16[192,512]{1,0:T(8,128)(2,1)}, bf16[192,512]{1,0:T(8,128)(2,1)S(1)}, u32[]{:S(2)}, u32[]{:S(2)}) collective-permute-start(bf16[192,512]{1,0:T(8,128)(2,1)} %get-tuple-element.41), channel_id=1, source_target_pairs={{0,1},{1,0},{2,3},{3,2},{4,5},{5,4},{6,7},{7,6},{8,9},{9,8},{10,11... | collective-permute-start | bytes 589832 | tf_op jit(solution)/shard_map/ppermute | solution.py:304
  38.1 1.3 collective-permute-start.1
  39.4 1.5 collective-permute-start.2
  40.9 1.3 collective-permute-start.3
  42.2 2.0 %collective-permute-start.4 = (bf16[192,512]{1,0:T(8,128)(2,1)}, bf16[192,512]{1,0:T(8,128)(2,1)S(1)}, u32[]{:S(2)}, u32[]{:S(2)}) collective-permute-start(bf16[192,512]{1,0:T(8,128)(2,1)} %get-tuple-element.49), channel_id=1, source_target_pairs={{0,5},{1,4},{2,7},{3,6},{4,1},{5,0},{6,3},{7,2},{8,13},{9,12},{10,... | collective-permute-start | bytes 589832 | tf_op jit(solution)/shard_map/ppermute | solution.py:304
  44.2 0.1 reduce_sum.25
  44.4 0.1 concatenate.8
  44.5 0.1 copy.20
  44.6 0.1 pad_add_fusion
  44.7 0.6 gather_fusion
  45.3 0.1 broadcast_in_dim.27
  45.3 0.1 broadcast_in_dim.28
  45.4 0.0 collective-permute-done.qb_ref
  45.4 1.5 collective-permute-start.5
  46.9 0.0 collective-permute-done.1.qa_ref
  46.9 1.8 %collective-permute-start.6 = (bf16[192,512]{1,0:T(8,128)(2,1)}, bf16[192,512]{1,0:T(8,128)(2,1)S(1)}, u32[]{:S(2)}, u32[]{:S(2)}) collective-permute-start(bf16[192,512]{1,0:T(8,128)(2,1)} %get-tuple-element.53), channel_id=1, source_target_pairs={{0,7},{1,6},{2,1},{3,0},{4,3},{5,2},{6,5},{7,4},{8,15},{9,14},{10,... | collective-permute-start | bytes 589832 | tf_op jit(solution)/shard_map/ppermute | solution.py:304
  48.7 0.1 broadcast_select_fusion
  48.8 0.1 slice.19.slots_ref
  48.9 0.5 copy-done.9
  49.4 5.5 %shard_map.66 = (f32[3,136,512]{2,1,0:T(8,128)}, bf16[3,512,128]{2,1,0:T(8,128)(2,1)}) custom-call(s32[12,5]{1,0:T(8,128)} %bitcast.10, s32[1]{0:T(128)} %bitcast.4.core_ref, bf16[192,512]{1,0:T(8,128)(2,1)} %get-tuple-element.40.qa_ref, bf16[192,512]{1,0:T(8,128)(2,1)} %copy-done.14, bf16[8192,128]{1,0:T(8,128)(2,1)} %k_ref.9, bf16[8192,128]{1,0:T(8,128)(2,1)} %v_ref.9), custom_call_target="tpu_custom_call" | custom-call | flops 503316480 | bytes 2555904 | tf_op jit(solution)/shard_map/pallas_call | solution.py:187
  54.9 0.0 collective-permute-done.2.qb_ref
  55.0 0.7 copy-done.13
  55.6 5.4 %shard_map.67 = (f32[3,136,512]{2,1,0:T(8,128)}, bf16[3,512,128]{2,1,0:T(8,128)(2,1)}) custom-call(s32[12,5]{1,0:T(8,128)} %bitcast.11, s32[1]{0:T(128)} %bitcast.4.core_ref, bf16[192,512]{1,0:T(8,128)(2,1)} %copy-done.12, bf16[192,512]{1,0:T(8,128)(2,1)} %copy-done.13, bf16[8192,128]{1,0:T(8,128)(2,1)} %k_ref.9, bf16[8192,128]{1,0:T(8,128)(2,1)} %v_ref.9), custom_call_target="tpu_custom_call" | custom-call | flops 503316480 | bytes 2555904 | tf_op jit(solution)/shard_map/pallas_call | solution.py:187
  61.0 0.0 collective-permute-done.3.qa_ref
  61.0 0.0 collective-permute-done.4.qb_ref
  61.0 0.7 copy-done.10
  61.7 0.7 copy-done.11
  62.4 5.4 %shard_map.68 = (f32[3,136,512]{2,1,0:T(8,128)}, bf16[3,512,128]{2,1,0:T(8,128)(2,1)}) custom-call(s32[12,5]{1,0:T(8,128)} %bitcast.12, s32[1]{0:T(128)} %bitcast.4.core_ref, bf16[192,512]{1,0:T(8,128)(2,1)} %copy-done.10, bf16[192,512]{1,0:T(8,128)(2,1)} %copy-done.11, bf16[8192,128]{1,0:T(8,128)(2,1)} %k_ref.9, bf16[8192,128]{1,0:T(8,128)(2,1)} %v_ref.9), custom_call_target="tpu_custom_call" | custom-call | flops 503316480 | bytes 2555904 | tf_op jit(solution)/shard_map/pallas_call | solution.py:187
  67.8 0.7 copy-done.15
  68.5 0.7 copy-done.16
  69.2 5.4 %shard_map.69 = (f32[3,136,512]{2,1,0:T(8,128)}, bf16[3,512,128]{2,1,0:T(8,128)(2,1)}) custom-call(s32[12,5]{1,0:T(8,128)} %bitcast.13, s32[1]{0:T(128)} %bitcast.4.core_ref, bf16[192,512]{1,0:T(8,128)(2,1)} %copy-done.15, bf16[192,512]{1,0:T(8,128)(2,1)} %copy-done.16, bf16[8192,128]{1,0:T(8,128)(2,1)} %k_ref.9, bf16[8192,128]{1,0:T(8,128)(2,1)} %v_ref.9), custom_call_target="tpu_custom_call" | custom-call | flops 503316480 | bytes 2555904 | tf_op jit(solution)/shard_map/pallas_call | solution.py:187
  74.6 54.5 %all-to-all-done.1 = bf16[32,2,2,128,128]{4,3,2,1,0:T(8,128)(2,1)} async-done(((bf16[32,2,2,128,128]{4,3,2,1,0:T(8,128)(2,1)}), bf16[32,2,2,128,128]{4,3,2,1,0:T(8,128)(2,1)}, u32[]{:S(2)}, u32[]{:S(2)}) %all-to-all-start.1) | async-done | bytes 4194336 | tf_op jit(solution)/shard_map/all_to_all | solution.py:293
  129.1 3.7 %shard_map.70 = bf16[2,192,512]{2,1,0:T(8,128)(2,1)S(1)} custom-call(s32[12,3]{1,0:T(8,128)S(1)} %slice.19.slots_ref, s32[1]{0:T(128)} %bitcast.4.core_ref, bf16[64,2,128,128]{3,2,1,0:T(8,128)(2,1)} %bitcast.2.got_ref, f32[3,136,512]{2,1,0:T(8,128)S(1)} %copy-done.2, bf16[3,512,128]{2,1,0:T(8,128)(2,1)S(1)} %copy-done.5), custom_call_target="tpu_custom_call" | custom-call | flops 1 | bytes 1 | tf_op jit(solution)/shard_map/pallas_call | solution.py:248
  132.9 3.2 %collective-permute-start.11 = (bf16[2,192,512]{2,1,0:T(8,128)(2,1)S(1)}, bf16[2,192,512]{2,1,0:T(8,128)(2,1)S(1)}, u32[]{:S(2)}, u32[]{:S(2)}) collective-permute-start(bf16[2,192,512]{2,1,0:T(8,128)(2,1)S(1)} %shard_map.70), channel_id=1, source_target_pairs={{0,4},{1,5},{2,6},{3,7},{4,0},{5,1},{6,2},{7,3},{8,12},{9,13},{10,... | collective-permute-start | bytes 1179656 | tf_op jit(solution)/shard_map/ppermute | solution.py:327
  136.1 5.7 %shard_map.71 = (bf16[2,192,512]{2,1,0:T(8,128)(2,1)S(1)}, bf16[2,192,512]{2,1,0:T(8,128)(2,1)S(1)}) custom-call(s32[12,3]{1,0:T(8,128)S(1)} %slice.19.slots_ref, s32[1]{0:T(128)} %bitcast.4.core_ref, bf16[64,2,128,128]{3,2,1,0:T(8,128)(2,1)} %bitcast.2.got_ref, f32[3,136,512]{2,1,0:T(8,128)S(1)} %copy-done.1, bf16[3,512,128]{2,1,0:T(8,128)(2,1)S(1)} %copy-done.6, ...), custom_call_target="tpu_custom_call" | custom-call | flops 1 | bytes 1 | tf_op jit(solution)/shard_map/pallas_call | solution.py:248
  141.8 0.9 collective-permute-start.7
  142.7 0.7 collective-permute-start.9
  143.3 0.4 collective-permute-done.11.refs_2_
  143.7 3.7 %shard_map.72.refs_0_ = bf16[2,192,512]{2,1,0:T(8,128)(2,1)S(1)} custom-call(s32[12,3]{1,0:T(8,128)S(1)} %slice.19.slots_ref, s32[1]{0:T(128)} %bitcast.4.core_ref, bf16[64,2,128,128]{3,2,1,0:T(8,128)(2,1)} %bitcast.2.got_ref, f32[3,136,512]{2,1,0:T(8,128)S(1)} %copy-done, bf16[3,512,128]{2,1,0:T(8,128)(2,1)S(1)} %copy-done.4), custom_call_target="tpu_custom_call" | custom-call | flops 1 | bytes 1 | tf_op jit(solution)/shard_map/pallas_call | solution.py:248
  147.4 3.0 %collective-permute-start.12 = (bf16[2,192,512]{2,1,0:T(8,128)(2,1)S(1)}, bf16[2,192,512]{2,1,0:T(8,128)(2,1)S(1)}, u32[]{:S(2)}, u32[]{:S(2)}) collective-permute-start(bf16[2,192,512]{2,1,0:T(8,128)(2,1)S(1)} %shard_map.72.refs_0_), channel_id=1, source_target_pairs={{0,1},{1,0},{2,3},{3,2},{4,5},{5,4},{6,7},{7,6},{8,9},{9,8},{10,11... | collective-permute-start | bytes 1179656 | tf_op jit(solution)/shard_map/ppermute | solution.py:330
  150.3 0.1 collective-permute-start.13
  150.4 2.6 %collective-permute-done.7.refs_0_ = bf16[2,192,512]{2,1,0:T(8,128)(2,1)S(1)} collective-permute-done((bf16[2,192,512]{2,1,0:T(8,128)(2,1)S(1)}, bf16[2,192,512]{2,1,0:T(8,128)(2,1)S(1)}, u32[]{:S(2)}, u32[]{:S(2)}) %collective-permute-start.7) | collective-permute-done | bytes 393248 | tf_op jit(solution)/shard_map/ppermute | solution.py:327
  153.1 1.9 %collective-permute-start.8 = (bf16[2,192,512]{2,1,0:T(8,128)(2,1)S(1)}, bf16[2,192,512]{2,1,0:T(8,128)(2,1)S(1)}, u32[]{:S(2)}, u32[]{:S(2)}) collective-permute-start(bf16[2,192,512]{2,1,0:T(8,128)(2,1)S(1)} %collective-permute-done.7.refs_0_), channel_id=1, source_target_pairs={{0,1},{1,0},{2,3},{3,2},{4,5},{5,4},{6,7},{7,6},{8,9},{9,8},{10,11... | collective-permute-start | bytes 1179656 | tf_op jit(solution)/shard_map/ppermute | solution.py:330
  154.9 0.0 collective-permute-done.9.refs_2_
  154.9 0.4 collective-permute-start.10
  155.4 0.0 collective-permute-done.13.refs_3_
  155.4 1.5 shard_map.73.refs_4_
  156.9 0.0 collective-permute-done.8.refs_1_
  156.9 0.0 collective-permute-done.10.refs_3_
  156.9 1.5 shard_map.74
  (45 shorter events, 0.2 us)
Async XLA Ops:
  27.5 5.1 %copy-start.18 = (s32[8]{0:T(128)S(1)}, s32[8]{0:T(128)}, u32[]{:S(2)}) copy-start(s32[8]{0:T(128)} %constant.114.clone) | copy-start | bytes 100
  27.5 5.1 %copy-start.19 = (s32[8]{0:T(128)S(1)}, s32[8]{0:T(128)}, u32[]{:S(2)}) copy-start(s32[8]{0:T(128)} %constant.115.clone) | copy-start | bytes 100
  27.5 16.9 %copy-start.17 = (s32[12,8]{0,1:T(8,128)S(1)}, s32[12,8]{0,1:T(8,128)}, u32[]{:S(2)}) copy-start(s32[12,8]{0,1:T(8,128)} %param.9) | copy-start | bytes 1156
  27.5 101.6 %all-to-all-start.1 = ((bf16[32,2,2,128,128]{4,3,2,1,0:T(8,128)(2,1)}), bf16[32,2,2,128,128]{4,3,2,1,0:T(8,128)(2,1)}, u32[]{:S(2)}, u32[]{:S(2)}) async-start(bf16[32,2,2,128,128]{4,3,2,1,0:T(8,128)(2,1)} %bitcast.9), calls=%async_computation.1 | async-start | bytes 8388608 | tf_op jit(solution)/shard_map/all_to_all | solution.py:293
  36.1 9.4 %collective-permute-start = (bf16[192,512]{1,0:T(8,128)(2,1)}, bf16[192,512]{1,0:T(8,128)(2,1)S(1)}, u32[]{:S(2)}, u32[]{:S(2)}) collective-permute-start(bf16[192,512]{1,0:T(8,128)(2,1)} %get-tuple-element.41), channel_id=1, source_target_pairs={{0,1},{1,0},{2,3},{3,2},{4,5},{5,4},{6,7},{7,6},{8,9},{9,8},{10,11... | collective-permute-start | bytes 589832 | tf_op jit(solution)/shard_map/ppermute | solution.py:304
  38.1 8.8 %collective-permute-start.1 = (bf16[192,512]{1,0:T(8,128)(2,1)}, bf16[192,512]{1,0:T(8,128)(2,1)S(1)}, u32[]{:S(2)}, u32[]{:S(2)}) collective-permute-start(bf16[192,512]{1,0:T(8,128)(2,1)} %get-tuple-element.44), channel_id=1, source_target_pairs={{0,2},{1,3},{2,4},{3,5},{4,6},{5,7},{6,0},{7,1},{8,10},{9,11},{10,... | collective-permute-start | bytes 589832 | tf_op jit(solution)/shard_map/ppermute | solution.py:304
  39.4 15.5 %collective-permute-start.2 = (bf16[192,512]{1,0:T(8,128)(2,1)}, bf16[192,512]{1,0:T(8,128)(2,1)S(1)}, u32[]{:S(2)}, u32[]{:S(2)}) collective-permute-start(bf16[192,512]{1,0:T(8,128)(2,1)} %get-tuple-element.45), channel_id=1, source_target_pairs={{0,3},{1,2},{2,5},{3,4},{4,7},{5,6},{6,1},{7,0},{8,11},{9,10},{10,... | collective-permute-start | bytes 589832 | tf_op jit(solution)/shard_map/ppermute | solution.py:304
  40.9 20.1 %collective-permute-start.3 = (bf16[192,512]{1,0:T(8,128)(2,1)}, bf16[192,512]{1,0:T(8,128)(2,1)S(1)}, u32[]{:S(2)}, u32[]{:S(2)}) collective-permute-start(bf16[192,512]{1,0:T(8,128)(2,1)} %get-tuple-element.48), channel_id=1, source_target_pairs={{0,4},{1,5},{2,6},{3,7},{4,0},{5,1},{6,2},{7,3},{8,12},{9,13},{10,... | collective-permute-start | bytes 589832 | tf_op jit(solution)/shard_map/ppermute | solution.py:304
  42.2 18.8 %collective-permute-start.4 = (bf16[192,512]{1,0:T(8,128)(2,1)}, bf16[192,512]{1,0:T(8,128)(2,1)S(1)}, u32[]{:S(2)}, u32[]{:S(2)}) collective-permute-start(bf16[192,512]{1,0:T(8,128)(2,1)} %get-tuple-element.49), channel_id=1, source_target_pairs={{0,5},{1,4},{2,7},{3,6},{4,1},{5,0},{6,3},{7,2},{8,13},{9,12},{10,... | collective-permute-start | bytes 589832 | tf_op jit(solution)/shard_map/ppermute | solution.py:304
  45.4 3.4 %copy-start.14 = (bf16[192,512]{1,0:T(8,128)(2,1)}, bf16[192,512]{1,0:T(8,128)(2,1)S(1)}, u32[]{:S(2)}) copy-start(bf16[192,512]{1,0:T(8,128)(2,1)S(1)} %collective-permute-done.qb_ref) | copy-start | bytes 589828
  45.4 22.3 %collective-permute-start.5 = (bf16[192,512]{1,0:T(8,128)(2,1)}, bf16[192,512]{1,0:T(8,128)(2,1)S(1)}, u32[]{:S(2)}, u32[]{:S(2)}) collective-permute-start(bf16[192,512]{1,0:T(8,128)(2,1)} %get-tuple-element.52), channel_id=1, source_target_pairs={{0,6},{1,7},{2,0},{3,1},{4,2},{5,3},{6,4},{7,5},{8,14},{9,15},{10,... | collective-permute-start | bytes 589832 | tf_op jit(solution)/shard_map/ppermute | solution.py:304
  46.9 8.0 %copy-start.12 = (bf16[192,512]{1,0:T(8,128)(2,1)}, bf16[192,512]{1,0:T(8,128)(2,1)S(1)}, u32[]{:S(2)}) copy-start(bf16[192,512]{1,0:T(8,128)(2,1)S(1)} %collective-permute-done.1.qa_ref) | copy-start | bytes 589828
  46.9 20.9 %collective-permute-start.6 = (bf16[192,512]{1,0:T(8,128)(2,1)}, bf16[192,512]{1,0:T(8,128)(2,1)S(1)}, u32[]{:S(2)}, u32[]{:S(2)}) collective-permute-start(bf16[192,512]{1,0:T(8,128)(2,1)} %get-tuple-element.53), channel_id=1, source_target_pairs={{0,7},{1,6},{2,1},{3,0},{4,3},{5,2},{6,5},{7,4},{8,15},{9,14},{10,... | collective-permute-start | bytes 589832 | tf_op jit(solution)/shard_map/ppermute | solution.py:304
  48.8 0.6 copy-start.9
  55.0 0.7 copy-start.13
  61.0 0.7 copy-start.10
  61.7 0.7 copy-start.11
  67.8 61.4 %copy-start.2 = (f32[3,136,512]{2,1,0:T(8,128)S(1)}, f32[3,136,512]{2,1,0:T(8,128)}, u32[]{:S(2)}) copy-start(f32[3,136,512]{2,1,0:T(8,128)} %get-tuple-element.58.refs_0_) | copy-start | bytes 2506756
  67.8 61.3 %copy-start.5 = (bf16[3,512,128]{2,1,0:T(8,128)(2,1)S(1)}, bf16[3,512,128]{2,1,0:T(8,128)(2,1)}, u32[]{:S(2)}) copy-start(bf16[3,512,128]{2,1,0:T(8,128)(2,1)} %get-tuple-element.59.refs_1_) | copy-start | bytes 1179652
  67.8 0.7 copy-start.15
  68.5 0.7 copy-start.16
  129.1 6.9 %copy-start.1 = (f32[3,136,512]{2,1,0:T(8,128)S(1)}, f32[3,136,512]{2,1,0:T(8,128)}, u32[]{:S(2)}) copy-start(f32[3,136,512]{2,1,0:T(8,128)} %get-tuple-element.61.refs_0_) | copy-start | bytes 2506756
  129.1 6.9 %copy-start.3 = (f32[3,136,512]{2,1,0:T(8,128)S(1)}, f32[3,136,512]{2,1,0:T(8,128)}, u32[]{:S(2)}) copy-start(f32[3,136,512]{2,1,0:T(8,128)} %get-tuple-element.63.refs_2_) | copy-start | bytes 2506756
  129.1 6.9 %copy-start.6 = (bf16[3,512,128]{2,1,0:T(8,128)(2,1)S(1)}, bf16[3,512,128]{2,1,0:T(8,128)(2,1)}, u32[]{:S(2)}) copy-start(bf16[3,512,128]{2,1,0:T(8,128)(2,1)} %get-tuple-element.62.refs_1_) | copy-start | bytes 1179652
  129.1 6.9 %copy-start.7 = (bf16[3,512,128]{2,1,0:T(8,128)(2,1)S(1)}, bf16[3,512,128]{2,1,0:T(8,128)(2,1)}, u32[]{:S(2)}) copy-start(bf16[3,512,128]{2,1,0:T(8,128)(2,1)} %get-tuple-element.64.refs_3_) | copy-start | bytes 1179652
  132.9 10.9 %copy-start = (f32[3,136,512]{2,1,0:T(8,128)S(1)}, f32[3,136,512]{2,1,0:T(8,128)}, u32[]{:S(2)}) copy-start(f32[3,136,512]{2,1,0:T(8,128)} %get-tuple-element.72.refs_0_) | copy-start | bytes 2506756
  132.9 10.9 %copy-start.4 = (bf16[3,512,128]{2,1,0:T(8,128)(2,1)S(1)}, bf16[3,512,128]{2,1,0:T(8,128)(2,1)}, u32[]{:S(2)}) copy-start(bf16[3,512,128]{2,1,0:T(8,128)(2,1)} %get-tuple-element.73.refs_1_) | copy-start | bytes 1179652
  132.9 10.8 %collective-permute-start.11 = (bf16[2,192,512]{2,1,0:T(8,128)(2,1)S(1)}, bf16[2,192,512]{2,1,0:T(8,128)(2,1)S(1)}, u32[]{:S(2)}, u32[]{:S(2)}) collective-permute-start(bf16[2,192,512]{2,1,0:T(8,128)(2,1)S(1)} %shard_map.70), channel_id=1, source_target_pairs={{0,4},{1,5},{2,6},{3,7},{4,0},{5,1},{6,2},{7,3},{8,12},{9,13},{10,... | collective-permute-start | bytes 1179656 | tf_op jit(solution)/shard_map/ppermute | solution.py:327
  141.8 13.6 %copy-start.8 = (s32[8]{0:T(128)S(1)}, s32[8]{0:T(128)}, u32[]{:S(2)}) copy-start(s32[8]{0:T(128)} %fusion.7.places_ref) | copy-start | bytes 100
  141.8 11.3 %collective-permute-start.7 = (bf16[2,192,512]{2,1,0:T(8,128)(2,1)S(1)}, bf16[2,192,512]{2,1,0:T(8,128)(2,1)S(1)}, u32[]{:S(2)}, u32[]{:S(2)}) collective-permute-start(bf16[2,192,512]{2,1,0:T(8,128)(2,1)S(1)} %get-tuple-element.67), channel_id=1, source_target_pairs={{0,6},{1,7},{2,0},{3,1},{4,2},{5,3},{6,4},{7,5},{8,14},{9,15},{10,... | collective-permute-start | bytes 1179656 | tf_op jit(solution)/shard_map/ppermute | solution.py:327
  142.7 12.3 %collective-permute-start.9 = (bf16[2,192,512]{2,1,0:T(8,128)(2,1)S(1)}, bf16[2,192,512]{2,1,0:T(8,128)(2,1)S(1)}, u32[]{:S(2)}, u32[]{:S(2)}) collective-permute-start(bf16[2,192,512]{2,1,0:T(8,128)(2,1)S(1)} %get-tuple-element.68), channel_id=1, source_target_pairs={{0,2},{1,3},{2,4},{3,5},{4,6},{5,7},{6,0},{7,1},{8,10},{9,11},{10,... | collective-permute-start | bytes 1179656 | tf_op jit(solution)/shard_map/ppermute | solution.py:327
  147.4 8.0 %collective-permute-start.12 = (bf16[2,192,512]{2,1,0:T(8,128)(2,1)S(1)}, bf16[2,192,512]{2,1,0:T(8,128)(2,1)S(1)}, u32[]{:S(2)}, u32[]{:S(2)}) collective-permute-start(bf16[2,192,512]{2,1,0:T(8,128)(2,1)S(1)} %shard_map.72.refs_0_), channel_id=1, source_target_pairs={{0,1},{1,0},{2,3},{3,2},{4,5},{5,4},{6,7},{7,6},{8,9},{9,8},{10,11... | collective-permute-start | bytes 1179656 | tf_op jit(solution)/shard_map/ppermute | solution.py:330
  150.3 5.1 %collective-permute-start.13 = (bf16[2,192,512]{2,1,0:T(8,128)(2,1)S(1)}, bf16[2,192,512]{2,1,0:T(8,128)(2,1)S(1)}, u32[]{:S(2)}, u32[]{:S(2)}) collective-permute-start(bf16[2,192,512]{2,1,0:T(8,128)(2,1)S(1)} %collective-permute-done.11.refs_2_), channel_id=1, source_target_pairs={{0,1},{1,0},{2,3},{3,2},{4,5},{5,4},{6,7},{7,6},{8,9},{9,8},{10,11... | collective-permute-start | bytes 1179656 | tf_op jit(solution)/shard_map/ppermute | solution.py:330
  153.1 3.8 %collective-permute-start.8 = (bf16[2,192,512]{2,1,0:T(8,128)(2,1)S(1)}, bf16[2,192,512]{2,1,0:T(8,128)(2,1)S(1)}, u32[]{:S(2)}, u32[]{:S(2)}) collective-permute-start(bf16[2,192,512]{2,1,0:T(8,128)(2,1)S(1)} %collective-permute-done.7.refs_0_), channel_id=1, source_target_pairs={{0,1},{1,0},{2,3},{3,2},{4,5},{5,4},{6,7},{7,6},{8,9},{9,8},{10,11... | collective-permute-start | bytes 1179656 | tf_op jit(solution)/shard_map/ppermute | solution.py:330
  154.9 2.0 %collective-permute-start.10 = (bf16[2,192,512]{2,1,0:T(8,128)(2,1)S(1)}, bf16[2,192,512]{2,1,0:T(8,128)(2,1)S(1)}, u32[]{:S(2)}, u32[]{:S(2)}) collective-permute-start(bf16[2,192,512]{2,1,0:T(8,128)(2,1)S(1)} %collective-permute-done.9.refs_2_), channel_id=1, source_target_pairs={{0,1},{1,0},{2,3},{3,2},{4,5},{5,4},{6,7},{7,6},{8,9},{9,8},{10,11... | collective-permute-start | bytes 1179656 | tf_op jit(solution)/shard_map/ppermute | solution.py:330

commit v6 on v5

--- a/solution.py
+++ b/solution.py
@@ -70,8 +70,9 @@
     width = out_ref.shape[1] // count
     copies = []
     for piece, i in zip(pieces, chosen):
+        piece = piece.at[i % CORES] if len(piece.shape) == 3 else piece
         start = pl.multiple_of(places_ref[i] * width, width)
-        copies.append(pltpu.make_async_copy(piece.at[i % CORES], out_ref.at[:, pl.ds(start, width)], sem.at[i]))
+        copies.append(pltpu.make_async_copy(piece, out_ref.at[:, pl.ds(start, width)], sem.at[i]))
     for copy in copies:
         copy.start()
     for copy in copies:
@@ -80,7 +81,7 @@
 
 def join_outputs(pieces, chosen, places, out=None):
     count = len(pieces)
-    _, rows, width = pieces[0].shape
+    rows, width = pieces[0].shape[-2:]
     rest = [] if out is None else [out]
     return pl.pallas_call(
         functools.partial(join_outputs_kernel, count, chosen),
@@ -202,22 +203,21 @@
     )(ids, core, qa, qb, keys, values)
 
 
-def far_kernel(firsts, slots_ref, core_ref, got_ref, *refs):
+def far_kernel(firsts, split, slots_ref, core_ref, got_ref, *refs):
     groups = len(firsts)
-    near_refs, o_refs = refs[: 2 * groups], refs[2 * groups : 3 * groups]
-    far_buf, far_sem = refs[3 * groups :]
-    picks, half = far_buf.shape[1], o_refs[0].shape[1]
-    ratio, blocks = o_refs[0].shape[2] // HD, far_buf.shape[0] // groups
+    near_refs, o_refs, far_buf, o_buf, far_sem = refs[: 2 * groups], refs[2 * groups : -3], *refs[-3:]
+    picks, half = far_buf.shape[1], o_buf.shape[2]
+    ratio, blocks = o_buf.shape[3] // HD, far_buf.shape[0] // groups
     factor = HD ** (-0.5) * LOG2E
     core = core_ref[0]
     for n in range(groups * blocks):
         g, i = divmod(n, blocks)
         for j in range(picks):
-            pltpu.make_async_copy(got_ref.at[slots_ref[firsts[g] + i, j]], far_buf.at[n, j], far_sem.at[n]).start()
+            pltpu.make_async_copy(got_ref.at[slots_ref[firsts[g] + i, j]], far_buf.at[n, j], far_sem).start()
+    wait_for(far_buf, far_sem)
     for n in range(groups * blocks):
         g, i = divmod(n, blocks)
         kept_ref, q_ref = near_refs[2 * g : 2 * g + 2]
-        wait_for(far_buf.at[n], far_sem.at[n])
         keys = jnp.concatenate([far_buf[n, j, 0] for j in range(picks)], axis=0)
         values = jnp.concatenate([far_buf[n, j, 1] for j in range(picks)], axis=0)
         for r in range(ratio):
@@ -230,27 +230,39 @@
             total = jnp.sum(exponent, axis=0, keepdims=True) + kept * kept_ref[i, TOTAL : TOTAL + 1, queries]
             partial = weighted(values, exponent.astype(jnp.bfloat16))
             merged = (partial + kept * kept_ref[i, 0:HD, queries]) * (1.0 / total)
-            turned = merged.T.astype(o_refs[g].dtype)
+            turned = merged.T.astype(o_buf.dtype)
             for part in range(CORES):
                 low, high = max(i * BLK, part * half), min((i + 1) * BLK, (part + 1) * half)
                 if low < high:
-                    place = core if part == 0 else 1 - core
                     rows = slice(low - part * half, high - part * half)
-                    o_refs[g][place, rows, r * HD : (r + 1) * HD] = turned[low - i * BLK : high - i * BLK]
-
-
-def far_attention(slots, firsts, core, got, near):
+                    o_buf[g, part, rows, r * HD : (r + 1) * HD] = turned[low - i * BLK : high - i * BLK]
+    for g in range(groups):
+        for part in range(CORES):
+            if split:
+                o_refs[CORES * g + part][...] = o_buf[g, core if part == 0 else 1 - core]
+            else:
+                o_refs[g][core if part == 0 else 1 - core] = o_buf[g, part]
+
+
+def far_attention(slots, firsts, split, core, got, near):
     groups, picks = len(firsts), slots.shape[1]
     _, q = near[0]
     blocks, wide = q.shape[0], q.shape[1]
     count = groups * blocks
     half, width = blocks * BLK // CORES, wide // BLK * HD
-    return pl.pallas_call(
-        functools.partial(far_kernel, firsts),
-        out_shape=[jax.ShapeDtypeStruct((CORES, half, width), q.dtype)] * groups,
+    out_shape = [jax.ShapeDtypeStruct((CORES, half, width), q.dtype)] * groups
+    if split:
+        out_shape = [jax.ShapeDtypeStruct((half, width), q.dtype)] * (CORES * groups)
+    return pl.pallas_call(
+        functools.partial(far_kernel, firsts, split),
+        out_shape=out_shape,
         in_specs=[SMEM, SMEM, HBM] + [VMEM] * (2 * groups),
-        out_specs=[VMEM] * groups,
-        scratch_shapes=[pltpu.VMEM((count, picks) + got.shape[1:], got.dtype), pltpu.SemaphoreType.DMA((count,))],
+        out_specs=[VMEM] * len(out_shape),
+        scratch_shapes=[
+            pltpu.VMEM((count, picks) + got.shape[1:], got.dtype),
+            pltpu.VMEM((groups, CORES, half, width), q.dtype),
+            pltpu.SemaphoreType.DMA,
+        ],
         compiler_params=room(16),
         cost_estimate=cost(1, 1),
     )(slots, core, got, *[array for group in near for array in group])
@@ -314,23 +326,28 @@
     ]
     got, near, slots = lax.optimization_barrier((got, near, slots))
 
-    results = [None] * chips
-    distance = lambda d: min(d, chips - d)
-    for hops in range(chips // 2, -1, -1):
-        group = [d for d in range(chips) if distance(d) == hops]
-        if not hops:
-            got, results[chips // 2] = lax.optimization_barrier((got, results[chips // 2]))
-        made = far_attention(slots, tuple(d * per_chip for d in group), core_operand, got, [near[d] for d in group])
-        if hops:
-            made, got = lax.optimization_barrier((made, got))
-        for d, rows in zip(group, made):
-            results[d] = lax.ppermute(rows, "head", offset_pairs(chips, -d, 0)) if d else rows
-    joined = []
-    for d in range(chips):
-        joined += [results[d], lax.ppermute(results[d], "head", offset_pairs(chips, 0, 1))]
-    early = tuple(i for i in range(heads) if i // CORES in (0, chips // 2))
-    late = tuple(i for i in range(heads) if i not in early)
-    return join_outputs(joined, late, ahead, join_outputs(joined, early, ahead))
+    joined = [None] * heads
+
+    def attend(group, split, got):
+        return far_attention(slots, tuple(d * per_chip for d in group), split, core_operand, got, [near[d] for d in group])
+
+    def send(rows, d, e):
+        return lax.ppermute(rows, "head", offset_pairs(chips, -d, e))
+
+    far_chip = chips // 2
+    made, got = lax.optimization_barrier((attend([far_chip], False, got), got))
+    farthest = send(made[0], far_chip, 0)
+    between = [d for d in range(1, chips) if d != far_chip]
+    made = attend(between + [0], True, got)
+    late = []
+    for e in range(CORES):
+        for n, d in enumerate(between):
+            joined[CORES * d + e] = send(made[CORES * n + e], d, e)
+            late.append(CORES * d + e)
+    joined[CORES * far_chip : CORES * (far_chip + 1)] = [farthest, send(farthest, 0, 1)]
+    joined[:CORES] = [made[-CORES], send(made[-1], 0, 1)]
+    early = [i for i in range(heads) if i not in late]
+    return join_outputs(joined, tuple(late + early), ahead)
 
 
 def solution(mesh):

time: 160 us -> 163 us (1.019)
  waiting for transfers between devices: 57.6 us -> 64.7 us
  Pallas kernels: 46.4 us -> 41.1 us
  starting transfers between devices: 26.6 us -> 28.3 us
    ppermute x7, waiting for transfers between devices: 3.02 us -> 10.1 us  [send(): return lax.ppermute(rows, 'head', offset_pairs(chips, -d, e))]
    pallas_call x3 -> x2, Pallas kernels: 13.1 us -> 8.74 us  [far_attention(): pl.pallas_call(functools.partial(far_kernel, firsts, split), out_shape=ou...]
    ppermute x7, starting transfers between devices: 10.1 us -> 11.9 us  [send(): return lax.ppermute(rows, 'head', offset_pairs(chips, -d, e))]
  transfers between devices with their start and end apart: 15 -> 15, of which waited for: 3 -> 5; matrix products, arithmetic and copies ran while one was open for 1% -> 1% of each run, Pallas kernels for 22% -> 18%
where the time goes in v6:
time: 163 us; the launch traced here: 162 us
  waiting for transfers between devices  64.7 us (40%)
  Pallas kernels  41.1 us (25%)
  starting transfers between devices  28.3 us (17%)
  blocking collectives  20.4 us (13%)
  local copies, waits for them, and re-layouts  6.03 us (4%)
    all_to_all x1, waiting for transfers between devices, shards(): lax.all_to_all(sent.reshape(seq_count, capacity, 2, BLK, HD), 'seq', spli...  54.6 us
    pallas_call x4, Pallas kernels, near_attention(): pl.pallas_call(functools.partial(near_kernel, first), out_shape=[jax.Shap...  21.6 us
    all_to_all x1, blocking collectives, shards(): lax.all_to_all(asked.reshape(seq_count, 1, capacity), 'seq', split_axis=0...  20.4 us
    ppermute x7, starting transfers between devices, send(): return lax.ppermute(rows, 'head', offset_pairs(chips, -d, e))  11.9 us
    ppermute x7, starting transfers between devices, shards(): lax.ppermute(piece, 'head', offset_pairs(chips, d, e))  11.5 us
    ppermute x7, waiting for transfers between devices, send(): return lax.ppermute(rows, 'head', offset_pairs(chips, -d, e))  10.1 us
    pallas_call x2, Pallas kernels, far_attention(): pl.pallas_call(functools.partial(far_kernel, firsts, split), out_shape=ou...  8.74 us
    pallas_call x1, Pallas kernels, pack(): pl.pallas_call(functools.partial(pack_kernel, chunks, ahead), out_shape=j...  6 us
  transfers between devices with their start and end apart: 15, of which 5 were waited for; matrix products, arithmetic and copies ran while one was open for 1% of the time, Pallas kernels for 18%

profile of v6, /device:TPU:1, one launch (start us, length us, event | category | flops | bytes accessed | tf_op | source)
XLA Modules:
  0.0 162.2 jit_solution(11876283567449275849)
XLA Ops:
  0.0 0.7 slice.12
  0.7 0.1 copy.22
  0.8 0.1 reshape.223
  0.9 0.2 convert_reduce_fusion
  1.1 0.1 select_reduce_fusion
  1.2 0.1 reduce_sum.24
  1.3 20.4 %all_to_all.10.wanted_ref = s32[32,1,2]{2,1,0:T(1,128)} all-to-all(s32[32,1,2]{2,1,0:T(1,128)S(1)} %fusion.1), channel_id=1, replica_groups=mesh['seq'=32,'head'=8] {'seq'}, dimensions={0} | all-to-all | bytes 512 | tf_op jit(solution)/shard_map/all_to_all | solution.py:302
  21.7 6.0 %shard_map.64 = bf16[64,2,128,128]{3,2,1,0:T(8,128)(2,1)} custom-call(s32[32,1,2]{2,1,0:T(1,128)} %all_to_all.10.wanted_ref, bf16[8192,128]{1,0:T(8,128)(2,1)} %k_ref.9, bf16[8192,128]{1,0:T(8,128)(2,1)} %v_ref.9), custom_call_target="tpu_custom_call" | custom-call | bytes 8388608 | tf_op jit(solution)/shard_map/pallas_call | solution.py:123
  27.7 0.0 copy-start.18
  27.8 0.0 copy-start.19
  27.8 0.0 copy-start.17
  27.8 5.0 %all-to-all-start.1 = ((bf16[32,2,2,128,128]{4,3,2,1,0:T(8,128)(2,1)}), bf16[32,2,2,128,128]{4,3,2,1,0:T(8,128)(2,1)}, u32[]{:S(2)}, u32[]{:S(2)}) async-start(bf16[32,2,2,128,128]{4,3,2,1,0:T(8,128)(2,1)} %bitcast.9), calls=%async_computation.1 | async-start | bytes 8388608 | tf_op jit(solution)/shard_map/all_to_all | solution.py:305
  32.8 0.5 fusion.7.places_ref
  33.4 3.0 %shard_map.65 = (bf16[192,512]{1,0:T(8,128)(2,1)}, bf16[192,512]{1,0:T(8,128)(2,1)}, bf16[192,512]{1,0:T(8,128)(2,1)}, bf16[192,512]{1,0:T(8,128)(2,1)}, bf16[19...) custom-call(s32[8]{0:T(128)} %fusion.7.places_ref, ...), custom_call_target="tpu_custom_call" | custom-call | bytes 3145728 | tf_op jit(solution)/shard_map/pallas_call | solution.py:54
  36.3 2.0 %collective-permute-start = (bf16[192,512]{1,0:T(8,128)(2,1)}, bf16[192,512]{1,0:T(8,128)(2,1)S(1)}, u32[]{:S(2)}, u32[]{:S(2)}) collective-permute-start(bf16[192,512]{1,0:T(8,128)(2,1)} %get-tuple-element.40), channel_id=1, source_target_pairs={{0,1},{1,0},{2,3},{3,2},{4,5},{5,4},{6,7},{7,6},{8,9},{9,8},{10,11... | collective-permute-start | bytes 589832 | tf_op jit(solution)/shard_map/ppermute | solution.py:316
  38.4 1.3 collective-permute-start.1
  39.7 1.5 collective-permute-start.2
  41.2 1.3 collective-permute-start.3
  42.5 2.0 %collective-permute-start.4 = (bf16[192,512]{1,0:T(8,128)(2,1)}, bf16[192,512]{1,0:T(8,128)(2,1)S(1)}, u32[]{:S(2)}, u32[]{:S(2)}) collective-permute-start(bf16[192,512]{1,0:T(8,128)(2,1)} %get-tuple-element.48), channel_id=1, source_target_pairs={{0,5},{1,4},{2,7},{3,6},{4,1},{5,0},{6,3},{7,2},{8,13},{9,12},{10,... | collective-permute-start | bytes 589832 | tf_op jit(solution)/shard_map/ppermute | solution.py:316
  44.5 0.1 reduce_sum.25
  44.7 0.1 concatenate.8
  44.7 0.1 copy.19
  44.9 0.1 pad_add_fusion
  44.9 0.6 gather_fusion
  45.5 0.1 broadcast_in_dim.27
  45.6 0.1 broadcast_in_dim.28
  45.7 0.0 collective-permute-done.qb_ref
  45.7 1.5 collective-permute-start.5
  47.2 0.0 collective-permute-done.1.qa_ref
  47.2 1.8 %collective-permute-start.6 = (bf16[192,512]{1,0:T(8,128)(2,1)}, bf16[192,512]{1,0:T(8,128)(2,1)S(1)}, u32[]{:S(2)}, u32[]{:S(2)}) collective-permute-start(bf16[192,512]{1,0:T(8,128)(2,1)} %get-tuple-element.52), channel_id=1, source_target_pairs={{0,7},{1,6},{2,1},{3,0},{4,3},{5,2},{6,5},{7,4},{8,15},{9,14},{10,... | collective-permute-start | bytes 589832 | tf_op jit(solution)/shard_map/ppermute | solution.py:316
  49.0 0.1 broadcast_select_fusion
  49.1 0.1 slice.19.slots_ref
  49.1 0.5 copy-done.9
  49.7 5.4 %shard_map.66 = (f32[3,136,512]{2,1,0:T(8,128)}, bf16[3,512,128]{2,1,0:T(8,128)(2,1)}) custom-call(s32[12,5]{1,0:T(8,128)} %bitcast.10, s32[1]{0:T(128)} %bitcast.4.core_ref, bf16[192,512]{1,0:T(8,128)(2,1)} %get-tuple-element.39.qa_ref, bf16[192,512]{1,0:T(8,128)(2,1)} %copy-done.14, bf16[8192,128]{1,0:T(8,128)(2,1)} %k_ref.9, bf16[8192,128]{1,0:T(8,128)(2,1)} %v_ref.9), custom_call_target="tpu_custom_call" | custom-call | flops 503316480 | bytes 2555904 | tf_op jit(solution)/shard_map/pallas_call | solution.py:188
  55.1 0.0 collective-permute-done.2.qb_ref
  55.1 0.7 copy-done.13
  55.8 5.4 %shard_map.67 = (f32[3,136,512]{2,1,0:T(8,128)}, bf16[3,512,128]{2,1,0:T(8,128)(2,1)}) custom-call(s32[12,5]{1,0:T(8,128)} %bitcast.11, s32[1]{0:T(128)} %bitcast.4.core_ref, bf16[192,512]{1,0:T(8,128)(2,1)} %copy-done.12, bf16[192,512]{1,0:T(8,128)(2,1)} %copy-done.13, bf16[8192,128]{1,0:T(8,128)(2,1)} %k_ref.9, bf16[8192,128]{1,0:T(8,128)(2,1)} %v_ref.9), custom_call_target="tpu_custom_call" | custom-call | flops 503316480 | bytes 2555904 | tf_op jit(solution)/shard_map/pallas_call | solution.py:188
  61.2 0.0 collective-permute-done.3.qa_ref
  61.2 0.0 collective-permute-done.4.qb_ref
  61.2 0.7 copy-done.10
  61.9 0.7 copy-done.11
  62.5 5.4 %shard_map.68 = (f32[3,136,512]{2,1,0:T(8,128)}, bf16[3,512,128]{2,1,0:T(8,128)(2,1)}) custom-call(s32[12,5]{1,0:T(8,128)} %bitcast.12, s32[1]{0:T(128)} %bitcast.4.core_ref, bf16[192,512]{1,0:T(8,128)(2,1)} %copy-done.10, bf16[192,512]{1,0:T(8,128)(2,1)} %copy-done.11, bf16[8192,128]{1,0:T(8,128)(2,1)} %k_ref.9, bf16[8192,128]{1,0:T(8,128)(2,1)} %v_ref.9), custom_call_target="tpu_custom_call" | custom-call | flops 503316480 | bytes 2555904 | tf_op jit(solution)/shard_map/pallas_call | solution.py:188
  68.0 0.0 collective-permute-done.6.qb_ref
  68.0 0.7 copy-done.15
  68.6 0.7 copy-done.16
  69.3 5.5 %shard_map.69 = (f32[3,136,512]{2,1,0:T(8,128)}, bf16[3,512,128]{2,1,0:T(8,128)(2,1)}) custom-call(s32[12,5]{1,0:T(8,128)} %bitcast.13, s32[1]{0:T(128)} %bitcast.4.core_ref, bf16[192,512]{1,0:T(8,128)(2,1)} %copy-done.15, bf16[192,512]{1,0:T(8,128)(2,1)} %copy-done.16, bf16[8192,128]{1,0:T(8,128)(2,1)} %k_ref.9, bf16[8192,128]{1,0:T(8,128)(2,1)} %v_ref.9), custom_call_target="tpu_custom_call" | custom-call | flops 503316480 | bytes 2555904 | tf_op jit(solution)/shard_map/pallas_call | solution.py:188
  74.8 54.6 %all-to-all-done.1 = bf16[32,2,2,128,128]{4,3,2,1,0:T(8,128)(2,1)} async-done(((bf16[32,2,2,128,128]{4,3,2,1,0:T(8,128)(2,1)}), bf16[32,2,2,128,128]{4,3,2,1,0:T(8,128)(2,1)}, u32[]{:S(2)}, u32[]{:S(2)}) %all-to-all-start.1) | async-done | bytes 4194336 | tf_op jit(solution)/shard_map/all_to_all | solution.py:305
  129.4 3.4 %shard_map.70 = bf16[2,192,512]{2,1,0:T(8,128)(2,1)S(1)} custom-call(s32[12,3]{1,0:T(8,128)S(1)} %slice.19.slots_ref, s32[1]{0:T(128)} %bitcast.4.core_ref, bf16[64,2,128,128]{3,2,1,0:T(8,128)(2,1)} %bitcast.2.got_ref, f32[3,136,512]{2,1,0:T(8,128)S(1)} %copy-done.3, bf16[3,512,128]{2,1,0:T(8,128)(2,1)S(1)} %copy-done.7), custom_call_target="tpu_custom_call" | custom-call | flops 1 | bytes 1 | tf_op jit(solution)/shard_map/pallas_call | solution.py:256
  132.9 3.2 %collective-permute-start.12 = (bf16[2,192,512]{2,1,0:T(8,128)(2,1)S(1)}, bf16[2,192,512]{2,1,0:T(8,128)(2,1)S(1)}, u32[]{:S(2)}, u32[]{:S(2)}) collective-permute-start(bf16[2,192,512]{2,1,0:T(8,128)(2,1)S(1)} %shard_map.70), channel_id=1, source_target_pairs={{0,4},{1,5},{2,6},{3,7},{4,0},{5,1},{6,2},{7,3},{8,12},{9,13},{10,... | collective-permute-start | bytes 1179656 | tf_op jit(solution)/shard_map/ppermute | solution.py:335
  136.1 5.3 %shard_map.71 = (bf16[192,512]{1,0:T(8,128)(2,1)S(1)}, bf16[192,512]{1,0:T(8,128)(2,1)S(1)}, bf16[192,512]{1,0:T(8,128)(2,1)S(1)}, bf16[192,512]{1,0:T(8,128)(2,...) custom-call(s32[12,3]{1,0:T(8,128)S(1)} %slice.19.slots_ref, s32[1]{0:T(128)} %bitcast.4.core_ref, ...), custom_call_target="tpu_custom_call" | custom-call | flops 1 | bytes 1 | tf_op jit(solution)/shard_map/pallas_call | solution.py:256
  141.4 0.8 collective-permute-start.7
  142.3 1.5 collective-permute-done.12.refs_6_
  143.7 2.5 %collective-permute-start.13 = (bf16[2,192,512]{2,1,0:T(8,128)(2,1)S(1)}, bf16[2,192,512]{2,1,0:T(8,128)(2,1)S(1)}, u32[]{:S(2)}, u32[]{:S(2)}) collective-permute-start(bf16[2,192,512]{2,1,0:T(8,128)(2,1)S(1)} %collective-permute-done.12.refs_6_), channel_id=1, source_target_pairs={{0,1},{1,0},{2,3},{3,2},{4,5},{5,4},{6,7},{7,6},{8,9},{9,8},{10,11... | collective-permute-start | bytes 1179656 | tf_op jit(solution)/shard_map/ppermute | solution.py:335
  146.2 3.4 %collective-permute-start.8 = (bf16[192,512]{1,0:T(8,128)(2,1)S(1)}, bf16[192,512]{1,0:T(8,128)(2,1)S(1)}, u32[]{:S(2)}, u32[]{:S(2)}) collective-permute-start(bf16[192,512]{1,0:T(8,128)(2,1)S(1)} %get-tuple-element.67), channel_id=1, source_target_pairs={{0,2},{1,3},{2,4},{3,5},{4,6},{5,7},{6,0},{7,1},{8,10},{9,11},{10,... | collective-permute-start | bytes 589832 | tf_op jit(solution)/shard_map/ppermute | solution.py:335
  149.5 1.1 collective-permute-start.9
  150.7 0.6 collective-permute-start.10
  151.3 0.0 collective-permute-done.7.refs_0_
  151.3 0.3 collective-permute-start.11
  151.6 4.5 %collective-permute-done.8.refs_1_ = bf16[192,512]{1,0:T(8,128)(2,1)S(1)} collective-permute-done((bf16[192,512]{1,0:T(8,128)(2,1)S(1)}, bf16[192,512]{1,0:T(8,128)(2,1)S(1)}, u32[]{:S(2)}, u32[]{:S(2)}) %collective-permute-start.8) | collective-permute-done | bytes 196640 | tf_op jit(solution)/shard_map/ppermute | solution.py:335
  156.0 0.6 collective-permute-done.9.refs_2_
  156.6 3.6 %collective-permute-done.10.refs_3_ = bf16[192,512]{1,0:T(8,128)(2,1)S(1)} collective-permute-done((bf16[192,512]{1,0:T(8,128)(2,1)S(1)}, bf16[192,512]{1,0:T(8,128)(2,1)S(1)}, u32[]{:S(2)}, u32[]{:S(2)}) %collective-permute-start.10) | collective-permute-done | bytes 196640 | tf_op jit(solution)/shard_map/ppermute | solution.py:335
  160.2 0.0 collective-permute-done.11.refs_5_
  160.2 0.0 collective-permute-done.13.refs_7_
  160.3 1.7 %shard_map.72 = bf16[192,4096]{1,0:T(8,128)(2,1)} custom-call(s32[8]{0:T(128)S(1)} %copy-done.8, bf16[192,512]{1,0:T(8,128)(2,1)S(1)} %collective-permute-done.7.refs_0_, bf16[192,512]{1,0:T(8,128)(2,1)S(1)} %collective-permute-done.8.refs_1_, bf16[192,512]{1,0:T(8,128)(2,1)S(1)} %collective-permute-done.9.refs_2_, ...), custom_call_target="tpu_custom_call" | custom-call | bytes 3145728 | tf_op jit(solution)/shard_map/pallas_call | solution.py:86
  (43 shorter events, 0.2 us)
Async XLA Ops:
  27.7 5.1 %copy-start.18 = (s32[8]{0:T(128)S(1)}, s32[8]{0:T(128)}, u32[]{:S(2)}) copy-start(s32[8]{0:T(128)} %constant.114.clone) | copy-start | bytes 100
  27.8 5.1 %copy-start.19 = (s32[8]{0:T(128)S(1)}, s32[8]{0:T(128)}, u32[]{:S(2)}) copy-start(s32[8]{0:T(128)} %constant.115.clone) | copy-start | bytes 100
  27.8 16.9 %copy-start.17 = (s32[12,8]{0,1:T(8,128)S(1)}, s32[12,8]{0,1:T(8,128)}, u32[]{:S(2)}) copy-start(s32[12,8]{0,1:T(8,128)} %param.9) | copy-start | bytes 1156
  27.8 101.6 %all-to-all-start.1 = ((bf16[32,2,2,128,128]{4,3,2,1,0:T(8,128)(2,1)}), bf16[32,2,2,128,128]{4,3,2,1,0:T(8,128)(2,1)}, u32[]{:S(2)}, u32[]{:S(2)}) async-start(bf16[32,2,2,128,128]{4,3,2,1,0:T(8,128)(2,1)} %bitcast.9), calls=%async_computation.1 | async-start | bytes 8388608 | tf_op jit(solution)/shard_map/all_to_all | solution.py:305
  36.3 9.4 %collective-permute-start = (bf16[192,512]{1,0:T(8,128)(2,1)}, bf16[192,512]{1,0:T(8,128)(2,1)S(1)}, u32[]{:S(2)}, u32[]{:S(2)}) collective-permute-start(bf16[192,512]{1,0:T(8,128)(2,1)} %get-tuple-element.40), channel_id=1, source_target_pairs={{0,1},{1,0},{2,3},{3,2},{4,5},{5,4},{6,7},{7,6},{8,9},{9,8},{10,11... | collective-permute-start | bytes 589832 | tf_op jit(solution)/shard_map/ppermute | solution.py:316
  38.4 8.8 %collective-permute-start.1 = (bf16[192,512]{1,0:T(8,128)(2,1)}, bf16[192,512]{1,0:T(8,128)(2,1)S(1)}, u32[]{:S(2)}, u32[]{:S(2)}) collective-permute-start(bf16[192,512]{1,0:T(8,128)(2,1)} %get-tuple-element.43), channel_id=1, source_target_pairs={{0,2},{1,3},{2,4},{3,5},{4,6},{5,7},{6,0},{7,1},{8,10},{9,11},{10,... | collective-permute-start | bytes 589832 | tf_op jit(solution)/shard_map/ppermute | solution.py:316
  39.7 15.4 %collective-permute-start.2 = (bf16[192,512]{1,0:T(8,128)(2,1)}, bf16[192,512]{1,0:T(8,128)(2,1)S(1)}, u32[]{:S(2)}, u32[]{:S(2)}) collective-permute-start(bf16[192,512]{1,0:T(8,128)(2,1)} %get-tuple-element.44), channel_id=1, source_target_pairs={{0,3},{1,2},{2,5},{3,4},{4,7},{5,6},{6,1},{7,0},{8,11},{9,10},{10,... | collective-permute-start | bytes 589832 | tf_op jit(solution)/shard_map/ppermute | solution.py:316
  41.2 20.0 %collective-permute-start.3 = (bf16[192,512]{1,0:T(8,128)(2,1)}, bf16[192,512]{1,0:T(8,128)(2,1)S(1)}, u32[]{:S(2)}, u32[]{:S(2)}) collective-permute-start(bf16[192,512]{1,0:T(8,128)(2,1)} %get-tuple-element.47), channel_id=1, source_target_pairs={{0,4},{1,5},{2,6},{3,7},{4,0},{5,1},{6,2},{7,3},{8,12},{9,13},{10,... | collective-permute-start | bytes 589832 | tf_op jit(solution)/shard_map/ppermute | solution.py:316
  42.5 18.7 %collective-permute-start.4 = (bf16[192,512]{1,0:T(8,128)(2,1)}, bf16[192,512]{1,0:T(8,128)(2,1)S(1)}, u32[]{:S(2)}, u32[]{:S(2)}) collective-permute-start(bf16[192,512]{1,0:T(8,128)(2,1)} %get-tuple-element.48), channel_id=1, source_target_pairs={{0,5},{1,4},{2,7},{3,6},{4,1},{5,0},{6,3},{7,2},{8,13},{9,12},{10,... | collective-permute-start | bytes 589832 | tf_op jit(solution)/shard_map/ppermute | solution.py:316
  45.7 3.4 %copy-start.14 = (bf16[192,512]{1,0:T(8,128)(2,1)}, bf16[192,512]{1,0:T(8,128)(2,1)S(1)}, u32[]{:S(2)}) copy-start(bf16[192,512]{1,0:T(8,128)(2,1)S(1)} %collective-permute-done.qb_ref) | copy-start | bytes 589828
  45.7 22.2 %collective-permute-start.5 = (bf16[192,512]{1,0:T(8,128)(2,1)}, bf16[192,512]{1,0:T(8,128)(2,1)S(1)}, u32[]{:S(2)}, u32[]{:S(2)}) collective-permute-start(bf16[192,512]{1,0:T(8,128)(2,1)} %get-tuple-element.51), channel_id=1, source_target_pairs={{0,6},{1,7},{2,0},{3,1},{4,2},{5,3},{6,4},{7,5},{8,14},{9,15},{10,... | collective-permute-start | bytes 589832 | tf_op jit(solution)/shard_map/ppermute | solution.py:316
  47.2 7.9 %copy-start.12 = (bf16[192,512]{1,0:T(8,128)(2,1)}, bf16[192,512]{1,0:T(8,128)(2,1)S(1)}, u32[]{:S(2)}) copy-start(bf16[192,512]{1,0:T(8,128)(2,1)S(1)} %collective-permute-done.1.qa_ref) | copy-start | bytes 589828
  47.2 20.8 %collective-permute-start.6 = (bf16[192,512]{1,0:T(8,128)(2,1)}, bf16[192,512]{1,0:T(8,128)(2,1)S(1)}, u32[]{:S(2)}, u32[]{:S(2)}) collective-permute-start(bf16[192,512]{1,0:T(8,128)(2,1)} %get-tuple-element.52), channel_id=1, source_target_pairs={{0,7},{1,6},{2,1},{3,0},{4,3},{5,2},{6,5},{7,4},{8,15},{9,14},{10,... | collective-permute-start | bytes 589832 | tf_op jit(solution)/shard_map/ppermute | solution.py:316
  49.1 0.6 copy-start.9
  55.1 0.7 copy-start.13
  61.2 0.7 copy-start.10
  61.9 0.7 copy-start.11
  67.9 61.5 %copy-start.3 = (f32[3,136,512]{2,1,0:T(8,128)S(1)}, f32[3,136,512]{2,1,0:T(8,128)}, u32[]{:S(2)}) copy-start(f32[3,136,512]{2,1,0:T(8,128)} %get-tuple-element.57.refs_0_) | copy-start | bytes 2506756
  67.9 61.5 %copy-start.7 = (bf16[3,512,128]{2,1,0:T(8,128)(2,1)S(1)}, bf16[3,512,128]{2,1,0:T(8,128)(2,1)}, u32[]{:S(2)}) copy-start(bf16[3,512,128]{2,1,0:T(8,128)(2,1)} %get-tuple-element.58.refs_1_) | copy-start | bytes 1179652
  68.0 0.7 copy-start.15
  68.6 0.7 copy-start.16
  129.4 6.7 %copy-start = (f32[3,136,512]{2,1,0:T(8,128)S(1)}, f32[3,136,512]{2,1,0:T(8,128)}, u32[]{:S(2)}) copy-start(f32[3,136,512]{2,1,0:T(8,128)} %get-tuple-element.64.refs_4_) | copy-start | bytes 2506756
  129.4 6.7 %copy-start.1 = (f32[3,136,512]{2,1,0:T(8,128)S(1)}, f32[3,136,512]{2,1,0:T(8,128)}, u32[]{:S(2)}) copy-start(f32[3,136,512]{2,1,0:T(8,128)} %get-tuple-element.60.refs_0_) | copy-start | bytes 2506756
  129.4 6.7 %copy-start.2 = (f32[3,136,512]{2,1,0:T(8,128)S(1)}, f32[3,136,512]{2,1,0:T(8,128)}, u32[]{:S(2)}) copy-start(f32[3,136,512]{2,1,0:T(8,128)} %get-tuple-element.62.refs_2_) | copy-start | bytes 2506756
  129.4 6.7 %copy-start.4 = (bf16[3,512,128]{2,1,0:T(8,128)(2,1)S(1)}, bf16[3,512,128]{2,1,0:T(8,128)(2,1)}, u32[]{:S(2)}) copy-start(bf16[3,512,128]{2,1,0:T(8,128)(2,1)} %get-tuple-element.65.refs_5_) | copy-start | bytes 1179652
  129.4 6.6 %copy-start.5 = (bf16[3,512,128]{2,1,0:T(8,128)(2,1)S(1)}, bf16[3,512,128]{2,1,0:T(8,128)(2,1)}, u32[]{:S(2)}) copy-start(bf16[3,512,128]{2,1,0:T(8,128)(2,1)} %get-tuple-element.61.refs_1_) | copy-start | bytes 1179652
  129.4 6.6 %copy-start.6 = (bf16[3,512,128]{2,1,0:T(8,128)(2,1)S(1)}, bf16[3,512,128]{2,1,0:T(8,128)(2,1)}, u32[]{:S(2)}) copy-start(bf16[3,512,128]{2,1,0:T(8,128)(2,1)} %get-tuple-element.63.refs_3_) | copy-start | bytes 1179652
  132.9 27.4 %copy-start.8 = (s32[8]{0:T(128)S(1)}, s32[8]{0:T(128)}, u32[]{:S(2)}) copy-start(s32[8]{0:T(128)} %fusion.7.places_ref) | copy-start | bytes 100
  132.9 10.8 %collective-permute-start.12 = (bf16[2,192,512]{2,1,0:T(8,128)(2,1)S(1)}, bf16[2,192,512]{2,1,0:T(8,128)(2,1)S(1)}, u32[]{:S(2)}, u32[]{:S(2)}) collective-permute-start(bf16[2,192,512]{2,1,0:T(8,128)(2,1)S(1)} %shard_map.70), channel_id=1, source_target_pairs={{0,4},{1,5},{2,6},{3,7},{4,0},{5,1},{6,2},{7,3},{8,12},{9,13},{10,... | collective-permute-start | bytes 1179656 | tf_op jit(solution)/shard_map/ppermute | solution.py:335
  141.4 9.9 %collective-permute-start.7 = (bf16[192,512]{1,0:T(8,128)(2,1)S(1)}, bf16[192,512]{1,0:T(8,128)(2,1)S(1)}, u32[]{:S(2)}, u32[]{:S(2)}) collective-permute-start(bf16[192,512]{1,0:T(8,128)(2,1)S(1)} %get-tuple-element.66), channel_id=1, source_target_pairs={{0,6},{1,7},{2,0},{3,1},{4,2},{5,3},{6,4},{7,5},{8,14},{9,15},{10,... | collective-permute-start | bytes 589832 | tf_op jit(solution)/shard_map/ppermute | solution.py:335
  143.7 16.5 %collective-permute-start.13 = (bf16[2,192,512]{2,1,0:T(8,128)(2,1)S(1)}, bf16[2,192,512]{2,1,0:T(8,128)(2,1)S(1)}, u32[]{:S(2)}, u32[]{:S(2)}) collective-permute-start(bf16[2,192,512]{2,1,0:T(8,128)(2,1)S(1)} %collective-permute-done.12.refs_6_), channel_id=1, source_target_pairs={{0,1},{1,0},{2,3},{3,2},{4,5},{5,4},{6,7},{7,6},{8,9},{9,8},{10,11... | collective-permute-start | bytes 1179656 | tf_op jit(solution)/shard_map/ppermute | solution.py:335
  146.2 9.9 %collective-permute-start.8 = (bf16[192,512]{1,0:T(8,128)(2,1)S(1)}, bf16[192,512]{1,0:T(8,128)(2,1)S(1)}, u32[]{:S(2)}, u32[]{:S(2)}) collective-permute-start(bf16[192,512]{1,0:T(8,128)(2,1)S(1)} %get-tuple-element.67), channel_id=1, source_target_pairs={{0,2},{1,3},{2,4},{3,5},{4,6},{5,7},{6,0},{7,1},{8,10},{9,11},{10,... | collective-permute-start | bytes 589832 | tf_op jit(solution)/shard_map/ppermute | solution.py:335
  149.5 7.1 %collective-permute-start.9 = (bf16[192,512]{1,0:T(8,128)(2,1)S(1)}, bf16[192,512]{1,0:T(8,128)(2,1)S(1)}, u32[]{:S(2)}, u32[]{:S(2)}) collective-permute-start(bf16[192,512]{1,0:T(8,128)(2,1)S(1)} %get-tuple-element.68), channel_id=1, source_target_pairs={{0,7},{1,6},{2,1},{3,0},{4,3},{5,2},{6,5},{7,4},{8,15},{9,14},{10,... | collective-permute-start | bytes 589832 | tf_op jit(solution)/shard_map/ppermute | solution.py:335
  150.7 9.6 %collective-permute-start.10 = (bf16[192,512]{1,0:T(8,128)(2,1)S(1)}, bf16[192,512]{1,0:T(8,128)(2,1)S(1)}, u32[]{:S(2)}, u32[]{:S(2)}) collective-permute-start(bf16[192,512]{1,0:T(8,128)(2,1)S(1)} %get-tuple-element.69), channel_id=1, source_target_pairs={{0,3},{1,2},{2,5},{3,4},{4,7},{5,6},{6,1},{7,0},{8,11},{9,10},{10,... | collective-permute-start | bytes 589832 | tf_op jit(solution)/shard_map/ppermute | solution.py:335
  151.3 9.0 %collective-permute-start.11 = (bf16[192,512]{1,0:T(8,128)(2,1)S(1)}, bf16[192,512]{1,0:T(8,128)(2,1)S(1)}, u32[]{:S(2)}, u32[]{:S(2)}) collective-permute-start(bf16[192,512]{1,0:T(8,128)(2,1)S(1)} %get-tuple-element.71), channel_id=1, source_target_pairs={{0,1},{1,0},{2,3},{3,2},{4,5},{5,4},{6,7},{7,6},{8,9},{9,8},{10,11... | collective-permute-start | bytes 589832 | tf_op jit(solution)/shard_map/ppermute | solution.py:335

commit v7 on v5

--- a/solution.py
+++ b/solution.py
@@ -94,33 +94,34 @@
     )(places, *[pieces[i] for i in chosen], *rest)
 
 
-def pack_kernel(chunks, ahead, wanted_ref, k_ref, v_ref, out_ref, buf, in_sem, out_sem):
+def pack_kernel(chunks, unroll, wanted_ref, k_ref, v_ref, out_ref, buf, in_sem, out_sem):
     span, capacity = out_ref.shape[0] // chunks, wanted_ref.shape[2]
-
-    def fetch(chunk):
-        for i in range(chunk * span, (chunk + 1) * span):
-            rows = pl.ds(pl.multiple_of(wanted_ref[i // capacity, 0, i % capacity] * BLK, BLK), BLK)
-            pltpu.make_async_copy(k_ref.at[rows], buf.at[i, 0], in_sem.at[chunk]).start()
-            pltpu.make_async_copy(v_ref.at[rows], buf.at[i, 1], in_sem.at[chunk]).start()
-
+    owners = span // capacity
     copies = []
-    for chunk in range(min(ahead, chunks)):
-        fetch(chunk)
+    for chunk in range(chunks):
+
+        def fetch(owner, carry):
+            for j in range(capacity):
+                rows = pl.ds(pl.multiple_of(wanted_ref[owner, 0, j] * BLK, BLK), BLK)
+                place = owner * capacity + j
+                pltpu.make_async_copy(k_ref.at[rows], buf.at[place, 0], in_sem.at[chunk]).start()
+                pltpu.make_async_copy(v_ref.at[rows], buf.at[place, 1], in_sem.at[chunk]).start()
+            return carry
+
+        lax.fori_loop(chunk * owners, (chunk + 1) * owners, fetch, 0, unroll=unroll)
     for chunk in range(chunks):
         part = pl.ds(chunk * span, span)
         wait_for(buf.at[part], in_sem.at[chunk])
         copies.append(pltpu.make_async_copy(buf.at[part], out_ref.at[part], out_sem.at[chunk]))
         copies[-1].start()
-        if chunk + ahead < chunks:
-            fetch(chunk + ahead)
     for copy in copies:
         copy.wait()
 
 
-def pack(wanted, keys, values, chunks=4, ahead=4):
+def pack(wanted, keys, values, chunks=4, unroll=2):
     count = wanted.shape[0] * wanted.shape[2]
     return pl.pallas_call(
-        functools.partial(pack_kernel, chunks, ahead),
+        functools.partial(pack_kernel, chunks, unroll),
         out_shape=jax.ShapeDtypeStruct((count, 2, BLK, HD), keys.dtype),
         in_specs=[SMEM, HBM, HBM],
         out_specs=HBM,
@@ -205,19 +206,19 @@
 def far_kernel(firsts, slots_ref, core_ref, got_ref, *refs):
     groups = len(firsts)
     near_refs, o_refs = refs[: 2 * groups], refs[2 * groups : 3 * groups]
-    far_buf, far_sem = refs[3 * groups :]
-    picks, half = far_buf.shape[1], o_refs[0].shape[1]
-    ratio, blocks = o_refs[0].shape[2] // HD, far_buf.shape[0] // groups
+    far_buf, o_buf, far_sem = refs[3 * groups :]
+    picks, half = far_buf.shape[1], o_buf.shape[2]
+    ratio, blocks = o_buf.shape[3] // HD, far_buf.shape[0] // groups
     factor = HD ** (-0.5) * LOG2E
     core = core_ref[0]
     for n in range(groups * blocks):
         g, i = divmod(n, blocks)
         for j in range(picks):
-            pltpu.make_async_copy(got_ref.at[slots_ref[firsts[g] + i, j]], far_buf.at[n, j], far_sem.at[n]).start()
+            pltpu.make_async_copy(got_ref.at[slots_ref[firsts[g] + i, j]], far_buf.at[n, j], far_sem).start()
+    wait_for(far_buf, far_sem)
     for n in range(groups * blocks):
         g, i = divmod(n, blocks)
         kept_ref, q_ref = near_refs[2 * g : 2 * g + 2]
-        wait_for(far_buf.at[n], far_sem.at[n])
         keys = jnp.concatenate([far_buf[n, j, 0] for j in range(picks)], axis=0)
         values = jnp.concatenate([far_buf[n, j, 1] for j in range(picks)], axis=0)
         for r in range(ratio):
@@ -230,13 +231,15 @@
             total = jnp.sum(exponent, axis=0, keepdims=True) + kept * kept_ref[i, TOTAL : TOTAL + 1, queries]
             partial = weighted(values, exponent.astype(jnp.bfloat16))
             merged = (partial + kept * kept_ref[i, 0:HD, queries]) * (1.0 / total)
-            turned = merged.T.astype(o_refs[g].dtype)
+            turned = merged.T.astype(o_buf.dtype)
             for part in range(CORES):
                 low, high = max(i * BLK, part * half), min((i + 1) * BLK, (part + 1) * half)
                 if low < high:
-                    place = core if part == 0 else 1 - core
                     rows = slice(low - part * half, high - part * half)
-                    o_refs[g][place, rows, r * HD : (r + 1) * HD] = turned[low - i * BLK : high - i * BLK]
+                    o_buf[g, part, rows, r * HD : (r + 1) * HD] = turned[low - i * BLK : high - i * BLK]
+    for g in range(groups):
+        for part in range(CORES):
+            o_refs[g][core if part == 0 else 1 - core] = o_buf[g, part]
 
 
 def far_attention(slots, firsts, core, got, near):
@@ -250,7 +253,11 @@
         out_shape=[jax.ShapeDtypeStruct((CORES, half, width), q.dtype)] * groups,
         in_specs=[SMEM, SMEM, HBM] + [VMEM] * (2 * groups),
         out_specs=[VMEM] * groups,
-        scratch_shapes=[pltpu.VMEM((count, picks) + got.shape[1:], got.dtype), pltpu.SemaphoreType.DMA((count,))],
+        scratch_shapes=[
+            pltpu.VMEM((count, picks) + got.shape[1:], got.dtype),
+            pltpu.VMEM((groups, CORES, half, width), q.dtype),
+            pltpu.SemaphoreType.DMA,
+        ],
         compiler_params=room(16),
         cost_estimate=cost(1, 1),
     )(slots, core, got, *[array for group in near for array in group])

time: 160 us -> 159 us (level)
  Pallas kernels: 46.4 us -> 44 us
    pallas_call x3, Pallas kernels: 13.1 us -> 10.4 us  [far_attention(): pl.pallas_call(functools.partial(far_kernel, firsts), out_shape=[jax.Shap...]
  transfers between devices with their start and end apart: 15 -> 15, of which waited for: 3 -> 4; matrix products, arithmetic and copies ran while one was open for 1% -> 1% of each run, Pallas kernels for 22% -> 21%
where the time goes in v7:
time: 159 us; the launch traced here: 158 us
  waiting for transfers between devices  58.4 us (37%)
  Pallas kernels  44 us (28%)
  starting transfers between devices  27.9 us (18%)
  blocking collectives  20.4 us (13%)
  local copies, waits for them, and re-layouts  6.03 us (4%)
    all_to_all x1, waiting for transfers between devices, shards(): lax.all_to_all(sent.reshape(seq_count, capacity, 2, BLK, HD), 'seq', spli...  54.7 us
    pallas_call x4, Pallas kernels, near_attention(): pl.pallas_call(functools.partial(near_kernel, first), out_shape=[jax.Shap...  21.5 us
    all_to_all x1, blocking collectives, shards(): lax.all_to_all(asked.reshape(seq_count, 1, capacity), 'seq', split_axis=0...  20.4 us
    ppermute x7, starting transfers between devices, shards(): lax.ppermute(piece, 'head', offset_pairs(chips, d, e))  11.5 us
    pallas_call x3, Pallas kernels, far_attention(): pl.pallas_call(functools.partial(far_kernel, firsts), out_shape=[jax.Shap...  10.4 us
    ppermute x4, starting transfers between devices, shards(): lax.ppermute(results[d], 'head', offset_pairs(chips, 0, 1))  6.74 us
    pallas_call x1, Pallas kernels, pack(): pl.pallas_call(functools.partial(pack_kernel, chunks, unroll), out_shape=...  6.17 us
    all_to_all x1, starting transfers between devices, shards(): lax.all_to_all(sent.reshape(seq_count, capacity, 2, BLK, HD), 'seq', spli...  5 us
  transfers between devices with their start and end apart: 15, of which 4 were waited for; matrix products, arithmetic and copies ran while one was open for 1% of the time, Pallas kernels for 21%

profile of v7, /device:TPU:1, one launch (start us, length us, event | category | flops | bytes accessed | tf_op | source)
XLA Modules:
  0.0 158.4 jit_solution(1155737386502555513)
XLA Ops:
  0.0 0.7 slice.12
  0.7 0.1 copy.23
  0.8 0.1 reshape.223
  0.9 0.2 convert_reduce_fusion
  1.1 0.1 select_reduce_fusion
  1.2 0.1 reduce_sum.24
  1.3 20.4 %all_to_all.10.wanted_ref = s32[32,1,2]{2,1,0:T(1,128)} all-to-all(s32[32,1,2]{2,1,0:T(1,128)S(1)} %fusion.1), channel_id=1, replica_groups=mesh['seq'=32,'head'=8] {'seq'}, dimensions={0} | all-to-all | bytes 512 | tf_op jit(solution)/shard_map/all_to_all | solution.py:297
  21.7 6.2 %shard_map.64 = bf16[64,2,128,128]{3,2,1,0:T(8,128)(2,1)} custom-call(s32[32,1,2]{2,1,0:T(1,128)} %all_to_all.10.wanted_ref, bf16[8192,128]{1,0:T(8,128)(2,1)} %k_ref.9, bf16[8192,128]{1,0:T(8,128)(2,1)} %v_ref.9), custom_call_target="tpu_custom_call" | custom-call | bytes 8388608 | tf_op jit(solution)/shard_map/pallas_call | solution.py:123
  27.9 0.0 copy-start.18
  27.9 0.0 copy-start.19
  27.9 0.0 copy-start.17
  27.9 5.0 %all-to-all-start.1 = ((bf16[32,2,2,128,128]{4,3,2,1,0:T(8,128)(2,1)}), bf16[32,2,2,128,128]{4,3,2,1,0:T(8,128)(2,1)}, u32[]{:S(2)}, u32[]{:S(2)}) async-start(bf16[32,2,2,128,128]{4,3,2,1,0:T(8,128)(2,1)} %bitcast.9), calls=%async_computation.1 | async-start | bytes 8388608 | tf_op jit(solution)/shard_map/all_to_all | solution.py:300
  33.0 0.5 fusion.7.places_ref
  33.5 3.0 %shard_map.65 = (bf16[192,512]{1,0:T(8,128)(2,1)}, bf16[192,512]{1,0:T(8,128)(2,1)}, bf16[192,512]{1,0:T(8,128)(2,1)}, bf16[192,512]{1,0:T(8,128)(2,1)}, bf16[19...) custom-call(s32[8]{0:T(128)} %fusion.7.places_ref, ...), custom_call_target="tpu_custom_call" | custom-call | bytes 3145728 | tf_op jit(solution)/shard_map/pallas_call | solution.py:54
  36.5 2.0 %collective-permute-start = (bf16[192,512]{1,0:T(8,128)(2,1)}, bf16[192,512]{1,0:T(8,128)(2,1)S(1)}, u32[]{:S(2)}, u32[]{:S(2)}) collective-permute-start(bf16[192,512]{1,0:T(8,128)(2,1)} %get-tuple-element.41), channel_id=1, source_target_pairs={{0,1},{1,0},{2,3},{3,2},{4,5},{5,4},{6,7},{7,6},{8,9},{9,8},{10,11... | collective-permute-start | bytes 589832 | tf_op jit(solution)/shard_map/ppermute | solution.py:311
  38.5 1.3 collective-permute-start.1
  39.8 1.5 collective-permute-start.2
  41.4 1.3 collective-permute-start.3
  42.7 2.0 %collective-permute-start.4 = (bf16[192,512]{1,0:T(8,128)(2,1)}, bf16[192,512]{1,0:T(8,128)(2,1)S(1)}, u32[]{:S(2)}, u32[]{:S(2)}) collective-permute-start(bf16[192,512]{1,0:T(8,128)(2,1)} %get-tuple-element.49), channel_id=1, source_target_pairs={{0,5},{1,4},{2,7},{3,6},{4,1},{5,0},{6,3},{7,2},{8,13},{9,12},{10,... | collective-permute-start | bytes 589832 | tf_op jit(solution)/shard_map/ppermute | solution.py:311
  44.7 0.1 reduce_sum.25
  44.8 0.1 concatenate.8
  44.9 0.1 copy.20
  45.0 0.1 pad_add_fusion
  45.1 0.6 gather_fusion
  45.7 0.1 broadcast_in_dim.27
  45.8 0.1 broadcast_in_dim.28
  45.9 0.0 collective-permute-done.qb_ref
  45.9 1.5 collective-permute-start.5
  47.3 0.0 collective-permute-done.1.qa_ref
  47.3 1.8 %collective-permute-start.6 = (bf16[192,512]{1,0:T(8,128)(2,1)}, bf16[192,512]{1,0:T(8,128)(2,1)S(1)}, u32[]{:S(2)}, u32[]{:S(2)}) collective-permute-start(bf16[192,512]{1,0:T(8,128)(2,1)} %get-tuple-element.53), channel_id=1, source_target_pairs={{0,7},{1,6},{2,1},{3,0},{4,3},{5,2},{6,5},{7,4},{8,15},{9,14},{10,... | collective-permute-start | bytes 589832 | tf_op jit(solution)/shard_map/ppermute | solution.py:311
  49.2 0.1 broadcast_select_fusion
  49.2 0.1 slice.19.slots_ref
  49.3 0.5 copy-done.9
  49.8 5.4 %shard_map.66 = (f32[3,136,512]{2,1,0:T(8,128)}, bf16[3,512,128]{2,1,0:T(8,128)(2,1)}) custom-call(s32[12,5]{1,0:T(8,128)} %bitcast.10, s32[1]{0:T(128)} %bitcast.4.core_ref, bf16[192,512]{1,0:T(8,128)(2,1)} %get-tuple-element.40.qa_ref, bf16[192,512]{1,0:T(8,128)(2,1)} %copy-done.14, bf16[8192,128]{1,0:T(8,128)(2,1)} %k_ref.9, bf16[8192,128]{1,0:T(8,128)(2,1)} %v_ref.9), custom_call_target="tpu_custom_call" | custom-call | flops 503316480 | bytes 2555904 | tf_op jit(solution)/shard_map/pallas_call | solution.py:188
  55.3 0.0 collective-permute-done.2.qb_ref
  55.3 0.7 copy-done.13
  56.0 5.4 %shard_map.67 = (f32[3,136,512]{2,1,0:T(8,128)}, bf16[3,512,128]{2,1,0:T(8,128)(2,1)}) custom-call(s32[12,5]{1,0:T(8,128)} %bitcast.11, s32[1]{0:T(128)} %bitcast.4.core_ref, bf16[192,512]{1,0:T(8,128)(2,1)} %copy-done.12, bf16[192,512]{1,0:T(8,128)(2,1)} %copy-done.13, bf16[8192,128]{1,0:T(8,128)(2,1)} %k_ref.9, bf16[8192,128]{1,0:T(8,128)(2,1)} %v_ref.9), custom_call_target="tpu_custom_call" | custom-call | flops 503316480 | bytes 2555904 | tf_op jit(solution)/shard_map/pallas_call | solution.py:188
  61.3 0.0 collective-permute-done.3.qa_ref
  61.4 0.0 collective-permute-done.4.qb_ref
  61.4 0.7 copy-done.10
  62.0 0.7 copy-done.11
  62.7 5.4 %shard_map.68 = (f32[3,136,512]{2,1,0:T(8,128)}, bf16[3,512,128]{2,1,0:T(8,128)(2,1)}) custom-call(s32[12,5]{1,0:T(8,128)} %bitcast.12, s32[1]{0:T(128)} %bitcast.4.core_ref, bf16[192,512]{1,0:T(8,128)(2,1)} %copy-done.10, bf16[192,512]{1,0:T(8,128)(2,1)} %copy-done.11, bf16[8192,128]{1,0:T(8,128)(2,1)} %k_ref.9, bf16[8192,128]{1,0:T(8,128)(2,1)} %v_ref.9), custom_call_target="tpu_custom_call" | custom-call | flops 503316480 | bytes 2555904 | tf_op jit(solution)/shard_map/pallas_call | solution.py:188
  68.1 0.0 collective-permute-done.5.qa_ref
  68.1 0.0 collective-permute-done.6.qb_ref
  68.1 0.7 copy-done.15
  68.8 0.7 copy-done.16
  69.5 5.4 %shard_map.69 = (f32[3,136,512]{2,1,0:T(8,128)}, bf16[3,512,128]{2,1,0:T(8,128)(2,1)}) custom-call(s32[12,5]{1,0:T(8,128)} %bitcast.13, s32[1]{0:T(128)} %bitcast.4.core_ref, bf16[192,512]{1,0:T(8,128)(2,1)} %copy-done.15, bf16[192,512]{1,0:T(8,128)(2,1)} %copy-done.16, bf16[8192,128]{1,0:T(8,128)(2,1)} %k_ref.9, bf16[8192,128]{1,0:T(8,128)(2,1)} %v_ref.9), custom_call_target="tpu_custom_call" | custom-call | flops 503316480 | bytes 2555904 | tf_op jit(solution)/shard_map/pallas_call | solution.py:188
  74.9 54.7 %all-to-all-done.1 = bf16[32,2,2,128,128]{4,3,2,1,0:T(8,128)(2,1)} async-done(((bf16[32,2,2,128,128]{4,3,2,1,0:T(8,128)(2,1)}), bf16[32,2,2,128,128]{4,3,2,1,0:T(8,128)(2,1)}, u32[]{:S(2)}, u32[]{:S(2)}) %all-to-all-start.1) | async-done | bytes 4194336 | tf_op jit(solution)/shard_map/all_to_all | solution.py:300
  129.6 3.1 %shard_map.70 = bf16[2,192,512]{2,1,0:T(8,128)(2,1)S(1)} custom-call(s32[12,3]{1,0:T(8,128)S(1)} %slice.19.slots_ref, s32[1]{0:T(128)} %bitcast.4.core_ref, bf16[64,2,128,128]{3,2,1,0:T(8,128)(2,1)} %bitcast.2.got_ref, f32[3,136,512]{2,1,0:T(8,128)S(1)} %copy-done.2, bf16[3,512,128]{2,1,0:T(8,128)(2,1)S(1)} %copy-done.5), custom_call_target="tpu_custom_call" | custom-call | flops 1 | bytes 1 | tf_op jit(solution)/shard_map/pallas_call | solution.py:251
  132.7 3.2 %collective-permute-start.11 = (bf16[2,192,512]{2,1,0:T(8,128)(2,1)S(1)}, bf16[2,192,512]{2,1,0:T(8,128)(2,1)S(1)}, u32[]{:S(2)}, u32[]{:S(2)}) collective-permute-start(bf16[2,192,512]{2,1,0:T(8,128)(2,1)S(1)} %shard_map.70), channel_id=1, source_target_pairs={{0,4},{1,5},{2,6},{3,7},{4,0},{5,1},{6,2},{7,3},{8,12},{9,13},{10,... | collective-permute-start | bytes 1179656 | tf_op jit(solution)/shard_map/ppermute | solution.py:334
  135.9 4.2 %shard_map.71 = (bf16[2,192,512]{2,1,0:T(8,128)(2,1)S(1)}, bf16[2,192,512]{2,1,0:T(8,128)(2,1)S(1)}) custom-call(s32[12,3]{1,0:T(8,128)S(1)} %slice.19.slots_ref, s32[1]{0:T(128)} %bitcast.4.core_ref, bf16[64,2,128,128]{3,2,1,0:T(8,128)(2,1)} %bitcast.2.got_ref, f32[3,136,512]{2,1,0:T(8,128)S(1)} %copy-done.1, bf16[3,512,128]{2,1,0:T(8,128)(2,1)S(1)} %copy-done.6, ...), custom_call_target="tpu_custom_call" | custom-call | flops 1 | bytes 1 | tf_op jit(solution)/shard_map/pallas_call | solution.py:251
  140.1 0.9 collective-permute-start.7
  141.0 0.7 collective-permute-start.9
  141.7 1.9 %collective-permute-done.11.refs_2_ = bf16[2,192,512]{2,1,0:T(8,128)(2,1)S(1)} collective-permute-done((bf16[2,192,512]{2,1,0:T(8,128)(2,1)S(1)}, bf16[2,192,512]{2,1,0:T(8,128)(2,1)S(1)}, u32[]{:S(2)}, u32[]{:S(2)}) %collective-permute-start.11) | collective-permute-done | bytes 393248 | tf_op jit(solution)/shard_map/ppermute | solution.py:334
  143.6 3.1 %shard_map.72.refs_0_ = bf16[2,192,512]{2,1,0:T(8,128)(2,1)S(1)} custom-call(s32[12,3]{1,0:T(8,128)S(1)} %slice.19.slots_ref, s32[1]{0:T(128)} %bitcast.4.core_ref, bf16[64,2,128,128]{3,2,1,0:T(8,128)(2,1)} %bitcast.2.got_ref, f32[3,136,512]{2,1,0:T(8,128)S(1)} %copy-done, bf16[3,512,128]{2,1,0:T(8,128)(2,1)S(1)} %copy-done.4), custom_call_target="tpu_custom_call" | custom-call | flops 1 | bytes 1 | tf_op jit(solution)/shard_map/pallas_call | solution.py:251
  146.7 4.5 %collective-permute-start.12 = (bf16[2,192,512]{2,1,0:T(8,128)(2,1)S(1)}, bf16[2,192,512]{2,1,0:T(8,128)(2,1)S(1)}, u32[]{:S(2)}, u32[]{:S(2)}) collective-permute-start(bf16[2,192,512]{2,1,0:T(8,128)(2,1)S(1)} %shard_map.72.refs_0_), channel_id=1, source_target_pairs={{0,1},{1,0},{2,3},{3,2},{4,5},{5,4},{6,7},{7,6},{8,9},{9,8},{10,11... | collective-permute-start | bytes 1179656 | tf_op jit(solution)/shard_map/ppermute | solution.py:337
  151.1 0.1 collective-permute-start.13
  151.2 1.6 %collective-permute-done.7.refs_0_ = bf16[2,192,512]{2,1,0:T(8,128)(2,1)S(1)} collective-permute-done((bf16[2,192,512]{2,1,0:T(8,128)(2,1)S(1)}, bf16[2,192,512]{2,1,0:T(8,128)(2,1)S(1)}, u32[]{:S(2)}, u32[]{:S(2)}) %collective-permute-start.7) | collective-permute-done | bytes 393248 | tf_op jit(solution)/shard_map/ppermute | solution.py:334
  152.9 1.9 %collective-permute-start.8 = (bf16[2,192,512]{2,1,0:T(8,128)(2,1)S(1)}, bf16[2,192,512]{2,1,0:T(8,128)(2,1)S(1)}, u32[]{:S(2)}, u32[]{:S(2)}) collective-permute-start(bf16[2,192,512]{2,1,0:T(8,128)(2,1)S(1)} %collective-permute-done.7.refs_0_), channel_id=1, source_target_pairs={{0,1},{1,0},{2,3},{3,2},{4,5},{5,4},{6,7},{7,6},{8,9},{9,8},{10,11... | collective-permute-start | bytes 1179656 | tf_op jit(solution)/shard_map/ppermute | solution.py:337
  154.8 0.3 collective-permute-start.10
  155.1 1.5 shard_map.73.refs_4_
  156.6 0.0 collective-permute-done.8.refs_1_
  156.6 0.1 collective-permute-done.10.refs_3_
  156.7 1.5 shard_map.74
  (45 shorter events, 0.2 us)
Async XLA Ops:
  27.9 5.1 %copy-start.18 = (s32[8]{0:T(128)S(1)}, s32[8]{0:T(128)}, u32[]{:S(2)}) copy-start(s32[8]{0:T(128)} %constant.114.clone) | copy-start | bytes 100
  27.9 5.1 %copy-start.19 = (s32[8]{0:T(128)S(1)}, s32[8]{0:T(128)}, u32[]{:S(2)}) copy-start(s32[8]{0:T(128)} %constant.115.clone) | copy-start | bytes 100
  27.9 16.9 %copy-start.17 = (s32[12,8]{0,1:T(8,128)S(1)}, s32[12,8]{0,1:T(8,128)}, u32[]{:S(2)}) copy-start(s32[12,8]{0,1:T(8,128)} %param.9) | copy-start | bytes 1156
  27.9 101.6 %all-to-all-start.1 = ((bf16[32,2,2,128,128]{4,3,2,1,0:T(8,128)(2,1)}), bf16[32,2,2,128,128]{4,3,2,1,0:T(8,128)(2,1)}, u32[]{:S(2)}, u32[]{:S(2)}) async-start(bf16[32,2,2,128,128]{4,3,2,1,0:T(8,128)(2,1)} %bitcast.9), calls=%async_computation.1 | async-start | bytes 8388608 | tf_op jit(solution)/shard_map/all_to_all | solution.py:300
  36.5 9.4 %collective-permute-start = (bf16[192,512]{1,0:T(8,128)(2,1)}, bf16[192,512]{1,0:T(8,128)(2,1)S(1)}, u32[]{:S(2)}, u32[]{:S(2)}) collective-permute-start(bf16[192,512]{1,0:T(8,128)(2,1)} %get-tuple-element.41), channel_id=1, source_target_pairs={{0,1},{1,0},{2,3},{3,2},{4,5},{5,4},{6,7},{7,6},{8,9},{9,8},{10,11... | collective-permute-start | bytes 589832 | tf_op jit(solution)/shard_map/ppermute | solution.py:311
  38.5 8.8 %collective-permute-start.1 = (bf16[192,512]{1,0:T(8,128)(2,1)}, bf16[192,512]{1,0:T(8,128)(2,1)S(1)}, u32[]{:S(2)}, u32[]{:S(2)}) collective-permute-start(bf16[192,512]{1,0:T(8,128)(2,1)} %get-tuple-element.44), channel_id=1, source_target_pairs={{0,2},{1,3},{2,4},{3,5},{4,6},{5,7},{6,0},{7,1},{8,10},{9,11},{10,... | collective-permute-start | bytes 589832 | tf_op jit(solution)/shard_map/ppermute | solution.py:311
  39.8 15.4 %collective-permute-start.2 = (bf16[192,512]{1,0:T(8,128)(2,1)}, bf16[192,512]{1,0:T(8,128)(2,1)S(1)}, u32[]{:S(2)}, u32[]{:S(2)}) collective-permute-start(bf16[192,512]{1,0:T(8,128)(2,1)} %get-tuple-element.45), channel_id=1, source_target_pairs={{0,3},{1,2},{2,5},{3,4},{4,7},{5,6},{6,1},{7,0},{8,11},{9,10},{10,... | collective-permute-start | bytes 589832 | tf_op jit(solution)/shard_map/ppermute | solution.py:311
  41.4 20.0 %collective-permute-start.3 = (bf16[192,512]{1,0:T(8,128)(2,1)}, bf16[192,512]{1,0:T(8,128)(2,1)S(1)}, u32[]{:S(2)}, u32[]{:S(2)}) collective-permute-start(bf16[192,512]{1,0:T(8,128)(2,1)} %get-tuple-element.48), channel_id=1, source_target_pairs={{0,4},{1,5},{2,6},{3,7},{4,0},{5,1},{6,2},{7,3},{8,12},{9,13},{10,... | collective-permute-start | bytes 589832 | tf_op jit(solution)/shard_map/ppermute | solution.py:311
  42.7 18.7 %collective-permute-start.4 = (bf16[192,512]{1,0:T(8,128)(2,1)}, bf16[192,512]{1,0:T(8,128)(2,1)S(1)}, u32[]{:S(2)}, u32[]{:S(2)}) collective-permute-start(bf16[192,512]{1,0:T(8,128)(2,1)} %get-tuple-element.49), channel_id=1, source_target_pairs={{0,5},{1,4},{2,7},{3,6},{4,1},{5,0},{6,3},{7,2},{8,13},{9,12},{10,... | collective-permute-start | bytes 589832 | tf_op jit(solution)/shard_map/ppermute | solution.py:311
  45.9 3.4 %copy-start.14 = (bf16[192,512]{1,0:T(8,128)(2,1)}, bf16[192,512]{1,0:T(8,128)(2,1)S(1)}, u32[]{:S(2)}) copy-start(bf16[192,512]{1,0:T(8,128)(2,1)S(1)} %collective-permute-done.qb_ref) | copy-start | bytes 589828
  45.9 22.2 %collective-permute-start.5 = (bf16[192,512]{1,0:T(8,128)(2,1)}, bf16[192,512]{1,0:T(8,128)(2,1)S(1)}, u32[]{:S(2)}, u32[]{:S(2)}) collective-permute-start(bf16[192,512]{1,0:T(8,128)(2,1)} %get-tuple-element.52), channel_id=1, source_target_pairs={{0,6},{1,7},{2,0},{3,1},{4,2},{5,3},{6,4},{7,5},{8,14},{9,15},{10,... | collective-permute-start | bytes 589832 | tf_op jit(solution)/shard_map/ppermute | solution.py:311
  47.3 7.9 %copy-start.12 = (bf16[192,512]{1,0:T(8,128)(2,1)}, bf16[192,512]{1,0:T(8,128)(2,1)S(1)}, u32[]{:S(2)}) copy-start(bf16[192,512]{1,0:T(8,128)(2,1)S(1)} %collective-permute-done.1.qa_ref) | copy-start | bytes 589828
  47.3 20.8 %collective-permute-start.6 = (bf16[192,512]{1,0:T(8,128)(2,1)}, bf16[192,512]{1,0:T(8,128)(2,1)S(1)}, u32[]{:S(2)}, u32[]{:S(2)}) collective-permute-start(bf16[192,512]{1,0:T(8,128)(2,1)} %get-tuple-element.53), channel_id=1, source_target_pairs={{0,7},{1,6},{2,1},{3,0},{4,3},{5,2},{6,5},{7,4},{8,15},{9,14},{10,... | collective-permute-start | bytes 589832 | tf_op jit(solution)/shard_map/ppermute | solution.py:311
  49.2 0.6 copy-start.9
  55.3 0.7 copy-start.13
  61.3 0.7 copy-start.10
  62.0 0.7 copy-start.11
  68.1 61.5 %copy-start.2 = (f32[3,136,512]{2,1,0:T(8,128)S(1)}, f32[3,136,512]{2,1,0:T(8,128)}, u32[]{:S(2)}) copy-start(f32[3,136,512]{2,1,0:T(8,128)} %get-tuple-element.58.refs_0_) | copy-start | bytes 2506756
  68.1 61.5 %copy-start.5 = (bf16[3,512,128]{2,1,0:T(8,128)(2,1)S(1)}, bf16[3,512,128]{2,1,0:T(8,128)(2,1)}, u32[]{:S(2)}) copy-start(bf16[3,512,128]{2,1,0:T(8,128)(2,1)} %get-tuple-element.59.refs_1_) | copy-start | bytes 1179652
  68.1 0.7 copy-start.15
  68.8 0.7 copy-start.16
  129.6 6.3 %copy-start.1 = (f32[3,136,512]{2,1,0:T(8,128)S(1)}, f32[3,136,512]{2,1,0:T(8,128)}, u32[]{:S(2)}) copy-start(f32[3,136,512]{2,1,0:T(8,128)} %get-tuple-element.61.refs_0_) | copy-start | bytes 2506756
  129.6 6.3 %copy-start.3 = (f32[3,136,512]{2,1,0:T(8,128)S(1)}, f32[3,136,512]{2,1,0:T(8,128)}, u32[]{:S(2)}) copy-start(f32[3,136,512]{2,1,0:T(8,128)} %get-tuple-element.63.refs_2_) | copy-start | bytes 2506756
  129.6 6.3 %copy-start.6 = (bf16[3,512,128]{2,1,0:T(8,128)(2,1)S(1)}, bf16[3,512,128]{2,1,0:T(8,128)(2,1)}, u32[]{:S(2)}) copy-start(bf16[3,512,128]{2,1,0:T(8,128)(2,1)} %get-tuple-element.62.refs_1_) | copy-start | bytes 1179652
  129.6 6.3 %copy-start.7 = (bf16[3,512,128]{2,1,0:T(8,128)(2,1)S(1)}, bf16[3,512,128]{2,1,0:T(8,128)(2,1)}, u32[]{:S(2)}) copy-start(bf16[3,512,128]{2,1,0:T(8,128)(2,1)} %get-tuple-element.64.refs_3_) | copy-start | bytes 1179652
  132.7 10.9 %copy-start = (f32[3,136,512]{2,1,0:T(8,128)S(1)}, f32[3,136,512]{2,1,0:T(8,128)}, u32[]{:S(2)}) copy-start(f32[3,136,512]{2,1,0:T(8,128)} %get-tuple-element.72.refs_0_) | copy-start | bytes 2506756
  132.7 10.9 %copy-start.4 = (bf16[3,512,128]{2,1,0:T(8,128)(2,1)S(1)}, bf16[3,512,128]{2,1,0:T(8,128)(2,1)}, u32[]{:S(2)}) copy-start(bf16[3,512,128]{2,1,0:T(8,128)(2,1)} %get-tuple-element.73.refs_1_) | copy-start | bytes 1179652
  132.7 10.8 %collective-permute-start.11 = (bf16[2,192,512]{2,1,0:T(8,128)(2,1)S(1)}, bf16[2,192,512]{2,1,0:T(8,128)(2,1)S(1)}, u32[]{:S(2)}, u32[]{:S(2)}) collective-permute-start(bf16[2,192,512]{2,1,0:T(8,128)(2,1)S(1)} %shard_map.70), channel_id=1, source_target_pairs={{0,4},{1,5},{2,6},{3,7},{4,0},{5,1},{6,2},{7,3},{8,12},{9,13},{10,... | collective-permute-start | bytes 1179656 | tf_op jit(solution)/shard_map/ppermute | solution.py:334
  140.1 14.9 %copy-start.8 = (s32[8]{0:T(128)S(1)}, s32[8]{0:T(128)}, u32[]{:S(2)}) copy-start(s32[8]{0:T(128)} %fusion.7.places_ref) | copy-start | bytes 100
  140.1 12.8 %collective-permute-start.7 = (bf16[2,192,512]{2,1,0:T(8,128)(2,1)S(1)}, bf16[2,192,512]{2,1,0:T(8,128)(2,1)S(1)}, u32[]{:S(2)}, u32[]{:S(2)}) collective-permute-start(bf16[2,192,512]{2,1,0:T(8,128)(2,1)S(1)} %get-tuple-element.67), channel_id=1, source_target_pairs={{0,6},{1,7},{2,0},{3,1},{4,2},{5,3},{6,4},{7,5},{8,14},{9,15},{10,... | collective-permute-start | bytes 1179656 | tf_op jit(solution)/shard_map/ppermute | solution.py:334
  141.0 13.8 %collective-permute-start.9 = (bf16[2,192,512]{2,1,0:T(8,128)(2,1)S(1)}, bf16[2,192,512]{2,1,0:T(8,128)(2,1)S(1)}, u32[]{:S(2)}, u32[]{:S(2)}) collective-permute-start(bf16[2,192,512]{2,1,0:T(8,128)(2,1)S(1)} %get-tuple-element.68), channel_id=1, source_target_pairs={{0,2},{1,3},{2,4},{3,5},{4,6},{5,7},{6,0},{7,1},{8,10},{9,11},{10,... | collective-permute-start | bytes 1179656 | tf_op jit(solution)/shard_map/ppermute | solution.py:334
  146.7 8.4 %collective-permute-start.12 = (bf16[2,192,512]{2,1,0:T(8,128)(2,1)S(1)}, bf16[2,192,512]{2,1,0:T(8,128)(2,1)S(1)}, u32[]{:S(2)}, u32[]{:S(2)}) collective-permute-start(bf16[2,192,512]{2,1,0:T(8,128)(2,1)S(1)} %shard_map.72.refs_0_), channel_id=1, source_target_pairs={{0,1},{1,0},{2,3},{3,2},{4,5},{5,4},{6,7},{7,6},{8,9},{9,8},{10,11... | collective-permute-start | bytes 1179656 | tf_op jit(solution)/shard_map/ppermute | solution.py:337
  151.1 3.9 %collective-permute-start.13 = (bf16[2,192,512]{2,1,0:T(8,128)(2,1)S(1)}, bf16[2,192,512]{2,1,0:T(8,128)(2,1)S(1)}, u32[]{:S(2)}, u32[]{:S(2)}) collective-permute-start(bf16[2,192,512]{2,1,0:T(8,128)(2,1)S(1)} %collective-permute-done.11.refs_2_), channel_id=1, source_target_pairs={{0,1},{1,0},{2,3},{3,2},{4,5},{5,4},{6,7},{7,6},{8,9},{9,8},{10,11... | collective-permute-start | bytes 1179656 | tf_op jit(solution)/shard_map/ppermute | solution.py:337
  152.9 3.7 %collective-permute-start.8 = (bf16[2,192,512]{2,1,0:T(8,128)(2,1)S(1)}, bf16[2,192,512]{2,1,0:T(8,128)(2,1)S(1)}, u32[]{:S(2)}, u32[]{:S(2)}) collective-permute-start(bf16[2,192,512]{2,1,0:T(8,128)(2,1)S(1)} %collective-permute-done.7.refs_0_), channel_id=1, source_target_pairs={{0,1},{1,0},{2,3},{3,2},{4,5},{5,4},{6,7},{7,6},{8,9},{9,8},{10,11... | collective-permute-start | bytes 1179656 | tf_op jit(solution)/shard_map/ppermute | solution.py:337
  154.8 1.9 %collective-permute-start.10 = (bf16[2,192,512]{2,1,0:T(8,128)(2,1)S(1)}, bf16[2,192,512]{2,1,0:T(8,128)(2,1)S(1)}, u32[]{:S(2)}, u32[]{:S(2)}) collective-permute-start(bf16[2,192,512]{2,1,0:T(8,128)(2,1)S(1)} %collective-permute-done.9.refs_2_), channel_id=1, source_target_pairs={{0,1},{1,0},{2,3},{3,2},{4,5},{5,4},{6,7},{7,6},{8,9},{9,8},{10,11... | collective-permute-start | bytes 1179656 | tf_op jit(solution)/shard_map/ppermute | solution.py:337

commit v8 on v7

--- a/solution.py
+++ b/solution.py
@@ -94,42 +94,41 @@
     )(places, *[pieces[i] for i in chosen], *rest)
 
 
-def pack_kernel(chunks, unroll, wanted_ref, k_ref, v_ref, out_ref, buf, in_sem, out_sem):
-    span, capacity = out_ref.shape[0] // chunks, wanted_ref.shape[2]
-    owners = span // capacity
-    copies = []
-    for chunk in range(chunks):
-
-        def fetch(owner, carry):
-            for j in range(capacity):
-                rows = pl.ds(pl.multiple_of(wanted_ref[owner, 0, j] * BLK, BLK), BLK)
-                place = owner * capacity + j
-                pltpu.make_async_copy(k_ref.at[rows], buf.at[place, 0], in_sem.at[chunk]).start()
-                pltpu.make_async_copy(v_ref.at[rows], buf.at[place, 1], in_sem.at[chunk]).start()
-            return carry
-
-        lax.fori_loop(chunk * owners, (chunk + 1) * owners, fetch, 0, unroll=unroll)
-    for chunk in range(chunks):
-        part = pl.ds(chunk * span, span)
-        wait_for(buf.at[part], in_sem.at[chunk])
-        copies.append(pltpu.make_async_copy(buf.at[part], out_ref.at[part], out_sem.at[chunk]))
-        copies[-1].start()
-    for copy in copies:
-        copy.wait()
-
-
-def pack(wanted, keys, values, chunks=4, unroll=2):
+def hold_kernel(k_ref, k_out, sem):
+    copy = pltpu.make_async_copy(k_ref, k_out, sem)
+    copy.start()
+    copy.wait()
+
+
+def hold(keys):
+    return pl.pallas_call(
+        hold_kernel,
+        out_shape=jax.ShapeDtypeStruct(keys.shape, keys.dtype),
+        in_specs=[HBM],
+        out_specs=VMEM,
+        scratch_shapes=[pltpu.SemaphoreType.DMA],
+        compiler_params=room(6),
+        cost_estimate=cost(0, 4 * keys.size),
+    )(keys)
+
+
+def pack_kernel(wanted_ref, k_ref, v_ref, out_ref):
+    capacity = wanted_ref.shape[2]
+    for place in range(out_ref.shape[0]):
+        wanted = wanted_ref[place // capacity, 0, place % capacity]
+        rows = pl.ds(pl.multiple_of(wanted * BLK, BLK), BLK)
+        out_ref[place, 0] = k_ref[rows, :]
+        out_ref[place, 1] = v_ref[rows, :]
+
+
+def pack(wanted, keys, values):
     count = wanted.shape[0] * wanted.shape[2]
     return pl.pallas_call(
-        functools.partial(pack_kernel, chunks, unroll),
+        pack_kernel,
         out_shape=jax.ShapeDtypeStruct((count, 2, BLK, HD), keys.dtype),
-        in_specs=[SMEM, HBM, HBM],
-        out_specs=HBM,
-        scratch_shapes=[
-            pltpu.VMEM((count, 2, BLK, HD), keys.dtype),
-            pltpu.SemaphoreType.DMA((chunks,)),
-            pltpu.SemaphoreType.DMA((chunks,)),
-        ],
+        in_specs=[SMEM, VMEM, VMEM],
+        out_specs=VMEM,
+        compiler_params=room(12),
         cost_estimate=cost(0, 8 * count * BLK * HD),
     )(wanted, keys, values)
 
@@ -296,7 +295,7 @@
     asked = unasked + jnp.sum(jnp.where(placed, far_within[:, None] - unasked[None, :], 0), axis=0)
     wanted = lax.all_to_all(asked.reshape(seq_count, 1, capacity), "seq", split_axis=0, concat_axis=0, tiled=True)
 
-    sent = pack(wanted, cache_keys, cache_values)
+    sent = pack(wanted, hold(cache_keys), cache_values)
     got = lax.all_to_all(
         sent.reshape(seq_count, capacity, 2, BLK, HD), "seq", split_axis=0, concat_axis=0, tiled=True
     ).reshape(slot_total, 2, BLK, HD)

time: 159 us -> 158 us (level)
  blocking collectives: 20.4 us -> 0 us
  starting transfers between devices: 27.9 us -> 40 us
  local copies, waits for them, and re-layouts: 6.03 us -> 12.6 us
  waiting for transfers between devices: 58.4 us -> 63.6 us
  Pallas kernels: 44 us -> 39.1 us
    all_to_all x1 -> x0, blocking collectives: 20.4 us -> none  [shards(): lax.all_to_all(asked.reshape(seq_count, 1, capacity), 'seq', split_axis=0...]
    all_to_all x0 -> x1, starting transfers between devices: none -> 11.9 us  [shards(): lax.all_to_all(asked.reshape(seq_count, 1, capacity), 'seq', split_axis=0...]
    unnamed x41 -> x51, local copies, waits for them, and re-layouts: 4.06 us -> 10.6 us
    all_to_all x0 -> x1, waiting for transfers between devices: none -> 5.45 us  [shards(): lax.all_to_all(asked.reshape(seq_count, 1, capacity), 'seq', split_axis=0...]
    pallas_call x1 -> x2, Pallas kernels: 6.17 us -> 1.23 us  [the longest x1 1.08 us: pack(): pl.pallas_call(pack_kernel, out_shape=jax.ShapeDtypeStruct((count, 2, BLK...]
  transfers between devices with their start and end apart: 15 -> 16, of which waited for: 4 -> 5; matrix products, arithmetic and copies ran while one was open for 1% -> 1% of each run, Pallas kernels for 21% -> 21%
where the time goes in v8:
time: 158 us; the launch traced here: 157 us
  waiting for transfers between devices  63.6 us (40%)
  starting transfers between devices  40 us (25%)
  Pallas kernels  39.1 us (25%)
  local copies, waits for them, and re-layouts  12.6 us (8%)
  other arithmetic  1.65 us (1%)
    all_to_all x1, waiting for transfers between devices, shards(): lax.all_to_all(sent.reshape(seq_count, capacity, 2, BLK, HD), 'seq', spli...  54.5 us
    pallas_call x4, Pallas kernels, near_attention(): pl.pallas_call(functools.partial(near_kernel, first), out_shape=[jax.Shap...  21.5 us
    all_to_all x1, starting transfers between devices, shards(): lax.all_to_all(asked.reshape(seq_count, 1, capacity), 'seq', split_axis=0...  11.9 us
    ppermute x7, starting transfers between devices, shards(): lax.ppermute(piece, 'head', offset_pairs(chips, d, e))  11.6 us
    unnamed x51, local copies, waits for them, and re-layouts  10.6 us
    pallas_call x3, Pallas kernels, far_attention(): pl.pallas_call(functools.partial(far_kernel, firsts), out_shape=[jax.Shap...  10.4 us
    ppermute x4, starting transfers between devices, shards(): lax.ppermute(results[d], 'head', offset_pairs(chips, 0, 1))  6.77 us
    all_to_all x1, waiting for transfers between devices, shards(): lax.all_to_all(asked.reshape(seq_count, 1, capacity), 'seq', split_axis=0...  5.45 us
  transfers between devices with their start and end apart: 16, of which 5 were waited for; matrix products, arithmetic and copies ran while one was open for 1% of the time, Pallas kernels for 21%

profile of v8, /device:TPU:1, one launch (start us, length us, event | category | flops | bytes accessed | tf_op | source)
XLA Modules:
  0.0 157.4 jit_solution(4916522460297151595)
XLA Ops:
  0.0 0.7 slice.12
  0.7 0.1 copy.23
  0.8 0.1 reshape.223
  0.9 0.2 convert_reduce_fusion
  1.1 0.1 select_reduce_fusion
  1.2 0.1 reduce_sum.24
  1.3 0.6 fusion.1
  1.9 11.9 %all-to-all-start = ((s32[32,1,2]{2,1,0:T(1,128)}), s32[32,1,2]{2,1,0:T(1,128)S(1)}, u32[]{:S(2)}, u32[]{:S(2)}) async-start(s32[32,1,2]{2,1,0:T(1,128)} %fusion.1), calls=%async_computation | async-start | bytes 32768 | tf_op jit(solution)/shard_map/all_to_all | solution.py:296
  13.8 0.0 copy-start
  13.8 1.6 %copy-done = bf16[8192,128]{1,0:T(8,128)(2,1)S(1)} copy-done((bf16[8192,128]{1,0:T(8,128)(2,1)S(1)}, bf16[8192,128]{1,0:T(8,128)(2,1)}, u32[]{:S(2)}) %copy-start) | copy-done | bytes 2097176
  15.4 0.1 shard_map.64.k_ref
  15.6 1.3 copy-done.3
  16.9 5.4 %all-to-all-done.wanted_ref = s32[32,1,2]{2,1,0:T(1,128)S(1)} async-done(((s32[32,1,2]{2,1,0:T(1,128)}), s32[32,1,2]{2,1,0:T(1,128)S(1)}, u32[]{:S(2)}, u32[]{:S(2)}) %all-to-all-start) | async-done | bytes 288 | tf_op jit(solution)/shard_map/all_to_all | solution.py:296
  22.4 1.6 %copy-done.4 = bf16[8192,128]{1,0:T(8,128)(2,1)S(1)} copy-done((bf16[8192,128]{1,0:T(8,128)(2,1)S(1)}, bf16[8192,128]{1,0:T(8,128)(2,1)}, u32[]{:S(2)}) %copy-start.4) | copy-done | bytes 2097176
  24.0 1.1 shard_map.65
  25.0 2.0 %copy-done.2 = bf16[64,2,128,128]{3,2,1,0:T(8,128)(2,1)} copy-done((bf16[64,2,128,128]{3,2,1,0:T(8,128)(2,1)}, bf16[64,2,128,128]{3,2,1,0:T(8,128)(2,1)S(1)}, u32[]{:S(2)}) %copy-start.2) | copy-done | bytes 4194328
  27.1 5.0 %all-to-all-start.1 = ((bf16[32,2,2,128,128]{4,3,2,1,0:T(8,128)(2,1)}), bf16[32,2,2,128,128]{4,3,2,1,0:T(8,128)(2,1)}, u32[]{:S(2)}, u32[]{:S(2)}) async-start(bf16[32,2,2,128,128]{4,3,2,1,0:T(8,128)(2,1)} %bitcast.9), calls=%async_computation.1 | async-start | bytes 8388608 | tf_op jit(solution)/shard_map/all_to_all | solution.py:299
  32.1 0.5 fusion.7.places_ref
  32.6 3.0 %shard_map.66 = (bf16[192,512]{1,0:T(8,128)(2,1)}, bf16[192,512]{1,0:T(8,128)(2,1)}, bf16[192,512]{1,0:T(8,128)(2,1)}, bf16[192,512]{1,0:T(8,128)(2,1)}, bf16[19...) custom-call(s32[8]{0:T(128)} %fusion.7.places_ref, ...), custom_call_target="tpu_custom_call" | custom-call | bytes 3145728 | tf_op jit(solution)/shard_map/pallas_call | solution.py:54
  35.6 2.2 %collective-permute-start = (bf16[192,512]{1,0:T(8,128)(2,1)}, bf16[192,512]{1,0:T(8,128)(2,1)S(1)}, u32[]{:S(2)}, u32[]{:S(2)}) collective-permute-start(bf16[192,512]{1,0:T(8,128)(2,1)} %get-tuple-element.41), channel_id=1, source_target_pairs={{0,1},{1,0},{2,3},{3,2},{4,5},{5,4},{6,7},{7,6},{8,9},{9,8},{10,11... | collective-permute-start | bytes 589832 | tf_op jit(solution)/shard_map/ppermute | solution.py:310
  37.8 1.3 collective-permute-start.1
  39.1 1.5 collective-permute-start.2
  40.7 1.3 collective-permute-start.3
  41.9 2.0 %collective-permute-start.4 = (bf16[192,512]{1,0:T(8,128)(2,1)}, bf16[192,512]{1,0:T(8,128)(2,1)S(1)}, u32[]{:S(2)}, u32[]{:S(2)}) collective-permute-start(bf16[192,512]{1,0:T(8,128)(2,1)} %get-tuple-element.49), channel_id=1, source_target_pairs={{0,5},{1,4},{2,7},{3,6},{4,1},{5,0},{6,3},{7,2},{8,13},{9,12},{10,... | collective-permute-start | bytes 589832 | tf_op jit(solution)/shard_map/ppermute | solution.py:310
  44.0 0.1 reduce_sum.25
  44.1 0.1 concatenate.8
  44.2 0.1 copy.20
  44.3 0.1 pad_add_fusion
  44.4 0.6 gather_fusion
  45.0 0.1 broadcast_in_dim.27
  45.1 0.1 broadcast_in_dim.28
  45.2 0.0 collective-permute-done.qb_ref
  45.2 1.5 collective-permute-start.5
  46.6 1.8 %collective-permute-start.6 = (bf16[192,512]{1,0:T(8,128)(2,1)}, bf16[192,512]{1,0:T(8,128)(2,1)S(1)}, u32[]{:S(2)}, u32[]{:S(2)}) collective-permute-start(bf16[192,512]{1,0:T(8,128)(2,1)} %get-tuple-element.53), channel_id=1, source_target_pairs={{0,7},{1,6},{2,1},{3,0},{4,3},{5,2},{6,5},{7,4},{8,15},{9,14},{10,... | collective-permute-start | bytes 589832 | tf_op jit(solution)/shard_map/ppermute | solution.py:310
  48.5 0.1 broadcast_select_fusion
  48.5 0.1 slice.19.slots_ref
  48.6 0.5 copy-done.14
  49.1 5.4 %shard_map.67 = (f32[3,136,512]{2,1,0:T(8,128)}, bf16[3,512,128]{2,1,0:T(8,128)(2,1)}) custom-call(s32[12,5]{1,0:T(8,128)} %bitcast.10, s32[1]{0:T(128)} %bitcast.4.core_ref, bf16[192,512]{1,0:T(8,128)(2,1)} %get-tuple-element.40.qa_ref, bf16[192,512]{1,0:T(8,128)(2,1)} %copy-done.19, bf16[8192,128]{1,0:T(8,128)(2,1)} %k_ref.9, bf16[8192,128]{1,0:T(8,128)(2,1)} %v_ref.9), custom_call_target="tpu_custom_call" | custom-call | flops 503316480 | bytes 2555904 | tf_op jit(solution)/shard_map/pallas_call | solution.py:187
  54.5 0.0 collective-permute-done.2.qb_ref
  54.5 0.7 copy-done.18
  55.2 5.4 %shard_map.68 = (f32[3,136,512]{2,1,0:T(8,128)}, bf16[3,512,128]{2,1,0:T(8,128)(2,1)}) custom-call(s32[12,5]{1,0:T(8,128)} %bitcast.11, s32[1]{0:T(128)} %bitcast.4.core_ref, bf16[192,512]{1,0:T(8,128)(2,1)} %copy-done.17, bf16[192,512]{1,0:T(8,128)(2,1)} %copy-done.18, bf16[8192,128]{1,0:T(8,128)(2,1)} %k_ref.9, bf16[8192,128]{1,0:T(8,128)(2,1)} %v_ref.9), custom_call_target="tpu_custom_call" | custom-call | flops 503316480 | bytes 2555904 | tf_op jit(solution)/shard_map/pallas_call | solution.py:187
  60.6 0.0 collective-permute-done.4.qb_ref
  60.6 0.7 copy-done.15
  61.3 0.7 copy-done.16
  62.0 5.4 %shard_map.69 = (f32[3,136,512]{2,1,0:T(8,128)}, bf16[3,512,128]{2,1,0:T(8,128)(2,1)}) custom-call(s32[12,5]{1,0:T(8,128)} %bitcast.12, s32[1]{0:T(128)} %bitcast.4.core_ref, bf16[192,512]{1,0:T(8,128)(2,1)} %copy-done.15, bf16[192,512]{1,0:T(8,128)(2,1)} %copy-done.16, bf16[8192,128]{1,0:T(8,128)(2,1)} %k_ref.9, bf16[8192,128]{1,0:T(8,128)(2,1)} %v_ref.9), custom_call_target="tpu_custom_call" | custom-call | flops 503316480 | bytes 2555904 | tf_op jit(solution)/shard_map/pallas_call | solution.py:187
  67.4 0.7 copy-done.20
  68.1 0.7 copy-done.21
  68.8 5.4 %shard_map.70 = (f32[3,136,512]{2,1,0:T(8,128)}, bf16[3,512,128]{2,1,0:T(8,128)(2,1)}) custom-call(s32[12,5]{1,0:T(8,128)} %bitcast.13, s32[1]{0:T(128)} %bitcast.4.core_ref, bf16[192,512]{1,0:T(8,128)(2,1)} %copy-done.20, bf16[192,512]{1,0:T(8,128)(2,1)} %copy-done.21, bf16[8192,128]{1,0:T(8,128)(2,1)} %k_ref.9, bf16[8192,128]{1,0:T(8,128)(2,1)} %v_ref.9), custom_call_target="tpu_custom_call" | custom-call | flops 503316480 | bytes 2555904 | tf_op jit(solution)/shard_map/pallas_call | solution.py:187
  74.1 54.5 %all-to-all-done.1 = bf16[32,2,2,128,128]{4,3,2,1,0:T(8,128)(2,1)} async-done(((bf16[32,2,2,128,128]{4,3,2,1,0:T(8,128)(2,1)}), bf16[32,2,2,128,128]{4,3,2,1,0:T(8,128)(2,1)}, u32[]{:S(2)}, u32[]{:S(2)}) %all-to-all-start.1) | async-done | bytes 4194336 | tf_op jit(solution)/shard_map/all_to_all | solution.py:299
  128.7 3.1 %shard_map.71 = bf16[2,192,512]{2,1,0:T(8,128)(2,1)S(1)} custom-call(s32[12,3]{1,0:T(8,128)S(1)} %slice.19.slots_ref, s32[1]{0:T(128)} %bitcast.4.core_ref, bf16[64,2,128,128]{3,2,1,0:T(8,128)(2,1)} %bitcast.2.got_ref, f32[3,136,512]{2,1,0:T(8,128)S(1)} %copy-done.7, bf16[3,512,128]{2,1,0:T(8,128)(2,1)S(1)} %copy-done.10), custom_call_target="tpu_custom_call" | custom-call | flops 1 | bytes 1 | tf_op jit(solution)/shard_map/pallas_call | solution.py:250
  131.8 3.2 %collective-permute-start.11 = (bf16[2,192,512]{2,1,0:T(8,128)(2,1)S(1)}, bf16[2,192,512]{2,1,0:T(8,128)(2,1)S(1)}, u32[]{:S(2)}, u32[]{:S(2)}) collective-permute-start(bf16[2,192,512]{2,1,0:T(8,128)(2,1)S(1)} %shard_map.71), channel_id=1, source_target_pairs={{0,4},{1,5},{2,6},{3,7},{4,0},{5,1},{6,2},{7,3},{8,12},{9,13},{10,... | collective-permute-start | bytes 1179656 | tf_op jit(solution)/shard_map/ppermute | solution.py:333
  135.0 4.2 %shard_map.72 = (bf16[2,192,512]{2,1,0:T(8,128)(2,1)S(1)}, bf16[2,192,512]{2,1,0:T(8,128)(2,1)S(1)}) custom-call(s32[12,3]{1,0:T(8,128)S(1)} %slice.19.slots_ref, s32[1]{0:T(128)} %bitcast.4.core_ref, bf16[64,2,128,128]{3,2,1,0:T(8,128)(2,1)} %bitcast.2.got_ref, f32[3,136,512]{2,1,0:T(8,128)S(1)} %copy-done.6, bf16[3,512,128]{2,1,0:T(8,128)(2,1)S(1)} %copy-done.11, ...), custom_call_target="tpu_custom_call" | custom-call | flops 1 | bytes 1 | tf_op jit(solution)/shard_map/pallas_call | solution.py:250
  139.2 0.8 collective-permute-start.7
  140.0 0.7 collective-permute-start.9
  140.7 1.9 %collective-permute-done.11.refs_2_ = bf16[2,192,512]{2,1,0:T(8,128)(2,1)S(1)} collective-permute-done((bf16[2,192,512]{2,1,0:T(8,128)(2,1)S(1)}, bf16[2,192,512]{2,1,0:T(8,128)(2,1)S(1)}, u32[]{:S(2)}, u32[]{:S(2)}) %collective-permute-start.11) | collective-permute-done | bytes 393248 | tf_op jit(solution)/shard_map/ppermute | solution.py:333
  142.6 3.1 %shard_map.73.refs_0_ = bf16[2,192,512]{2,1,0:T(8,128)(2,1)S(1)} custom-call(s32[12,3]{1,0:T(8,128)S(1)} %slice.19.slots_ref, s32[1]{0:T(128)} %bitcast.4.core_ref, bf16[64,2,128,128]{3,2,1,0:T(8,128)(2,1)} %bitcast.2.got_ref, f32[3,136,512]{2,1,0:T(8,128)S(1)} %copy-done.5, bf16[3,512,128]{2,1,0:T(8,128)(2,1)S(1)} %copy-done.9), custom_call_target="tpu_custom_call" | custom-call | flops 1 | bytes 1 | tf_op jit(solution)/shard_map/pallas_call | solution.py:250
  145.7 4.5 %collective-permute-start.12 = (bf16[2,192,512]{2,1,0:T(8,128)(2,1)S(1)}, bf16[2,192,512]{2,1,0:T(8,128)(2,1)S(1)}, u32[]{:S(2)}, u32[]{:S(2)}) collective-permute-start(bf16[2,192,512]{2,1,0:T(8,128)(2,1)S(1)} %shard_map.73.refs_0_), channel_id=1, source_target_pairs={{0,1},{1,0},{2,3},{3,2},{4,5},{5,4},{6,7},{7,6},{8,9},{9,8},{10,11... | collective-permute-start | bytes 1179656 | tf_op jit(solution)/shard_map/ppermute | solution.py:336
  150.1 0.1 collective-permute-start.13
  150.2 1.6 %collective-permute-done.7.refs_0_ = bf16[2,192,512]{2,1,0:T(8,128)(2,1)S(1)} collective-permute-done((bf16[2,192,512]{2,1,0:T(8,128)(2,1)S(1)}, bf16[2,192,512]{2,1,0:T(8,128)(2,1)S(1)}, u32[]{:S(2)}, u32[]{:S(2)}) %collective-permute-start.7) | collective-permute-done | bytes 393248 | tf_op jit(solution)/shard_map/ppermute | solution.py:333
  151.9 1.9 %collective-permute-start.8 = (bf16[2,192,512]{2,1,0:T(8,128)(2,1)S(1)}, bf16[2,192,512]{2,1,0:T(8,128)(2,1)S(1)}, u32[]{:S(2)}, u32[]{:S(2)}) collective-permute-start(bf16[2,192,512]{2,1,0:T(8,128)(2,1)S(1)} %collective-permute-done.7.refs_0_), channel_id=1, source_target_pairs={{0,1},{1,0},{2,3},{3,2},{4,5},{5,4},{6,7},{7,6},{8,9},{9,8},{10,11... | collective-permute-start | bytes 1179656 | tf_op jit(solution)/shard_map/ppermute | solution.py:336
  153.8 0.3 collective-permute-start.10
  154.1 1.5 shard_map.74.refs_4_
  155.6 0.1 collective-permute-done.10.refs_3_
  155.8 1.5 shard_map.75
  (57 shorter events, 0.2 us)
Async XLA Ops:
  1.9 20.4 %all-to-all-start = ((s32[32,1,2]{2,1,0:T(1,128)}), s32[32,1,2]{2,1,0:T(1,128)S(1)}, u32[]{:S(2)}, u32[]{:S(2)}) async-start(s32[32,1,2]{2,1,0:T(1,128)} %fusion.1), calls=%async_computation | async-start | bytes 32768 | tf_op jit(solution)/shard_map/all_to_all | solution.py:296
  13.8 1.6 %copy-start = (bf16[8192,128]{1,0:T(8,128)(2,1)S(1)}, bf16[8192,128]{1,0:T(8,128)(2,1)}, u32[]{:S(2)}) copy-start(bf16[8192,128]{1,0:T(8,128)(2,1)} %k_ref.9) | copy-start | bytes 6291460
  15.4 7.0 %copy-start.1 = (bf16[8192,128]{1,0:T(8,128)(2,1)S(1)}, bf16[8192,128]{1,0:T(8,128)(2,1)}, u32[]{:S(2)}) copy-start(bf16[8192,128]{1,0:T(8,128)(2,1)} %v_ref.9) | copy-start | bytes 6291460
  15.5 1.4 copy-start.3
  22.4 1.6 %copy-start.4 = (bf16[8192,128]{1,0:T(8,128)(2,1)S(1)}, bf16[8192,128]{1,0:T(8,128)(2,1)}, u32[]{:S(2)}) copy-start(bf16[8192,128]{1,0:T(8,128)(2,1)} %copy-done.3) | copy-start | bytes 6291460
  25.0 2.0 %copy-start.2 = (bf16[64,2,128,128]{3,2,1,0:T(8,128)(2,1)}, bf16[64,2,128,128]{3,2,1,0:T(8,128)(2,1)S(1)}, u32[]{:S(2)}) copy-start(bf16[64,2,128,128]{3,2,1,0:T(8,128)(2,1)S(1)} %shard_map.65) | copy-start | bytes 12582916
  27.1 5.0 %copy-start.23 = (s32[8]{0:T(128)S(1)}, s32[8]{0:T(128)}, u32[]{:S(2)}) copy-start(s32[8]{0:T(128)} %constant.114.clone) | copy-start | bytes 100
  27.1 5.0 %copy-start.24 = (s32[8]{0:T(128)S(1)}, s32[8]{0:T(128)}, u32[]{:S(2)}) copy-start(s32[8]{0:T(128)} %constant.115.clone) | copy-start | bytes 100
  27.1 17.0 %copy-start.22 = (s32[12,8]{0,1:T(8,128)S(1)}, s32[12,8]{0,1:T(8,128)}, u32[]{:S(2)}) copy-start(s32[12,8]{0,1:T(8,128)} %param.9) | copy-start | bytes 1156
  27.1 101.5 %all-to-all-start.1 = ((bf16[32,2,2,128,128]{4,3,2,1,0:T(8,128)(2,1)}), bf16[32,2,2,128,128]{4,3,2,1,0:T(8,128)(2,1)}, u32[]{:S(2)}, u32[]{:S(2)}) async-start(bf16[32,2,2,128,128]{4,3,2,1,0:T(8,128)(2,1)} %bitcast.9), calls=%async_computation.1 | async-start | bytes 8388608 | tf_op jit(solution)/shard_map/all_to_all | solution.py:299
  35.6 9.5 %collective-permute-start = (bf16[192,512]{1,0:T(8,128)(2,1)}, bf16[192,512]{1,0:T(8,128)(2,1)S(1)}, u32[]{:S(2)}, u32[]{:S(2)}) collective-permute-start(bf16[192,512]{1,0:T(8,128)(2,1)} %get-tuple-element.41), channel_id=1, source_target_pairs={{0,1},{1,0},{2,3},{3,2},{4,5},{5,4},{6,7},{7,6},{8,9},{9,8},{10,11... | collective-permute-start | bytes 589832 | tf_op jit(solution)/shard_map/ppermute | solution.py:310
  37.8 8.8 %collective-permute-start.1 = (bf16[192,512]{1,0:T(8,128)(2,1)}, bf16[192,512]{1,0:T(8,128)(2,1)S(1)}, u32[]{:S(2)}, u32[]{:S(2)}) collective-permute-start(bf16[192,512]{1,0:T(8,128)(2,1)} %get-tuple-element.44), channel_id=1, source_target_pairs={{0,2},{1,3},{2,4},{3,5},{4,6},{5,7},{6,0},{7,1},{8,10},{9,11},{10,... | collective-permute-start | bytes 589832 | tf_op jit(solution)/shard_map/ppermute | solution.py:310
  39.1 15.4 %collective-permute-start.2 = (bf16[192,512]{1,0:T(8,128)(2,1)}, bf16[192,512]{1,0:T(8,128)(2,1)S(1)}, u32[]{:S(2)}, u32[]{:S(2)}) collective-permute-start(bf16[192,512]{1,0:T(8,128)(2,1)} %get-tuple-element.45), channel_id=1, source_target_pairs={{0,3},{1,2},{2,5},{3,4},{4,7},{5,6},{6,1},{7,0},{8,11},{9,10},{10,... | collective-permute-start | bytes 589832 | tf_op jit(solution)/shard_map/ppermute | solution.py:310
  40.7 19.9 %collective-permute-start.3 = (bf16[192,512]{1,0:T(8,128)(2,1)}, bf16[192,512]{1,0:T(8,128)(2,1)S(1)}, u32[]{:S(2)}, u32[]{:S(2)}) collective-permute-start(bf16[192,512]{1,0:T(8,128)(2,1)} %get-tuple-element.48), channel_id=1, source_target_pairs={{0,4},{1,5},{2,6},{3,7},{4,0},{5,1},{6,2},{7,3},{8,12},{9,13},{10,... | collective-permute-start | bytes 589832 | tf_op jit(solution)/shard_map/ppermute | solution.py:310
  41.9 18.7 %collective-permute-start.4 = (bf16[192,512]{1,0:T(8,128)(2,1)}, bf16[192,512]{1,0:T(8,128)(2,1)S(1)}, u32[]{:S(2)}, u32[]{:S(2)}) collective-permute-start(bf16[192,512]{1,0:T(8,128)(2,1)} %get-tuple-element.49), channel_id=1, source_target_pairs={{0,5},{1,4},{2,7},{3,6},{4,1},{5,0},{6,3},{7,2},{8,13},{9,12},{10,... | collective-permute-start | bytes 589832 | tf_op jit(solution)/shard_map/ppermute | solution.py:310
  45.2 3.4 %copy-start.19 = (bf16[192,512]{1,0:T(8,128)(2,1)}, bf16[192,512]{1,0:T(8,128)(2,1)S(1)}, u32[]{:S(2)}) copy-start(bf16[192,512]{1,0:T(8,128)(2,1)S(1)} %collective-permute-done.qb_ref) | copy-start | bytes 589828
  45.2 22.2 %collective-permute-start.5 = (bf16[192,512]{1,0:T(8,128)(2,1)}, bf16[192,512]{1,0:T(8,128)(2,1)S(1)}, u32[]{:S(2)}, u32[]{:S(2)}) collective-permute-start(bf16[192,512]{1,0:T(8,128)(2,1)} %get-tuple-element.52), channel_id=1, source_target_pairs={{0,6},{1,7},{2,0},{3,1},{4,2},{5,3},{6,4},{7,5},{8,14},{9,15},{10,... | collective-permute-start | bytes 589832 | tf_op jit(solution)/shard_map/ppermute | solution.py:310
  46.6 7.9 %copy-start.17 = (bf16[192,512]{1,0:T(8,128)(2,1)}, bf16[192,512]{1,0:T(8,128)(2,1)S(1)}, u32[]{:S(2)}) copy-start(bf16[192,512]{1,0:T(8,128)(2,1)S(1)} %collective-permute-done.1.qa_ref) | copy-start | bytes 589828
  46.6 20.8 %collective-permute-start.6 = (bf16[192,512]{1,0:T(8,128)(2,1)}, bf16[192,512]{1,0:T(8,128)(2,1)S(1)}, u32[]{:S(2)}, u32[]{:S(2)}) collective-permute-start(bf16[192,512]{1,0:T(8,128)(2,1)} %get-tuple-element.53), channel_id=1, source_target_pairs={{0,7},{1,6},{2,1},{3,0},{4,3},{5,2},{6,5},{7,4},{8,15},{9,14},{10,... | collective-permute-start | bytes 589832 | tf_op jit(solution)/shard_map/ppermute | solution.py:310
  48.5 0.6 copy-start.14
  54.5 0.7 copy-start.18
  60.6 0.7 copy-start.15
  61.3 0.7 copy-start.16
  67.4 61.2 %copy-start.7 = (f32[3,136,512]{2,1,0:T(8,128)S(1)}, f32[3,136,512]{2,1,0:T(8,128)}, u32[]{:S(2)}) copy-start(f32[3,136,512]{2,1,0:T(8,128)} %get-tuple-element.58.refs_0_) | copy-start | bytes 2506756
  67.4 61.2 %copy-start.10 = (bf16[3,512,128]{2,1,0:T(8,128)(2,1)S(1)}, bf16[3,512,128]{2,1,0:T(8,128)(2,1)}, u32[]{:S(2)}) copy-start(bf16[3,512,128]{2,1,0:T(8,128)(2,1)} %get-tuple-element.59.refs_1_) | copy-start | bytes 1179652
  67.4 0.7 copy-start.20
  68.1 0.7 copy-start.21
  128.6 6.3 %copy-start.6 = (f32[3,136,512]{2,1,0:T(8,128)S(1)}, f32[3,136,512]{2,1,0:T(8,128)}, u32[]{:S(2)}) copy-start(f32[3,136,512]{2,1,0:T(8,128)} %get-tuple-element.61.refs_0_) | copy-start | bytes 2506756
  128.6 6.3 %copy-start.8 = (f32[3,136,512]{2,1,0:T(8,128)S(1)}, f32[3,136,512]{2,1,0:T(8,128)}, u32[]{:S(2)}) copy-start(f32[3,136,512]{2,1,0:T(8,128)} %get-tuple-element.63.refs_2_) | copy-start | bytes 2506756
  128.6 6.3 %copy-start.11 = (bf16[3,512,128]{2,1,0:T(8,128)(2,1)S(1)}, bf16[3,512,128]{2,1,0:T(8,128)(2,1)}, u32[]{:S(2)}) copy-start(bf16[3,512,128]{2,1,0:T(8,128)(2,1)} %get-tuple-element.62.refs_1_) | copy-start | bytes 1179652
  128.6 6.3 %copy-start.12 = (bf16[3,512,128]{2,1,0:T(8,128)(2,1)S(1)}, bf16[3,512,128]{2,1,0:T(8,128)(2,1)}, u32[]{:S(2)}) copy-start(bf16[3,512,128]{2,1,0:T(8,128)(2,1)} %get-tuple-element.64.refs_3_) | copy-start | bytes 1179652
  131.7 10.8 %copy-start.5 = (f32[3,136,512]{2,1,0:T(8,128)S(1)}, f32[3,136,512]{2,1,0:T(8,128)}, u32[]{:S(2)}) copy-start(f32[3,136,512]{2,1,0:T(8,128)} %get-tuple-element.72.refs_0_) | copy-start | bytes 2506756
  131.8 10.8 %copy-start.9 = (bf16[3,512,128]{2,1,0:T(8,128)(2,1)S(1)}, bf16[3,512,128]{2,1,0:T(8,128)(2,1)}, u32[]{:S(2)}) copy-start(bf16[3,512,128]{2,1,0:T(8,128)(2,1)} %get-tuple-element.73.refs_1_) | copy-start | bytes 1179652
  131.8 10.8 %collective-permute-start.11 = (bf16[2,192,512]{2,1,0:T(8,128)(2,1)S(1)}, bf16[2,192,512]{2,1,0:T(8,128)(2,1)S(1)}, u32[]{:S(2)}, u32[]{:S(2)}) collective-permute-start(bf16[2,192,512]{2,1,0:T(8,128)(2,1)S(1)} %shard_map.71), channel_id=1, source_target_pairs={{0,4},{1,5},{2,6},{3,7},{4,0},{5,1},{6,2},{7,3},{8,12},{9,13},{10,... | collective-permute-start | bytes 1179656 | tf_op jit(solution)/shard_map/ppermute | solution.py:333
  139.2 14.9 %copy-start.13 = (s32[8]{0:T(128)S(1)}, s32[8]{0:T(128)}, u32[]{:S(2)}) copy-start(s32[8]{0:T(128)} %fusion.7.places_ref) | copy-start | bytes 100
  139.2 12.7 %collective-permute-start.7 = (bf16[2,192,512]{2,1,0:T(8,128)(2,1)S(1)}, bf16[2,192,512]{2,1,0:T(8,128)(2,1)S(1)}, u32[]{:S(2)}, u32[]{:S(2)}) collective-permute-start(bf16[2,192,512]{2,1,0:T(8,128)(2,1)S(1)} %get-tuple-element.67), channel_id=1, source_target_pairs={{0,6},{1,7},{2,0},{3,1},{4,2},{5,3},{6,4},{7,5},{8,14},{9,15},{10,... | collective-permute-start | bytes 1179656 | tf_op jit(solution)/shard_map/ppermute | solution.py:333
  140.0 13.8 %collective-permute-start.9 = (bf16[2,192,512]{2,1,0:T(8,128)(2,1)S(1)}, bf16[2,192,512]{2,1,0:T(8,128)(2,1)S(1)}, u32[]{:S(2)}, u32[]{:S(2)}) collective-permute-start(bf16[2,192,512]{2,1,0:T(8,128)(2,1)S(1)} %get-tuple-element.68), channel_id=1, source_target_pairs={{0,2},{1,3},{2,4},{3,5},{4,6},{5,7},{6,0},{7,1},{8,10},{9,11},{10,... | collective-permute-start | bytes 1179656 | tf_op jit(solution)/shard_map/ppermute | solution.py:333
  145.7 8.4 %collective-permute-start.12 = (bf16[2,192,512]{2,1,0:T(8,128)(2,1)S(1)}, bf16[2,192,512]{2,1,0:T(8,128)(2,1)S(1)}, u32[]{:S(2)}, u32[]{:S(2)}) collective-permute-start(bf16[2,192,512]{2,1,0:T(8,128)(2,1)S(1)} %shard_map.73.refs_0_), channel_id=1, source_target_pairs={{0,1},{1,0},{2,3},{3,2},{4,5},{5,4},{6,7},{7,6},{8,9},{9,8},{10,11... | collective-permute-start | bytes 1179656 | tf_op jit(solution)/shard_map/ppermute | solution.py:336
  150.1 4.0 %collective-permute-start.13 = (bf16[2,192,512]{2,1,0:T(8,128)(2,1)S(1)}, bf16[2,192,512]{2,1,0:T(8,128)(2,1)S(1)}, u32[]{:S(2)}, u32[]{:S(2)}) collective-permute-start(bf16[2,192,512]{2,1,0:T(8,128)(2,1)S(1)} %collective-permute-done.11.refs_2_), channel_id=1, source_target_pairs={{0,1},{1,0},{2,3},{3,2},{4,5},{5,4},{6,7},{7,6},{8,9},{9,8},{10,11... | collective-permute-start | bytes 1179656 | tf_op jit(solution)/shard_map/ppermute | solution.py:336
  151.9 3.7 %collective-permute-start.8 = (bf16[2,192,512]{2,1,0:T(8,128)(2,1)S(1)}, bf16[2,192,512]{2,1,0:T(8,128)(2,1)S(1)}, u32[]{:S(2)}, u32[]{:S(2)}) collective-permute-start(bf16[2,192,512]{2,1,0:T(8,128)(2,1)S(1)} %collective-permute-done.7.refs_0_), channel_id=1, source_target_pairs={{0,1},{1,0},{2,3},{3,2},{4,5},{5,4},{6,7},{7,6},{8,9},{9,8},{10,11... | collective-permute-start | bytes 1179656 | tf_op jit(solution)/shard_map/ppermute | solution.py:336
  153.8 1.9 %collective-permute-start.10 = (bf16[2,192,512]{2,1,0:T(8,128)(2,1)S(1)}, bf16[2,192,512]{2,1,0:T(8,128)(2,1)S(1)}, u32[]{:S(2)}, u32[]{:S(2)}) collective-permute-start(bf16[2,192,512]{2,1,0:T(8,128)(2,1)S(1)} %collective-permute-done.9.refs_2_), channel_id=1, source_target_pairs={{0,1},{1,0},{2,3},{3,2},{4,5},{5,4},{6,7},{7,6},{8,9},{9,8},{10,11... | collective-permute-start | bytes 1179656 | tf_op jit(solution)/shard_map/ppermute | solution.py:336

commit v9 on v8

--- a/solution.py
+++ b/solution.py
@@ -283,16 +283,16 @@
     capacity = max(2, (far_count * q_count + seq_count - 2) // (seq_count - 1))
     slot_total = seq_count * capacity
 
-    far_ids = block_ids[:, NEAR:].reshape(-1)
+    far_ids = block_ids.T[NEAR:]
     far_owner = far_ids // k_count
     far_within = far_ids - far_owner * k_count
-    entry = jnp.arange(far_ids.shape[0], dtype=jnp.int32)
-    earlier = (far_owner[:, None] == far_owner[None, :]) & (entry[None, :] < entry[:, None])
-    far_slot = far_owner * capacity + jnp.sum(earlier.astype(jnp.int32), axis=1)
+    entry = lax.broadcasted_iota(jnp.int32, far_ids.shape, 1) * far_count + lax.broadcasted_iota(jnp.int32, far_ids.shape, 0)
+    earlier = (far_owner[:, :, None, None] == far_owner[None, None]) & (entry[None, None] < entry[:, :, None, None])
+    far_slot = far_owner * capacity + jnp.sum(earlier.astype(jnp.int32), axis=(2, 3))
     slot_range = jnp.arange(slot_total, dtype=jnp.int32)
     unasked = slot_range % k_count
-    placed = far_slot[:, None] == slot_range[None, :]
-    asked = unasked + jnp.sum(jnp.where(placed, far_within[:, None] - unasked[None, :], 0), axis=0)
+    placed = far_slot[:, :, None] == slot_range
+    asked = unasked + jnp.sum(jnp.where(placed, far_within[:, :, None] - unasked, 0), axis=(0, 1))
     wanted = lax.all_to_all(asked.reshape(seq_count, 1, capacity), "seq", split_axis=0, concat_axis=0, tiled=True)
 
     sent = pack(wanted, hold(cache_keys), cache_values)
@@ -310,7 +310,7 @@
         rows_of[d, e] = piece if d == e == 0 else lax.ppermute(piece, "head", offset_pairs(chips, d, e))
 
     order = (chip - jnp.arange(chips, dtype=jnp.int32)) % chips
-    own_ids = jnp.concatenate([block_ids[:, :NEAR] - seq_place * k_count, far_slot.reshape(q_count, far_count)], axis=1)
+    own_ids = jnp.concatenate([block_ids[:, :NEAR] - seq_place * k_count, far_slot.T], axis=1)
     own_ids = jnp.take(own_ids.reshape(chips, per_chip, -1), order, axis=0).reshape(q_count, -1)
     near_ids, slots = own_ids[:, :NEAR], own_ids[:, NEAR:]
     core_operand = core.astype(jnp.int32).reshape(1)

time: 158 us -> 158 us (level)
    unnamed x51 -> x50, local copies, waits for them, and re-layouts: 10.6 us -> 10.5 us
where the time goes in v9:
time: 158 us; the launch traced here: 157 us
  waiting for transfers between devices  63.6 us (40%)
  starting transfers between devices  40.3 us (26%)
  Pallas kernels  39.1 us (25%)
  local copies, waits for them, and re-layouts  11.5 us (7%)
  other arithmetic  2.31 us (1%)
    all_to_all x1, waiting for transfers between devices, shards(): lax.all_to_all(sent.reshape(seq_count, capacity, 2, BLK, HD), 'seq', spli...  54.5 us
    pallas_call x4, Pallas kernels, near_attention(): pl.pallas_call(functools.partial(near_kernel, first), out_shape=[jax.Shap...  21.5 us
    ppermute x7, starting transfers between devices, shards(): lax.ppermute(piece, 'head', offset_pairs(chips, d, e))  11.9 us
    all_to_all x1, starting transfers between devices, shards(): lax.all_to_all(asked.reshape(seq_count, 1, capacity), 'seq', split_axis=0...  11.9 us
    unnamed x50, local copies, waits for them, and re-layouts  10.5 us
    pallas_call x3, Pallas kernels, far_attention(): pl.pallas_call(functools.partial(far_kernel, firsts), out_shape=[jax.Shap...  10.4 us
    ppermute x4, starting transfers between devices, shards(): lax.ppermute(results[d], 'head', offset_pairs(chips, 0, 1))  6.78 us
    all_to_all x1, waiting for transfers between devices, shards(): lax.all_to_all(asked.reshape(seq_count, 1, capacity), 'seq', split_axis=0...  5.45 us
  transfers between devices with their start and end apart: 16, of which 5 were waited for; matrix products, arithmetic and copies ran while one was open for 1% of the time, Pallas kernels for 21%

profile of v9, /device:TPU:1, one launch (start us, length us, event | category | flops | bytes accessed | tf_op | source)
XLA Modules:
  0.0 157.2 jit_solution(8893564694087879203)
XLA Ops:
  0.0 0.7 multiply_subtract_fusion
  0.7 0.2 convert_reduce_fusion
  0.9 0.1 select_reduce_fusion
  1.0 0.1 reduce_sum.22
  1.1 0.6 fusion
  1.8 11.9 %all-to-all-start = ((s32[32,1,2]{2,1,0:T(1,128)}), s32[32,1,2]{2,1,0:T(1,128)S(1)}, u32[]{:S(2)}, u32[]{:S(2)}) async-start(s32[32,1,2]{2,1,0:T(1,128)} %fusion), calls=%async_computation | async-start | bytes 32768 | tf_op jit(solution)/shard_map/all_to_all | solution.py:296
  13.6 0.0 copy-start
  13.7 1.6 %copy-done = bf16[8192,128]{1,0:T(8,128)(2,1)S(1)} copy-done((bf16[8192,128]{1,0:T(8,128)(2,1)S(1)}, bf16[8192,128]{1,0:T(8,128)(2,1)}, u32[]{:S(2)}) %copy-start) | copy-done | bytes 2097176
  15.2 0.1 shard_map.64.k_ref
  15.4 1.3 copy-done.3
  16.8 5.4 %all-to-all-done.wanted_ref = s32[32,1,2]{2,1,0:T(1,128)S(1)} async-done(((s32[32,1,2]{2,1,0:T(1,128)}), s32[32,1,2]{2,1,0:T(1,128)S(1)}, u32[]{:S(2)}, u32[]{:S(2)}) %all-to-all-start) | async-done | bytes 288 | tf_op jit(solution)/shard_map/all_to_all | solution.py:296
  22.2 1.6 %copy-done.4 = bf16[8192,128]{1,0:T(8,128)(2,1)S(1)} copy-done((bf16[8192,128]{1,0:T(8,128)(2,1)S(1)}, bf16[8192,128]{1,0:T(8,128)(2,1)}, u32[]{:S(2)}) %copy-start.4) | copy-done | bytes 2097176
  23.8 1.1 shard_map.65
  24.9 2.0 %copy-done.2 = bf16[64,2,128,128]{3,2,1,0:T(8,128)(2,1)} copy-done((bf16[64,2,128,128]{3,2,1,0:T(8,128)(2,1)}, bf16[64,2,128,128]{3,2,1,0:T(8,128)(2,1)S(1)}, u32[]{:S(2)}) %copy-start.2) | copy-done | bytes 4194328
  26.9 5.0 %all-to-all-start.1 = ((bf16[32,2,2,128,128]{4,3,2,1,0:T(8,128)(2,1)}), bf16[32,2,2,128,128]{4,3,2,1,0:T(8,128)(2,1)}, u32[]{:S(2)}, u32[]{:S(2)}) async-start(bf16[32,2,2,128,128]{4,3,2,1,0:T(8,128)(2,1)} %bitcast.9), calls=%async_computation.1 | async-start | bytes 8388608 | tf_op jit(solution)/shard_map/all_to_all | solution.py:299
  32.0 0.5 fusion.4.places_ref
  32.5 3.0 %shard_map.66 = (bf16[192,512]{1,0:T(8,128)(2,1)}, bf16[192,512]{1,0:T(8,128)(2,1)}, bf16[192,512]{1,0:T(8,128)(2,1)}, bf16[192,512]{1,0:T(8,128)(2,1)}, bf16[19...) custom-call(s32[8]{0:T(128)} %fusion.4.places_ref, ...), custom_call_target="tpu_custom_call" | custom-call | bytes 3145728 | tf_op jit(solution)/shard_map/pallas_call | solution.py:54
  35.5 2.2 %collective-permute-start = (bf16[192,512]{1,0:T(8,128)(2,1)}, bf16[192,512]{1,0:T(8,128)(2,1)S(1)}, u32[]{:S(2)}, u32[]{:S(2)}) collective-permute-start(bf16[192,512]{1,0:T(8,128)(2,1)} %get-tuple-element.41), channel_id=1, source_target_pairs={{0,1},{1,0},{2,3},{3,2},{4,5},{5,4},{6,7},{7,6},{8,9},{9,8},{10,11... | collective-permute-start | bytes 589832 | tf_op jit(solution)/shard_map/ppermute | solution.py:310
  37.7 1.3 collective-permute-start.1
  39.0 1.5 collective-permute-start.2
  40.5 1.3 collective-permute-start.3
  41.8 2.0 %collective-permute-start.4 = (bf16[192,512]{1,0:T(8,128)(2,1)}, bf16[192,512]{1,0:T(8,128)(2,1)S(1)}, u32[]{:S(2)}, u32[]{:S(2)}) collective-permute-start(bf16[192,512]{1,0:T(8,128)(2,1)} %get-tuple-element.49), channel_id=1, source_target_pairs={{0,5},{1,4},{2,7},{3,6},{4,1},{5,0},{6,3},{7,2},{8,13},{9,12},{10,... | collective-permute-start | bytes 589832 | tf_op jit(solution)/shard_map/ppermute | solution.py:310
  43.8 0.1 copy.13
  44.0 0.6 gather_fusion
  44.6 0.1 broadcast_in_dim.27
  44.6 0.1 broadcast_in_dim.28
  44.7 0.0 collective-permute-done.qb_ref
  44.7 1.5 collective-permute-start.5
  46.2 0.0 collective-permute-done.1.qa_ref
  46.2 2.1 %collective-permute-start.6 = (bf16[192,512]{1,0:T(8,128)(2,1)}, bf16[192,512]{1,0:T(8,128)(2,1)S(1)}, u32[]{:S(2)}, u32[]{:S(2)}) collective-permute-start(bf16[192,512]{1,0:T(8,128)(2,1)} %get-tuple-element.53), channel_id=1, source_target_pairs={{0,7},{1,6},{2,1},{3,0},{4,3},{5,2},{6,5},{7,4},{8,15},{9,14},{10,... | collective-permute-start | bytes 589832 | tf_op jit(solution)/shard_map/ppermute | solution.py:310
  48.3 0.1 broadcast_select_fusion
  48.4 0.1 slice.19.slots_ref
  48.5 0.5 copy-done.14
  49.0 5.4 %shard_map.67 = (f32[3,136,512]{2,1,0:T(8,128)}, bf16[3,512,128]{2,1,0:T(8,128)(2,1)}) custom-call(s32[12,5]{1,0:T(8,128)} %bitcast.10, s32[1]{0:T(128)} %bitcast.6.core_ref, bf16[192,512]{1,0:T(8,128)(2,1)} %get-tuple-element.40.qa_ref, bf16[192,512]{1,0:T(8,128)(2,1)} %copy-done.19, bf16[8192,128]{1,0:T(8,128)(2,1)} %k_ref.9, bf16[8192,128]{1,0:T(8,128)(2,1)} %v_ref.9), custom_call_target="tpu_custom_call" | custom-call | flops 503316480 | bytes 2555904 | tf_op jit(solution)/shard_map/pallas_call | solution.py:187
  54.4 0.0 collective-permute-done.2.qb_ref
  54.4 0.7 copy-done.18
  55.1 5.4 %shard_map.68 = (f32[3,136,512]{2,1,0:T(8,128)}, bf16[3,512,128]{2,1,0:T(8,128)(2,1)}) custom-call(s32[12,5]{1,0:T(8,128)} %bitcast.11, s32[1]{0:T(128)} %bitcast.6.core_ref, bf16[192,512]{1,0:T(8,128)(2,1)} %copy-done.17, bf16[192,512]{1,0:T(8,128)(2,1)} %copy-done.18, bf16[8192,128]{1,0:T(8,128)(2,1)} %k_ref.9, bf16[8192,128]{1,0:T(8,128)(2,1)} %v_ref.9), custom_call_target="tpu_custom_call" | custom-call | flops 503316480 | bytes 2555904 | tf_op jit(solution)/shard_map/pallas_call | solution.py:187
  60.4 0.0 collective-permute-done.3.qa_ref
  60.5 0.7 copy-done.15
  61.1 0.7 copy-done.16
  61.8 5.4 %shard_map.69 = (f32[3,136,512]{2,1,0:T(8,128)}, bf16[3,512,128]{2,1,0:T(8,128)(2,1)}) custom-call(s32[12,5]{1,0:T(8,128)} %bitcast.12, s32[1]{0:T(128)} %bitcast.6.core_ref, bf16[192,512]{1,0:T(8,128)(2,1)} %copy-done.15, bf16[192,512]{1,0:T(8,128)(2,1)} %copy-done.16, bf16[8192,128]{1,0:T(8,128)(2,1)} %k_ref.9, bf16[8192,128]{1,0:T(8,128)(2,1)} %v_ref.9), custom_call_target="tpu_custom_call" | custom-call | flops 503316480 | bytes 2555904 | tf_op jit(solution)/shard_map/pallas_call | solution.py:187
  67.2 0.0 collective-permute-done.5.qa_ref
  67.3 0.7 copy-done.20
  67.9 0.7 copy-done.21
  68.6 5.4 %shard_map.70 = (f32[3,136,512]{2,1,0:T(8,128)}, bf16[3,512,128]{2,1,0:T(8,128)(2,1)}) custom-call(s32[12,5]{1,0:T(8,128)} %bitcast.13, s32[1]{0:T(128)} %bitcast.6.core_ref, bf16[192,512]{1,0:T(8,128)(2,1)} %copy-done.20, bf16[192,512]{1,0:T(8,128)(2,1)} %copy-done.21, bf16[8192,128]{1,0:T(8,128)(2,1)} %k_ref.9, bf16[8192,128]{1,0:T(8,128)(2,1)} %v_ref.9), custom_call_target="tpu_custom_call" | custom-call | flops 503316480 | bytes 2555904 | tf_op jit(solution)/shard_map/pallas_call | solution.py:187
  74.0 54.5 %all-to-all-done.1 = bf16[32,2,2,128,128]{4,3,2,1,0:T(8,128)(2,1)} async-done(((bf16[32,2,2,128,128]{4,3,2,1,0:T(8,128)(2,1)}), bf16[32,2,2,128,128]{4,3,2,1,0:T(8,128)(2,1)}, u32[]{:S(2)}, u32[]{:S(2)}) %all-to-all-start.1) | async-done | bytes 4194336 | tf_op jit(solution)/shard_map/all_to_all | solution.py:299
  128.5 3.1 %shard_map.71 = bf16[2,192,512]{2,1,0:T(8,128)(2,1)S(1)} custom-call(s32[12,3]{1,0:T(8,128)S(1)} %slice.19.slots_ref, s32[1]{0:T(128)} %bitcast.6.core_ref, bf16[64,2,128,128]{3,2,1,0:T(8,128)(2,1)} %bitcast.3.got_ref, f32[3,136,512]{2,1,0:T(8,128)S(1)} %copy-done.7, bf16[3,512,128]{2,1,0:T(8,128)(2,1)S(1)} %copy-done.10), custom_call_target="tpu_custom_call" | custom-call | flops 1 | bytes 1 | tf_op jit(solution)/shard_map/pallas_call | solution.py:250
  131.6 3.2 %collective-permute-start.11 = (bf16[2,192,512]{2,1,0:T(8,128)(2,1)S(1)}, bf16[2,192,512]{2,1,0:T(8,128)(2,1)S(1)}, u32[]{:S(2)}, u32[]{:S(2)}) collective-permute-start(bf16[2,192,512]{2,1,0:T(8,128)(2,1)S(1)} %shard_map.71), channel_id=1, source_target_pairs={{0,4},{1,5},{2,6},{3,7},{4,0},{5,1},{6,2},{7,3},{8,12},{9,13},{10,... | collective-permute-start | bytes 1179656 | tf_op jit(solution)/shard_map/ppermute | solution.py:333
  134.8 4.2 %shard_map.72 = (bf16[2,192,512]{2,1,0:T(8,128)(2,1)S(1)}, bf16[2,192,512]{2,1,0:T(8,128)(2,1)S(1)}) custom-call(s32[12,3]{1,0:T(8,128)S(1)} %slice.19.slots_ref, s32[1]{0:T(128)} %bitcast.6.core_ref, bf16[64,2,128,128]{3,2,1,0:T(8,128)(2,1)} %bitcast.3.got_ref, f32[3,136,512]{2,1,0:T(8,128)S(1)} %copy-done.6, bf16[3,512,128]{2,1,0:T(8,128)(2,1)S(1)} %copy-done.11, ...), custom_call_target="tpu_custom_call" | custom-call | flops 1 | bytes 1 | tf_op jit(solution)/shard_map/pallas_call | solution.py:250
  139.0 0.8 collective-permute-start.7
  139.9 0.7 collective-permute-start.9
  140.6 1.9 %collective-permute-done.11.refs_2_ = bf16[2,192,512]{2,1,0:T(8,128)(2,1)S(1)} collective-permute-done((bf16[2,192,512]{2,1,0:T(8,128)(2,1)S(1)}, bf16[2,192,512]{2,1,0:T(8,128)(2,1)S(1)}, u32[]{:S(2)}, u32[]{:S(2)}) %collective-permute-start.11) | collective-permute-done | bytes 393248 | tf_op jit(solution)/shard_map/ppermute | solution.py:333
  142.4 3.1 %shard_map.73.refs_0_ = bf16[2,192,512]{2,1,0:T(8,128)(2,1)S(1)} custom-call(s32[12,3]{1,0:T(8,128)S(1)} %slice.19.slots_ref, s32[1]{0:T(128)} %bitcast.6.core_ref, bf16[64,2,128,128]{3,2,1,0:T(8,128)(2,1)} %bitcast.3.got_ref, f32[3,136,512]{2,1,0:T(8,128)S(1)} %copy-done.5, bf16[3,512,128]{2,1,0:T(8,128)(2,1)S(1)} %copy-done.9), custom_call_target="tpu_custom_call" | custom-call | flops 1 | bytes 1 | tf_op jit(solution)/shard_map/pallas_call | solution.py:250
  145.5 4.5 %collective-permute-start.12 = (bf16[2,192,512]{2,1,0:T(8,128)(2,1)S(1)}, bf16[2,192,512]{2,1,0:T(8,128)(2,1)S(1)}, u32[]{:S(2)}, u32[]{:S(2)}) collective-permute-start(bf16[2,192,512]{2,1,0:T(8,128)(2,1)S(1)} %shard_map.73.refs_0_), channel_id=1, source_target_pairs={{0,1},{1,0},{2,3},{3,2},{4,5},{5,4},{6,7},{7,6},{8,9},{9,8},{10,11... | collective-permute-start | bytes 1179656 | tf_op jit(solution)/shard_map/ppermute | solution.py:336
  150.0 0.1 collective-permute-start.13
  150.1 1.6 %collective-permute-done.7.refs_0_ = bf16[2,192,512]{2,1,0:T(8,128)(2,1)S(1)} collective-permute-done((bf16[2,192,512]{2,1,0:T(8,128)(2,1)S(1)}, bf16[2,192,512]{2,1,0:T(8,128)(2,1)S(1)}, u32[]{:S(2)}, u32[]{:S(2)}) %collective-permute-start.7) | collective-permute-done | bytes 393248 | tf_op jit(solution)/shard_map/ppermute | solution.py:333
  151.7 1.9 %collective-permute-start.8 = (bf16[2,192,512]{2,1,0:T(8,128)(2,1)S(1)}, bf16[2,192,512]{2,1,0:T(8,128)(2,1)S(1)}, u32[]{:S(2)}, u32[]{:S(2)}) collective-permute-start(bf16[2,192,512]{2,1,0:T(8,128)(2,1)S(1)} %collective-permute-done.7.refs_0_), channel_id=1, source_target_pairs={{0,1},{1,0},{2,3},{3,2},{4,5},{5,4},{6,7},{7,6},{8,9},{9,8},{10,11... | collective-permute-start | bytes 1179656 | tf_op jit(solution)/shard_map/ppermute | solution.py:336
  153.7 0.0 collective-permute-done.9.refs_2_
  153.7 0.3 collective-permute-start.10
  153.9 0.0 collective-permute-done.12.refs_1_
  154.0 0.0 collective-permute-done.13.refs_3_
  154.0 1.5 shard_map.74.refs_4_
  155.5 0.1 collective-permute-done.10.refs_3_
  155.6 1.5 shard_map.75
  (52 shorter events, 0.2 us)
Async XLA Ops:
  1.8 20.4 %all-to-all-start = ((s32[32,1,2]{2,1,0:T(1,128)}), s32[32,1,2]{2,1,0:T(1,128)S(1)}, u32[]{:S(2)}, u32[]{:S(2)}) async-start(s32[32,1,2]{2,1,0:T(1,128)} %fusion), calls=%async_computation | async-start | bytes 32768 | tf_op jit(solution)/shard_map/all_to_all | solution.py:296
  13.6 1.6 %copy-start = (bf16[8192,128]{1,0:T(8,128)(2,1)S(1)}, bf16[8192,128]{1,0:T(8,128)(2,1)}, u32[]{:S(2)}) copy-start(bf16[8192,128]{1,0:T(8,128)(2,1)} %k_ref.9) | copy-start | bytes 6291460
  15.2 7.0 %copy-start.1 = (bf16[8192,128]{1,0:T(8,128)(2,1)S(1)}, bf16[8192,128]{1,0:T(8,128)(2,1)}, u32[]{:S(2)}) copy-start(bf16[8192,128]{1,0:T(8,128)(2,1)} %v_ref.9) | copy-start | bytes 6291460
  15.4 1.4 copy-start.3
  22.2 1.6 %copy-start.4 = (bf16[8192,128]{1,0:T(8,128)(2,1)S(1)}, bf16[8192,128]{1,0:T(8,128)(2,1)}, u32[]{:S(2)}) copy-start(bf16[8192,128]{1,0:T(8,128)(2,1)} %copy-done.3) | copy-start | bytes 6291460
  24.9 2.0 %copy-start.2 = (bf16[64,2,128,128]{3,2,1,0:T(8,128)(2,1)}, bf16[64,2,128,128]{3,2,1,0:T(8,128)(2,1)S(1)}, u32[]{:S(2)}) copy-start(bf16[64,2,128,128]{3,2,1,0:T(8,128)(2,1)S(1)} %shard_map.65) | copy-start | bytes 12582916
  26.9 5.0 %copy-start.23 = (s32[8]{0:T(128)S(1)}, s32[8]{0:T(128)}, u32[]{:S(2)}) copy-start(s32[8]{0:T(128)} %constant.115.clone) | copy-start | bytes 100
  26.9 5.0 %copy-start.24 = (s32[8]{0:T(128)S(1)}, s32[8]{0:T(128)}, u32[]{:S(2)}) copy-start(s32[8]{0:T(128)} %constant.116.clone) | copy-start | bytes 100
  26.9 16.9 %copy-start.22 = (s32[12,8]{0,1:T(8,128)S(1)}, s32[12,8]{0,1:T(8,128)}, u32[]{:S(2)}) copy-start(s32[12,8]{0,1:T(8,128)} %param.9) | copy-start | bytes 1156
  26.9 101.5 %all-to-all-start.1 = ((bf16[32,2,2,128,128]{4,3,2,1,0:T(8,128)(2,1)}), bf16[32,2,2,128,128]{4,3,2,1,0:T(8,128)(2,1)}, u32[]{:S(2)}, u32[]{:S(2)}) async-start(bf16[32,2,2,128,128]{4,3,2,1,0:T(8,128)(2,1)} %bitcast.9), calls=%async_computation.1 | async-start | bytes 8388608 | tf_op jit(solution)/shard_map/all_to_all | solution.py:299
  35.5 9.3 %collective-permute-start = (bf16[192,512]{1,0:T(8,128)(2,1)}, bf16[192,512]{1,0:T(8,128)(2,1)S(1)}, u32[]{:S(2)}, u32[]{:S(2)}) collective-permute-start(bf16[192,512]{1,0:T(8,128)(2,1)} %get-tuple-element.41), channel_id=1, source_target_pairs={{0,1},{1,0},{2,3},{3,2},{4,5},{5,4},{6,7},{7,6},{8,9},{9,8},{10,11... | collective-permute-start | bytes 589832 | tf_op jit(solution)/shard_map/ppermute | solution.py:310
  37.7 8.5 %collective-permute-start.1 = (bf16[192,512]{1,0:T(8,128)(2,1)}, bf16[192,512]{1,0:T(8,128)(2,1)S(1)}, u32[]{:S(2)}, u32[]{:S(2)}) collective-permute-start(bf16[192,512]{1,0:T(8,128)(2,1)} %get-tuple-element.44), channel_id=1, source_target_pairs={{0,2},{1,3},{2,4},{3,5},{4,6},{5,7},{6,0},{7,1},{8,10},{9,11},{10,... | collective-permute-start | bytes 589832 | tf_op jit(solution)/shard_map/ppermute | solution.py:310
  39.0 15.4 %collective-permute-start.2 = (bf16[192,512]{1,0:T(8,128)(2,1)}, bf16[192,512]{1,0:T(8,128)(2,1)S(1)}, u32[]{:S(2)}, u32[]{:S(2)}) collective-permute-start(bf16[192,512]{1,0:T(8,128)(2,1)} %get-tuple-element.45), channel_id=1, source_target_pairs={{0,3},{1,2},{2,5},{3,4},{4,7},{5,6},{6,1},{7,0},{8,11},{9,10},{10,... | collective-permute-start | bytes 589832 | tf_op jit(solution)/shard_map/ppermute | solution.py:310
  40.5 19.9 %collective-permute-start.3 = (bf16[192,512]{1,0:T(8,128)(2,1)}, bf16[192,512]{1,0:T(8,128)(2,1)S(1)}, u32[]{:S(2)}, u32[]{:S(2)}) collective-permute-start(bf16[192,512]{1,0:T(8,128)(2,1)} %get-tuple-element.48), channel_id=1, source_target_pairs={{0,4},{1,5},{2,6},{3,7},{4,0},{5,1},{6,2},{7,3},{8,12},{9,13},{10,... | collective-permute-start | bytes 589832 | tf_op jit(solution)/shard_map/ppermute | solution.py:310
  41.8 18.7 %collective-permute-start.4 = (bf16[192,512]{1,0:T(8,128)(2,1)}, bf16[192,512]{1,0:T(8,128)(2,1)S(1)}, u32[]{:S(2)}, u32[]{:S(2)}) collective-permute-start(bf16[192,512]{1,0:T(8,128)(2,1)} %get-tuple-element.49), channel_id=1, source_target_pairs={{0,5},{1,4},{2,7},{3,6},{4,1},{5,0},{6,3},{7,2},{8,13},{9,12},{10,... | collective-permute-start | bytes 589832 | tf_op jit(solution)/shard_map/ppermute | solution.py:310
  44.7 3.7 %copy-start.19 = (bf16[192,512]{1,0:T(8,128)(2,1)}, bf16[192,512]{1,0:T(8,128)(2,1)S(1)}, u32[]{:S(2)}) copy-start(bf16[192,512]{1,0:T(8,128)(2,1)S(1)} %collective-permute-done.qb_ref) | copy-start | bytes 589828
  44.7 22.5 %collective-permute-start.5 = (bf16[192,512]{1,0:T(8,128)(2,1)}, bf16[192,512]{1,0:T(8,128)(2,1)S(1)}, u32[]{:S(2)}, u32[]{:S(2)}) collective-permute-start(bf16[192,512]{1,0:T(8,128)(2,1)} %get-tuple-element.52), channel_id=1, source_target_pairs={{0,6},{1,7},{2,0},{3,1},{4,2},{5,3},{6,4},{7,5},{8,14},{9,15},{10,... | collective-permute-start | bytes 589832 | tf_op jit(solution)/shard_map/ppermute | solution.py:310
  46.2 8.2 %copy-start.17 = (bf16[192,512]{1,0:T(8,128)(2,1)}, bf16[192,512]{1,0:T(8,128)(2,1)S(1)}, u32[]{:S(2)}) copy-start(bf16[192,512]{1,0:T(8,128)(2,1)S(1)} %collective-permute-done.1.qa_ref) | copy-start | bytes 589828
  46.2 21.1 %collective-permute-start.6 = (bf16[192,512]{1,0:T(8,128)(2,1)}, bf16[192,512]{1,0:T(8,128)(2,1)S(1)}, u32[]{:S(2)}, u32[]{:S(2)}) collective-permute-start(bf16[192,512]{1,0:T(8,128)(2,1)} %get-tuple-element.53), channel_id=1, source_target_pairs={{0,7},{1,6},{2,1},{3,0},{4,3},{5,2},{6,5},{7,4},{8,15},{9,14},{10,... | collective-permute-start | bytes 589832 | tf_op jit(solution)/shard_map/ppermute | solution.py:310
  48.4 0.6 copy-start.14
  54.4 0.7 copy-start.18
  60.5 0.7 copy-start.15
  61.1 0.7 copy-start.16
  67.2 61.2 %copy-start.7 = (f32[3,136,512]{2,1,0:T(8,128)S(1)}, f32[3,136,512]{2,1,0:T(8,128)}, u32[]{:S(2)}) copy-start(f32[3,136,512]{2,1,0:T(8,128)} %get-tuple-element.58.refs_0_) | copy-start | bytes 2506756
  67.2 61.2 %copy-start.10 = (bf16[3,512,128]{2,1,0:T(8,128)(2,1)S(1)}, bf16[3,512,128]{2,1,0:T(8,128)(2,1)}, u32[]{:S(2)}) copy-start(bf16[3,512,128]{2,1,0:T(8,128)(2,1)} %get-tuple-element.59.refs_1_) | copy-start | bytes 1179652
  67.3 0.7 copy-start.20
  67.9 0.7 copy-start.21
  128.5 6.3 %copy-start.6 = (f32[3,136,512]{2,1,0:T(8,128)S(1)}, f32[3,136,512]{2,1,0:T(8,128)}, u32[]{:S(2)}) copy-start(f32[3,136,512]{2,1,0:T(8,128)} %get-tuple-element.61.refs_0_) | copy-start | bytes 2506756
  128.5 6.3 %copy-start.8 = (f32[3,136,512]{2,1,0:T(8,128)S(1)}, f32[3,136,512]{2,1,0:T(8,128)}, u32[]{:S(2)}) copy-start(f32[3,136,512]{2,1,0:T(8,128)} %get-tuple-element.63.refs_2_) | copy-start | bytes 2506756
  128.5 6.3 %copy-start.11 = (bf16[3,512,128]{2,1,0:T(8,128)(2,1)S(1)}, bf16[3,512,128]{2,1,0:T(8,128)(2,1)}, u32[]{:S(2)}) copy-start(bf16[3,512,128]{2,1,0:T(8,128)(2,1)} %get-tuple-element.62.refs_1_) | copy-start | bytes 1179652
  128.5 6.3 %copy-start.12 = (bf16[3,512,128]{2,1,0:T(8,128)(2,1)S(1)}, bf16[3,512,128]{2,1,0:T(8,128)(2,1)}, u32[]{:S(2)}) copy-start(bf16[3,512,128]{2,1,0:T(8,128)(2,1)} %get-tuple-element.64.refs_3_) | copy-start | bytes 1179652
  131.6 10.8 %copy-start.5 = (f32[3,136,512]{2,1,0:T(8,128)S(1)}, f32[3,136,512]{2,1,0:T(8,128)}, u32[]{:S(2)}) copy-start(f32[3,136,512]{2,1,0:T(8,128)} %get-tuple-element.72.refs_0_) | copy-start | bytes 2506756
  131.6 10.8 %copy-start.9 = (bf16[3,512,128]{2,1,0:T(8,128)(2,1)S(1)}, bf16[3,512,128]{2,1,0:T(8,128)(2,1)}, u32[]{:S(2)}) copy-start(bf16[3,512,128]{2,1,0:T(8,128)(2,1)} %get-tuple-element.73.refs_1_) | copy-start | bytes 1179652
  131.6 10.8 %collective-permute-start.11 = (bf16[2,192,512]{2,1,0:T(8,128)(2,1)S(1)}, bf16[2,192,512]{2,1,0:T(8,128)(2,1)S(1)}, u32[]{:S(2)}, u32[]{:S(2)}) collective-permute-start(bf16[2,192,512]{2,1,0:T(8,128)(2,1)S(1)} %shard_map.71), channel_id=1, source_target_pairs={{0,4},{1,5},{2,6},{3,7},{4,0},{5,1},{6,2},{7,3},{8,12},{9,13},{10,... | collective-permute-start | bytes 1179656 | tf_op jit(solution)/shard_map/ppermute | solution.py:333
  139.0 14.9 %copy-start.13 = (s32[8]{0:T(128)S(1)}, s32[8]{0:T(128)}, u32[]{:S(2)}) copy-start(s32[8]{0:T(128)} %fusion.4.places_ref) | copy-start | bytes 100
  139.0 12.7 %collective-permute-start.7 = (bf16[2,192,512]{2,1,0:T(8,128)(2,1)S(1)}, bf16[2,192,512]{2,1,0:T(8,128)(2,1)S(1)}, u32[]{:S(2)}, u32[]{:S(2)}) collective-permute-start(bf16[2,192,512]{2,1,0:T(8,128)(2,1)S(1)} %get-tuple-element.67), channel_id=1, source_target_pairs={{0,6},{1,7},{2,0},{3,1},{4,2},{5,3},{6,4},{7,5},{8,14},{9,15},{10,... | collective-permute-start | bytes 1179656 | tf_op jit(solution)/shard_map/ppermute | solution.py:333
  139.9 13.8 %collective-permute-start.9 = (bf16[2,192,512]{2,1,0:T(8,128)(2,1)S(1)}, bf16[2,192,512]{2,1,0:T(8,128)(2,1)S(1)}, u32[]{:S(2)}, u32[]{:S(2)}) collective-permute-start(bf16[2,192,512]{2,1,0:T(8,128)(2,1)S(1)} %get-tuple-element.68), channel_id=1, source_target_pairs={{0,2},{1,3},{2,4},{3,5},{4,6},{5,7},{6,0},{7,1},{8,10},{9,11},{10,... | collective-permute-start | bytes 1179656 | tf_op jit(solution)/shard_map/ppermute | solution.py:333
  145.5 8.4 %collective-permute-start.12 = (bf16[2,192,512]{2,1,0:T(8,128)(2,1)S(1)}, bf16[2,192,512]{2,1,0:T(8,128)(2,1)S(1)}, u32[]{:S(2)}, u32[]{:S(2)}) collective-permute-start(bf16[2,192,512]{2,1,0:T(8,128)(2,1)S(1)} %shard_map.73.refs_0_), channel_id=1, source_target_pairs={{0,1},{1,0},{2,3},{3,2},{4,5},{5,4},{6,7},{7,6},{8,9},{9,8},{10,11... | collective-permute-start | bytes 1179656 | tf_op jit(solution)/shard_map/ppermute | solution.py:336
  150.0 4.0 %collective-permute-start.13 = (bf16[2,192,512]{2,1,0:T(8,128)(2,1)S(1)}, bf16[2,192,512]{2,1,0:T(8,128)(2,1)S(1)}, u32[]{:S(2)}, u32[]{:S(2)}) collective-permute-start(bf16[2,192,512]{2,1,0:T(8,128)(2,1)S(1)} %collective-permute-done.11.refs_2_), channel_id=1, source_target_pairs={{0,1},{1,0},{2,3},{3,2},{4,5},{5,4},{6,7},{7,6},{8,9},{9,8},{10,11... | collective-permute-start | bytes 1179656 | tf_op jit(solution)/shard_map/ppermute | solution.py:336
  151.7 3.7 %collective-permute-start.8 = (bf16[2,192,512]{2,1,0:T(8,128)(2,1)S(1)}, bf16[2,192,512]{2,1,0:T(8,128)(2,1)S(1)}, u32[]{:S(2)}, u32[]{:S(2)}) collective-permute-start(bf16[2,192,512]{2,1,0:T(8,128)(2,1)S(1)} %collective-permute-done.7.refs_0_), channel_id=1, source_target_pairs={{0,1},{1,0},{2,3},{3,2},{4,5},{5,4},{6,7},{7,6},{8,9},{9,8},{10,11... | collective-permute-start | bytes 1179656 | tf_op jit(solution)/shard_map/ppermute | solution.py:336
  153.7 1.9 %collective-permute-start.10 = (bf16[2,192,512]{2,1,0:T(8,128)(2,1)S(1)}, bf16[2,192,512]{2,1,0:T(8,128)(2,1)S(1)}, u32[]{:S(2)}, u32[]{:S(2)}) collective-permute-start(bf16[2,192,512]{2,1,0:T(8,128)(2,1)S(1)} %collective-permute-done.9.refs_2_), channel_id=1, source_target_pairs={{0,1},{1,0},{2,3},{3,2},{4,5},{5,4},{6,7},{7,6},{8,9},{9,8},{10,11... | collective-permute-start | bytes 1179656 | tf_op jit(solution)/shard_map/ppermute | solution.py:336

commit v10 on v7

--- a/solution.py
+++ b/solution.py
@@ -284,16 +284,16 @@
     capacity = max(2, (far_count * q_count + seq_count - 2) // (seq_count - 1))
     slot_total = seq_count * capacity
 
-    far_ids = block_ids[:, NEAR:].reshape(-1)
+    far_ids = block_ids.T[NEAR:]
     far_owner = far_ids // k_count
     far_within = far_ids - far_owner * k_count
-    entry = jnp.arange(far_ids.shape[0], dtype=jnp.int32)
-    earlier = (far_owner[:, None] == far_owner[None, :]) & (entry[None, :] < entry[:, None])
-    far_slot = far_owner * capacity + jnp.sum(earlier.astype(jnp.int32), axis=1)
+    entry = lax.broadcasted_iota(jnp.int32, far_ids.shape, 1) * far_count + lax.broadcasted_iota(jnp.int32, far_ids.shape, 0)
+    earlier = (far_owner[:, :, None, None] == far_owner[None, None]) & (entry[None, None] < entry[:, :, None, None])
+    far_slot = far_owner * capacity + jnp.sum(earlier.astype(jnp.int32), axis=(2, 3))
     slot_range = jnp.arange(slot_total, dtype=jnp.int32)
     unasked = slot_range % k_count
-    placed = far_slot[:, None] == slot_range[None, :]
-    asked = unasked + jnp.sum(jnp.where(placed, far_within[:, None] - unasked[None, :], 0), axis=0)
+    placed = far_slot[:, :, None] == slot_range
+    asked = unasked + jnp.sum(jnp.where(placed, far_within[:, :, None] - unasked, 0), axis=(0, 1))
     wanted = lax.all_to_all(asked.reshape(seq_count, 1, capacity), "seq", split_axis=0, concat_axis=0, tiled=True)
 
     sent = pack(wanted, cache_keys, cache_values)
@@ -311,7 +311,7 @@
         rows_of[d, e] = piece if d == e == 0 else lax.ppermute(piece, "head", offset_pairs(chips, d, e))
 
     order = (chip - jnp.arange(chips, dtype=jnp.int32)) % chips
-    own_ids = jnp.concatenate([block_ids[:, :NEAR] - seq_place * k_count, far_slot.reshape(q_count, far_count)], axis=1)
+    own_ids = jnp.concatenate([block_ids[:, :NEAR] - seq_place * k_count, far_slot.T], axis=1)
     own_ids = jnp.take(own_ids.reshape(chips, per_chip, -1), order, axis=0).reshape(q_count, -1)
     near_ids, slots = own_ids[:, :NEAR], own_ids[:, NEAR:]
     core_operand = core.astype(jnp.int32).reshape(1)

time: 159 us -> 159 us (level)
    unnamed x41 -> x40, local copies, waits for them, and re-layouts: 4.06 us -> 3.96 us
where the time goes in v10:
time: 159 us; the launch traced here: 158 us
  waiting for transfers between devices  58.4 us (37%)
  Pallas kernels  43.8 us (28%)
  starting transfers between devices  28.2 us (18%)
  blocking collectives  20.4 us (13%)
  local copies, waits for them, and re-layouts  4.98 us (3%)
  other arithmetic  1.71 us (1%)
    all_to_all x1, waiting for transfers between devices, shards(): lax.all_to_all(sent.reshape(seq_count, capacity, 2, BLK, HD), 'seq', spli...  54.7 us
    pallas_call x4, Pallas kernels, near_attention(): pl.pallas_call(functools.partial(near_kernel, first), out_shape=[jax.Shap...  21.5 us
    all_to_all x1, blocking collectives, shards(): lax.all_to_all(asked.reshape(seq_count, 1, capacity), 'seq', split_axis=0...  20.4 us
    ppermute x7, starting transfers between devices, shards(): lax.ppermute(piece, 'head', offset_pairs(chips, d, e))  11.7 us
    pallas_call x3, Pallas kernels, far_attention(): pl.pallas_call(functools.partial(far_kernel, firsts), out_shape=[jax.Shap...  10.4 us
    ppermute x4, starting transfers between devices, shards(): lax.ppermute(results[d], 'head', offset_pairs(chips, 0, 1))  6.76 us
    pallas_call x1, Pallas kernels, pack(): pl.pallas_call(functools.partial(pack_kernel, chunks, unroll), out_shape=...  5.93 us
    all_to_all x1, starting transfers between devices, shards(): lax.all_to_all(sent.reshape(seq_count, capacity, 2, BLK, HD), 'seq', spli...  5 us
  transfers between devices with their start and end apart: 15, of which 4 were waited for; matrix products, arithmetic and copies ran while one was open for 1% of the time, Pallas kernels for 21%

profile of v10, /device:TPU:1, one launch (start us, length us, event | category | flops | bytes accessed | tf_op | source)
XLA Modules:
  0.0 158.0 jit_solution(8646999221051769365)
XLA Ops:
  0.0 0.7 multiply_subtract_fusion
  0.7 0.2 convert_reduce_fusion
  0.9 0.1 select_reduce_fusion
  1.0 0.1 reduce_sum.22
  1.2 20.4 %all_to_all.10.wanted_ref = s32[32,1,2]{2,1,0:T(1,128)} all-to-all(s32[32,1,2]{2,1,0:T(1,128)S(1)} %fusion), channel_id=1, replica_groups=mesh['seq'=32,'head'=8] {'seq'}, dimensions={0} | all-to-all | bytes 512 | tf_op jit(solution)/shard_map/all_to_all | solution.py:297
  21.6 5.9 %shard_map.64 = bf16[64,2,128,128]{3,2,1,0:T(8,128)(2,1)} custom-call(s32[32,1,2]{2,1,0:T(1,128)} %all_to_all.10.wanted_ref, bf16[8192,128]{1,0:T(8,128)(2,1)} %k_ref.9, bf16[8192,128]{1,0:T(8,128)(2,1)} %v_ref.9), custom_call_target="tpu_custom_call" | custom-call | bytes 8388608 | tf_op jit(solution)/shard_map/pallas_call | solution.py:123
  27.5 0.0 copy-start.18
  27.5 0.0 copy-start.19
  27.6 0.0 copy-start.17
  27.6 5.0 %all-to-all-start.1 = ((bf16[32,2,2,128,128]{4,3,2,1,0:T(8,128)(2,1)}), bf16[32,2,2,128,128]{4,3,2,1,0:T(8,128)(2,1)}, u32[]{:S(2)}, u32[]{:S(2)}) async-start(bf16[32,2,2,128,128]{4,3,2,1,0:T(8,128)(2,1)} %bitcast.9), calls=%async_computation.1 | async-start | bytes 8388608 | tf_op jit(solution)/shard_map/all_to_all | solution.py:300
  32.6 0.5 fusion.4.places_ref
  33.1 3.0 %shard_map.65 = (bf16[192,512]{1,0:T(8,128)(2,1)}, bf16[192,512]{1,0:T(8,128)(2,1)}, bf16[192,512]{1,0:T(8,128)(2,1)}, bf16[192,512]{1,0:T(8,128)(2,1)}, bf16[19...) custom-call(s32[8]{0:T(128)} %fusion.4.places_ref, ...), custom_call_target="tpu_custom_call" | custom-call | bytes 3145728 | tf_op jit(solution)/shard_map/pallas_call | solution.py:54
  36.1 2.0 %collective-permute-start = (bf16[192,512]{1,0:T(8,128)(2,1)}, bf16[192,512]{1,0:T(8,128)(2,1)S(1)}, u32[]{:S(2)}, u32[]{:S(2)}) collective-permute-start(bf16[192,512]{1,0:T(8,128)(2,1)} %get-tuple-element.41), channel_id=1, source_target_pairs={{0,1},{1,0},{2,3},{3,2},{4,5},{5,4},{6,7},{7,6},{8,9},{9,8},{10,11... | collective-permute-start | bytes 589832 | tf_op jit(solution)/shard_map/ppermute | solution.py:311
  38.2 1.3 collective-permute-start.1
  39.5 1.5 collective-permute-start.2
  41.0 1.3 collective-permute-start.3
  42.3 2.0 %collective-permute-start.4 = (bf16[192,512]{1,0:T(8,128)(2,1)}, bf16[192,512]{1,0:T(8,128)(2,1)S(1)}, u32[]{:S(2)}, u32[]{:S(2)}) collective-permute-start(bf16[192,512]{1,0:T(8,128)(2,1)} %get-tuple-element.49), channel_id=1, source_target_pairs={{0,5},{1,4},{2,7},{3,6},{4,1},{5,0},{6,3},{7,2},{8,13},{9,12},{10,... | collective-permute-start | bytes 589832 | tf_op jit(solution)/shard_map/ppermute | solution.py:311
  44.3 0.0 copy-done.17
  44.3 0.1 copy.13
  44.4 0.6 gather_fusion
  45.0 0.1 broadcast_in_dim.27
  45.1 0.1 broadcast_in_dim.28
  45.2 0.0 collective-permute-done.qb_ref
  45.2 1.5 collective-permute-start.5
  46.7 0.0 collective-permute-done.1.qa_ref
  46.7 2.1 %collective-permute-start.6 = (bf16[192,512]{1,0:T(8,128)(2,1)}, bf16[192,512]{1,0:T(8,128)(2,1)S(1)}, u32[]{:S(2)}, u32[]{:S(2)}) collective-permute-start(bf16[192,512]{1,0:T(8,128)(2,1)} %get-tuple-element.53), channel_id=1, source_target_pairs={{0,7},{1,6},{2,1},{3,0},{4,3},{5,2},{6,5},{7,4},{8,15},{9,14},{10,... | collective-permute-start | bytes 589832 | tf_op jit(solution)/shard_map/ppermute | solution.py:311
  48.8 0.1 broadcast_select_fusion
  48.9 0.1 slice.19.slots_ref
  48.9 0.5 copy-done.9
  49.5 5.4 %shard_map.66 = (f32[3,136,512]{2,1,0:T(8,128)}, bf16[3,512,128]{2,1,0:T(8,128)(2,1)}) custom-call(s32[12,5]{1,0:T(8,128)} %bitcast.10, s32[1]{0:T(128)} %bitcast.6.core_ref, bf16[192,512]{1,0:T(8,128)(2,1)} %get-tuple-element.40.qa_ref, bf16[192,512]{1,0:T(8,128)(2,1)} %copy-done.14, bf16[8192,128]{1,0:T(8,128)(2,1)} %k_ref.9, bf16[8192,128]{1,0:T(8,128)(2,1)} %v_ref.9), custom_call_target="tpu_custom_call" | custom-call | flops 503316480 | bytes 2555904 | tf_op jit(solution)/shard_map/pallas_call | solution.py:188
  54.9 0.0 collective-permute-done.2.qb_ref
  54.9 0.0 copy-done.12
  54.9 0.7 copy-done.13
  55.6 5.4 %shard_map.67 = (f32[3,136,512]{2,1,0:T(8,128)}, bf16[3,512,128]{2,1,0:T(8,128)(2,1)}) custom-call(s32[12,5]{1,0:T(8,128)} %bitcast.11, s32[1]{0:T(128)} %bitcast.6.core_ref, bf16[192,512]{1,0:T(8,128)(2,1)} %copy-done.12, bf16[192,512]{1,0:T(8,128)(2,1)} %copy-done.13, bf16[8192,128]{1,0:T(8,128)(2,1)} %k_ref.9, bf16[8192,128]{1,0:T(8,128)(2,1)} %v_ref.9), custom_call_target="tpu_custom_call" | custom-call | flops 503316480 | bytes 2555904 | tf_op jit(solution)/shard_map/pallas_call | solution.py:188
  61.0 0.0 collective-permute-done.3.qa_ref
  61.0 0.0 collective-permute-done.4.qb_ref
  61.0 0.7 copy-done.10
  61.6 0.7 copy-done.11
  62.3 5.4 %shard_map.68 = (f32[3,136,512]{2,1,0:T(8,128)}, bf16[3,512,128]{2,1,0:T(8,128)(2,1)}) custom-call(s32[12,5]{1,0:T(8,128)} %bitcast.12, s32[1]{0:T(128)} %bitcast.6.core_ref, bf16[192,512]{1,0:T(8,128)(2,1)} %copy-done.10, bf16[192,512]{1,0:T(8,128)(2,1)} %copy-done.11, bf16[8192,128]{1,0:T(8,128)(2,1)} %k_ref.9, bf16[8192,128]{1,0:T(8,128)(2,1)} %v_ref.9), custom_call_target="tpu_custom_call" | custom-call | flops 503316480 | bytes 2555904 | tf_op jit(solution)/shard_map/pallas_call | solution.py:188
  67.7 0.0 collective-permute-done.5.qa_ref
  67.7 0.0 collective-permute-done.6.qb_ref
  67.8 0.7 copy-done.15
  68.4 0.7 copy-done.16
  69.1 5.4 %shard_map.69 = (f32[3,136,512]{2,1,0:T(8,128)}, bf16[3,512,128]{2,1,0:T(8,128)(2,1)}) custom-call(s32[12,5]{1,0:T(8,128)} %bitcast.13, s32[1]{0:T(128)} %bitcast.6.core_ref, bf16[192,512]{1,0:T(8,128)(2,1)} %copy-done.15, bf16[192,512]{1,0:T(8,128)(2,1)} %copy-done.16, bf16[8192,128]{1,0:T(8,128)(2,1)} %k_ref.9, bf16[8192,128]{1,0:T(8,128)(2,1)} %v_ref.9), custom_call_target="tpu_custom_call" | custom-call | flops 503316480 | bytes 2555904 | tf_op jit(solution)/shard_map/pallas_call | solution.py:188
  74.5 54.7 %all-to-all-done.1 = bf16[32,2,2,128,128]{4,3,2,1,0:T(8,128)(2,1)} async-done(((bf16[32,2,2,128,128]{4,3,2,1,0:T(8,128)(2,1)}), bf16[32,2,2,128,128]{4,3,2,1,0:T(8,128)(2,1)}, u32[]{:S(2)}, u32[]{:S(2)}) %all-to-all-start.1) | async-done | bytes 4194336 | tf_op jit(solution)/shard_map/all_to_all | solution.py:300
  129.2 3.1 %shard_map.70 = bf16[2,192,512]{2,1,0:T(8,128)(2,1)S(1)} custom-call(s32[12,3]{1,0:T(8,128)S(1)} %slice.19.slots_ref, s32[1]{0:T(128)} %bitcast.6.core_ref, bf16[64,2,128,128]{3,2,1,0:T(8,128)(2,1)} %bitcast.3.got_ref, f32[3,136,512]{2,1,0:T(8,128)S(1)} %copy-done.2, bf16[3,512,128]{2,1,0:T(8,128)(2,1)S(1)} %copy-done.5), custom_call_target="tpu_custom_call" | custom-call | flops 1 | bytes 1 | tf_op jit(solution)/shard_map/pallas_call | solution.py:251
  132.3 3.2 %collective-permute-start.11 = (bf16[2,192,512]{2,1,0:T(8,128)(2,1)S(1)}, bf16[2,192,512]{2,1,0:T(8,128)(2,1)S(1)}, u32[]{:S(2)}, u32[]{:S(2)}) collective-permute-start(bf16[2,192,512]{2,1,0:T(8,128)(2,1)S(1)} %shard_map.70), channel_id=1, source_target_pairs={{0,4},{1,5},{2,6},{3,7},{4,0},{5,1},{6,2},{7,3},{8,12},{9,13},{10,... | collective-permute-start | bytes 1179656 | tf_op jit(solution)/shard_map/ppermute | solution.py:334
  135.5 4.2 %shard_map.71 = (bf16[2,192,512]{2,1,0:T(8,128)(2,1)S(1)}, bf16[2,192,512]{2,1,0:T(8,128)(2,1)S(1)}) custom-call(s32[12,3]{1,0:T(8,128)S(1)} %slice.19.slots_ref, s32[1]{0:T(128)} %bitcast.6.core_ref, bf16[64,2,128,128]{3,2,1,0:T(8,128)(2,1)} %bitcast.3.got_ref, f32[3,136,512]{2,1,0:T(8,128)S(1)} %copy-done.1, bf16[3,512,128]{2,1,0:T(8,128)(2,1)S(1)} %copy-done.6, ...), custom_call_target="tpu_custom_call" | custom-call | flops 1 | bytes 1 | tf_op jit(solution)/shard_map/pallas_call | solution.py:251
  139.7 0.9 collective-permute-start.7
  140.6 0.7 collective-permute-start.9
  141.3 1.9 %collective-permute-done.11.refs_2_ = bf16[2,192,512]{2,1,0:T(8,128)(2,1)S(1)} collective-permute-done((bf16[2,192,512]{2,1,0:T(8,128)(2,1)S(1)}, bf16[2,192,512]{2,1,0:T(8,128)(2,1)S(1)}, u32[]{:S(2)}, u32[]{:S(2)}) %collective-permute-start.11) | collective-permute-done | bytes 393248 | tf_op jit(solution)/shard_map/ppermute | solution.py:334
  143.2 3.1 %shard_map.72.refs_0_ = bf16[2,192,512]{2,1,0:T(8,128)(2,1)S(1)} custom-call(s32[12,3]{1,0:T(8,128)S(1)} %slice.19.slots_ref, s32[1]{0:T(128)} %bitcast.6.core_ref, bf16[64,2,128,128]{3,2,1,0:T(8,128)(2,1)} %bitcast.3.got_ref, f32[3,136,512]{2,1,0:T(8,128)S(1)} %copy-done, bf16[3,512,128]{2,1,0:T(8,128)(2,1)S(1)} %copy-done.4), custom_call_target="tpu_custom_call" | custom-call | flops 1 | bytes 1 | tf_op jit(solution)/shard_map/pallas_call | solution.py:251
  146.3 4.5 %collective-permute-start.12 = (bf16[2,192,512]{2,1,0:T(8,128)(2,1)S(1)}, bf16[2,192,512]{2,1,0:T(8,128)(2,1)S(1)}, u32[]{:S(2)}, u32[]{:S(2)}) collective-permute-start(bf16[2,192,512]{2,1,0:T(8,128)(2,1)S(1)} %shard_map.72.refs_0_), channel_id=1, source_target_pairs={{0,1},{1,0},{2,3},{3,2},{4,5},{5,4},{6,7},{7,6},{8,9},{9,8},{10,11... | collective-permute-start | bytes 1179656 | tf_op jit(solution)/shard_map/ppermute | solution.py:337
  150.8 0.1 collective-permute-start.13
  150.9 1.6 %collective-permute-done.7.refs_0_ = bf16[2,192,512]{2,1,0:T(8,128)(2,1)S(1)} collective-permute-done((bf16[2,192,512]{2,1,0:T(8,128)(2,1)S(1)}, bf16[2,192,512]{2,1,0:T(8,128)(2,1)S(1)}, u32[]{:S(2)}, u32[]{:S(2)}) %collective-permute-start.7) | collective-permute-done | bytes 393248 | tf_op jit(solution)/shard_map/ppermute | solution.py:334
  152.5 1.9 %collective-permute-start.8 = (bf16[2,192,512]{2,1,0:T(8,128)(2,1)S(1)}, bf16[2,192,512]{2,1,0:T(8,128)(2,1)S(1)}, u32[]{:S(2)}, u32[]{:S(2)}) collective-permute-start(bf16[2,192,512]{2,1,0:T(8,128)(2,1)S(1)} %collective-permute-done.7.refs_0_), channel_id=1, source_target_pairs={{0,1},{1,0},{2,3},{3,2},{4,5},{5,4},{6,7},{7,6},{8,9},{9,8},{10,11... | collective-permute-start | bytes 1179656 | tf_op jit(solution)/shard_map/ppermute | solution.py:337
  154.4 0.0 collective-permute-done.9.refs_2_
  154.4 0.3 collective-permute-start.10
  154.7 0.0 collective-permute-done.12.refs_1_
  154.7 0.0 collective-permute-done.13.refs_3_
  154.7 1.5 shard_map.73.refs_4_
  156.2 0.0 collective-permute-done.8.refs_1_
  156.2 0.1 collective-permute-done.10.refs_3_
  156.3 1.5 shard_map.74
  (40 shorter events, 0.2 us)
Async XLA Ops:
  27.5 5.1 %copy-start.18 = (s32[8]{0:T(128)S(1)}, s32[8]{0:T(128)}, u32[]{:S(2)}) copy-start(s32[8]{0:T(128)} %constant.115.clone) | copy-start | bytes 100
  27.5 5.1 %copy-start.19 = (s32[8]{0:T(128)S(1)}, s32[8]{0:T(128)}, u32[]{:S(2)}) copy-start(s32[8]{0:T(128)} %constant.116.clone) | copy-start | bytes 100
  27.6 16.8 %copy-start.17 = (s32[12,8]{0,1:T(8,128)S(1)}, s32[12,8]{0,1:T(8,128)}, u32[]{:S(2)}) copy-start(s32[12,8]{0,1:T(8,128)} %param.9) | copy-start | bytes 1156
  27.6 101.6 %all-to-all-start.1 = ((bf16[32,2,2,128,128]{4,3,2,1,0:T(8,128)(2,1)}), bf16[32,2,2,128,128]{4,3,2,1,0:T(8,128)(2,1)}, u32[]{:S(2)}, u32[]{:S(2)}) async-start(bf16[32,2,2,128,128]{4,3,2,1,0:T(8,128)(2,1)} %bitcast.9), calls=%async_computation.1 | async-start | bytes 8388608 | tf_op jit(solution)/shard_map/all_to_all | solution.py:300
  36.1 9.1 %collective-permute-start = (bf16[192,512]{1,0:T(8,128)(2,1)}, bf16[192,512]{1,0:T(8,128)(2,1)S(1)}, u32[]{:S(2)}, u32[]{:S(2)}) collective-permute-start(bf16[192,512]{1,0:T(8,128)(2,1)} %get-tuple-element.41), channel_id=1, source_target_pairs={{0,1},{1,0},{2,3},{3,2},{4,5},{5,4},{6,7},{7,6},{8,9},{9,8},{10,11... | collective-permute-start | bytes 589832 | tf_op jit(solution)/shard_map/ppermute | solution.py:311
  38.2 8.5 %collective-permute-start.1 = (bf16[192,512]{1,0:T(8,128)(2,1)}, bf16[192,512]{1,0:T(8,128)(2,1)S(1)}, u32[]{:S(2)}, u32[]{:S(2)}) collective-permute-start(bf16[192,512]{1,0:T(8,128)(2,1)} %get-tuple-element.44), channel_id=1, source_target_pairs={{0,2},{1,3},{2,4},{3,5},{4,6},{5,7},{6,0},{7,1},{8,10},{9,11},{10,... | collective-permute-start | bytes 589832 | tf_op jit(solution)/shard_map/ppermute | solution.py:311
  39.5 15.4 %collective-permute-start.2 = (bf16[192,512]{1,0:T(8,128)(2,1)}, bf16[192,512]{1,0:T(8,128)(2,1)S(1)}, u32[]{:S(2)}, u32[]{:S(2)}) collective-permute-start(bf16[192,512]{1,0:T(8,128)(2,1)} %get-tuple-element.45), channel_id=1, source_target_pairs={{0,3},{1,2},{2,5},{3,4},{4,7},{5,6},{6,1},{7,0},{8,11},{9,10},{10,... | collective-permute-start | bytes 589832 | tf_op jit(solution)/shard_map/ppermute | solution.py:311
  41.0 20.0 %collective-permute-start.3 = (bf16[192,512]{1,0:T(8,128)(2,1)}, bf16[192,512]{1,0:T(8,128)(2,1)S(1)}, u32[]{:S(2)}, u32[]{:S(2)}) collective-permute-start(bf16[192,512]{1,0:T(8,128)(2,1)} %get-tuple-element.48), channel_id=1, source_target_pairs={{0,4},{1,5},{2,6},{3,7},{4,0},{5,1},{6,2},{7,3},{8,12},{9,13},{10,... | collective-permute-start | bytes 589832 | tf_op jit(solution)/shard_map/ppermute | solution.py:311
  42.3 18.7 %collective-permute-start.4 = (bf16[192,512]{1,0:T(8,128)(2,1)}, bf16[192,512]{1,0:T(8,128)(2,1)S(1)}, u32[]{:S(2)}, u32[]{:S(2)}) collective-permute-start(bf16[192,512]{1,0:T(8,128)(2,1)} %get-tuple-element.49), channel_id=1, source_target_pairs={{0,5},{1,4},{2,7},{3,6},{4,1},{5,0},{6,3},{7,2},{8,13},{9,12},{10,... | collective-permute-start | bytes 589832 | tf_op jit(solution)/shard_map/ppermute | solution.py:311
  45.2 3.7 %copy-start.14 = (bf16[192,512]{1,0:T(8,128)(2,1)}, bf16[192,512]{1,0:T(8,128)(2,1)S(1)}, u32[]{:S(2)}) copy-start(bf16[192,512]{1,0:T(8,128)(2,1)S(1)} %collective-permute-done.qb_ref) | copy-start | bytes 589828
  45.2 22.5 %collective-permute-start.5 = (bf16[192,512]{1,0:T(8,128)(2,1)}, bf16[192,512]{1,0:T(8,128)(2,1)S(1)}, u32[]{:S(2)}, u32[]{:S(2)}) collective-permute-start(bf16[192,512]{1,0:T(8,128)(2,1)} %get-tuple-element.52), channel_id=1, source_target_pairs={{0,6},{1,7},{2,0},{3,1},{4,2},{5,3},{6,4},{7,5},{8,14},{9,15},{10,... | collective-permute-start | bytes 589832 | tf_op jit(solution)/shard_map/ppermute | solution.py:311
  46.7 8.2 %copy-start.12 = (bf16[192,512]{1,0:T(8,128)(2,1)}, bf16[192,512]{1,0:T(8,128)(2,1)S(1)}, u32[]{:S(2)}) copy-start(bf16[192,512]{1,0:T(8,128)(2,1)S(1)} %collective-permute-done.1.qa_ref) | copy-start | bytes 589828
  46.7 21.1 %collective-permute-start.6 = (bf16[192,512]{1,0:T(8,128)(2,1)}, bf16[192,512]{1,0:T(8,128)(2,1)S(1)}, u32[]{:S(2)}, u32[]{:S(2)}) collective-permute-start(bf16[192,512]{1,0:T(8,128)(2,1)} %get-tuple-element.53), channel_id=1, source_target_pairs={{0,7},{1,6},{2,1},{3,0},{4,3},{5,2},{6,5},{7,4},{8,15},{9,14},{10,... | collective-permute-start | bytes 589832 | tf_op jit(solution)/shard_map/ppermute | solution.py:311
  48.9 0.6 copy-start.9
  54.9 0.7 copy-start.13
  61.0 0.7 copy-start.10
  61.6 0.7 copy-start.11
  67.7 61.5 %copy-start.2 = (f32[3,136,512]{2,1,0:T(8,128)S(1)}, f32[3,136,512]{2,1,0:T(8,128)}, u32[]{:S(2)}) copy-start(f32[3,136,512]{2,1,0:T(8,128)} %get-tuple-element.58.refs_0_) | copy-start | bytes 2506756
  67.7 61.5 %copy-start.5 = (bf16[3,512,128]{2,1,0:T(8,128)(2,1)S(1)}, bf16[3,512,128]{2,1,0:T(8,128)(2,1)}, u32[]{:S(2)}) copy-start(bf16[3,512,128]{2,1,0:T(8,128)(2,1)} %get-tuple-element.59.refs_1_) | copy-start | bytes 1179652
  67.7 0.7 copy-start.15
  68.4 0.7 copy-start.16
  129.2 6.3 %copy-start.1 = (f32[3,136,512]{2,1,0:T(8,128)S(1)}, f32[3,136,512]{2,1,0:T(8,128)}, u32[]{:S(2)}) copy-start(f32[3,136,512]{2,1,0:T(8,128)} %get-tuple-element.61.refs_0_) | copy-start | bytes 2506756
  129.2 6.3 %copy-start.3 = (f32[3,136,512]{2,1,0:T(8,128)S(1)}, f32[3,136,512]{2,1,0:T(8,128)}, u32[]{:S(2)}) copy-start(f32[3,136,512]{2,1,0:T(8,128)} %get-tuple-element.63.refs_2_) | copy-start | bytes 2506756
  129.2 6.3 %copy-start.6 = (bf16[3,512,128]{2,1,0:T(8,128)(2,1)S(1)}, bf16[3,512,128]{2,1,0:T(8,128)(2,1)}, u32[]{:S(2)}) copy-start(bf16[3,512,128]{2,1,0:T(8,128)(2,1)} %get-tuple-element.62.refs_1_) | copy-start | bytes 1179652
  129.2 6.3 %copy-start.7 = (bf16[3,512,128]{2,1,0:T(8,128)(2,1)S(1)}, bf16[3,512,128]{2,1,0:T(8,128)(2,1)}, u32[]{:S(2)}) copy-start(bf16[3,512,128]{2,1,0:T(8,128)(2,1)} %get-tuple-element.64.refs_3_) | copy-start | bytes 1179652
  132.3 10.9 %copy-start = (f32[3,136,512]{2,1,0:T(8,128)S(1)}, f32[3,136,512]{2,1,0:T(8,128)}, u32[]{:S(2)}) copy-start(f32[3,136,512]{2,1,0:T(8,128)} %get-tuple-element.72.refs_0_) | copy-start | bytes 2506756
  132.3 10.9 %copy-start.4 = (bf16[3,512,128]{2,1,0:T(8,128)(2,1)S(1)}, bf16[3,512,128]{2,1,0:T(8,128)(2,1)}, u32[]{:S(2)}) copy-start(bf16[3,512,128]{2,1,0:T(8,128)(2,1)} %get-tuple-element.73.refs_1_) | copy-start | bytes 1179652
  132.3 10.8 %collective-permute-start.11 = (bf16[2,192,512]{2,1,0:T(8,128)(2,1)S(1)}, bf16[2,192,512]{2,1,0:T(8,128)(2,1)S(1)}, u32[]{:S(2)}, u32[]{:S(2)}) collective-permute-start(bf16[2,192,512]{2,1,0:T(8,128)(2,1)S(1)} %shard_map.70), channel_id=1, source_target_pairs={{0,4},{1,5},{2,6},{3,7},{4,0},{5,1},{6,2},{7,3},{8,12},{9,13},{10,... | collective-permute-start | bytes 1179656 | tf_op jit(solution)/shard_map/ppermute | solution.py:334
  139.7 14.9 %copy-start.8 = (s32[8]{0:T(128)S(1)}, s32[8]{0:T(128)}, u32[]{:S(2)}) copy-start(s32[8]{0:T(128)} %fusion.4.places_ref) | copy-start | bytes 100
  139.7 12.8 %collective-permute-start.7 = (bf16[2,192,512]{2,1,0:T(8,128)(2,1)S(1)}, bf16[2,192,512]{2,1,0:T(8,128)(2,1)S(1)}, u32[]{:S(2)}, u32[]{:S(2)}) collective-permute-start(bf16[2,192,512]{2,1,0:T(8,128)(2,1)S(1)} %get-tuple-element.67), channel_id=1, source_target_pairs={{0,6},{1,7},{2,0},{3,1},{4,2},{5,3},{6,4},{7,5},{8,14},{9,15},{10,... | collective-permute-start | bytes 1179656 | tf_op jit(solution)/shard_map/ppermute | solution.py:334
  140.6 13.8 %collective-permute-start.9 = (bf16[2,192,512]{2,1,0:T(8,128)(2,1)S(1)}, bf16[2,192,512]{2,1,0:T(8,128)(2,1)S(1)}, u32[]{:S(2)}, u32[]{:S(2)}) collective-permute-start(bf16[2,192,512]{2,1,0:T(8,128)(2,1)S(1)} %get-tuple-element.68), channel_id=1, source_target_pairs={{0,2},{1,3},{2,4},{3,5},{4,6},{5,7},{6,0},{7,1},{8,10},{9,11},{10,... | collective-permute-start | bytes 1179656 | tf_op jit(solution)/shard_map/ppermute | solution.py:334
  146.3 8.4 %collective-permute-start.12 = (bf16[2,192,512]{2,1,0:T(8,128)(2,1)S(1)}, bf16[2,192,512]{2,1,0:T(8,128)(2,1)S(1)}, u32[]{:S(2)}, u32[]{:S(2)}) collective-permute-start(bf16[2,192,512]{2,1,0:T(8,128)(2,1)S(1)} %shard_map.72.refs_0_), channel_id=1, source_target_pairs={{0,1},{1,0},{2,3},{3,2},{4,5},{5,4},{6,7},{7,6},{8,9},{9,8},{10,11... | collective-permute-start | bytes 1179656 | tf_op jit(solution)/shard_map/ppermute | solution.py:337
  150.8 3.9 %collective-permute-start.13 = (bf16[2,192,512]{2,1,0:T(8,128)(2,1)S(1)}, bf16[2,192,512]{2,1,0:T(8,128)(2,1)S(1)}, u32[]{:S(2)}, u32[]{:S(2)}) collective-permute-start(bf16[2,192,512]{2,1,0:T(8,128)(2,1)S(1)} %collective-permute-done.11.refs_2_), channel_id=1, source_target_pairs={{0,1},{1,0},{2,3},{3,2},{4,5},{5,4},{6,7},{7,6},{8,9},{9,8},{10,11... | collective-permute-start | bytes 1179656 | tf_op jit(solution)/shard_map/ppermute | solution.py:337
  152.5 3.7 %collective-permute-start.8 = (bf16[2,192,512]{2,1,0:T(8,128)(2,1)S(1)}, bf16[2,192,512]{2,1,0:T(8,128)(2,1)S(1)}, u32[]{:S(2)}, u32[]{:S(2)}) collective-permute-start(bf16[2,192,512]{2,1,0:T(8,128)(2,1)S(1)} %collective-permute-done.7.refs_0_), channel_id=1, source_target_pairs={{0,1},{1,0},{2,3},{3,2},{4,5},{5,4},{6,7},{7,6},{8,9},{9,8},{10,11... | collective-permute-start | bytes 1179656 | tf_op jit(solution)/shard_map/ppermute | solution.py:337
  154.4 1.9 %collective-permute-start.10 = (bf16[2,192,512]{2,1,0:T(8,128)(2,1)S(1)}, bf16[2,192,512]{2,1,0:T(8,128)(2,1)S(1)}, u32[]{:S(2)}, u32[]{:S(2)}) collective-permute-start(bf16[2,192,512]{2,1,0:T(8,128)(2,1)S(1)} %collective-permute-done.9.refs_2_), channel_id=1, source_target_pairs={{0,1},{1,0},{2,3},{3,2},{4,5},{5,4},{6,7},{7,6},{8,9},{9,8},{10,11... | collective-permute-start | bytes 1179656 | tf_op jit(solution)/shard_map/ppermute | solution.py:337
